TPU v7x, 512 devices: a whole 4x4x16 slice. The times are simulated.
512 devices in a mesh: row: 16 (over z), col: 8 (over x_lo, y), depth: 4 (over x_hi, core).
Axes of the slice: x: 4 (x_hi: 2, x_lo: 2; x = x_hi * 2 + x_lo), y: 4, z: 16, core: 2. Of those that a mesh axis runs over, the one named last changes fastest.
Arguments:
- h_blocks: bfloat16 [16, 16, 4, 12, 128, 128], P('row', 'col', 'depth'), may hold values from -0.25 to 0.25
- h_rows: int32 [16, 16, 4, 12], P('row', 'col', 'depth'), may hold values from 0 to 31, as said below
- h_cols: int32 [16, 16, 4, 12], P('row', 'col', 'depth'), may hold values from 0 to 7
- h_flags: int32 [16, 16, 4, 12], P('row', 'col', 'depth'), may hold values from 0 to 1
- x_blocks: bfloat16 [16, 4, 8, 8, 2, 128, 128], P('row', 'depth', 'col'), may hold values from -6 to 6
- x_cols: int32 [16, 4, 8, 8, 2], P('row', 'depth', 'col'), may hold values from 0 to 7, as said below
- x_flags: int32 [16, 4, 8, 8, 2], P('row', 'depth', 'col'), may hold values from 0 to 1
- previous: bfloat16 [16, 4, 8, 8, 2, 128, 128], P('row', 'depth', 'col'), may hold values from -6 to 6
Outputs:
- next_term: bfloat16 [16, 4, 8, 8, 2, 128, 128], P('row', 'depth', 'col')
Inputs may be any that keep to these rules, and one draw needn't show every extreme that they name: The slots of one tile (g, p, e) name distinct positions (h_rows, h_cols); live slots come first; every tile with g = p has all 12 slots live. `x_cols`: the 2 slots of one block row in one column group name distinct columns.
All inputs are finite; a program needn't handle non-finite values.
Results may differ from a plain program's by a relative error of at most 0.0095.
Values may be sent and summed in bfloat16 or wider, within the bound.
No kernel may reach another device: no remote copies, remote signals or barrier semaphores. Data moves between devices by JAX's collectives and lax.ppermute only.
A program may use at most 64 MiB of HBM per device.

v0:
```python
import jax
import jax.numpy as jnp
from jax import lax
from jax.sharding import PartitionSpec as P


def add_piece(summed, ham_part, iter_part, aim_cols, aim_flags):
    blocks, ham_rows, ham_cols, ham_flags = ham_part
    iter_blocks, iter_cols, iter_flags = iter_part
    iter_width = iter_cols.shape[-1]
    picked = jnp.take(iter_blocks, ham_cols, axis=0)
    picked_cols = jnp.take(iter_cols, ham_cols, axis=0)
    picked_flags = jnp.take(iter_flags, ham_cols, axis=0)
    wanted_cols = jnp.take(aim_cols, ham_rows, axis=0)
    wanted_flags = jnp.take(aim_flags, ham_rows, axis=0)
    paired = picked_cols[:, :, None] == wanted_cols[:, None, :]
    paired = paired & (picked_flags[:, :, None] > 0) & (wanted_flags[:, None, :] > 0)
    paired = paired & (ham_flags[:, None, None] > 0)
    chosen = jnp.einsum(
        "awv,awkm->avkm", paired.astype(jnp.bfloat16), picked, preferred_element_type=jnp.float32
    ).astype(jnp.bfloat16)
    products = jnp.einsum("akl,avlm->avkm", blocks, chosen, preferred_element_type=jnp.float32)
    target = ham_rows[:, None] * iter_width + jnp.arange(iter_width, dtype=jnp.int32)[None, :]
    return summed.at[target.reshape(-1)].add(products.reshape((-1,) + products.shape[2:]))


def run_pieces(summed, ham_part, iter_part, aim_cols, aim_flags):

    def one_piece(running, element):
        ham_item, iter_item = element
        running = add_piece(running, ham_item, iter_item, aim_cols, aim_flags)
        return (running, None)

    summed, _ = lax.scan(one_piece, summed, (ham_part, iter_part))
    return summed


def body(h_blocks, h_rows, h_cols, h_flags, x_blocks, x_cols, x_flags, previous):
    aim_cols, aim_flags = (
        lax.all_gather(x_cols, "depth", axis=1, tiled=True),
        lax.all_gather(x_flags, "depth", axis=1, tiled=True),
    )
    iter_width = x_cols.shape[-1]
    piece_rows = x_cols.shape[3]
    block_size = x_blocks.shape[-1]
    aim_cols = aim_cols.reshape(-1, iter_width)
    aim_flags = aim_flags.reshape(-1, iter_width)
    group_rows = aim_cols.shape[0]
    summed = jnp.zeros((group_rows * iter_width, block_size, block_size), jnp.float32)
    ham_all = (
        lax.all_gather(h_blocks, "col", axis=1, tiled=True),
        lax.all_gather(h_rows, "col", axis=1, tiled=True),
        lax.all_gather(h_cols, "col", axis=1, tiled=True),
        lax.all_gather(h_flags, "col", axis=1, tiled=True),
    )
    ham_all = tuple((member[0, :, 0] for member in ham_all))
    pieces = (
        lax.all_gather(x_blocks, "row", axis=0, tiled=True),
        lax.all_gather(x_cols, "row", axis=0, tiled=True),
        lax.all_gather(x_flags, "row", axis=0, tiled=True),
    )
    ham_part = tuple((member for member in ham_all))
    iter_part = tuple((member[:, 0, 0] for member in pieces))
    summed = run_pieces(summed, ham_part, iter_part, aim_cols, aim_flags)
    rounded = lax.optimization_barrier(summed.astype(jnp.bfloat16)).astype(jnp.float32)
    rounded = rounded.reshape(
        (lax.axis_size("depth"), piece_rows, iter_width, block_size, block_size)
    )
    shares = lax.psum_scatter(
        rounded.astype(jnp.bfloat16), "depth", scatter_dimension=0, tiled=True
    ).astype(jnp.float32)
    prior = previous[0, 0, 0].astype(jnp.float32)
    live = x_flags[0, 0, 0].astype(jnp.float32)[..., None, None]
    result = (2.0 * shares[0] - prior) * live
    return result.astype(jnp.bfloat16).reshape(previous.shape)


def solution(mesh):
    placed = (
        P("row", "col", "depth", None, None, None),
        P("row", "col", "depth", None),
        P("row", "col", "depth", None),
        P("row", "col", "depth", None),
        P("row", "depth", "col", None, None, None, None),
        P("row", "depth", "col", None, None),
        P("row", "depth", "col", None, None),
        P("row", "depth", "col", None, None, None, None),
    )
    return jax.shard_map(
        body,
        mesh=mesh,
        in_specs=placed,
        out_specs=P("row", "depth", "col", None, None, None, None),
        check_vma=False,
    )
```

profile of v0, /device:TPU:1, one launch (start us, length us, event | category | flops | bytes accessed | tf_op | source)
XLA Modules:
  0.0 491.9 jit_solution(9868348673197642162)
XLA Ops:
  8.1 13.5 %all_gather.30 = s32[1,4,1,8,2]{3,4,2,0,1:T(2,128)S(1)} all-gather(s32[1,1,1,8,2]{3,4,2,0,1:T(2,128)} %bitcast.95), channel_id=1, replica_groups=mesh['row'=16,'col'=8,'depth'=4] {'depth'}, dimensions={1}, use_global_device_ids=true | all-gather | bytes 320 | tf_op jit(solution)/shard_map/all_gather | solution.py:40
  21.6 6.8 %all_gather.32 = s32[1,4,1,8,2]{3,4,2,0,1:T(2,128)S(1)} all-gather(s32[1,1,1,8,2]{3,4,2,0,1:T(2,128)} %bitcast.93), channel_id=1, replica_groups=mesh['row'=16,'col'=8,'depth'=4] {'depth'}, dimensions={1}, use_global_device_ids=true | all-gather | bytes 320 | tf_op jit(solution)/shard_map/all_gather | solution.py:41
  28.5 12.7 %all_gather.27 = s32[1,16,1,12]{3,2,0,1:T(1,128)S(1)} all-gather(s32[1,2,1,12]{3,2,0,1:T(1,128)} %bitcast.96), channel_id=1, replica_groups=mesh['row'=16,'col'=8,'depth'=4] {'col'}, dimensions={1}, use_global_device_ids=true | all-gather | bytes 864 | tf_op jit(solution)/shard_map/all_gather | solution.py:52
  41.2 15.2 %all_gather.29 = s32[1,16,1,12]{3,2,0,1:T(1,128)S(1)} all-gather(s32[1,2,1,12]{3,2,0,1:T(1,128)} %bitcast.97), channel_id=1, replica_groups=mesh['row'=16,'col'=8,'depth'=4] {'col'}, dimensions={1}, use_global_device_ids=true | all-gather | bytes 864 | tf_op jit(solution)/shard_map/all_gather | solution.py:53
  56.4 13.5 %all_gather.33 = s32[1,16,1,12]{3,2,0,1:T(1,128)S(1)} all-gather(s32[1,2,1,12]{3,2,0,1:T(1,128)} %bitcast.98), channel_id=1, replica_groups=mesh['row'=16,'col'=8,'depth'=4] {'col'}, dimensions={1}, use_global_device_ids=true | all-gather | bytes 864 | tf_op jit(solution)/shard_map/all_gather | solution.py:54
  70.0 29.6 %all_gather.28 = s32[16,1,1,8,2]{3,4,2,1,0:T(2,128)S(1)} all-gather(s32[1,1,1,8,2]{3,4,2,1,0:T(2,128)} %param.19), channel_id=1, replica_groups=mesh['row'=16,'col'=8,'depth'=4] {'row'}, dimensions={0}, use_global_device_ids=true | all-gather | bytes 1088 | tf_op jit(solution)/shard_map/all_gather | solution.py:59
  99.5 20.1 %all_gather.31 = s32[16,1,1,8,2]{3,4,2,1,0:T(2,128)S(1)} all-gather(s32[1,1,1,8,2]{3,4,2,1,0:T(2,128)} %param.20), channel_id=1, replica_groups=mesh['row'=16,'col'=8,'depth'=4] {'row'}, dimensions={0}, use_global_device_ids=true | all-gather | bytes 1088 | tf_op jit(solution)/shard_map/all_gather | solution.py:60
  119.6 82.3 %all-gather.3.cloned.1.call-done = bf16[16,1,1,8,2,128,128]{6,5,4,3,2,1,0:T(8,128)(2,1)} async-done(((bf16[1,1,1,8,2,128,128]{6,5,4,3,2,1,0:T(8,128)(2,1)}), bf16[16,1,1,8,2,128,128]{6,5,4,3,2,1,0:T(8,128)(2,1)}) %all-gather.3.cloned.1.call-update) | async-done | bytes 8388624 | tf_op jit(solution)/shard_map/all_gather | solution.py:58
  204.4 222.7 %while.10 = (s32[]{:T(128)}, f32[64,128,128]{2,1,0:T(8,128)}, s32[16,12]{1,0:T(8,128)S(1)}, s32[16,8,2]{1,2,0:T(2,128)S(1)}, s32[16,12]{1,0:T(8,128)S(1)}, /*ind...) while((s32[]{:T(128)}, f32[64,128,128]{2,1,0:T(8,128)}, ...), condition=%wide.region_2.5_spmd, body=%wide.region_0.4_spmd.sunk | while | flops 103419520 | bytes 16400633 | solution.py:34
  226.1 6.0 %scatter_fusion = f32[64,128,128]{2,1,0:T(8,128)} fusion(f32[64,128,128]{2,1,0:T(8,128)} %get-tuple-element.231, s32[24]{0:T(128)S(1)} %fusion.31, f32[24,128,128]{2,1,0:T(8,128)S(1)} %copy.89), kind=kCustom, calls=%fused_computation.5.clone.1 | custom fusion | flops 393216 | bytes 4718688 | tf_op jit(solution)/shard_map/while/body/eval_jaxpr/scatter-add | solution.py:24
  240.0 6.0 %scatter_fusion = f32[64,128,128]{2,1,0:T(8,128)} fusion(f32[64,128,128]{2,1,0:T(8,128)} %get-tuple-element.231, s32[24]{0:T(128)S(1)} %fusion.31, f32[24,128,128]{2,1,0:T(8,128)S(1)} %copy.89), kind=kCustom, calls=%fused_computation.5.clone.1 | custom fusion | flops 393216 | bytes 4718688 | tf_op jit(solution)/shard_map/while/body/eval_jaxpr/scatter-add | solution.py:24
  253.9 6.1 %scatter_fusion = f32[64,128,128]{2,1,0:T(8,128)} fusion(f32[64,128,128]{2,1,0:T(8,128)} %get-tuple-element.231, s32[24]{0:T(128)S(1)} %fusion.31, f32[24,128,128]{2,1,0:T(8,128)S(1)} %copy.89), kind=kCustom, calls=%fused_computation.5.clone.1 | custom fusion | flops 393216 | bytes 4718688 | tf_op jit(solution)/shard_map/while/body/eval_jaxpr/scatter-add | solution.py:24
  267.9 6.1 %scatter_fusion = f32[64,128,128]{2,1,0:T(8,128)} fusion(f32[64,128,128]{2,1,0:T(8,128)} %get-tuple-element.231, s32[24]{0:T(128)S(1)} %fusion.31, f32[24,128,128]{2,1,0:T(8,128)S(1)} %copy.89), kind=kCustom, calls=%fused_computation.5.clone.1 | custom fusion | flops 393216 | bytes 4718688 | tf_op jit(solution)/shard_map/while/body/eval_jaxpr/scatter-add | solution.py:24
  281.8 6.1 %scatter_fusion = f32[64,128,128]{2,1,0:T(8,128)} fusion(f32[64,128,128]{2,1,0:T(8,128)} %get-tuple-element.231, s32[24]{0:T(128)S(1)} %fusion.31, f32[24,128,128]{2,1,0:T(8,128)S(1)} %copy.89), kind=kCustom, calls=%fused_computation.5.clone.1 | custom fusion | flops 393216 | bytes 4718688 | tf_op jit(solution)/shard_map/while/body/eval_jaxpr/scatter-add | solution.py:24
  295.7 6.1 %scatter_fusion = f32[64,128,128]{2,1,0:T(8,128)} fusion(f32[64,128,128]{2,1,0:T(8,128)} %get-tuple-element.231, s32[24]{0:T(128)S(1)} %fusion.31, f32[24,128,128]{2,1,0:T(8,128)S(1)} %copy.89), kind=kCustom, calls=%fused_computation.5.clone.1 | custom fusion | flops 393216 | bytes 4718688 | tf_op jit(solution)/shard_map/while/body/eval_jaxpr/scatter-add | solution.py:24
  309.7 6.1 %scatter_fusion = f32[64,128,128]{2,1,0:T(8,128)} fusion(f32[64,128,128]{2,1,0:T(8,128)} %get-tuple-element.231, s32[24]{0:T(128)S(1)} %fusion.31, f32[24,128,128]{2,1,0:T(8,128)S(1)} %copy.89), kind=kCustom, calls=%fused_computation.5.clone.1 | custom fusion | flops 393216 | bytes 4718688 | tf_op jit(solution)/shard_map/while/body/eval_jaxpr/scatter-add | solution.py:24
  323.6 6.1 %scatter_fusion = f32[64,128,128]{2,1,0:T(8,128)} fusion(f32[64,128,128]{2,1,0:T(8,128)} %get-tuple-element.231, s32[24]{0:T(128)S(1)} %fusion.31, f32[24,128,128]{2,1,0:T(8,128)S(1)} %copy.89), kind=kCustom, calls=%fused_computation.5.clone.1 | custom fusion | flops 393216 | bytes 4718688 | tf_op jit(solution)/shard_map/while/body/eval_jaxpr/scatter-add | solution.py:24
  337.6 6.1 %scatter_fusion = f32[64,128,128]{2,1,0:T(8,128)} fusion(f32[64,128,128]{2,1,0:T(8,128)} %get-tuple-element.231, s32[24]{0:T(128)S(1)} %fusion.31, f32[24,128,128]{2,1,0:T(8,128)S(1)} %copy.89), kind=kCustom, calls=%fused_computation.5.clone.1 | custom fusion | flops 393216 | bytes 4718688 | tf_op jit(solution)/shard_map/while/body/eval_jaxpr/scatter-add | solution.py:24
  365.4 6.0 %scatter_fusion = f32[64,128,128]{2,1,0:T(8,128)} fusion(f32[64,128,128]{2,1,0:T(8,128)} %get-tuple-element.231, s32[24]{0:T(128)S(1)} %fusion.31, f32[24,128,128]{2,1,0:T(8,128)S(1)} %copy.89), kind=kCustom, calls=%fused_computation.5.clone.1 | custom fusion | flops 393216 | bytes 4718688 | tf_op jit(solution)/shard_map/while/body/eval_jaxpr/scatter-add | solution.py:24
  379.3 6.1 %scatter_fusion = f32[64,128,128]{2,1,0:T(8,128)} fusion(f32[64,128,128]{2,1,0:T(8,128)} %get-tuple-element.231, s32[24]{0:T(128)S(1)} %fusion.31, f32[24,128,128]{2,1,0:T(8,128)S(1)} %copy.89), kind=kCustom, calls=%fused_computation.5.clone.1 | custom fusion | flops 393216 | bytes 4718688 | tf_op jit(solution)/shard_map/while/body/eval_jaxpr/scatter-add | solution.py:24
  393.2 6.0 %scatter_fusion = f32[64,128,128]{2,1,0:T(8,128)} fusion(f32[64,128,128]{2,1,0:T(8,128)} %get-tuple-element.231, s32[24]{0:T(128)S(1)} %fusion.31, f32[24,128,128]{2,1,0:T(8,128)S(1)} %copy.89), kind=kCustom, calls=%fused_computation.5.clone.1 | custom fusion | flops 393216 | bytes 4718688 | tf_op jit(solution)/shard_map/while/body/eval_jaxpr/scatter-add | solution.py:24
  407.1 6.0 %scatter_fusion = f32[64,128,128]{2,1,0:T(8,128)} fusion(f32[64,128,128]{2,1,0:T(8,128)} %get-tuple-element.231, s32[24]{0:T(128)S(1)} %fusion.31, f32[24,128,128]{2,1,0:T(8,128)S(1)} %copy.89), kind=kCustom, calls=%fused_computation.5.clone.1 | custom fusion | flops 393216 | bytes 4718688 | tf_op jit(solution)/shard_map/while/body/eval_jaxpr/scatter-add | solution.py:24
  421.0 6.1 %scatter_fusion = f32[64,128,128]{2,1,0:T(8,128)} fusion(f32[64,128,128]{2,1,0:T(8,128)} %get-tuple-element.231, s32[24]{0:T(128)S(1)} %fusion.31, f32[24,128,128]{2,1,0:T(8,128)S(1)} %copy.89), kind=kCustom, calls=%fused_computation.5.clone.1 | custom fusion | flops 393216 | bytes 4718688 | tf_op jit(solution)/shard_map/while/body/eval_jaxpr/scatter-add | solution.py:24
  431.2 52.1 %reduce-scatter.2.cloned.1.call-done = bf16[1,8,2,128,128]{4,3,2,1,0:T(8,128)(2,1)} async-done(((bf16[4,8,2,128,128]{4,3,2,1,0:T(8,128)(2,1)}), bf16[1,8,2,128,128]{4,3,2,1,0:T(8,128)(2,1)}) %reduce-scatter.2.cloned.1.call-update) | async-done | bytes 524304 | tf_op jit(solution)/shard_map/reduce_scatter | solution.py:69
  (452 shorter events, 146.4 us)
Async XLA Ops:
  6.5 113.1 %all-gather.5.cloned.1.call-start = ((), (), s32[]{:S(2)}) async-start(), calls=%async_computation.2 | async-start | bytes 7077888 | tf_op jit(solution)/shard_map/all_gather | solution.py:51
  7.3 194.6 %all-gather.3.cloned.1.call-start = ((), (), s32[]{:S(2)}) async-start(), calls=%async_computation.1 | async-start | bytes 8912896 | tf_op jit(solution)/shard_map/all_gather | solution.py:58
  8.0 475.3 %reduce-scatter.2.cloned.1.call-start = ((), (), s32[]{:S(2)}) async-start(), calls=%async_computation.3 | async-start | bytes 2621440 | tf_op jit(solution)/shard_map/reduce_scatter | solution.py:69
  427.1 4.0 copy-start.1
  427.1 56.2 %copy-start = (bf16[1,1,1,8,2,128,128]{6,5,4,3,2,1,0:T(8,128)(2,1)S(1)}, bf16[1,1,1,8,2,128,128]{6,5,4,3,2,1,0:T(8,128)(2,1)}, u32[]{:S(2)}) copy-start(bf16[1,1,1,8,2,128,128]{6,5,4,3,2,1,0:T(8,128)(2,1)} %param.21) | copy-start | bytes 1572868
Sparse Core Ops, SparseCore 0:
  9.4 85.4 all-gather.4
  97.0 104.8 all-gather.2
  431.2 52.0 reduce-scatter.1
where the time goes:
time: 496 us; the launch traced here: 492 us
  waiting for transfers between devices  136 us (27%)
  other arithmetic  112 us (23%)
  blocking collectives  111 us (22%)
  local copies, waits for them, and re-layouts  78.5 us (16%)
  matrix products  39.2 us (8%)
  between operations  13.1 us (3%)
    scatter-add x16, other arithmetic, add_piece(): summed.at[target.reshape(-1)]  96.7 us
    all_gather x1, waiting for transfers between devices, body(): lax.all_gather(x_blocks, 'row', axis=0, tiled=True)  82.3 us
    reduce_scatter x1, waiting for transfers between devices, body(): lax.psum_scatter(rounded.astype(jnp.bfloat16), 'depth', scatter_dimension...  52.1 us
    all_gather x1, blocking collectives, body(): lax.all_gather(x_cols, 'row', axis=0, tiled=True)  29.6 us
    dot_general x16, matrix products, add_piece(): jnp.einsum('akl,avlm->avkm', blocks, chosen, preferred_element_type=jnp.f...  22.5 us
    all_gather x1, blocking collectives, body(): lax.all_gather(x_flags, 'row', axis=0, tiled=True)  20.1 us
    squeeze x64, local copies, waits for them, and re-layouts, run_pieces(): summed, _ = lax.scan(one_piece, summed, (ham_part, iter_part))  20.1 us
    dot_general x16, matrix products, add_piece(): jnp.einsum('awv,awkm->avkm', paired.astype(jnp.bfloat16), picked, preferr...  16.7 us
  transfers between devices with their start and end apart: 3, of which 2 were waited for; matrix products, arithmetic and copies ran while one was open for 0% of the time, Pallas kernels for 0%

commit v1 on v0

v1 whole, which is shorter than its diff:
```python
import jax
import jax.numpy as jnp
from jax import lax
from jax.experimental import pallas as pl
from jax.experimental.pallas import tpu as pltpu
from jax.sharding import PartitionSpec as P

WINDOW = 16


def pair_kernel(where, ham, iterate, aim, pairs):
    cols, width = ham.shape[0], iterate.shape[1] // 2
    slots = ham.shape[1] // 3
    per_tile = slots // (iterate.shape[0] // cols)
    near = where[0] // 4
    step = where[0] % 4

    def one_slot(at, count):
        col = at // slots
        slot = at % slots
        row = ham[col, slot]
        inner = ham[col, slots + slot]
        live = ham[col, 2 * slots + slot] > 0
        piece = col * (slots // per_tile) + slot // per_tile
        array = ((col // 4) ^ near) * 4 + (step - col % 4 + 4) % 4
        owner = row // 8
        for w in range(2):
            spot = inner * 2 + w
            there = iterate[piece, spot]
            on = live & (iterate[piece, width + spot] > 0)
            for v in range(2):
                place = (row % 8) * 2 + v
                match = on & (aim[owner, place] == there) & (aim[owner, width + place] > 0)
                pairs[count] = (array * slots + slot) + (piece * width + spot) * 256 + (row * 2 + v) * 65536
                count = count + match.astype(jnp.int32)
        return count

    pairs[pairs.shape[0] - 1] = lax.fori_loop(0, cols * slots, one_slot, jnp.int32(0))


def product_kernel(pairs, where, iterate, *rest):
    hams, (sent, kept, total, ham_buf, it_buf, ham_sem, it_sem) = rest[:8], rest[8:]
    slots = hams[0].shape[0]
    count = pairs[pairs.shape[0] - 1]

    def start(at):
        code = pairs[at]
        ham_at = code % 256
        slot = at % WINDOW
        for k, ham in enumerate(hams):

            @pl.when(ham_at // slots == k)
            def _():
                pltpu.make_async_copy(ham.at[ham_at % slots], ham_buf.at[slot], ham_sem.at[slot]).start()

        pltpu.make_async_copy(iterate.at[(code // 256) % 256], it_buf.at[slot], it_sem.at[slot]).start()

    def first(at, carry):
        start(at)
        return carry

    lax.fori_loop(0, jnp.minimum(count, WINDOW), first, 0)

    def clear(at, carry):
        total[at] = jnp.zeros(total.shape[1:], total.dtype)
        return carry

    lax.fori_loop(0, total.shape[0], clear, 0, unroll=4)

    def multiply(at, carry):
        slot = at % WINDOW
        pltpu.make_async_copy(hams[0].at[0], ham_buf.at[slot], ham_sem.at[slot]).wait()
        pltpu.make_async_copy(iterate.at[0], it_buf.at[slot], it_sem.at[slot]).wait()
        goal = pairs[at] // 65536
        total[goal] += jnp.dot(ham_buf[slot], it_buf[slot], preferred_element_type=jnp.float32)

        @pl.when(at + WINDOW < count)
        def _():
            start(at + WINDOW)

        return carry

    lax.fori_loop(0, count, multiply, 0)
    half = sent.shape[0] // 2
    core = where[1] % 2
    high = where[1] // 2
    for part in range(2):
        target_high = high if part else 1 - high

        def finish(at, carry):
            sent[part * half + at] = total[(target_high * 2 + 1 - core) * half + at].astype(sent.dtype)
            kept[part * half + at] = total[(target_high * 2 + core) * half + at].astype(kept.dtype)
            return carry

        lax.fori_loop(0, half, finish, 0, unroll=2)


def body(h_blocks, h_rows, h_cols, h_flags, x_blocks, x_cols, x_flags, previous):
    block = x_blocks.shape[-1]
    n_row, n_col, n_depth = lax.axis_size("row"), lax.axis_size("col"), lax.axis_size("depth")
    where = jnp.stack([lax.axis_index("col"), lax.axis_index("depth")]).astype(jnp.int32)
    iterate = lax.all_gather(x_blocks[0, 0, 0], "row", axis=0)
    iterate = iterate.reshape(-1, block, block)
    mine = h_blocks[0].reshape(-1, block, block)
    hams = []
    for flip in range(2):
        for step in range(4):
            route = [(c, ((c // 4) ^ flip) * 4 + (c % 4 + step) % 4) for c in range(n_col)]
            hams.append(lax.ppermute(mine, "col", route) if flip or step else mine)
    ham_ints = jnp.concatenate([h_rows.reshape(-1), h_cols.reshape(-1), h_flags.reshape(-1)])
    it_ints = jnp.concatenate([x_cols.reshape(-1), x_flags.reshape(-1)])
    ham_ints = lax.all_gather(ham_ints.reshape(1, 1, -1), "col", axis=0, tiled=True)[:, 0]
    aim_ints = lax.all_gather(it_ints.reshape(1, 1, -1), "depth", axis=0, tiled=True)[:, 0]
    it_ints = lax.all_gather(it_ints.reshape(1, 1, -1), "row", axis=0, tiled=True)[:, 0]
    smem = pl.BlockSpec(memory_space=pltpu.SMEM)
    anywhere = pl.BlockSpec(memory_space=pl.ANY)
    vmem = pl.BlockSpec(memory_space=pltpu.VMEM)
    pairs = pl.pallas_call(
        pair_kernel,
        out_shape=jax.ShapeDtypeStruct((512,), jnp.int32),
        in_specs=[smem] * 4,
        out_specs=smem,
        name="pairs",
    )(where, ham_ints, it_ints, aim_ints)
    results = x_cols.shape[3] * x_cols.shape[4]
    half_shape = jax.ShapeDtypeStruct((2 * results, block, block), jnp.bfloat16)
    sent, kept = pl.pallas_call(
        product_kernel,
        out_shape=(half_shape, half_shape),
        in_specs=[smem, smem] + [anywhere] * 9,
        out_specs=(vmem, vmem),
        scratch_shapes=[
            pltpu.VMEM((n_depth * results, block, block), jnp.float32),
            pltpu.VMEM((WINDOW, block, block), jnp.bfloat16),
            pltpu.VMEM((WINDOW, block, block), jnp.bfloat16),
            pltpu.SemaphoreType.DMA((WINDOW,)),
            pltpu.SemaphoreType.DMA((WINDOW,)),
        ],
        compiler_params=pltpu.CompilerParams(vmem_limit_bytes=24 << 20),
        name="products",
    )(pairs, where, *[pltpu.with_memory_space_constraint(x, pltpu.HBM) for x in (iterate, hams[0])], *hams[1:])
    near = lax.ppermute(sent, "depth", [(d, d ^ 1) for d in range(n_depth)])
    onward = kept[:results].astype(jnp.float32) + near[:results].astype(jnp.float32)
    far = lax.ppermute(onward.astype(jnp.bfloat16), "depth", [(d, d ^ 2) for d in range(n_depth)])
    summed = kept[results:].astype(jnp.float32) + near[results:].astype(jnp.float32)
    summed = summed + far.astype(jnp.float32)
    prior = previous.reshape(results, block, block).astype(jnp.float32)
    live = x_flags.reshape(results, 1, 1).astype(jnp.float32)
    result = (2.0 * summed - prior) * live
    return result.astype(jnp.bfloat16).reshape(previous.shape)


def solution(mesh):
    placed = (
        P("row", "col", "depth", None, None, None),
        P("row", "col", "depth", None),
        P("row", "col", "depth", None),
        P("row", "col", "depth", None),
        P("row", "depth", "col", None, None, None, None),
        P("row", "depth", "col", None, None),
        P("row", "depth", "col", None, None),
        P("row", "depth", "col", None, None, None, None),
    )
    return jax.shard_map(
        body,
        mesh=mesh,
        in_specs=placed,
        out_specs=P("row", "depth", "col", None, None, None, None),
        check_vma=False,
    )
```

time: 496 us -> 184 us (0.37)
  other arithmetic: 112 us -> 6.09 us
  waiting for transfers between devices: 136 us -> 32.6 us
  local copies, waits for them, and re-layouts: 78.5 us -> 9.56 us
  blocking collectives: 111 us -> 62.5 us
  matrix products: 39.2 us -> 0 us
  starting transfers between devices: 0.08 us -> 36.7 us
  Pallas kernels: 0 us -> 17.4 us
    all_gather x7 -> x0, blocking collectives: 111 us -> none  [the longest x1 29.6 us: body(): lax.all_gather(x_cols, 'row', axis=0, tiled=True)]
    scatter-add x16 -> x0, other arithmetic: 96.7 us -> none  [add_piece(): summed.at[target.reshape(-1)]]
    all_gather x2 -> x1, waiting for transfers between devices: 82.3 us -> 0.02 us  [body(): iterate = lax.all_gather(x_blocks[0, 0, 0], 'row', axis=0)]
    unnamed x0 -> x3, blocking collectives: none -> 62.5 us
    reduce_scatter x1 -> x0, waiting for transfers between devices: 52.1 us -> none  [body(): lax.psum_scatter(rounded.astype(jnp.bfloat16), 'depth', scatter_dimension...]
    gather x80 -> x0, local copies, waits for them, and re-layouts: 46.8 us -> none  [the longest x16 11.2 us: add_piece(): picked = jnp.take(iter_blocks, ham_cols, axis=0)]
    dot_general x32 -> x0, matrix products: 39.2 us -> none  [the longest x16 22.5 us: add_piece(): jnp.einsum('akl,avlm->avkm', blocks, chosen, preferred_element_type=jnp.f...]
    ppermute x0 -> x9, starting transfers between devices: none -> 36.7 us  [the longest x7 26.4 us: body(): hams.append(lax.ppermute(mine, 'col', route) if flip or step else mine)]
  transfers between devices with their start and end apart: 3 -> 10, of which waited for: 2 -> 4; matrix products, arithmetic and copies ran while one was open for 0% -> 7% of each run, Pallas kernels for 0% -> 8%
where the time goes in v1:
time: 184 us; the launch traced here: 180 us
  blocking collectives  62.5 us (34%)
  starting transfers between devices  36.7 us (20%)
  waiting for transfers between devices  32.6 us (18%)
  Pallas kernels  17.4 us (9%)
  between operations  15.6 us (8%)
  local copies, waits for them, and re-layouts  9.56 us (5%)
  other arithmetic  6.09 us (3%)
    unnamed x3, blocking collectives  62.5 us
    ppermute x7, starting transfers between devices, body(): hams.append(lax.ppermute(mine, 'col', route) if flip or step else mine)  26.4 us
    ppermute x7, waiting for transfers between devices, body(): hams.append(lax.ppermute(mine, 'col', route) if flip or step else mine)  16.9 us
    pallas_call x1, Pallas kernels, body(): pl.pallas_call(pair_kernel, out_shape=jax.ShapeDtypeStruct((512,), jnp.in...  14.7 us
    ppermute x1, waiting for transfers between devices, body(): lax.ppermute(onward.astype(jnp.bfloat16), 'depth', [(d, d ^ 2) for d in r...  12.7 us
    unnamed x15, local copies, waits for them, and re-layouts  7.12 us
    ppermute x1, starting transfers between devices, body(): near = lax.ppermute(sent, 'depth', [(d, d ^ 1) for d in range(n_depth)])  6.44 us
    unnamed x5, other arithmetic  4.14 us
  transfers between devices with their start and end apart: 10, of which 4 were waited for; matrix products, arithmetic and copies ran while one was open for 7% of the time, Pallas kernels for 8%

profile of v1, /device:TPU:1, one launch (start us, length us, event | category | flops | bytes accessed | tf_op | source)
XLA Modules:
  0.0 180.3 jit_solution(15597354634558510799)
XLA Ops:
  7.3 6.4 %collective-permute-start.6 = (bf16[24,128,128]{2,1,0:T(8,128)(2,1)}, bf16[24,128,128]{2,1,0:T(8,128)(2,1)S(1)}, u32[]{:S(2)}, u32[]{:S(2)}) collective-permute-start(bf16[24,128,128]{2,1,0:T(8,128)(2,1)} %bitcast.16), channel_id=1, source_target_pairs={{0,28},{4,16},{8,20},{12,24},{16,12},{20,0},{24,4},{28,8},{1,29},{... | collective-permute-start | bytes 2359304 | tf_op jit(solution)/shard_map/ppermute | solution.py:109
  13.7 2.3 %collective-permute-start.5 = (bf16[24,128,128]{2,1,0:T(8,128)(2,1)}, bf16[24,128,128]{2,1,0:T(8,128)(2,1)S(1)}, u32[]{:S(2)}, u32[]{:S(2)}) collective-permute-start(bf16[24,128,128]{2,1,0:T(8,128)(2,1)} %bitcast.17), channel_id=1, source_target_pairs={{0,24},{4,28},{8,16},{12,20},{16,8},{20,12},{24,0},{28,4},{1,25},{... | collective-permute-start | bytes 2359304 | tf_op jit(solution)/shard_map/ppermute | solution.py:109
  15.9 3.5 %collective-permute-start.4 = (bf16[24,128,128]{2,1,0:T(8,128)(2,1)}, bf16[24,128,128]{2,1,0:T(8,128)(2,1)S(1)}, u32[]{:S(2)}, u32[]{:S(2)}) collective-permute-start(bf16[24,128,128]{2,1,0:T(8,128)(2,1)} %bitcast.18), channel_id=1, source_target_pairs={{0,20},{4,24},{8,28},{12,16},{16,4},{20,8},{24,12},{28,0},{1,21},{... | collective-permute-start | bytes 2359304 | tf_op jit(solution)/shard_map/ppermute | solution.py:109
  19.4 2.2 %collective-permute-start.3 = (bf16[24,128,128]{2,1,0:T(8,128)(2,1)}, bf16[24,128,128]{2,1,0:T(8,128)(2,1)S(1)}, u32[]{:S(2)}, u32[]{:S(2)}) collective-permute-start(bf16[24,128,128]{2,1,0:T(8,128)(2,1)} %bitcast.19), channel_id=1, source_target_pairs={{0,16},{4,20},{8,24},{12,28},{16,0},{20,4},{24,8},{28,12},{1,17},{... | collective-permute-start | bytes 2359304 | tf_op jit(solution)/shard_map/ppermute | solution.py:109
  21.6 3.9 %collective-permute-start.2 = (bf16[24,128,128]{2,1,0:T(8,128)(2,1)}, bf16[24,128,128]{2,1,0:T(8,128)(2,1)}, u32[]{:S(2)}, u32[]{:S(2)}) collective-permute-start(bf16[24,128,128]{2,1,0:T(8,128)(2,1)} %bitcast.20), channel_id=1, source_target_pairs={{0,12},{4,0},{8,4},{12,8},{16,28},{20,16},{24,20},{28,24},{1,13},{... | collective-permute-start | bytes 2359304 | tf_op jit(solution)/shard_map/ppermute | solution.py:109
  25.5 3.2 %collective-permute-done.6.rest_7_ = bf16[24,128,128]{2,1,0:T(8,128)(2,1)S(1)} collective-permute-done((bf16[24,128,128]{2,1,0:T(8,128)(2,1)}, bf16[24,128,128]{2,1,0:T(8,128)(2,1)S(1)}, u32[]{:S(2)}, u32[]{:S(2)}) %collective-permute-start.6) | collective-permute-done | bytes 786464 | tf_op jit(solution)/shard_map/ppermute | solution.py:109
  28.7 5.6 %collective-permute-start.1 = (bf16[24,128,128]{2,1,0:T(8,128)(2,1)}, bf16[24,128,128]{2,1,0:T(8,128)(2,1)}, u32[]{:S(2)}, u32[]{:S(2)}) collective-permute-start(bf16[24,128,128]{2,1,0:T(8,128)(2,1)} %bitcast.21), channel_id=1, source_target_pairs={{0,8},{4,12},{8,0},{12,4},{16,24},{20,28},{24,16},{28,20},{1,9},{5... | collective-permute-start | bytes 2359304 | tf_op jit(solution)/shard_map/ppermute | solution.py:109
  34.4 13.7 %collective-permute-done.5.rest_6_ = bf16[24,128,128]{2,1,0:T(8,128)(2,1)S(1)} collective-permute-done((bf16[24,128,128]{2,1,0:T(8,128)(2,1)}, bf16[24,128,128]{2,1,0:T(8,128)(2,1)S(1)}, u32[]{:S(2)}, u32[]{:S(2)}) %collective-permute-start.5) | collective-permute-done | bytes 786464 | tf_op jit(solution)/shard_map/ppermute | solution.py:109
  48.1 2.5 %collective-permute-start = (bf16[24,128,128]{2,1,0:T(8,128)(2,1)}, bf16[24,128,128]{2,1,0:T(8,128)(2,1)}, u32[]{:S(2)}, u32[]{:S(2)}) collective-permute-start(bf16[24,128,128]{2,1,0:T(8,128)(2,1)} %bitcast.22), channel_id=1, source_target_pairs={{0,4},{4,8},{8,12},{12,0},{16,20},{20,24},{24,28},{28,16},{1,5},{5... | collective-permute-start | bytes 2359304 | tf_op jit(solution)/shard_map/ppermute | solution.py:109
  50.6 1.3 dynamic-slice.2
  51.9 1.3 dynamic-slice.1
  54.6 1.3 dynamic-slice
  56.3 1.3 reduce.11
  57.7 1.3 reduce.10
  59.0 1.3 reduce.9
  62.2 21.9 %all-reduce.2 = s32[128]{0:T(128)S(1)} all-reduce(s32[128]{0:T(128)S(1)} %get-tuple-element.9), channel_id=4, replica_groups=mesh['row'=16,'col'=8,'depth'=4] {'depth'}, use_global_device_ids=true, to_apply=%add.2 | all-reduce | flops 128 | bytes 1024
  85.7 23.6 %all-reduce = s32[576]{0:T(1024)S(1)} all-reduce(s32[576]{0:T(1024)S(1)} %add_dynamic-update-slice_fusion), channel_id=2, replica_groups=mesh['row'=16,'col'=8,'depth'=4] {'col'}, use_global_device_ids=true, to_apply=%add | all-reduce | flops 576 | bytes 4608
  110.0 16.9 %all-reduce.1 = s32[512]{0:T(512)S(1)} all-reduce(s32[512]{0:T(512)S(1)} %get-tuple-element.10), channel_id=3, replica_groups=mesh['row'=16,'col'=8,'depth'=4] {'row'}, use_global_device_ids=true, to_apply=%add.1 | all-reduce | flops 512 | bytes 4096
  128.1 14.7 %pairs.1 = s32[512]{0:T(512)} custom-call(s32[2]{0:T(128)} %pad_add_fusion.where, s32[8,72]{1,0:T(8,128)} %squeeze.9.ham, s32[16,32]{1,0:T(8,128)} %squeeze.10.iterate, s32[4,32]{1,0:T(4,128)} %squeeze.11.aim), custom_call_target="tpu_custom_call" | custom-call | tf_op jit(solution)/shard_map/pairs/pallas_call | solution.py:118
  144.2 2.7 %products.1 = (bf16[32,128,128]{2,1,0:T(8,128)(2,1)S(1)}, bf16[32,128,128]{2,1,0:T(8,128)(2,1)S(1)}) custom-call(s32[512]{0:T(512)S(1)} %copy-done, s32[2]{0:T(128)S(1)} %copy-done.1, bf16[256,128,128]{2,1,0:T(8,128)(2,1)} %bitcast.15, bf16[24,128,128]{2,1,0:T(8,128)(2,1)} %bitcast.23, bf16[24,128,128]{2,1,0:T(8,128)(2,1)} %collective-permute-done.rest_1_, ...), custom_call_target="tpu_custom_call" | custom-call | tf_op jit(solution)/shard_map/products/pallas_call | solution.py:127
  146.9 6.4 %collective-permute-start.7 = (bf16[32,128,128]{2,1,0:T(8,128)(2,1)S(1)}, bf16[32,128,128]{2,1,0:T(8,128)(2,1)S(1)}, u32[]{:S(2)}, u32[]{:S(2)}) collective-permute-start(bf16[32,128,128]{2,1,0:T(8,128)(2,1)S(1)} %get-tuple-element.8), channel_id=1, source_target_pairs={{0,1},{1,0},{2,3},{3,2},{4,5},{5,4},{6,7},{7,6},{8,9},{9,8},{10,11... | collective-permute-start | bytes 3145736 | tf_op jit(solution)/shard_map/ppermute | solution.py:142
  153.3 2.3 %collective-permute-done.7 = bf16[32,128,128]{2,1,0:T(8,128)(2,1)S(1)} collective-permute-done((bf16[32,128,128]{2,1,0:T(8,128)(2,1)S(1)}, bf16[32,128,128]{2,1,0:T(8,128)(2,1)S(1)}, u32[]{:S(2)}, u32[]{:S(2)}) %collective-permute-start.7) | collective-permute-done | bytes 1048608 | tf_op jit(solution)/shard_map/ppermute | solution.py:142
  155.7 3.8 %collective-permute-start.8 = (bf16[16,128,128]{2,1,0:T(8,128)(2,1)S(1)}, bf16[16,128,128]{2,1,0:T(8,128)(2,1)S(1)}, u32[]{:S(2)}, u32[]{:S(2)}) collective-permute-start(bf16[16,128,128]{2,1,0:T(8,128)(2,1)S(1)} %add_convert_fusion), channel_id=1, source_target_pairs={{0,2},{1,3},{2,0},{3,1},{4,6},{5,7},{6,4},{7,5},{8,10},{9,11},{10,... | collective-permute-start | bytes 1572872 | tf_op jit(solution)/shard_map/ppermute | solution.py:144
  159.5 12.7 %collective-permute-done.8 = bf16[16,128,128]{2,1,0:T(8,128)(2,1)S(1)} collective-permute-done((bf16[16,128,128]{2,1,0:T(8,128)(2,1)S(1)}, bf16[16,128,128]{2,1,0:T(8,128)(2,1)S(1)}, u32[]{:S(2)}, u32[]{:S(2)}) %collective-permute-start.8) | collective-permute-done | bytes 524320 | tf_op jit(solution)/shard_map/ppermute | solution.py:144
  (34 shorter events, 8.8 us)
Async XLA Ops:
  6.5 136.4 %all-gather.6.cloned.1.call-start = ((), (), s32[]{:S(2)}) async-start(), calls=%async_computation | async-start | bytes 8912896 | tf_op jit(solution)/shard_map/all_gather | solution.py:102
  7.3 21.5 %collective-permute-start.6 = (bf16[24,128,128]{2,1,0:T(8,128)(2,1)}, bf16[24,128,128]{2,1,0:T(8,128)(2,1)S(1)}, u32[]{:S(2)}, u32[]{:S(2)}) collective-permute-start(bf16[24,128,128]{2,1,0:T(8,128)(2,1)} %bitcast.16), channel_id=1, source_target_pairs={{0,28},{4,16},{8,20},{12,24},{16,12},{20,0},{24,4},{28,8},{1,29},{... | collective-permute-start | bytes 2359304 | tf_op jit(solution)/shard_map/ppermute | solution.py:109
  13.7 34.4 %collective-permute-start.5 = (bf16[24,128,128]{2,1,0:T(8,128)(2,1)}, bf16[24,128,128]{2,1,0:T(8,128)(2,1)S(1)}, u32[]{:S(2)}, u32[]{:S(2)}) collective-permute-start(bf16[24,128,128]{2,1,0:T(8,128)(2,1)} %bitcast.17), channel_id=1, source_target_pairs={{0,24},{4,28},{8,16},{12,20},{16,8},{20,12},{24,0},{28,4},{1,25},{... | collective-permute-start | bytes 2359304 | tf_op jit(solution)/shard_map/ppermute | solution.py:109
  15.9 127.0 %collective-permute-start.4 = (bf16[24,128,128]{2,1,0:T(8,128)(2,1)}, bf16[24,128,128]{2,1,0:T(8,128)(2,1)S(1)}, u32[]{:S(2)}, u32[]{:S(2)}) collective-permute-start(bf16[24,128,128]{2,1,0:T(8,128)(2,1)} %bitcast.18), channel_id=1, source_target_pairs={{0,20},{4,24},{8,28},{12,16},{16,4},{20,8},{24,12},{28,0},{1,21},{... | collective-permute-start | bytes 2359304 | tf_op jit(solution)/shard_map/ppermute | solution.py:109
  19.4 123.5 %collective-permute-start.3 = (bf16[24,128,128]{2,1,0:T(8,128)(2,1)}, bf16[24,128,128]{2,1,0:T(8,128)(2,1)S(1)}, u32[]{:S(2)}, u32[]{:S(2)}) collective-permute-start(bf16[24,128,128]{2,1,0:T(8,128)(2,1)} %bitcast.19), channel_id=1, source_target_pairs={{0,16},{4,20},{8,24},{12,28},{16,0},{20,4},{24,8},{28,12},{1,17},{... | collective-permute-start | bytes 2359304 | tf_op jit(solution)/shard_map/ppermute | solution.py:109
  21.6 121.3 %collective-permute-start.2 = (bf16[24,128,128]{2,1,0:T(8,128)(2,1)}, bf16[24,128,128]{2,1,0:T(8,128)(2,1)}, u32[]{:S(2)}, u32[]{:S(2)}) collective-permute-start(bf16[24,128,128]{2,1,0:T(8,128)(2,1)} %bitcast.20), channel_id=1, source_target_pairs={{0,12},{4,0},{8,4},{12,8},{16,28},{20,16},{24,20},{28,24},{1,13},{... | collective-permute-start | bytes 2359304 | tf_op jit(solution)/shard_map/ppermute | solution.py:109
  28.7 114.2 %collective-permute-start.1 = (bf16[24,128,128]{2,1,0:T(8,128)(2,1)}, bf16[24,128,128]{2,1,0:T(8,128)(2,1)}, u32[]{:S(2)}, u32[]{:S(2)}) collective-permute-start(bf16[24,128,128]{2,1,0:T(8,128)(2,1)} %bitcast.21), channel_id=1, source_target_pairs={{0,8},{4,12},{8,0},{12,4},{16,24},{20,28},{24,16},{28,20},{1,9},{5... | collective-permute-start | bytes 2359304 | tf_op jit(solution)/shard_map/ppermute | solution.py:109
  48.1 94.9 %collective-permute-start = (bf16[24,128,128]{2,1,0:T(8,128)(2,1)}, bf16[24,128,128]{2,1,0:T(8,128)(2,1)}, u32[]{:S(2)}, u32[]{:S(2)}) collective-permute-start(bf16[24,128,128]{2,1,0:T(8,128)(2,1)} %bitcast.22), channel_id=1, source_target_pairs={{0,4},{4,8},{8,12},{12,0},{16,20},{20,24},{24,28},{28,16},{1,5},{5... | collective-permute-start | bytes 2359304 | tf_op jit(solution)/shard_map/ppermute | solution.py:109
  143.0 0.6 copy-start
  143.6 0.6 copy-start.1
  144.2 28.1 %copy-start.2 = (bf16[1,1,1,8,2,128,128]{6,5,4,3,2,1,0:T(8,128)(2,1)S(1)}, bf16[1,1,1,8,2,128,128]{6,5,4,3,2,1,0:T(8,128)(2,1)}, u32[]{:S(2)}) copy-start(bf16[1,1,1,8,2,128,128]{6,5,4,3,2,1,0:T(8,128)(2,1)} %param.15) | copy-start | bytes 1572868
  146.9 8.7 %collective-permute-start.7 = (bf16[32,128,128]{2,1,0:T(8,128)(2,1)S(1)}, bf16[32,128,128]{2,1,0:T(8,128)(2,1)S(1)}, u32[]{:S(2)}, u32[]{:S(2)}) collective-permute-start(bf16[32,128,128]{2,1,0:T(8,128)(2,1)S(1)} %get-tuple-element.8), channel_id=1, source_target_pairs={{0,1},{1,0},{2,3},{3,2},{4,5},{5,4},{6,7},{7,6},{8,9},{9,8},{10,11... | collective-permute-start | bytes 3145736 | tf_op jit(solution)/shard_map/ppermute | solution.py:142
  155.7 16.5 %collective-permute-start.8 = (bf16[16,128,128]{2,1,0:T(8,128)(2,1)S(1)}, bf16[16,128,128]{2,1,0:T(8,128)(2,1)S(1)}, u32[]{:S(2)}, u32[]{:S(2)}) collective-permute-start(bf16[16,128,128]{2,1,0:T(8,128)(2,1)S(1)} %add_convert_fusion), channel_id=1, source_target_pairs={{0,2},{1,3},{2,0},{3,1},{4,6},{5,7},{6,4},{7,5},{8,10},{9,11},{10,... | collective-permute-start | bytes 1572872 | tf_op jit(solution)/shard_map/ppermute | solution.py:144
Sparse Core Ops, SparseCore 0:
  9.4 111.2 all-gather.5

commit v2 on v1

--- a/solution.py
+++ b/solution.py
@@ -9,36 +9,40 @@
 
 
 def pair_kernel(where, ham, iterate, aim, pairs):
-    cols, width = ham.shape[0], iterate.shape[1] // 2
-    slots = ham.shape[1] // 3
-    per_tile = slots // (iterate.shape[0] // cols)
+    pieces, slots = ham.shape
+    per_col = pieces // 8
+    width = iterate.shape[1]
     near = where[0] // 4
     step = where[0] % 4
 
-    def one_slot(at, count):
-        col = at // slots
-        slot = at % slots
-        row = ham[col, slot]
-        inner = ham[col, slots + slot]
-        live = ham[col, 2 * slots + slot] > 0
-        piece = col * (slots // per_tile) + slot // per_tile
+    def one_piece(piece, count):
+        col = piece // per_col
         array = ((col // 4) ^ near) * 4 + (step - col % 4 + 4) % 4
-        owner = row // 8
-        for w in range(2):
-            spot = inner * 2 + w
-            there = iterate[piece, spot]
-            on = live & (iterate[piece, width + spot] > 0)
-            for v in range(2):
-                place = (row % 8) * 2 + v
-                match = on & (aim[owner, place] == there) & (aim[owner, width + place] > 0)
-                pairs[count] = (array * slots + slot) + (piece * width + spot) * 256 + (row * 2 + v) * 65536
-                count = count + match.astype(jnp.int32)
-        return count
+        base = (array * per_col + piece % per_col) * slots + piece * width * 256
 
-    pairs[pairs.shape[0] - 1] = lax.fori_loop(0, cols * slots, one_slot, jnp.int32(0))
+        def live(state):
+            slot, _ = state
+            return (slot < slots) & (ham[piece, jnp.minimum(slot, slots - 1)] >= 0)
+
+        def one_slot(state):
+            slot, count = state
+            key = ham[piece, slot]
+            row = key // 8
+            inner = key % 8
+            for w in range(2):
+                there = iterate[piece, inner * 2 + w]
+                for v in range(2):
+                    pairs[count] = base + slot + (inner * 2 + w) * 256 + (row * 2 + v) * 65536
+                    count = count + (aim[row * 2 + v] == there).astype(jnp.int32)
+            return slot + 1, count
+
+        return lax.while_loop(live, one_slot, (jnp.int32(0), count))[1]
+
+    pairs[pairs.shape[0] - 1] = lax.fori_loop(0, pieces, one_piece, jnp.int32(0))
+    pairs[pairs.shape[0] - 2] = where[1]
 
 
-def product_kernel(pairs, where, iterate, *rest):
+def product_kernel(pairs, iterate, *rest):
     hams, (sent, kept, total, ham_buf, it_buf, ham_sem, it_sem) = rest[:8], rest[8:]
     slots = hams[0].shape[0]
     count = pairs[pairs.shape[0] - 1]
@@ -82,8 +86,9 @@
 
     lax.fori_loop(0, count, multiply, 0)
     half = sent.shape[0] // 2
-    core = where[1] % 2
-    high = where[1] // 2
+    depth = pairs[pairs.shape[0] - 2]
+    core = depth % 2
+    high = depth // 2
     for part in range(2):
         target_high = high if part else 1 - high
 
@@ -101,17 +106,23 @@
     where = jnp.stack([lax.axis_index("col"), lax.axis_index("depth")]).astype(jnp.int32)
     iterate = lax.all_gather(x_blocks[0, 0, 0], "row", axis=0)
     iterate = iterate.reshape(-1, block, block)
+    ham_ints = jnp.stack([h_rows, h_cols, h_flags], axis=2)
+    ham_ints = lax.all_gather(ham_ints, "col", axis=1, tiled=True)
+    it_ints = jnp.concatenate([x_cols, x_flags], axis=2)
+    aim_ints = lax.all_gather(it_ints, "depth", axis=1, tiled=True)
+    it_ints = lax.all_gather(it_ints, "row", axis=0, tiled=True)
     mine = h_blocks[0].reshape(-1, block, block)
+    late, ham_ints, aim_ints, it_ints = lax.optimization_barrier((mine, ham_ints, aim_ints, it_ints))
     hams = []
     for flip in range(2):
-        for step in range(4):
+        for step in range(n_col // 2):
             route = [(c, ((c // 4) ^ flip) * 4 + (c % 4 + step) % 4) for c in range(n_col)]
-            hams.append(lax.ppermute(mine, "col", route) if flip or step else mine)
-    ham_ints = jnp.concatenate([h_rows.reshape(-1), h_cols.reshape(-1), h_flags.reshape(-1)])
-    it_ints = jnp.concatenate([x_cols.reshape(-1), x_flags.reshape(-1)])
-    ham_ints = lax.all_gather(ham_ints.reshape(1, 1, -1), "col", axis=0, tiled=True)[:, 0]
-    aim_ints = lax.all_gather(it_ints.reshape(1, 1, -1), "depth", axis=0, tiled=True)[:, 0]
-    it_ints = lax.all_gather(it_ints.reshape(1, 1, -1), "row", axis=0, tiled=True)[:, 0]
+            source = late if step % 2 and not flip else mine
+            hams.append(lax.ppermute(source, "col", route) if flip or step else mine)
+    ham_ints = ham_ints.reshape(-1, 3, ham_ints.shape[-1])
+    ham_keys = jnp.where(ham_ints[:, 2] > 0, ham_ints[:, 0] * 8 + ham_ints[:, 1], -1)
+    it_keys = jnp.where(it_ints[:, 0, 1] > 0, it_ints[:, 0, 0], -1).reshape(n_row, -1)
+    aim_keys = jnp.where(aim_ints[0, :, 1] > 0, aim_ints[0, :, 0], -2).reshape(-1)
     smem = pl.BlockSpec(memory_space=pltpu.SMEM)
     anywhere = pl.BlockSpec(memory_space=pl.ANY)
     vmem = pl.BlockSpec(memory_space=pltpu.VMEM)
@@ -121,13 +132,13 @@
         in_specs=[smem] * 4,
         out_specs=smem,
         name="pairs",
-    )(where, ham_ints, it_ints, aim_ints)
+    )(where, ham_keys, it_keys, aim_keys)
     results = x_cols.shape[3] * x_cols.shape[4]
     half_shape = jax.ShapeDtypeStruct((2 * results, block, block), jnp.bfloat16)
     sent, kept = pl.pallas_call(
         product_kernel,
         out_shape=(half_shape, half_shape),
-        in_specs=[smem, smem] + [anywhere] * 9,
+        in_specs=[smem] + [anywhere] * 9,
         out_specs=(vmem, vmem),
         scratch_shapes=[
             pltpu.VMEM((n_depth * results, block, block), jnp.float32),
@@ -138,7 +149,7 @@
         ],
         compiler_params=pltpu.CompilerParams(vmem_limit_bytes=24 << 20),
         name="products",
-    )(pairs, where, *[pltpu.with_memory_space_constraint(x, pltpu.HBM) for x in (iterate, hams[0])], *hams[1:])
+    )(*[pltpu.with_memory_space_constraint(x, pltpu.HBM) for x in (pairs, iterate, *hams)])
     near = lax.ppermute(sent, "depth", [(d, d ^ 1) for d in range(n_depth)])
     onward = kept[:results].astype(jnp.float32) + near[:results].astype(jnp.float32)
     far = lax.ppermute(onward.astype(jnp.bfloat16), "depth", [(d, d ^ 2) for d in range(n_depth)])

time: 184 us -> 191 us (1.038)
  waiting for transfers between devices: 32.6 us -> 55 us
  Pallas kernels: 17.4 us -> 5.99 us
  starting transfers between devices: 36.7 us -> 45.1 us
  local copies, waits for them, and re-layouts: 9.56 us -> 1.69 us
  between operations: 15.6 us -> 13.6 us
    unnamed x3 -> x0, blocking collectives: 62.5 us -> none
    all_gather x0 -> x3, blocking collectives: none -> 61.1 us  [the longest x1 24.4 us: body(): it_ints = lax.all_gather(it_ints, 'row', axis=0, tiled=True)]
    ppermute x7, waiting for transfers between devices: 16.9 us -> 38 us  [body(): hams.append(lax.ppermute(source, 'col', route) if flip or step else mine)]
    pallas_call x1, Pallas kernels: 14.7 us -> 3.37 us  [body(): pl.pallas_call(pair_kernel, out_shape=jax.ShapeDtypeStruct((512,), jnp.in...]
    ppermute x1, starting transfers between devices: 6.44 us -> 17.3 us  [body(): near = lax.ppermute(sent, 'depth', [(d, d ^ 1) for d in range(n_depth)])]
    unnamed x15 -> x10, local copies, waits for them, and re-layouts: 7.12 us -> 0.02 us
    unnamed x5 -> x0, other arithmetic: 4.14 us -> none
    squeeze x3 -> x0, local copies, waits for them, and re-layouts: 2.03 us -> none  [the longest x1 0.68 us: body(): lax.all_gather(it_ints.reshape(1, 1, -1), 'depth', axis=0, tiled=True)[:, 0]]
  transfers between devices with their start and end apart: 10 -> 10, of which waited for: 4 -> 6; matrix products, arithmetic and copies ran while one was open for 7% -> 2% of each run, Pallas kernels for 8% -> 2%
where the time goes in v2:
time: 191 us; the launch traced here: 187 us
  blocking collectives  61.1 us (32%)
  waiting for transfers between devices  55 us (29%)
  starting transfers between devices  45.1 us (24%)
  between operations  13.6 us (7%)
  Pallas kernels  5.99 us (3%)
  other arithmetic  5 us (3%)
    ppermute x7, waiting for transfers between devices, body(): hams.append(lax.ppermute(source, 'col', route) if flip or step else mine)  38 us
    ppermute x7, starting transfers between devices, body(): hams.append(lax.ppermute(source, 'col', route) if flip or step else mine)  25.6 us
    all_gather x1, blocking collectives, body(): it_ints = lax.all_gather(it_ints, 'row', axis=0, tiled=True)  24.4 us
    all_gather x1, blocking collectives, body(): ham_ints = lax.all_gather(ham_ints, 'col', axis=1, tiled=True)  23.4 us
    ppermute x1, starting transfers between devices, body(): near = lax.ppermute(sent, 'depth', [(d, d ^ 1) for d in range(n_depth)])  17.3 us
    ppermute x1, waiting for transfers between devices, body(): lax.ppermute(onward.astype(jnp.bfloat16), 'depth', [(d, d ^ 2) for d in r...  14.1 us
    all_gather x1, blocking collectives, body(): aim_ints = lax.all_gather(it_ints, 'depth', axis=1, tiled=True)  13.3 us
  transfers between devices with their start and end apart: 10, of which 6 were waited for; matrix products, arithmetic and copies ran while one was open for 2% of the time, Pallas kernels for 2%

profile of v2, /device:TPU:1, one launch (start us, length us, event | category | flops | bytes accessed | tf_op | source)
XLA Modules:
  0.0 187.5 jit_solution(13421704485522256469)
XLA Ops:
  6.5 0.7 all-gather.3.cloned.1.call-update
  7.3 0.7 pad_add_fusion
  8.0 0.7 fusion.4
  8.7 13.3 %all_gather.13 = s32[1,4,2,8,2]{3,4,2,0,1:T(2,128)S(1)} all-gather(s32[1,1,2,8,2]{3,4,2,0,1:T(2,128)S(1)} %get-tuple-element.18), channel_id=1, replica_groups=mesh['row'=16,'col'=8,'depth'=4] {'depth'}, dimensions={1}, use_global_device_ids=true | all-gather | bytes 640 | tf_op jit(solution)/shard_map/all_gather | solution.py:112
  22.0 24.4 %all_gather.14 = s32[16,1,2,8,2]{3,4,2,1,0:T(2,128)S(1)} all-gather(s32[1,1,2,8,2]{3,4,2,1,0:T(2,128)S(1)} %get-tuple-element.17), channel_id=1, replica_groups=mesh['row'=16,'col'=8,'depth'=4] {'row'}, dimensions={0}, use_global_device_ids=true | all-gather | bytes 2176 | tf_op jit(solution)/shard_map/all_gather | solution.py:113
  46.4 23.4 %all_gather.12 = s32[1,16,3,1,12]{4,3,2,0,1:T(1,128)S(1)} all-gather(s32[1,2,3,1,12]{4,3,2,0,1:T(1,128)S(1)} %copy.22), channel_id=1, replica_groups=mesh['row'=16,'col'=8,'depth'=4] {'col'}, dimensions={1}, use_global_device_ids=true | all-gather | bytes 2592 | tf_op jit(solution)/shard_map/all_gather | solution.py:110
  69.8 3.1 %collective-permute-start = (bf16[24,128,128]{2,1,0:T(8,128)(2,1)}, bf16[24,128,128]{2,1,0:T(8,128)(2,1)S(1)}, u32[]{:S(2)}, u32[]{:S(2)}) collective-permute-start(bf16[24,128,128]{2,1,0:T(8,128)(2,1)} %bitcast.28), channel_id=1, source_target_pairs={{0,4},{4,8},{8,12},{12,0},{16,20},{20,24},{24,28},{28,16},{1,5},{5... | collective-permute-start | bytes 2359304 | tf_op jit(solution)/shard_map/ppermute | solution.py:121
  72.9 3.4 %collective-permute-start.2 = (bf16[24,128,128]{2,1,0:T(8,128)(2,1)}, bf16[24,128,128]{2,1,0:T(8,128)(2,1)S(1)}, u32[]{:S(2)}, u32[]{:S(2)}) collective-permute-start(bf16[24,128,128]{2,1,0:T(8,128)(2,1)} %bitcast.29), channel_id=1, source_target_pairs={{0,12},{4,0},{8,4},{12,8},{16,28},{20,16},{24,20},{28,24},{1,13},{... | collective-permute-start | bytes 2359304 | tf_op jit(solution)/shard_map/ppermute | solution.py:121
  76.3 2.5 %collective-permute-start.1 = (bf16[24,128,128]{2,1,0:T(8,128)(2,1)}, bf16[24,128,128]{2,1,0:T(8,128)(2,1)S(1)}, u32[]{:S(2)}, u32[]{:S(2)}) collective-permute-start(bf16[24,128,128]{2,1,0:T(8,128)(2,1)} %bitcast.30), channel_id=1, source_target_pairs={{0,8},{4,12},{8,0},{12,4},{16,24},{20,28},{24,16},{28,20},{1,9},{5... | collective-permute-start | bytes 2359304 | tf_op jit(solution)/shard_map/ppermute | solution.py:121
  78.8 3.1 %collective-permute-start.3 = (bf16[24,128,128]{2,1,0:T(8,128)(2,1)}, bf16[24,128,128]{2,1,0:T(8,128)(2,1)S(1)}, u32[]{:S(2)}, u32[]{:S(2)}) collective-permute-start(bf16[24,128,128]{2,1,0:T(8,128)(2,1)} %bitcast.31), channel_id=1, source_target_pairs={{0,16},{4,20},{8,24},{12,28},{16,0},{20,4},{24,8},{28,12},{1,17},{... | collective-permute-start | bytes 2359304 | tf_op jit(solution)/shard_map/ppermute | solution.py:121
  81.9 2.8 %collective-permute-start.4 = (bf16[24,128,128]{2,1,0:T(8,128)(2,1)}, bf16[24,128,128]{2,1,0:T(8,128)(2,1)}, u32[]{:S(2)}, u32[]{:S(2)}) collective-permute-start(bf16[24,128,128]{2,1,0:T(8,128)(2,1)} %bitcast.32), channel_id=1, source_target_pairs={{0,20},{4,24},{8,28},{12,16},{16,4},{20,8},{24,12},{28,0},{1,21},{... | collective-permute-start | bytes 2359304 | tf_op jit(solution)/shard_map/ppermute | solution.py:121
  84.7 4.0 %collective-permute-start.5 = (bf16[24,128,128]{2,1,0:T(8,128)(2,1)}, bf16[24,128,128]{2,1,0:T(8,128)(2,1)}, u32[]{:S(2)}, u32[]{:S(2)}) collective-permute-start(bf16[24,128,128]{2,1,0:T(8,128)(2,1)} %bitcast.33), channel_id=1, source_target_pairs={{0,24},{4,28},{8,16},{12,20},{16,8},{20,12},{24,0},{28,4},{1,25},{... | collective-permute-start | bytes 2359304 | tf_op jit(solution)/shard_map/ppermute | solution.py:121
  88.8 6.7 %collective-permute-start.6 = (bf16[24,128,128]{2,1,0:T(8,128)(2,1)}, bf16[24,128,128]{2,1,0:T(8,128)(2,1)}, u32[]{:S(2)}, u32[]{:S(2)}) collective-permute-start(bf16[24,128,128]{2,1,0:T(8,128)(2,1)} %bitcast.34), channel_id=1, source_target_pairs={{0,28},{4,16},{8,20},{12,24},{16,12},{20,0},{24,4},{28,8},{1,29},{... | collective-permute-start | bytes 2359304 | tf_op jit(solution)/shard_map/ppermute | solution.py:121
  95.5 0.7 copy.29.iterate
  98.2 3.4 %pairs.1 = s32[512]{0:T(512)} custom-call(s32[2]{0:T(128)} %pad_add_fusion.2.where, s32[16,12]{1,0:T(8,128)} %fusion.3.ham, s32[16,16]{1,0:T(8,128)} %copy.29.iterate, s32[64]{0:T(128)} %select_n.27.aim), custom_call_target="tpu_custom_call" | custom-call | tf_op jit(solution)/shard_map/pairs/pallas_call | solution.py:129
  101.5 5.1 %collective-permute-done.1.rest_2_ = bf16[24,128,128]{2,1,0:T(8,128)(2,1)S(1)} collective-permute-done((bf16[24,128,128]{2,1,0:T(8,128)(2,1)}, bf16[24,128,128]{2,1,0:T(8,128)(2,1)S(1)}, u32[]{:S(2)}, u32[]{:S(2)}) %collective-permute-start.1) | collective-permute-done | bytes 786464 | tf_op jit(solution)/shard_map/ppermute | solution.py:121
  106.7 17.1 %collective-permute-done.5.rest_6_ = bf16[24,128,128]{2,1,0:T(8,128)(2,1)} collective-permute-done((bf16[24,128,128]{2,1,0:T(8,128)(2,1)}, bf16[24,128,128]{2,1,0:T(8,128)(2,1)}, u32[]{:S(2)}, u32[]{:S(2)}) %collective-permute-start.5) | collective-permute-done | bytes 786464 | tf_op jit(solution)/shard_map/ppermute | solution.py:121
  123.8 15.7 %collective-permute-done.6.rest_7_ = bf16[24,128,128]{2,1,0:T(8,128)(2,1)} collective-permute-done((bf16[24,128,128]{2,1,0:T(8,128)(2,1)}, bf16[24,128,128]{2,1,0:T(8,128)(2,1)}, u32[]{:S(2)}, u32[]{:S(2)}) %collective-permute-start.6) | collective-permute-done | bytes 786464 | tf_op jit(solution)/shard_map/ppermute | solution.py:121
  139.5 2.6 %products.1 = (bf16[32,128,128]{2,1,0:T(8,128)(2,1)S(1)}, bf16[32,128,128]{2,1,0:T(8,128)(2,1)S(1)}) custom-call(s32[512]{0:T(512)} %pairs.1, bf16[256,128,128]{2,1,0:T(8,128)(2,1)} %bitcast.27, bf16[24,128,128]{2,1,0:T(8,128)(2,1)} %bitcast.35, bf16[24,128,128]{2,1,0:T(8,128)(2,1)} %copy-done, bf16[24,128,128]{2,1,0:T(8,128)(2,1)} %copy-done.2, ...), custom_call_target="tpu_custom_call" | custom-call | tf_op jit(solution)/shard_map/products/pallas_call | solution.py:138
  142.2 17.3 %collective-permute-start.7 = (bf16[32,128,128]{2,1,0:T(8,128)(2,1)S(1)}, bf16[32,128,128]{2,1,0:T(8,128)(2,1)S(1)}, u32[]{:S(2)}, u32[]{:S(2)}) collective-permute-start(bf16[32,128,128]{2,1,0:T(8,128)(2,1)S(1)} %get-tuple-element.16), channel_id=1, source_target_pairs={{0,1},{1,0},{2,3},{3,2},{4,5},{5,4},{6,7},{7,6},{8,9},{9,8},{10,11... | collective-permute-start | bytes 3145736 | tf_op jit(solution)/shard_map/ppermute | solution.py:153
  159.4 2.3 %collective-permute-done.7 = bf16[32,128,128]{2,1,0:T(8,128)(2,1)S(1)} collective-permute-done((bf16[32,128,128]{2,1,0:T(8,128)(2,1)S(1)}, bf16[32,128,128]{2,1,0:T(8,128)(2,1)S(1)}, u32[]{:S(2)}, u32[]{:S(2)}) %collective-permute-start.7) | collective-permute-done | bytes 1048608 | tf_op jit(solution)/shard_map/ppermute | solution.py:153
  161.9 2.3 %collective-permute-start.8 = (bf16[16,128,128]{2,1,0:T(8,128)(2,1)S(1)}, bf16[16,128,128]{2,1,0:T(8,128)(2,1)S(1)}, u32[]{:S(2)}, u32[]{:S(2)}) collective-permute-start(bf16[16,128,128]{2,1,0:T(8,128)(2,1)S(1)} %add_convert_fusion), channel_id=1, source_target_pairs={{0,2},{1,3},{2,0},{3,1},{4,6},{5,7},{6,4},{7,5},{8,10},{9,11},{10,... | collective-permute-start | bytes 1572872 | tf_op jit(solution)/shard_map/ppermute | solution.py:155
  164.3 14.1 %collective-permute-done.8 = bf16[16,128,128]{2,1,0:T(8,128)(2,1)S(1)} collective-permute-done((bf16[16,128,128]{2,1,0:T(8,128)(2,1)S(1)}, bf16[16,128,128]{2,1,0:T(8,128)(2,1)S(1)}, u32[]{:S(2)}, u32[]{:S(2)}) %collective-permute-start.8) | collective-permute-done | bytes 524320 | tf_op jit(solution)/shard_map/ppermute | solution.py:155
  178.4 2.2 %fusion.1 = bf16[16,128,128]{2,1,0:T(8,128)(2,1)} fusion(bf16[16,128,128]{2,1,0:T(8,128)(2,1)S(1)} %collective-permute-done.8, bf16[32,128,128]{2,1,0:T(8,128)(2,1)S(1)} %collective-permute-done.7, bf16[1,1,1,8,2,128,128]{6,5,4,3,2,1,0:T(8,128)(2,1)} %param.15, f32[16]{0:T(128)S(1)} %convert_element_type.47, bf16[32,128,128]{2,1,0:T(8,128)(2,1)S(1)} %get-tuple-element.15), kind=kLoop, calls=%fused_computation.2 | loop fusion | flops 2621440 | bytes 2621504 | tf_op jit(solution)/shard_map/convert_element_type | solution.py:161
  (29 shorter events, 2.5 us)
Async XLA Ops:
  6.5 133.0 %all-gather.3.cloned.1.call-start = ((), (), s32[]{:S(2)}) async-start(), calls=%async_computation | async-start | bytes 8912896 | tf_op jit(solution)/shard_map/all_gather | solution.py:107
  7.3 156.9 %copy-start.4 = (s32[1,1,1,8,2]{3,4,2,1,0:T(2,128)S(1)}, s32[1,1,1,8,2]{3,4,2,1,0:T(2,128)}, u32[]{:S(2)}) copy-start(s32[1,1,1,8,2]{3,4,2,1,0:T(2,128)} %param.14) | copy-start | bytes 196
  69.8 14.9 %collective-permute-start = (bf16[24,128,128]{2,1,0:T(8,128)(2,1)}, bf16[24,128,128]{2,1,0:T(8,128)(2,1)S(1)}, u32[]{:S(2)}, u32[]{:S(2)}) collective-permute-start(bf16[24,128,128]{2,1,0:T(8,128)(2,1)} %bitcast.28), channel_id=1, source_target_pairs={{0,4},{4,8},{8,12},{12,0},{16,20},{20,24},{24,28},{28,16},{1,5},{5... | collective-permute-start | bytes 2359304 | tf_op jit(solution)/shard_map/ppermute | solution.py:121
  72.9 15.8 %collective-permute-start.2 = (bf16[24,128,128]{2,1,0:T(8,128)(2,1)}, bf16[24,128,128]{2,1,0:T(8,128)(2,1)S(1)}, u32[]{:S(2)}, u32[]{:S(2)}) collective-permute-start(bf16[24,128,128]{2,1,0:T(8,128)(2,1)} %bitcast.29), channel_id=1, source_target_pairs={{0,12},{4,0},{8,4},{12,8},{16,28},{20,16},{24,20},{28,24},{1,13},{... | collective-permute-start | bytes 2359304 | tf_op jit(solution)/shard_map/ppermute | solution.py:121
  76.3 30.4 %collective-permute-start.1 = (bf16[24,128,128]{2,1,0:T(8,128)(2,1)}, bf16[24,128,128]{2,1,0:T(8,128)(2,1)S(1)}, u32[]{:S(2)}, u32[]{:S(2)}) collective-permute-start(bf16[24,128,128]{2,1,0:T(8,128)(2,1)} %bitcast.30), channel_id=1, source_target_pairs={{0,8},{4,12},{8,0},{12,4},{16,24},{20,28},{24,16},{28,20},{1,9},{5... | collective-permute-start | bytes 2359304 | tf_op jit(solution)/shard_map/ppermute | solution.py:121
  78.8 27.8 %collective-permute-start.3 = (bf16[24,128,128]{2,1,0:T(8,128)(2,1)}, bf16[24,128,128]{2,1,0:T(8,128)(2,1)S(1)}, u32[]{:S(2)}, u32[]{:S(2)}) collective-permute-start(bf16[24,128,128]{2,1,0:T(8,128)(2,1)} %bitcast.31), channel_id=1, source_target_pairs={{0,16},{4,20},{8,24},{12,28},{16,0},{20,4},{24,8},{28,12},{1,17},{... | collective-permute-start | bytes 2359304 | tf_op jit(solution)/shard_map/ppermute | solution.py:121
  81.9 24.8 %collective-permute-start.4 = (bf16[24,128,128]{2,1,0:T(8,128)(2,1)}, bf16[24,128,128]{2,1,0:T(8,128)(2,1)}, u32[]{:S(2)}, u32[]{:S(2)}) collective-permute-start(bf16[24,128,128]{2,1,0:T(8,128)(2,1)} %bitcast.32), channel_id=1, source_target_pairs={{0,20},{4,24},{8,28},{12,16},{16,4},{20,8},{24,12},{28,0},{1,21},{... | collective-permute-start | bytes 2359304 | tf_op jit(solution)/shard_map/ppermute | solution.py:121
  84.7 54.8 %copy-start = (bf16[24,128,128]{2,1,0:T(8,128)(2,1)}, bf16[24,128,128]{2,1,0:T(8,128)(2,1)S(1)}, u32[]{:S(2)}) copy-start(bf16[24,128,128]{2,1,0:T(8,128)(2,1)S(1)} %collective-permute-done.rest_1_) | copy-start | bytes 2359300
  84.7 39.1 %collective-permute-start.5 = (bf16[24,128,128]{2,1,0:T(8,128)(2,1)}, bf16[24,128,128]{2,1,0:T(8,128)(2,1)}, u32[]{:S(2)}, u32[]{:S(2)}) collective-permute-start(bf16[24,128,128]{2,1,0:T(8,128)(2,1)} %bitcast.33), channel_id=1, source_target_pairs={{0,24},{4,28},{8,16},{12,20},{16,8},{20,12},{24,0},{28,4},{1,25},{... | collective-permute-start | bytes 2359304 | tf_op jit(solution)/shard_map/ppermute | solution.py:121
  88.8 50.8 %copy-start.1 = (bf16[24,128,128]{2,1,0:T(8,128)(2,1)}, bf16[24,128,128]{2,1,0:T(8,128)(2,1)S(1)}, u32[]{:S(2)}) copy-start(bf16[24,128,128]{2,1,0:T(8,128)(2,1)S(1)} %collective-permute-done.2.rest_3_) | copy-start | bytes 2359300
  88.8 50.7 %collective-permute-start.6 = (bf16[24,128,128]{2,1,0:T(8,128)(2,1)}, bf16[24,128,128]{2,1,0:T(8,128)(2,1)}, u32[]{:S(2)}, u32[]{:S(2)}) collective-permute-start(bf16[24,128,128]{2,1,0:T(8,128)(2,1)} %bitcast.34), channel_id=1, source_target_pairs={{0,28},{4,16},{8,20},{12,24},{16,12},{20,0},{24,4},{28,8},{1,29},{... | collective-permute-start | bytes 2359304 | tf_op jit(solution)/shard_map/ppermute | solution.py:121
  106.6 32.9 %copy-start.2 = (bf16[24,128,128]{2,1,0:T(8,128)(2,1)}, bf16[24,128,128]{2,1,0:T(8,128)(2,1)S(1)}, u32[]{:S(2)}) copy-start(bf16[24,128,128]{2,1,0:T(8,128)(2,1)S(1)} %collective-permute-done.1.rest_2_) | copy-start | bytes 2359300
  106.6 32.9 %copy-start.3 = (bf16[24,128,128]{2,1,0:T(8,128)(2,1)}, bf16[24,128,128]{2,1,0:T(8,128)(2,1)S(1)}, u32[]{:S(2)}) copy-start(bf16[24,128,128]{2,1,0:T(8,128)(2,1)S(1)} %collective-permute-done.3.rest_4_) | copy-start | bytes 2359300
  142.2 19.6 %collective-permute-start.7 = (bf16[32,128,128]{2,1,0:T(8,128)(2,1)S(1)}, bf16[32,128,128]{2,1,0:T(8,128)(2,1)S(1)}, u32[]{:S(2)}, u32[]{:S(2)}) collective-permute-start(bf16[32,128,128]{2,1,0:T(8,128)(2,1)S(1)} %get-tuple-element.16), channel_id=1, source_target_pairs={{0,1},{1,0},{2,3},{3,2},{4,5},{5,4},{6,7},{7,6},{8,9},{9,8},{10,11... | collective-permute-start | bytes 3145736 | tf_op jit(solution)/shard_map/ppermute | solution.py:153
  161.9 16.5 %collective-permute-start.8 = (bf16[16,128,128]{2,1,0:T(8,128)(2,1)S(1)}, bf16[16,128,128]{2,1,0:T(8,128)(2,1)S(1)}, u32[]{:S(2)}, u32[]{:S(2)}) collective-permute-start(bf16[16,128,128]{2,1,0:T(8,128)(2,1)S(1)} %add_convert_fusion), channel_id=1, source_target_pairs={{0,2},{1,3},{2,0},{3,1},{4,6},{5,7},{6,4},{7,5},{8,10},{9,11},{10,... | collective-permute-start | bytes 1572872 | tf_op jit(solution)/shard_map/ppermute | solution.py:155
Sparse Core Ops, SparseCore 0:
  9.4 111.4 all-gather.2

commit v3 on v2

--- a/solution.py
+++ b/solution.py
@@ -106,19 +106,18 @@
     where = jnp.stack([lax.axis_index("col"), lax.axis_index("depth")]).astype(jnp.int32)
     iterate = lax.all_gather(x_blocks[0, 0, 0], "row", axis=0)
     iterate = iterate.reshape(-1, block, block)
-    ham_ints = jnp.stack([h_rows, h_cols, h_flags], axis=2)
-    ham_ints = lax.all_gather(ham_ints, "col", axis=1, tiled=True)
-    it_ints = jnp.concatenate([x_cols, x_flags], axis=2)
-    aim_ints = lax.all_gather(it_ints, "depth", axis=1, tiled=True)
-    it_ints = lax.all_gather(it_ints, "row", axis=0, tiled=True)
     mine = h_blocks[0].reshape(-1, block, block)
-    late, ham_ints, aim_ints, it_ints = lax.optimization_barrier((mine, ham_ints, aim_ints, it_ints))
     hams = []
     for flip in range(2):
         for step in range(n_col // 2):
             route = [(c, ((c // 4) ^ flip) * 4 + (c % 4 + step) % 4) for c in range(n_col)]
-            source = late if step % 2 and not flip else mine
-            hams.append(lax.ppermute(source, "col", route) if flip or step else mine)
+            hams.append(lax.ppermute(mine, "col", route) if flip or step else mine)
+    ham_ints = jnp.stack([h_rows, h_cols, h_flags], axis=2)
+    it_ints = jnp.concatenate([x_cols, x_flags], axis=2)
+    hams[4], ham_ints, it_ints = lax.optimization_barrier((hams[4], ham_ints, it_ints))
+    ham_ints = lax.all_gather(ham_ints, "col", axis=1, tiled=True)
+    aim_ints = lax.all_gather(it_ints, "depth", axis=1, tiled=True)
+    it_ints = lax.all_gather(it_ints, "row", axis=0, tiled=True)
     ham_ints = ham_ints.reshape(-1, 3, ham_ints.shape[-1])
     ham_keys = jnp.where(ham_ints[:, 2] > 0, ham_ints[:, 0] * 8 + ham_ints[:, 1], -1)
     it_keys = jnp.where(it_ints[:, 0, 1] > 0, it_ints[:, 0, 0], -1).reshape(n_row, -1)

time: 191 us -> 199 us (1.042); the launches traced: 187 us -> 198 us
  waiting for transfers between devices: 55 us -> 16.6 us
  starting transfers between devices: 45.1 us -> 70.7 us
  blocking collectives: 61.1 us -> 80.4 us
  Pallas kernels: 5.99 us -> 8.56 us
    ppermute x7, waiting for transfers between devices: 38 us -> 0.02 us  [body(): hams.append(lax.ppermute(mine, 'col', route) if flip or step else mine)]
    ppermute x7, starting transfers between devices: 25.6 us -> 61.1 us  [body(): hams.append(lax.ppermute(mine, 'col', route) if flip or step else mine)]
    all_gather x1, blocking collectives: 23.4 us -> 34.8 us  [body(): ham_ints = lax.all_gather(ham_ints, 'col', axis=1, tiled=True)]
    ppermute x1, starting transfers between devices: 17.3 us -> 6.88 us  [body(): near = lax.ppermute(sent, 'depth', [(d, d ^ 1) for d in range(n_depth)])]
    all_gather x1, blocking collectives: 24.4 us -> 31.6 us  [body(): it_ints = lax.all_gather(it_ints, 'row', axis=0, tiled=True)]
  transfers between devices with their start and end apart: 10 -> 10, of which waited for: 6 -> 2; matrix products, arithmetic and copies ran while one was open for 2% -> 2% of each run, Pallas kernels for 2% -> 2%
where the time goes in v3:
time: 199 us; the launch traced here: 198 us
  blocking collectives  80.4 us (40%)
  starting transfers between devices  70.7 us (36%)
  waiting for transfers between devices  16.6 us (8%)
  between operations  13.6 us (7%)
  Pallas kernels  8.56 us (4%)
  other arithmetic  5.06 us (3%)
  local copies, waits for them, and re-layouts  2.79 us (1%)
    ppermute x7, starting transfers between devices, body(): hams.append(lax.ppermute(mine, 'col', route) if flip or step else mine)  61.1 us
    all_gather x1, blocking collectives, body(): ham_ints = lax.all_gather(ham_ints, 'col', axis=1, tiled=True)  34.8 us
    all_gather x1, blocking collectives, body(): it_ints = lax.all_gather(it_ints, 'row', axis=0, tiled=True)  31.6 us
    all_gather x1, blocking collectives, body(): aim_ints = lax.all_gather(it_ints, 'depth', axis=1, tiled=True)  14 us
    ppermute x1, waiting for transfers between devices, body(): lax.ppermute(onward.astype(jnp.bfloat16), 'depth', [(d, d ^ 2) for d in r...  13.6 us
    ppermute x1, starting transfers between devices, body(): near = lax.ppermute(sent, 'depth', [(d, d ^ 1) for d in range(n_depth)])  6.88 us
    pallas_call x1, Pallas kernels, body(): pl.pallas_call(pair_kernel, out_shape=jax.ShapeDtypeStruct((512,), jnp.in...  4.68 us
  transfers between devices with their start and end apart: 10, of which 2 were waited for; matrix products, arithmetic and copies ran while one was open for 2% of the time, Pallas kernels for 2%

profile of v3, /device:TPU:1, one launch (start us, length us, event | category | flops | bytes accessed | tf_op | source)
XLA Modules:
  0.0 197.7 jit_solution(4865926733892326068)
XLA Ops:
  6.5 0.7 all-gather.3.cloned.1.call-update
  7.3 4.0 %collective-permute-start = (bf16[24,128,128]{2,1,0:T(8,128)(2,1)}, bf16[24,128,128]{2,1,0:T(8,128)(2,1)S(1)}, u32[]{:S(2)}, u32[]{:S(2)}) collective-permute-start(bf16[24,128,128]{2,1,0:T(8,128)(2,1)} %bitcast.25), channel_id=1, source_target_pairs={{0,16},{4,20},{8,24},{12,28},{16,0},{20,4},{24,8},{28,12},{1,17},{... | collective-permute-start | bytes 2359304 | tf_op jit(solution)/shard_map/ppermute | solution.py:114
  11.2 3.2 %collective-permute-start.1 = (bf16[24,128,128]{2,1,0:T(8,128)(2,1)}, bf16[24,128,128]{2,1,0:T(8,128)(2,1)S(1)}, u32[]{:S(2)}, u32[]{:S(2)}) collective-permute-start(bf16[24,128,128]{2,1,0:T(8,128)(2,1)} %bitcast.26), channel_id=1, source_target_pairs={{0,4},{4,8},{8,12},{12,0},{16,20},{20,24},{24,28},{28,16},{1,5},{5... | collective-permute-start | bytes 2359304 | tf_op jit(solution)/shard_map/ppermute | solution.py:114
  14.4 4.5 %collective-permute-start.2 = (bf16[24,128,128]{2,1,0:T(8,128)(2,1)}, bf16[24,128,128]{2,1,0:T(8,128)(2,1)S(1)}, u32[]{:S(2)}, u32[]{:S(2)}) collective-permute-start(bf16[24,128,128]{2,1,0:T(8,128)(2,1)} %bitcast.27), channel_id=1, source_target_pairs={{0,8},{4,12},{8,0},{12,4},{16,24},{20,28},{24,16},{28,20},{1,9},{5... | collective-permute-start | bytes 2359304 | tf_op jit(solution)/shard_map/ppermute | solution.py:114
  19.0 3.0 %collective-permute-start.3 = (bf16[24,128,128]{2,1,0:T(8,128)(2,1)}, bf16[24,128,128]{2,1,0:T(8,128)(2,1)S(1)}, u32[]{:S(2)}, u32[]{:S(2)}) collective-permute-start(bf16[24,128,128]{2,1,0:T(8,128)(2,1)} %bitcast.28), channel_id=1, source_target_pairs={{0,12},{4,0},{8,4},{12,8},{16,28},{20,16},{24,20},{28,24},{1,13},{... | collective-permute-start | bytes 2359304 | tf_op jit(solution)/shard_map/ppermute | solution.py:114
  22.0 2.3 %collective-permute-start.4 = (bf16[24,128,128]{2,1,0:T(8,128)(2,1)}, bf16[24,128,128]{2,1,0:T(8,128)(2,1)}, u32[]{:S(2)}, u32[]{:S(2)}) collective-permute-start(bf16[24,128,128]{2,1,0:T(8,128)(2,1)} %bitcast.29), channel_id=1, source_target_pairs={{0,20},{4,24},{8,28},{12,16},{16,4},{20,8},{24,12},{28,0},{1,21},{... | collective-permute-start | bytes 2359304 | tf_op jit(solution)/shard_map/ppermute | solution.py:114
  24.3 0.7 pad_add_fusion.1
  25.0 0.7 pad_add_fusion
  25.7 8.7 %collective-permute-start.5 = (bf16[24,128,128]{2,1,0:T(8,128)(2,1)}, bf16[24,128,128]{2,1,0:T(8,128)(2,1)}, u32[]{:S(2)}, u32[]{:S(2)}) collective-permute-start(bf16[24,128,128]{2,1,0:T(8,128)(2,1)} %bitcast.30), channel_id=1, source_target_pairs={{0,24},{4,28},{8,16},{12,20},{16,8},{20,12},{24,0},{28,4},{1,25},{... | collective-permute-start | bytes 2359304 | tf_op jit(solution)/shard_map/ppermute | solution.py:114
  34.4 35.5 %collective-permute-start.6 = (bf16[24,128,128]{2,1,0:T(8,128)(2,1)}, bf16[24,128,128]{2,1,0:T(8,128)(2,1)}, u32[]{:S(2)}, u32[]{:S(2)}) collective-permute-start(bf16[24,128,128]{2,1,0:T(8,128)(2,1)} %bitcast.31), channel_id=1, source_target_pairs={{0,28},{4,16},{8,20},{12,24},{16,12},{20,0},{24,4},{28,8},{1,29},{... | collective-permute-start | bytes 2359304 | tf_op jit(solution)/shard_map/ppermute | solution.py:114
  69.8 0.7 pad_add_fusion.2.where
  70.5 31.6 %all_gather.13 = s32[16,1,2,8,2]{3,4,2,1,0:T(2,128)S(1)} all-gather(s32[1,1,2,8,2]{3,4,2,1,0:T(2,128)S(1)} %pad_add_fusion.1), channel_id=1, replica_groups=mesh['row'=16,'col'=8,'depth'=4] {'row'}, dimensions={0}, use_global_device_ids=true | all-gather | bytes 2176 | tf_op jit(solution)/shard_map/all_gather | solution.py:120
  102.2 0.7 copy.27.iterate
  102.8 14.0 %all_gather.14 = s32[1,4,2,8,2]{3,4,2,0,1:T(2,128)S(1)} all-gather(s32[1,1,2,8,2]{3,4,2,0,1:T(2,128)S(1)} %bitcast.35), channel_id=1, replica_groups=mesh['row'=16,'col'=8,'depth'=4] {'depth'}, dimensions={1}, use_global_device_ids=true | all-gather | bytes 640 | tf_op jit(solution)/shard_map/all_gather | solution.py:119
  117.0 0.7 select_n.27.aim
  117.6 34.8 %all_gather.12 = s32[1,16,3,1,12]{4,3,2,0,1:T(1,128)S(1)} all-gather(s32[1,2,3,1,12]{4,3,2,0,1:T(1,128)S(1)} %copy.22), channel_id=1, replica_groups=mesh['row'=16,'col'=8,'depth'=4] {'col'}, dimensions={1}, use_global_device_ids=true | all-gather | bytes 2592 | tf_op jit(solution)/shard_map/all_gather | solution.py:118
  153.0 4.7 %pairs.1 = s32[512]{0:T(512)} custom-call(s32[2]{0:T(128)} %pad_add_fusion.2.where, s32[16,12]{1,0:T(8,128)} %fusion.3.ham, s32[16,16]{1,0:T(8,128)} %copy.27.iterate, s32[64]{0:T(128)} %select_n.27.aim), custom_call_target="tpu_custom_call" | custom-call | tf_op jit(solution)/shard_map/pairs/pallas_call | solution.py:128
  157.8 0.9 copy-done.3
  158.9 3.9 %products.1 = (bf16[32,128,128]{2,1,0:T(8,128)(2,1)S(1)}, bf16[32,128,128]{2,1,0:T(8,128)(2,1)S(1)}) custom-call(s32[512]{0:T(512)} %pairs.1, bf16[256,128,128]{2,1,0:T(8,128)(2,1)} %bitcast.24, bf16[24,128,128]{2,1,0:T(8,128)(2,1)} %bitcast.32, bf16[24,128,128]{2,1,0:T(8,128)(2,1)} %copy-done.1, bf16[24,128,128]{2,1,0:T(8,128)(2,1)} %copy-done.2, ...), custom_call_target="tpu_custom_call" | custom-call | tf_op jit(solution)/shard_map/products/pallas_call | solution.py:137
  162.8 6.9 %collective-permute-start.7 = (bf16[32,128,128]{2,1,0:T(8,128)(2,1)S(1)}, bf16[32,128,128]{2,1,0:T(8,128)(2,1)S(1)}, u32[]{:S(2)}, u32[]{:S(2)}) collective-permute-start(bf16[32,128,128]{2,1,0:T(8,128)(2,1)S(1)} %get-tuple-element.14), channel_id=1, source_target_pairs={{0,1},{1,0},{2,3},{3,2},{4,5},{5,4},{6,7},{7,6},{8,9},{9,8},{10,11... | collective-permute-start | bytes 3145736 | tf_op jit(solution)/shard_map/ppermute | solution.py:152
  169.7 2.3 %collective-permute-done.7 = bf16[32,128,128]{2,1,0:T(8,128)(2,1)S(1)} collective-permute-done((bf16[32,128,128]{2,1,0:T(8,128)(2,1)S(1)}, bf16[32,128,128]{2,1,0:T(8,128)(2,1)S(1)}, u32[]{:S(2)}, u32[]{:S(2)}) %collective-permute-start.7) | collective-permute-done | bytes 1048608 | tf_op jit(solution)/shard_map/ppermute | solution.py:152
  172.1 2.7 %collective-permute-start.8 = (bf16[16,128,128]{2,1,0:T(8,128)(2,1)S(1)}, bf16[16,128,128]{2,1,0:T(8,128)(2,1)S(1)}, u32[]{:S(2)}, u32[]{:S(2)}) collective-permute-start(bf16[16,128,128]{2,1,0:T(8,128)(2,1)S(1)} %add_convert_fusion), channel_id=1, source_target_pairs={{0,2},{1,3},{2,0},{3,1},{4,6},{5,7},{6,4},{7,5},{8,10},{9,11},{10,... | collective-permute-start | bytes 1572872 | tf_op jit(solution)/shard_map/ppermute | solution.py:154
  175.0 13.6 %collective-permute-done.8 = bf16[16,128,128]{2,1,0:T(8,128)(2,1)S(1)} collective-permute-done((bf16[16,128,128]{2,1,0:T(8,128)(2,1)S(1)}, bf16[16,128,128]{2,1,0:T(8,128)(2,1)S(1)}, u32[]{:S(2)}, u32[]{:S(2)}) %collective-permute-start.8) | collective-permute-done | bytes 524320 | tf_op jit(solution)/shard_map/ppermute | solution.py:154
  188.6 2.2 %fusion.1 = bf16[16,128,128]{2,1,0:T(8,128)(2,1)} fusion(bf16[16,128,128]{2,1,0:T(8,128)(2,1)S(1)} %collective-permute-done.8, bf16[32,128,128]{2,1,0:T(8,128)(2,1)S(1)} %collective-permute-done.7, bf16[1,1,1,8,2,128,128]{6,5,4,3,2,1,0:T(8,128)(2,1)} %param.15, f32[16]{0:T(128)S(1)} %convert_element_type.47, bf16[32,128,128]{2,1,0:T(8,128)(2,1)S(1)} %get-tuple-element.13), kind=kLoop, calls=%fused_computation.2 | loop fusion | flops 2621440 | bytes 2621504 | tf_op jit(solution)/shard_map/convert_element_type | solution.py:160
  (29 shorter events, 1.4 us)
Async XLA Ops:
  6.5 151.3 %all-gather.3.cloned.1.call-start = ((), (), s32[]{:S(2)}) async-start(), calls=%async_computation | async-start | bytes 8912896 | tf_op jit(solution)/shard_map/all_gather | solution.py:107
  7.3 167.6 %copy-start.4 = (s32[1,1,1,8,2]{3,4,2,1,0:T(2,128)S(1)}, s32[1,1,1,8,2]{3,4,2,1,0:T(2,128)}, u32[]{:S(2)}) copy-start(s32[1,1,1,8,2]{3,4,2,1,0:T(2,128)} %param.14) | copy-start | bytes 196
  7.3 18.4 %collective-permute-start = (bf16[24,128,128]{2,1,0:T(8,128)(2,1)}, bf16[24,128,128]{2,1,0:T(8,128)(2,1)S(1)}, u32[]{:S(2)}, u32[]{:S(2)}) collective-permute-start(bf16[24,128,128]{2,1,0:T(8,128)(2,1)} %bitcast.25), channel_id=1, source_target_pairs={{0,16},{4,20},{8,24},{12,28},{16,0},{20,4},{24,8},{28,12},{1,17},{... | collective-permute-start | bytes 2359304 | tf_op jit(solution)/shard_map/ppermute | solution.py:114
  11.2 23.1 %collective-permute-start.1 = (bf16[24,128,128]{2,1,0:T(8,128)(2,1)}, bf16[24,128,128]{2,1,0:T(8,128)(2,1)S(1)}, u32[]{:S(2)}, u32[]{:S(2)}) collective-permute-start(bf16[24,128,128]{2,1,0:T(8,128)(2,1)} %bitcast.26), channel_id=1, source_target_pairs={{0,4},{4,8},{8,12},{12,0},{16,20},{20,24},{24,28},{28,16},{1,5},{5... | collective-permute-start | bytes 2359304 | tf_op jit(solution)/shard_map/ppermute | solution.py:114
  14.4 143.3 %collective-permute-start.2 = (bf16[24,128,128]{2,1,0:T(8,128)(2,1)}, bf16[24,128,128]{2,1,0:T(8,128)(2,1)S(1)}, u32[]{:S(2)}, u32[]{:S(2)}) collective-permute-start(bf16[24,128,128]{2,1,0:T(8,128)(2,1)} %bitcast.27), channel_id=1, source_target_pairs={{0,8},{4,12},{8,0},{12,4},{16,24},{20,28},{24,16},{28,20},{1,9},{5... | collective-permute-start | bytes 2359304 | tf_op jit(solution)/shard_map/ppermute | solution.py:114
  19.0 138.8 %collective-permute-start.3 = (bf16[24,128,128]{2,1,0:T(8,128)(2,1)}, bf16[24,128,128]{2,1,0:T(8,128)(2,1)S(1)}, u32[]{:S(2)}, u32[]{:S(2)}) collective-permute-start(bf16[24,128,128]{2,1,0:T(8,128)(2,1)} %bitcast.28), channel_id=1, source_target_pairs={{0,12},{4,0},{8,4},{12,8},{16,28},{20,16},{24,20},{28,24},{1,13},{... | collective-permute-start | bytes 2359304 | tf_op jit(solution)/shard_map/ppermute | solution.py:114
  22.0 135.8 %collective-permute-start.4 = (bf16[24,128,128]{2,1,0:T(8,128)(2,1)}, bf16[24,128,128]{2,1,0:T(8,128)(2,1)}, u32[]{:S(2)}, u32[]{:S(2)}) collective-permute-start(bf16[24,128,128]{2,1,0:T(8,128)(2,1)} %bitcast.29), channel_id=1, source_target_pairs={{0,20},{4,24},{8,28},{12,16},{16,4},{20,8},{24,12},{28,0},{1,21},{... | collective-permute-start | bytes 2359304 | tf_op jit(solution)/shard_map/ppermute | solution.py:114
  25.7 133.0 %copy-start = (bf16[24,128,128]{2,1,0:T(8,128)(2,1)}, bf16[24,128,128]{2,1,0:T(8,128)(2,1)S(1)}, u32[]{:S(2)}) copy-start(bf16[24,128,128]{2,1,0:T(8,128)(2,1)S(1)} %collective-permute-done.rest_4_) | copy-start | bytes 2359300
  25.7 132.1 %collective-permute-start.5 = (bf16[24,128,128]{2,1,0:T(8,128)(2,1)}, bf16[24,128,128]{2,1,0:T(8,128)(2,1)}, u32[]{:S(2)}, u32[]{:S(2)}) collective-permute-start(bf16[24,128,128]{2,1,0:T(8,128)(2,1)} %bitcast.30), channel_id=1, source_target_pairs={{0,24},{4,28},{8,16},{12,20},{16,8},{20,12},{24,0},{28,4},{1,25},{... | collective-permute-start | bytes 2359304 | tf_op jit(solution)/shard_map/ppermute | solution.py:114
  34.4 124.3 %copy-start.1 = (bf16[24,128,128]{2,1,0:T(8,128)(2,1)}, bf16[24,128,128]{2,1,0:T(8,128)(2,1)S(1)}, u32[]{:S(2)}) copy-start(bf16[24,128,128]{2,1,0:T(8,128)(2,1)S(1)} %collective-permute-done.1.rest_1_) | copy-start | bytes 2359300
  34.4 123.4 %collective-permute-start.6 = (bf16[24,128,128]{2,1,0:T(8,128)(2,1)}, bf16[24,128,128]{2,1,0:T(8,128)(2,1)}, u32[]{:S(2)}, u32[]{:S(2)}) collective-permute-start(bf16[24,128,128]{2,1,0:T(8,128)(2,1)} %bitcast.31), channel_id=1, source_target_pairs={{0,28},{4,16},{8,20},{12,24},{16,12},{20,0},{24,4},{28,8},{1,29},{... | collective-permute-start | bytes 2359304 | tf_op jit(solution)/shard_map/ppermute | solution.py:114
  157.7 1.2 copy-start.2
  157.7 0.9 copy-start.3
  162.8 9.2 %collective-permute-start.7 = (bf16[32,128,128]{2,1,0:T(8,128)(2,1)S(1)}, bf16[32,128,128]{2,1,0:T(8,128)(2,1)S(1)}, u32[]{:S(2)}, u32[]{:S(2)}) collective-permute-start(bf16[32,128,128]{2,1,0:T(8,128)(2,1)S(1)} %get-tuple-element.14), channel_id=1, source_target_pairs={{0,1},{1,0},{2,3},{3,2},{4,5},{5,4},{6,7},{7,6},{8,9},{9,8},{10,11... | collective-permute-start | bytes 3145736 | tf_op jit(solution)/shard_map/ppermute | solution.py:152
  172.1 16.5 %collective-permute-start.8 = (bf16[16,128,128]{2,1,0:T(8,128)(2,1)S(1)}, bf16[16,128,128]{2,1,0:T(8,128)(2,1)S(1)}, u32[]{:S(2)}, u32[]{:S(2)}) collective-permute-start(bf16[16,128,128]{2,1,0:T(8,128)(2,1)S(1)} %add_convert_fusion), channel_id=1, source_target_pairs={{0,2},{1,3},{2,0},{3,1},{4,6},{5,7},{6,4},{7,5},{8,10},{9,11},{10,... | collective-permute-start | bytes 1572872 | tf_op jit(solution)/shard_map/ppermute | solution.py:154
Sparse Core Ops, SparseCore 0:
  9.4 111.5 all-gather.2

commit v4 on v3

v4 whole, which is shorter than its diff:
```python
import jax
import jax.numpy as jnp
from jax import lax
from jax.experimental import pallas as pl
from jax.experimental.pallas import tpu as pltpu
from jax.sharding import PartitionSpec as P

WINDOW = 16


def key_kernel(*refs):
    hams, (keys, slab, sem) = refs[:8], refs[8:]
    tail = slab.shape[1]
    copies = [
        pltpu.make_async_copy(ham.at[pl.ds(ham.shape[0] - tail, tail)], slab.at[k], sem.at[k])
        for k, ham in enumerate(hams)
    ]
    for copy in copies:
        copy.start()
    for k, copy in enumerate(copies):
        copy.wait()
        held = slab[k].astype(jnp.float32)
        place = jnp.where(held[4:6] > 0, held[0:2] * 8 + held[2:4], -1.0)
        keys[2 * k : 2 * k + 2] = place.astype(jnp.int32)


def pair_kernel(where, ham, iterate, aim, pairs):
    pieces = ham.shape[0]
    slots = 12
    per_col = pieces // 8
    width = iterate.shape[1]
    near = where[0] // 4
    step = where[0] % 4

    def one_tile(tile, count):
        array = tile // per_col
        col = ((array // 4) ^ near) * 4 + (step - array % 4 + 4) % 4
        piece = col * per_col + tile % per_col
        base = tile * slots + piece * width * 256

        def live(state):
            slot, _ = state
            return (slot < slots) & (ham[tile, slot] >= 0)

        def one_slot(state):
            slot, count = state
            key = ham[tile, slot]
            row = key // 8
            inner = key % 8
            for w in range(2):
                there = iterate[piece, inner * 2 + w]
                for v in range(2):
                    pairs[count] = base + slot + (inner * 2 + w) * 256 + (row * 2 + v) * 65536
                    count = count + (aim[row * 2 + v] == there).astype(jnp.int32)
            return slot + 1, count

        return lax.while_loop(live, one_slot, (jnp.int32(0), count))[1]

    pairs[pairs.shape[0] - 1] = lax.fori_loop(0, pieces, one_tile, jnp.int32(0))
    pairs[pairs.shape[0] - 2] = where[1]


def product_kernel(pairs, iterate, *rest):
    hams, (sent_on, sent_keep, kept_on, kept_keep, total, ham_buf, it_buf, ham_sem, it_sem) = rest[:8], rest[8:]
    size = ham_buf.shape[1]
    slots = hams[0].shape[0] // size
    count = pairs[pairs.shape[0] - 1]

    def start(at):
        code = pairs[at]
        ham_at = code % 256
        slot = at % WINDOW
        rows = pl.ds(pl.multiple_of((ham_at % slots) * size, size), size)
        for k, ham in enumerate(hams):

            @pl.when(ham_at // slots == k)
            def _():
                pltpu.make_async_copy(ham.at[rows], ham_buf.at[slot], ham_sem.at[slot]).start()

        pltpu.make_async_copy(iterate.at[(code // 256) % 256], it_buf.at[slot], it_sem.at[slot]).start()

    def first(at, carry):
        start(at)
        return carry

    lax.fori_loop(0, jnp.minimum(count, WINDOW), first, 0)

    def clear(at, carry):
        total[at] = jnp.zeros(total.shape[1:], total.dtype)
        return carry

    lax.fori_loop(0, total.shape[0], clear, 0, unroll=4)

    def multiply(at, carry):
        slot = at % WINDOW
        pltpu.make_async_copy(hams[0].at[pl.ds(0, size)], ham_buf.at[slot], ham_sem.at[slot]).wait()
        pltpu.make_async_copy(iterate.at[0], it_buf.at[slot], it_sem.at[slot]).wait()
        goal = pairs[at] // 65536
        total[goal] += jnp.dot(ham_buf[slot], it_buf[slot], preferred_element_type=jnp.float32)

        @pl.when(at + WINDOW < count)
        def _():
            start(at + WINDOW)

        return carry

    lax.fori_loop(0, count, multiply, 0)
    half = sent_on.shape[0]
    depth = pairs[pairs.shape[0] - 2]
    core = depth % 2
    high = depth // 2

    def finish(at, carry):
        away = (1 - high) * 2
        home = high * 2
        sent_on[at] = total[(away + 1 - core) * half + at].astype(sent_on.dtype)
        kept_on[at] = total[(away + core) * half + at].astype(kept_on.dtype)
        sent_keep[at] = total[(home + 1 - core) * half + at].astype(sent_keep.dtype)
        kept_keep[at] = total[(home + core) * half + at].astype(kept_keep.dtype)
        return carry

    lax.fori_loop(0, half, finish, 0, unroll=2)


def body(h_blocks, h_rows, h_cols, h_flags, x_blocks, x_cols, x_flags, previous):
    block = x_blocks.shape[-1]
    n_row, n_col, n_depth = lax.axis_size("row"), lax.axis_size("col"), lax.axis_size("depth")
    where = jnp.stack([lax.axis_index("col"), lax.axis_index("depth")]).astype(jnp.int32)
    iterate = lax.all_gather(x_blocks[0, 0, 0], "row", axis=0)
    iterate = iterate.reshape(-1, block, block)
    it_ints = jnp.concatenate([x_cols, x_flags], axis=2)
    slots = h_rows.shape[-1]
    ham_ints = jnp.concatenate([ints.reshape(-1, slots) for ints in (h_rows, h_cols, h_flags)], axis=0)
    ham_ints = ham_ints.astype(jnp.bfloat16)
    ham_ints = jnp.pad(ham_ints, ((0, 16 - ham_ints.shape[0]), (0, block - slots)))
    mine = jnp.concatenate([h_blocks.reshape(-1, block), ham_ints], axis=0)

    def send(source, flip, step):
        route = [(c, ((c // 4) ^ flip) * 4 + (c % 4 + step) % 4) for c in range(n_col)]
        return lax.ppermute(source, "col", route)

    hams = [mine] + [None] * (n_col - 1)
    for flip, step in ((1, 0), (1, 2), (0, 2), (1, 1), (1, 3)):
        hams[flip * 4 + step] = send(mine, flip, step)
    hams[4], it_ints = lax.optimization_barrier((hams[4], it_ints))
    aim_ints = lax.all_gather(it_ints, "depth", axis=1, tiled=True)
    it_ints = lax.all_gather(it_ints, "row", axis=0, tiled=True)
    late, aim_ints, it_ints = lax.optimization_barrier((mine, aim_ints, it_ints))
    for flip, step in ((0, 1), (0, 3)):
        hams[flip * 4 + step] = send(late, flip, step)
    hams = [pltpu.with_memory_space_constraint(ham, pltpu.HBM) for ham in hams]
    it_keys = jnp.where(it_ints[:, 0, 1] > 0, it_ints[:, 0, 0], -1).reshape(n_row, -1)
    aim_keys = jnp.where(aim_ints[0, :, 1] > 0, aim_ints[0, :, 0], -2).reshape(-1)
    smem = pl.BlockSpec(memory_space=pltpu.SMEM)
    anywhere = pl.BlockSpec(memory_space=pl.ANY)
    vmem = pl.BlockSpec(memory_space=pltpu.VMEM)
    ham_keys = pl.pallas_call(
        key_kernel,
        out_shape=jax.ShapeDtypeStruct((n_row, block), jnp.int32),
        in_specs=[anywhere] * n_col,
        out_specs=vmem,
        scratch_shapes=[pltpu.VMEM((n_col, 16, block), jnp.bfloat16), pltpu.SemaphoreType.DMA((n_col,))],
        name="keys",
    )(*hams)
    pairs = pl.pallas_call(
        pair_kernel,
        out_shape=jax.ShapeDtypeStruct((512,), jnp.int32),
        in_specs=[smem] * 4,
        out_specs=smem,
        name="pairs",
    )(where, ham_keys, it_keys, aim_keys)
    results = x_cols.shape[3] * x_cols.shape[4]
    part = jax.ShapeDtypeStruct((results, block, block), jnp.bfloat16)
    sent_on, sent_keep, kept_on, kept_keep = pl.pallas_call(
        product_kernel,
        out_shape=(part,) * 4,
        in_specs=[smem] + [anywhere] * 9,
        out_specs=(vmem,) * 4,
        scratch_shapes=[
            pltpu.VMEM((n_depth * results, block, block), jnp.float32),
            pltpu.VMEM((WINDOW, block, block), jnp.bfloat16),
            pltpu.VMEM((WINDOW, block, block), jnp.bfloat16),
            pltpu.SemaphoreType.DMA((WINDOW,)),
            pltpu.SemaphoreType.DMA((WINDOW,)),
        ],
        compiler_params=pltpu.CompilerParams(vmem_limit_bytes=24 << 20),
        name="products",
    )(*[pltpu.with_memory_space_constraint(x, pltpu.HBM) for x in (pairs, iterate)], *hams)
    to_core = [(d, d ^ 1) for d in range(n_depth)]
    near_on = lax.ppermute(sent_on, "depth", to_core)
    onward = (kept_on.astype(jnp.float32) + near_on.astype(jnp.float32)).astype(jnp.bfloat16)
    onward, sent_keep = lax.optimization_barrier((onward, sent_keep))
    far = lax.ppermute(onward, "depth", [(d, d ^ 2) for d in range(n_depth)])
    near_keep = lax.ppermute(sent_keep, "depth", to_core)
    prior = previous.reshape(results, block, block).astype(jnp.float32)
    live = x_flags.reshape(results, 1, 1).astype(jnp.float32)
    summed = kept_keep.astype(jnp.float32) + near_keep.astype(jnp.float32)
    base = lax.optimization_barrier(2.0 * summed - prior)
    result = (base + 2.0 * far.astype(jnp.float32)) * live
    return result.astype(jnp.bfloat16).reshape(previous.shape)


def solution(mesh):
    placed = (
        P("row", "col", "depth", None, None, None),
        P("row", "col", "depth", None),
        P("row", "col", "depth", None),
        P("row", "col", "depth", None),
        P("row", "depth", "col", None, None, None, None),
        P("row", "depth", "col", None, None),
        P("row", "depth", "col", None, None),
        P("row", "depth", "col", None, None, None, None),
    )
    return jax.shard_map(
        body,
        mesh=mesh,
        in_specs=placed,
        out_specs=P("row", "depth", "col", None, None, None, None),
        check_vma=False,
    )
```

time: 199 us -> 190 us (0.955)
  the two profiles are of different devices: /device:TPU:1 before, /device:TPU:38 now
where the time goes in v4:
time: 190 us; the launch traced here: 189 us
  blocking collectives  87.5 us (46%)
  starting transfers between devices  38.9 us (20%)
  waiting for transfers between devices  34.1 us (18%)
  between operations  13.6 us (7%)
  Pallas kernels  7.75 us (4%)
  other arithmetic  5.3 us (3%)
    all_gather x1, blocking collectives, body(): aim_ints = lax.all_gather(it_ints, 'depth', axis=1, tiled=True)  51.5 us
    all_gather x1, blocking collectives, body(): it_ints = lax.all_gather(it_ints, 'row', axis=0, tiled=True)  36 us
    ppermute x7, starting transfers between devices, send(): return lax.ppermute(source, 'col', route)  32.8 us
    ppermute x7, waiting for transfers between devices, send(): return lax.ppermute(source, 'col', route)  16.2 us
    ppermute x1, waiting for transfers between devices, body(): far = lax.ppermute(onward, 'depth', [(d, d ^ 2) for d in range(n_depth)])  15.2 us
  transfers between devices with their start and end apart: 11, of which 5 were waited for; matrix products, arithmetic and copies ran while one was open for 3% of the time, Pallas kernels for 3%

profile of v4, /device:TPU:38, one launch (start us, length us, event | category | flops | bytes accessed | tf_op | source)
XLA Modules:
  0.0 188.8 jit_solution(7917944405871237220)
XLA Ops:
  6.5 0.7 all-gather.3.cloned.1.call-update
  9.3 1.2 pad_maximum_fusion.refs_0_.rest_0_
  10.5 2.7 %collective-permute-start = (bf16[3088,128]{1,0:T(8,128)(2,1)S(1)}, bf16[3088,128]{1,0:T(8,128)(2,1)S(1)}, u32[]{:S(2)}, u32[]{:S(2)}) collective-permute-start(bf16[3088,128]{1,0:T(8,128)(2,1)S(1)} %pad_maximum_fusion.refs_0_.rest_0_), channel_id=1, source_target_pairs={{0,16},{4,20},{8,24},{12,28},{16,0},{20,4},{24,8},{28,12},{1,17},{... | collective-permute-start | bytes 2371592 | tf_op jit(solution)/shard_map/ppermute | solution.py:140
  13.3 5.1 %collective-permute-start.2 = (bf16[3088,128]{1,0:T(8,128)(2,1)S(1)}, bf16[3088,128]{1,0:T(8,128)(2,1)S(1)}, u32[]{:S(2)}, u32[]{:S(2)}) collective-permute-start(bf16[3088,128]{1,0:T(8,128)(2,1)S(1)} %pad_maximum_fusion.refs_0_.rest_0_), channel_id=1, source_target_pairs={{0,8},{4,12},{8,0},{12,4},{16,24},{20,28},{24,16},{28,20},{1,9},{5... | collective-permute-start | bytes 2371592 | tf_op jit(solution)/shard_map/ppermute | solution.py:140
  18.4 3.2 %collective-permute-start.4 = (bf16[3088,128]{1,0:T(8,128)(2,1)S(1)}, bf16[3088,128]{1,0:T(8,128)(2,1)S(1)}, u32[]{:S(2)}, u32[]{:S(2)}) collective-permute-start(bf16[3088,128]{1,0:T(8,128)(2,1)S(1)} %pad_maximum_fusion.refs_0_.rest_0_), channel_id=1, source_target_pairs={{0,20},{4,24},{8,28},{12,16},{16,4},{20,8},{24,12},{28,0},{1,21},{... | collective-permute-start | bytes 2371592 | tf_op jit(solution)/shard_map/ppermute | solution.py:140
  21.6 4.0 %collective-permute-start.5 = (bf16[3088,128]{1,0:T(8,128)(2,1)S(1)}, bf16[3088,128]{1,0:T(8,128)(2,1)}, u32[]{:S(2)}, u32[]{:S(2)}) collective-permute-start(bf16[3088,128]{1,0:T(8,128)(2,1)S(1)} %pad_maximum_fusion.refs_0_.rest_0_), channel_id=1, source_target_pairs={{0,24},{4,28},{8,16},{12,20},{16,8},{20,12},{24,0},{28,4},{1,25},{... | collective-permute-start | bytes 2371592 | tf_op jit(solution)/shard_map/ppermute | solution.py:140
  25.6 3.0 %collective-permute-start.6 = (bf16[3088,128]{1,0:T(8,128)(2,1)S(1)}, bf16[3088,128]{1,0:T(8,128)(2,1)}, u32[]{:S(2)}, u32[]{:S(2)}) collective-permute-start(bf16[3088,128]{1,0:T(8,128)(2,1)S(1)} %pad_maximum_fusion.refs_0_.rest_0_), channel_id=1, source_target_pairs={{0,28},{4,16},{8,20},{12,24},{16,12},{20,0},{24,4},{28,8},{1,29},{... | collective-permute-start | bytes 2371592 | tf_op jit(solution)/shard_map/ppermute | solution.py:140
  28.7 4.3 %collective-permute-done.refs_4_.rest_4_ = bf16[3088,128]{1,0:T(8,128)(2,1)S(1)} collective-permute-done((bf16[3088,128]{1,0:T(8,128)(2,1)S(1)}, bf16[3088,128]{1,0:T(8,128)(2,1)S(1)}, u32[]{:S(2)}, u32[]{:S(2)}) %collective-permute-start) | collective-permute-done | bytes 790560 | tf_op jit(solution)/shard_map/ppermute | solution.py:140
  32.9 51.5 %all_gather.9 = s32[1,4,2,8,2]{3,4,2,0,1:T(2,128)S(1)} all-gather(s32[1,1,2,8,2]{3,4,2,0,1:T(2,128)S(1)} %pad_add_fusion), channel_id=1, replica_groups=mesh['row'=16,'col'=8,'depth'=4] {'depth'}, dimensions={1}, use_global_device_ids=true | all-gather | bytes 640 | tf_op jit(solution)/shard_map/all_gather | solution.py:146
  84.4 36.0 %all_gather.10 = s32[16,1,2,8,2]{3,4,2,1,0:T(2,128)S(1)} all-gather(s32[1,1,2,8,2]{3,4,2,1,0:T(2,128)S(1)} %bitcast.28), channel_id=1, replica_groups=mesh['row'=16,'col'=8,'depth'=4] {'row'}, dimensions={0}, use_global_device_ids=true | all-gather | bytes 2176 | tf_op jit(solution)/shard_map/all_gather | solution.py:147
  120.4 12.9 %collective-permute-start.1 = (bf16[3088,128]{1,0:T(8,128)(2,1)S(1)}, bf16[3088,128]{1,0:T(8,128)(2,1)}, u32[]{:S(2)}, u32[]{:S(2)}) collective-permute-start(bf16[3088,128]{1,0:T(8,128)(2,1)S(1)} %pad_maximum_fusion.refs_0_.rest_0_), channel_id=1, source_target_pairs={{0,4},{4,8},{8,12},{12,0},{16,20},{20,24},{24,28},{28,16},{1,5},{5... | collective-permute-start | bytes 2371592 | tf_op jit(solution)/shard_map/ppermute | solution.py:140
  133.3 1.9 %collective-permute-start.3 = (bf16[3088,128]{1,0:T(8,128)(2,1)S(1)}, bf16[3088,128]{1,0:T(8,128)(2,1)}, u32[]{:S(2)}, u32[]{:S(2)}) collective-permute-start(bf16[3088,128]{1,0:T(8,128)(2,1)S(1)} %pad_maximum_fusion.refs_0_.rest_0_), channel_id=1, source_target_pairs={{0,12},{4,0},{8,4},{12,8},{16,28},{20,16},{24,20},{28,24},{1,13},{... | collective-permute-start | bytes 2371592 | tf_op jit(solution)/shard_map/ppermute | solution.py:140
  136.8 0.7 select_n.19.aim
  137.5 7.7 %collective-permute-done.1.refs_1_.rest_1_ = bf16[3088,128]{1,0:T(8,128)(2,1)} collective-permute-done((bf16[3088,128]{1,0:T(8,128)(2,1)S(1)}, bf16[3088,128]{1,0:T(8,128)(2,1)}, u32[]{:S(2)}, u32[]{:S(2)}) %collective-permute-start.1) | collective-permute-done | bytes 790560 | tf_op jit(solution)/shard_map/ppermute | solution.py:140
  145.2 4.2 %collective-permute-done.3.refs_3_.rest_3_ = bf16[3088,128]{1,0:T(8,128)(2,1)} collective-permute-done((bf16[3088,128]{1,0:T(8,128)(2,1)S(1)}, bf16[3088,128]{1,0:T(8,128)(2,1)}, u32[]{:S(2)}, u32[]{:S(2)}) %collective-permute-start.3) | collective-permute-done | bytes 790560 | tf_op jit(solution)/shard_map/ppermute | solution.py:140
  149.5 1.4 keys.1.ham
  150.9 3.4 %pairs.1 = s32[512]{0:T(512)} custom-call(s32[2]{0:T(128)} %pad_add_fusion.1.where, s32[16,128]{1,0:T(8,128)} %keys.1.ham, s32[16,16]{1,0:T(8,128)} %copy.21.iterate, s32[64]{0:T(128)} %select_n.19.aim), custom_call_target="tpu_custom_call" | custom-call | tf_op jit(solution)/shard_map/pairs/pallas_call | solution.py:165
  154.4 2.9 %products.1 = (bf16[16,128,128]{2,1,0:T(8,128)(2,1)S(1)}, bf16[16,128,128]{2,1,0:T(8,128)(2,1)S(1)}, bf16[16,128,128]{2,1,0:T(8,128)(2,1)S(1)}, bf16[16,128,128]{2,1,0:T(8,128)(2,1)S(1)}) custom-call(s32[512]{0:T(512)} %pairs.1, bf16[256,128,128]{2,1,0:T(8,128)(2,1)} %bitcast.25, bf16[3088,128]{1,0:T(8,128)(2,1)} %copy-done, ...), custom_call_target="tpu_custom_call" | custom-call | tf_op jit(solution)/shard_map/products/pallas_call | solution.py:174
  157.3 2.1 %collective-permute-start.7 = (bf16[16,128,128]{2,1,0:T(8,128)(2,1)S(1)}, bf16[16,128,128]{2,1,0:T(8,128)(2,1)S(1)}, u32[]{:S(2)}, u32[]{:S(2)}) collective-permute-start(bf16[16,128,128]{2,1,0:T(8,128)(2,1)S(1)} %get-tuple-element.23), channel_id=1, source_target_pairs={{0,1},{1,0},{2,3},{3,2},{4,5},{5,4},{6,7},{7,6},{8,9},{9,8},{10,11... | collective-permute-start | bytes 1572872 | tf_op jit(solution)/shard_map/ppermute | solution.py:190
  159.3 1.9 collective-permute-done.7
  161.4 2.0 %collective-permute-start.8 = (bf16[16,128,128]{2,1,0:T(8,128)(2,1)S(1)}, bf16[16,128,128]{2,1,0:T(8,128)(2,1)S(1)}, u32[]{:S(2)}, u32[]{:S(2)}) collective-permute-start(bf16[16,128,128]{2,1,0:T(8,128)(2,1)S(1)} %get-tuple-element.25), channel_id=1, source_target_pairs={{0,1},{1,0},{2,3},{3,2},{4,5},{5,4},{6,7},{7,6},{8,9},{9,8},{10,11... | collective-permute-start | bytes 1572872 | tf_op jit(solution)/shard_map/ppermute | solution.py:194
  163.4 1.9 %collective-permute-start.9 = (bf16[16,128,128]{2,1,0:T(8,128)(2,1)S(1)}, bf16[16,128,128]{2,1,0:T(8,128)(2,1)S(1)}, u32[]{:S(2)}, u32[]{:S(2)}) collective-permute-start(bf16[16,128,128]{2,1,0:T(8,128)(2,1)S(1)} %add_convert_fusion), channel_id=1, source_target_pairs={{0,2},{1,3},{2,0},{3,1},{4,6},{5,7},{6,4},{7,5},{8,10},{9,11},{10,... | collective-permute-start | bytes 1572872 | tf_op jit(solution)/shard_map/ppermute | solution.py:193
  165.8 15.2 %collective-permute-done.9 = bf16[16,128,128]{2,1,0:T(8,128)(2,1)S(1)} collective-permute-done((bf16[16,128,128]{2,1,0:T(8,128)(2,1)S(1)}, bf16[16,128,128]{2,1,0:T(8,128)(2,1)S(1)}, u32[]{:S(2)}, u32[]{:S(2)}) %collective-permute-start.9) | collective-permute-done | bytes 524320 | tf_op jit(solution)/shard_map/ppermute | solution.py:193
  181.0 1.0 multiply_convert_fusion
  (39 shorter events, 4.2 us)
Async XLA Ops:
  6.5 22.1 %copy-start.6 = (s32[1,1,1,8,2]{3,4,2,1,0:T(2,128)S(1)}, s32[1,1,1,8,2]{3,4,2,1,0:T(2,128)}, u32[]{:S(2)}) copy-start(s32[1,1,1,8,2]{3,4,2,1,0:T(2,128)} %param.13) | copy-start | bytes 196
  6.5 22.1 %copy-start.5 = (s32[1,1,1,8,2]{3,4,2,1,0:T(2,128)S(1)}, s32[1,1,1,8,2]{3,4,2,1,0:T(2,128)}, u32[]{:S(2)}) copy-start(s32[1,1,1,8,2]{3,4,2,1,0:T(2,128)} %param.14) | copy-start | bytes 196
  6.5 147.8 %all-gather.3.cloned.1.call-start = ((), (), s32[]{:S(2)}) async-start(), calls=%async_computation | async-start | bytes 8912896 | tf_op jit(solution)/shard_map/all_gather | solution.py:129
  10.5 138.9 %copy-start = (bf16[3088,128]{1,0:T(8,128)(2,1)}, bf16[3088,128]{1,0:T(8,128)(2,1)S(1)}, u32[]{:S(2)}) copy-start(bf16[3088,128]{1,0:T(8,128)(2,1)S(1)} %pad_maximum_fusion.refs_0_.rest_0_) | copy-start | bytes 2371588
  10.5 22.4 %collective-permute-start = (bf16[3088,128]{1,0:T(8,128)(2,1)S(1)}, bf16[3088,128]{1,0:T(8,128)(2,1)S(1)}, u32[]{:S(2)}, u32[]{:S(2)}) collective-permute-start(bf16[3088,128]{1,0:T(8,128)(2,1)S(1)} %pad_maximum_fusion.refs_0_.rest_0_), channel_id=1, source_target_pairs={{0,16},{4,20},{8,24},{12,28},{16,0},{20,4},{24,8},{28,12},{1,17},{... | collective-permute-start | bytes 2371592 | tf_op jit(solution)/shard_map/ppermute | solution.py:140
  13.3 120.0 %collective-permute-start.2 = (bf16[3088,128]{1,0:T(8,128)(2,1)S(1)}, bf16[3088,128]{1,0:T(8,128)(2,1)S(1)}, u32[]{:S(2)}, u32[]{:S(2)}) collective-permute-start(bf16[3088,128]{1,0:T(8,128)(2,1)S(1)} %pad_maximum_fusion.refs_0_.rest_0_), channel_id=1, source_target_pairs={{0,8},{4,12},{8,0},{12,4},{16,24},{20,28},{24,16},{28,20},{1,9},{5... | collective-permute-start | bytes 2371592 | tf_op jit(solution)/shard_map/ppermute | solution.py:140
  18.4 119.1 %collective-permute-start.4 = (bf16[3088,128]{1,0:T(8,128)(2,1)S(1)}, bf16[3088,128]{1,0:T(8,128)(2,1)S(1)}, u32[]{:S(2)}, u32[]{:S(2)}) collective-permute-start(bf16[3088,128]{1,0:T(8,128)(2,1)S(1)} %pad_maximum_fusion.refs_0_.rest_0_), channel_id=1, source_target_pairs={{0,20},{4,24},{8,28},{12,16},{16,4},{20,8},{24,12},{28,0},{1,21},{... | collective-permute-start | bytes 2371592 | tf_op jit(solution)/shard_map/ppermute | solution.py:140
  21.6 115.8 %collective-permute-start.5 = (bf16[3088,128]{1,0:T(8,128)(2,1)S(1)}, bf16[3088,128]{1,0:T(8,128)(2,1)}, u32[]{:S(2)}, u32[]{:S(2)}) collective-permute-start(bf16[3088,128]{1,0:T(8,128)(2,1)S(1)} %pad_maximum_fusion.refs_0_.rest_0_), channel_id=1, source_target_pairs={{0,24},{4,28},{8,16},{12,20},{16,8},{20,12},{24,0},{28,4},{1,25},{... | collective-permute-start | bytes 2371592 | tf_op jit(solution)/shard_map/ppermute | solution.py:140
  25.6 111.8 %collective-permute-start.6 = (bf16[3088,128]{1,0:T(8,128)(2,1)S(1)}, bf16[3088,128]{1,0:T(8,128)(2,1)}, u32[]{:S(2)}, u32[]{:S(2)}) collective-permute-start(bf16[3088,128]{1,0:T(8,128)(2,1)S(1)} %pad_maximum_fusion.refs_0_.rest_0_), channel_id=1, source_target_pairs={{0,28},{4,16},{8,20},{12,24},{16,12},{20,0},{24,4},{28,8},{1,29},{... | collective-permute-start | bytes 2371592 | tf_op jit(solution)/shard_map/ppermute | solution.py:140
  32.9 116.5 %copy-start.1 = (bf16[3088,128]{1,0:T(8,128)(2,1)}, bf16[3088,128]{1,0:T(8,128)(2,1)S(1)}, u32[]{:S(2)}) copy-start(bf16[3088,128]{1,0:T(8,128)(2,1)S(1)} %collective-permute-done.refs_4_.rest_4_) | copy-start | bytes 2371588
  120.4 24.8 %collective-permute-start.1 = (bf16[3088,128]{1,0:T(8,128)(2,1)S(1)}, bf16[3088,128]{1,0:T(8,128)(2,1)}, u32[]{:S(2)}, u32[]{:S(2)}) collective-permute-start(bf16[3088,128]{1,0:T(8,128)(2,1)S(1)} %pad_maximum_fusion.refs_0_.rest_0_), channel_id=1, source_target_pairs={{0,4},{4,8},{8,12},{12,0},{16,20},{20,24},{24,28},{28,16},{1,5},{5... | collective-permute-start | bytes 2371592 | tf_op jit(solution)/shard_map/ppermute | solution.py:140
  133.3 16.2 %copy-start.2 = (bf16[3088,128]{1,0:T(8,128)(2,1)}, bf16[3088,128]{1,0:T(8,128)(2,1)S(1)}, u32[]{:S(2)}) copy-start(bf16[3088,128]{1,0:T(8,128)(2,1)S(1)} %collective-permute-done.2.refs_2_.rest_2_) | copy-start | bytes 2371588
  133.3 16.1 %collective-permute-start.3 = (bf16[3088,128]{1,0:T(8,128)(2,1)S(1)}, bf16[3088,128]{1,0:T(8,128)(2,1)}, u32[]{:S(2)}, u32[]{:S(2)}) collective-permute-start(bf16[3088,128]{1,0:T(8,128)(2,1)S(1)} %pad_maximum_fusion.refs_0_.rest_0_), channel_id=1, source_target_pairs={{0,12},{4,0},{8,4},{12,8},{16,28},{20,16},{24,20},{28,24},{1,13},{... | collective-permute-start | bytes 2371592 | tf_op jit(solution)/shard_map/ppermute | solution.py:140
  137.5 12.0 %copy-start.3 = (bf16[3088,128]{1,0:T(8,128)(2,1)}, bf16[3088,128]{1,0:T(8,128)(2,1)S(1)}, u32[]{:S(2)}) copy-start(bf16[3088,128]{1,0:T(8,128)(2,1)S(1)} %collective-permute-done.4.refs_5_.rest_5_) | copy-start | bytes 2371588
  157.3 8.3 %copy-start.4 = (bf16[1,1,1,8,2,128,128]{6,5,4,3,2,1,0:T(8,128)(2,1)S(1)}, bf16[1,1,1,8,2,128,128]{6,5,4,3,2,1,0:T(8,128)(2,1)}, u32[]{:S(2)}) copy-start(bf16[1,1,1,8,2,128,128]{6,5,4,3,2,1,0:T(8,128)(2,1)} %param.15) | copy-start | bytes 1572868
  157.3 3.9 %collective-permute-start.7 = (bf16[16,128,128]{2,1,0:T(8,128)(2,1)S(1)}, bf16[16,128,128]{2,1,0:T(8,128)(2,1)S(1)}, u32[]{:S(2)}, u32[]{:S(2)}) collective-permute-start(bf16[16,128,128]{2,1,0:T(8,128)(2,1)S(1)} %get-tuple-element.23), channel_id=1, source_target_pairs={{0,1},{1,0},{2,3},{3,2},{4,5},{5,4},{6,7},{7,6},{8,9},{9,8},{10,11... | collective-permute-start | bytes 1572872 | tf_op jit(solution)/shard_map/ppermute | solution.py:190
  161.4 4.2 %collective-permute-start.8 = (bf16[16,128,128]{2,1,0:T(8,128)(2,1)S(1)}, bf16[16,128,128]{2,1,0:T(8,128)(2,1)S(1)}, u32[]{:S(2)}, u32[]{:S(2)}) collective-permute-start(bf16[16,128,128]{2,1,0:T(8,128)(2,1)S(1)} %get-tuple-element.25), channel_id=1, source_target_pairs={{0,1},{1,0},{2,3},{3,2},{4,5},{5,4},{6,7},{7,6},{8,9},{9,8},{10,11... | collective-permute-start | bytes 1572872 | tf_op jit(solution)/shard_map/ppermute | solution.py:194
  163.4 17.6 %collective-permute-start.9 = (bf16[16,128,128]{2,1,0:T(8,128)(2,1)S(1)}, bf16[16,128,128]{2,1,0:T(8,128)(2,1)S(1)}, u32[]{:S(2)}, u32[]{:S(2)}) collective-permute-start(bf16[16,128,128]{2,1,0:T(8,128)(2,1)S(1)} %add_convert_fusion), channel_id=1, source_target_pairs={{0,2},{1,3},{2,0},{3,1},{4,6},{5,7},{6,4},{7,5},{8,10},{9,11},{10,... | collective-permute-start | bytes 1572872 | tf_op jit(solution)/shard_map/ppermute | solution.py:193
Sparse Core Ops, SparseCore 0:
  9.4 107.9 all-gather.2

commit v5 on v4

--- a/solution.py
+++ b/solution.py
@@ -20,8 +20,10 @@
     for k, copy in enumerate(copies):
         copy.wait()
         held = slab[k].astype(jnp.float32)
-        place = jnp.where(held[4:6] > 0, held[0:2] * 8 + held[2:4], -1.0)
-        keys[2 * k : 2 * k + 2] = place.astype(jnp.int32)
+        for t in range(2):
+            row, col, flag = (held[3 * t + i : 3 * t + i + 1] for i in range(3))
+            place = jnp.where(flag > 0, row * 8 + col, -1.0)
+            keys[2 * k + t : 2 * k + t + 1] = place.astype(jnp.int32)
 
 
 def pair_kernel(where, ham, iterate, aim, pairs):
@@ -61,7 +63,7 @@
 
 
 def product_kernel(pairs, iterate, *rest):
-    hams, (sent_on, sent_keep, kept_on, kept_keep, total, ham_buf, it_buf, ham_sem, it_sem) = rest[:8], rest[8:]
+    hams, (sent, kept, total, ham_buf, it_buf, ham_sem, it_sem) = rest[:8], rest[8:]
     size = ham_buf.shape[1]
     slots = hams[0].shape[0] // size
     count = pairs[pairs.shape[0] - 1]
@@ -105,18 +107,15 @@
         return carry
 
     lax.fori_loop(0, count, multiply, 0)
-    half = sent_on.shape[0]
+    half = sent.shape[1]
     depth = pairs[pairs.shape[0] - 2]
     core = depth % 2
     high = depth // 2
 
     def finish(at, carry):
-        away = (1 - high) * 2
-        home = high * 2
-        sent_on[at] = total[(away + 1 - core) * half + at].astype(sent_on.dtype)
-        kept_on[at] = total[(away + core) * half + at].astype(kept_on.dtype)
-        sent_keep[at] = total[(home + 1 - core) * half + at].astype(sent_keep.dtype)
-        kept_keep[at] = total[(home + core) * half + at].astype(kept_keep.dtype)
+        for part, far in enumerate((1 - high, high)):
+            sent[part, at] = total[(far * 2 + 1 - core) * half + at].astype(sent.dtype)
+            kept[part, at] = total[(far * 2 + core) * half + at].astype(kept.dtype)
         return carry
 
     lax.fori_loop(0, half, finish, 0, unroll=2)
@@ -129,11 +128,13 @@
     iterate = lax.all_gather(x_blocks[0, 0, 0], "row", axis=0)
     iterate = iterate.reshape(-1, block, block)
     it_ints = jnp.concatenate([x_cols, x_flags], axis=2)
+    aim_ints = lax.all_gather(it_ints, "depth", axis=1, tiled=True)
     slots = h_rows.shape[-1]
-    ham_ints = jnp.concatenate([ints.reshape(-1, slots) for ints in (h_rows, h_cols, h_flags)], axis=0)
+    ham_ints = jnp.concatenate([h_rows, h_cols, h_flags], axis=2).reshape(-1, slots)
     ham_ints = ham_ints.astype(jnp.bfloat16)
     ham_ints = jnp.pad(ham_ints, ((0, 16 - ham_ints.shape[0]), (0, block - slots)))
     mine = jnp.concatenate([h_blocks.reshape(-1, block), ham_ints], axis=0)
+    mine, aim_ints = lax.optimization_barrier((mine, aim_ints))
 
     def send(source, flip, step):
         route = [(c, ((c // 4) ^ flip) * 4 + (c % 4 + step) % 4) for c in range(n_col)]
@@ -143,9 +144,8 @@
     for flip, step in ((1, 0), (1, 2), (0, 2), (1, 1), (1, 3)):
         hams[flip * 4 + step] = send(mine, flip, step)
     hams[4], it_ints = lax.optimization_barrier((hams[4], it_ints))
-    aim_ints = lax.all_gather(it_ints, "depth", axis=1, tiled=True)
     it_ints = lax.all_gather(it_ints, "row", axis=0, tiled=True)
-    late, aim_ints, it_ints = lax.optimization_barrier((mine, aim_ints, it_ints))
+    late, it_ints = lax.optimization_barrier((mine, it_ints))
     for flip, step in ((0, 1), (0, 3)):
         hams[flip * 4 + step] = send(late, flip, step)
     hams = [pltpu.with_memory_space_constraint(ham, pltpu.HBM) for ham in hams]
@@ -170,12 +170,12 @@
         name="pairs",
     )(where, ham_keys, it_keys, aim_keys)
     results = x_cols.shape[3] * x_cols.shape[4]
-    part = jax.ShapeDtypeStruct((results, block, block), jnp.bfloat16)
-    sent_on, sent_keep, kept_on, kept_keep = pl.pallas_call(
+    halves = jax.ShapeDtypeStruct((2, results, block, block), jnp.bfloat16)
+    sent, kept = pl.pallas_call(
         product_kernel,
-        out_shape=(part,) * 4,
+        out_shape=(halves,) * 2,
         in_specs=[smem] + [anywhere] * 9,
-        out_specs=(vmem,) * 4,
+        out_specs=(vmem,) * 2,
         scratch_shapes=[
             pltpu.VMEM((n_depth * results, block, block), jnp.float32),
             pltpu.VMEM((WINDOW, block, block), jnp.bfloat16),
@@ -186,16 +186,13 @@
         compiler_params=pltpu.CompilerParams(vmem_limit_bytes=24 << 20),
         name="products",
     )(*[pltpu.with_memory_space_constraint(x, pltpu.HBM) for x in (pairs, iterate)], *hams)
-    to_core = [(d, d ^ 1) for d in range(n_depth)]
-    near_on = lax.ppermute(sent_on, "depth", to_core)
-    onward = (kept_on.astype(jnp.float32) + near_on.astype(jnp.float32)).astype(jnp.bfloat16)
-    onward, sent_keep = lax.optimization_barrier((onward, sent_keep))
+    near = lax.ppermute(sent, "depth", [(d, d ^ 1) for d in range(n_depth)])
+    onward = (kept[0].astype(jnp.float32) + near[0].astype(jnp.float32)).astype(jnp.bfloat16)
     far = lax.ppermute(onward, "depth", [(d, d ^ 2) for d in range(n_depth)])
-    near_keep = lax.ppermute(sent_keep, "depth", to_core)
     prior = previous.reshape(results, block, block).astype(jnp.float32)
     live = x_flags.reshape(results, 1, 1).astype(jnp.float32)
-    summed = kept_keep.astype(jnp.float32) + near_keep.astype(jnp.float32)
-    base = lax.optimization_barrier(2.0 * summed - prior)
+    base = 2.0 * (kept[1].astype(jnp.float32) + near[1].astype(jnp.float32)) - prior
+    base = lax.optimization_barrier(base)
     result = (base + 2.0 * far.astype(jnp.float32)) * live
     return result.astype(jnp.bfloat16).reshape(previous.shape)
 

time: 190 us -> 156 us (0.82)
  the two profiles are of different devices: /device:TPU:38 before, /device:TPU:1 now
where the time goes in v5:
time: 156 us; the launch traced here: 155 us
  waiting for transfers between devices  56.3 us (36%)
  blocking collectives  39.4 us (25%)
  starting transfers between devices  29.9 us (19%)
  between operations  13.6 us (9%)
  Pallas kernels  7.17 us (5%)
  other arithmetic  6.8 us (4%)
  local copies, waits for them, and re-layouts  1.75 us (1%)
    ppermute x7, waiting for transfers between devices, send(): return lax.ppermute(source, 'col', route)  37.9 us
    all_gather x1, blocking collectives, body(): it_ints = lax.all_gather(it_ints, 'row', axis=0, tiled=True)  26.1 us
    ppermute x7, starting transfers between devices, send(): return lax.ppermute(source, 'col', route)  21.8 us
    all_gather x1, blocking collectives, body(): aim_ints = lax.all_gather(it_ints, 'depth', axis=1, tiled=True)  13.3 us
    ppermute x1, waiting for transfers between devices, body(): far = lax.ppermute(onward, 'depth', [(d, d ^ 2) for d in range(n_depth)])  11.4 us
    ppermute x1, starting transfers between devices, body(): far = lax.ppermute(onward, 'depth', [(d, d ^ 2) for d in range(n_depth)])  4.87 us
    all_gather x1, waiting for transfers between devices, body(): iterate = lax.all_gather(x_blocks[0, 0, 0], 'row', axis=0)  3.95 us
    ppermute x1, starting transfers between devices, body(): near = lax.ppermute(sent, 'depth', [(d, d ^ 1) for d in range(n_depth)])  3.14 us
  transfers between devices with their start and end apart: 10, of which 8 were waited for; matrix products, arithmetic and copies ran while one was open for 4% of the time, Pallas kernels for 3%

profile of v5, /device:TPU:1, one launch (start us, length us, event | category | flops | bytes accessed | tf_op | source)
XLA Modules:
  0.0 154.9 jit_solution(12179789360509492795)
XLA Ops:
  10.0 13.3 %all_gather.9 = s32[1,4,2,8,2]{3,4,2,0,1:T(2,128)S(1)} all-gather(s32[1,1,2,8,2]{3,4,2,0,1:T(2,128)S(1)} %pad_add_fusion), channel_id=1, replica_groups=mesh['row'=16,'col'=8,'depth'=4] {'depth'}, dimensions={1}, use_global_device_ids=true | all-gather | bytes 640 | tf_op jit(solution)/shard_map/all_gather | solution.py:131
  23.4 1.2 fusion.1.refs_0_.rest_0_
  24.6 1.9 %collective-permute-start = (bf16[3088,128]{1,0:T(8,128)(2,1)S(1)}, bf16[3088,128]{1,0:T(8,128)(2,1)S(1)}, u32[]{:S(2)}, u32[]{:S(2)}) collective-permute-start(bf16[3088,128]{1,0:T(8,128)(2,1)S(1)} %fusion.1.refs_0_.rest_0_), channel_id=1, source_target_pairs={{0,16},{4,20},{8,24},{12,28},{16,0},{20,4},{24,8},{28,12},{1,17},{... | collective-permute-start | bytes 2371592 | tf_op jit(solution)/shard_map/ppermute | solution.py:141
  26.5 1.9 %collective-permute-start.2 = (bf16[3088,128]{1,0:T(8,128)(2,1)S(1)}, bf16[3088,128]{1,0:T(8,128)(2,1)S(1)}, u32[]{:S(2)}, u32[]{:S(2)}) collective-permute-start(bf16[3088,128]{1,0:T(8,128)(2,1)S(1)} %fusion.1.refs_0_.rest_0_), channel_id=1, source_target_pairs={{0,8},{4,12},{8,0},{12,4},{16,24},{20,28},{24,16},{28,20},{1,9},{5... | collective-permute-start | bytes 2371592 | tf_op jit(solution)/shard_map/ppermute | solution.py:141
  28.4 1.9 %collective-permute-start.4 = (bf16[3088,128]{1,0:T(8,128)(2,1)S(1)}, bf16[3088,128]{1,0:T(8,128)(2,1)S(1)}, u32[]{:S(2)}, u32[]{:S(2)}) collective-permute-start(bf16[3088,128]{1,0:T(8,128)(2,1)S(1)} %fusion.1.refs_0_.rest_0_), channel_id=1, source_target_pairs={{0,20},{4,24},{8,28},{12,16},{16,4},{20,8},{24,12},{28,0},{1,21},{... | collective-permute-start | bytes 2371592 | tf_op jit(solution)/shard_map/ppermute | solution.py:141
  30.3 6.0 %collective-permute-start.5 = (bf16[3088,128]{1,0:T(8,128)(2,1)S(1)}, bf16[3088,128]{1,0:T(8,128)(2,1)}, u32[]{:S(2)}, u32[]{:S(2)}) collective-permute-start(bf16[3088,128]{1,0:T(8,128)(2,1)S(1)} %fusion.1.refs_0_.rest_0_), channel_id=1, source_target_pairs={{0,24},{4,28},{8,16},{12,20},{16,8},{20,12},{24,0},{28,4},{1,25},{... | collective-permute-start | bytes 2371592 | tf_op jit(solution)/shard_map/ppermute | solution.py:141
  36.4 4.9 %collective-permute-start.6 = (bf16[3088,128]{1,0:T(8,128)(2,1)S(1)}, bf16[3088,128]{1,0:T(8,128)(2,1)}, u32[]{:S(2)}, u32[]{:S(2)}) collective-permute-start(bf16[3088,128]{1,0:T(8,128)(2,1)S(1)} %fusion.1.refs_0_.rest_0_), channel_id=1, source_target_pairs={{0,28},{4,16},{8,20},{12,24},{16,12},{20,0},{24,4},{28,8},{1,29},{... | collective-permute-start | bytes 2371592 | tf_op jit(solution)/shard_map/ppermute | solution.py:141
  41.3 4.3 %collective-permute-done.refs_4_.rest_4_ = bf16[3088,128]{1,0:T(8,128)(2,1)S(1)} collective-permute-done((bf16[3088,128]{1,0:T(8,128)(2,1)S(1)}, bf16[3088,128]{1,0:T(8,128)(2,1)S(1)}, u32[]{:S(2)}, u32[]{:S(2)}) %collective-permute-start) | collective-permute-done | bytes 790560 | tf_op jit(solution)/shard_map/ppermute | solution.py:141
  45.6 26.1 %all_gather.10 = s32[16,1,2,8,2]{3,4,2,1,0:T(2,128)S(1)} all-gather(s32[1,1,2,8,2]{3,4,2,1,0:T(2,128)S(1)} %bitcast.25), channel_id=1, replica_groups=mesh['row'=16,'col'=8,'depth'=4] {'row'}, dimensions={0}, use_global_device_ids=true | all-gather | bytes 2176 | tf_op jit(solution)/shard_map/all_gather | solution.py:147
  71.7 3.3 %collective-permute-start.1 = (bf16[3088,128]{1,0:T(8,128)(2,1)S(1)}, bf16[3088,128]{1,0:T(8,128)(2,1)}, u32[]{:S(2)}, u32[]{:S(2)}) collective-permute-start(bf16[3088,128]{1,0:T(8,128)(2,1)S(1)} %fusion.1.refs_0_.rest_0_), channel_id=1, source_target_pairs={{0,4},{4,8},{8,12},{12,0},{16,20},{20,24},{24,28},{28,16},{1,5},{5... | collective-permute-start | bytes 2371592 | tf_op jit(solution)/shard_map/ppermute | solution.py:141
  75.0 7.9 %collective-permute-done.2.refs_2_.rest_2_ = bf16[3088,128]{1,0:T(8,128)(2,1)S(1)} collective-permute-done((bf16[3088,128]{1,0:T(8,128)(2,1)S(1)}, bf16[3088,128]{1,0:T(8,128)(2,1)S(1)}, u32[]{:S(2)}, u32[]{:S(2)}) %collective-permute-start.2) | collective-permute-done | bytes 790560 | tf_op jit(solution)/shard_map/ppermute | solution.py:141
  82.8 1.9 %collective-permute-start.3 = (bf16[3088,128]{1,0:T(8,128)(2,1)S(1)}, bf16[3088,128]{1,0:T(8,128)(2,1)}, u32[]{:S(2)}, u32[]{:S(2)}) collective-permute-start(bf16[3088,128]{1,0:T(8,128)(2,1)S(1)} %fusion.1.refs_0_.rest_0_), channel_id=1, source_target_pairs={{0,12},{4,0},{8,4},{12,8},{16,28},{20,16},{24,20},{28,24},{1,13},{... | collective-permute-start | bytes 2371592 | tf_op jit(solution)/shard_map/ppermute | solution.py:141
  87.0 8.3 %collective-permute-done.6.refs_7_.rest_7_ = bf16[3088,128]{1,0:T(8,128)(2,1)} collective-permute-done((bf16[3088,128]{1,0:T(8,128)(2,1)S(1)}, bf16[3088,128]{1,0:T(8,128)(2,1)}, u32[]{:S(2)}, u32[]{:S(2)}) %collective-permute-start.6) | collective-permute-done | bytes 790560 | tf_op jit(solution)/shard_map/ppermute | solution.py:141
  95.3 4.6 %collective-permute-done.1.refs_1_.rest_1_ = bf16[3088,128]{1,0:T(8,128)(2,1)} collective-permute-done((bf16[3088,128]{1,0:T(8,128)(2,1)S(1)}, bf16[3088,128]{1,0:T(8,128)(2,1)}, u32[]{:S(2)}, u32[]{:S(2)}) %collective-permute-start.1) | collective-permute-done | bytes 790560 | tf_op jit(solution)/shard_map/ppermute | solution.py:141
  100.0 12.8 %collective-permute-done.3.refs_3_.rest_3_ = bf16[3088,128]{1,0:T(8,128)(2,1)} collective-permute-done((bf16[3088,128]{1,0:T(8,128)(2,1)S(1)}, bf16[3088,128]{1,0:T(8,128)(2,1)}, u32[]{:S(2)}, u32[]{:S(2)}) %collective-permute-start.3) | collective-permute-done | bytes 790560 | tf_op jit(solution)/shard_map/ppermute | solution.py:141
  112.8 1.4 keys.1.ham
  114.2 2.9 %pairs.1 = s32[512]{0:T(512)} custom-call(s32[2]{0:T(128)} %pad_add_fusion.1.where, s32[16,128]{1,0:T(8,128)} %keys.1.ham, s32[16,16]{1,0:T(8,128)} %copy.21.iterate, s32[64]{0:T(128)} %select_n.19.aim), custom_call_target="tpu_custom_call" | custom-call | tf_op jit(solution)/shard_map/pairs/pallas_call | solution.py:165
  117.1 4.0 %all-gather.3.cloned.1.call-done = bf16[16,1,1,8,2,128,128]{6,5,4,3,2,1,0:T(8,128)(2,1)} async-done(((bf16[1,1,1,8,2,128,128]{6,5,4,3,2,1,0:T(8,128)(2,1)}), bf16[16,1,1,8,2,128,128]{6,5,4,3,2,1,0:T(8,128)(2,1)}) %all-gather.3.cloned.1.call-update) | async-done | bytes 8388624 | tf_op jit(solution)/shard_map/all_gather | solution.py:128
  121.1 2.8 %products.1 = (bf16[2,16,128,128]{3,2,1,0:T(8,128)(2,1)S(1)}, bf16[2,16,128,128]{3,2,1,0:T(8,128)(2,1)S(1)}) custom-call(s32[512]{0:T(512)} %pairs.1, bf16[256,128,128]{2,1,0:T(8,128)(2,1)} %bitcast.22, bf16[3088,128]{1,0:T(8,128)(2,1)} %copy-done, bf16[3088,128]{1,0:T(8,128)(2,1)} %collective-permute-done.1.refs_1_.rest_1_, bf16[3088,128]{1,0:T(8,128)(2,1)} %copy-done.2, ...), custom_call_target="tpu_custom_call" | custom-call | tf_op jit(solution)/shard_map/products/pallas_call | solution.py:174
  123.9 3.1 %collective-permute-start.7 = (bf16[2,16,128,128]{3,2,1,0:T(8,128)(2,1)S(1)}, bf16[2,16,128,128]{3,2,1,0:T(8,128)(2,1)S(1)}, u32[]{:S(2)}, u32[]{:S(2)}) collective-permute-start(bf16[2,16,128,128]{3,2,1,0:T(8,128)(2,1)S(1)} %get-tuple-element.20), channel_id=1, source_target_pairs={{0,1},{1,0},{2,3},{3,2},{4,5},{5,4},{6,7},{7,6},{8,9},{9,8},{10,11... | collective-permute-start | bytes 3145736 | tf_op jit(solution)/shard_map/ppermute | solution.py:189
  127.1 2.3 %collective-permute-done.7 = bf16[2,16,128,128]{3,2,1,0:T(8,128)(2,1)S(1)} collective-permute-done((bf16[2,16,128,128]{3,2,1,0:T(8,128)(2,1)S(1)}, bf16[2,16,128,128]{3,2,1,0:T(8,128)(2,1)S(1)}, u32[]{:S(2)}, u32[]{:S(2)}) %collective-permute-start.7) | collective-permute-done | bytes 1048608 | tf_op jit(solution)/shard_map/ppermute | solution.py:189
  130.3 4.9 %collective-permute-start.8 = (bf16[16,128,128]{2,1,0:T(8,128)(2,1)}, bf16[16,128,128]{2,1,0:T(8,128)(2,1)S(1)}, u32[]{:S(2)}, u32[]{:S(2)}) collective-permute-start(bf16[16,128,128]{2,1,0:T(8,128)(2,1)} %fusion.2), channel_id=1, source_target_pairs={{0,2},{1,3},{2,0},{3,1},{4,6},{5,7},{6,4},{7,5},{8,10},{9,11},{10,... | collective-permute-start | bytes 1572872 | tf_op jit(solution)/shard_map/ppermute | solution.py:191
  135.6 11.4 %collective-permute-done.8 = bf16[16,128,128]{2,1,0:T(8,128)(2,1)S(1)} collective-permute-done((bf16[16,128,128]{2,1,0:T(8,128)(2,1)}, bf16[16,128,128]{2,1,0:T(8,128)(2,1)S(1)}, u32[]{:S(2)}, u32[]{:S(2)}) %collective-permute-start.8) | collective-permute-done | bytes 524320 | tf_op jit(solution)/shard_map/ppermute | solution.py:191
  147.1 1.0 multiply_convert_fusion
  (34 shorter events, 7.1 us)
Async XLA Ops:
  6.5 114.5 %all-gather.3.cloned.1.call-start = ((), (), s32[]{:S(2)}) async-start(), calls=%async_computation | async-start | bytes 8912896 | tf_op jit(solution)/shard_map/all_gather | solution.py:128
  24.5 88.2 %copy-start = (bf16[3088,128]{1,0:T(8,128)(2,1)}, bf16[3088,128]{1,0:T(8,128)(2,1)S(1)}, u32[]{:S(2)}) copy-start(bf16[3088,128]{1,0:T(8,128)(2,1)S(1)} %fusion.1.refs_0_.rest_0_) | copy-start | bytes 2371588
  24.6 21.0 %collective-permute-start = (bf16[3088,128]{1,0:T(8,128)(2,1)S(1)}, bf16[3088,128]{1,0:T(8,128)(2,1)S(1)}, u32[]{:S(2)}, u32[]{:S(2)}) collective-permute-start(bf16[3088,128]{1,0:T(8,128)(2,1)S(1)} %fusion.1.refs_0_.rest_0_), channel_id=1, source_target_pairs={{0,16},{4,20},{8,24},{12,28},{16,0},{20,4},{24,8},{28,12},{1,17},{... | collective-permute-start | bytes 2371592 | tf_op jit(solution)/shard_map/ppermute | solution.py:141
  26.5 56.4 %collective-permute-start.2 = (bf16[3088,128]{1,0:T(8,128)(2,1)S(1)}, bf16[3088,128]{1,0:T(8,128)(2,1)S(1)}, u32[]{:S(2)}, u32[]{:S(2)}) collective-permute-start(bf16[3088,128]{1,0:T(8,128)(2,1)S(1)} %fusion.1.refs_0_.rest_0_), channel_id=1, source_target_pairs={{0,8},{4,12},{8,0},{12,4},{16,24},{20,28},{24,16},{28,20},{1,9},{5... | collective-permute-start | bytes 2371592 | tf_op jit(solution)/shard_map/ppermute | solution.py:141
  28.4 58.6 %collective-permute-start.4 = (bf16[3088,128]{1,0:T(8,128)(2,1)S(1)}, bf16[3088,128]{1,0:T(8,128)(2,1)S(1)}, u32[]{:S(2)}, u32[]{:S(2)}) collective-permute-start(bf16[3088,128]{1,0:T(8,128)(2,1)S(1)} %fusion.1.refs_0_.rest_0_), channel_id=1, source_target_pairs={{0,20},{4,24},{8,28},{12,16},{16,4},{20,8},{24,12},{28,0},{1,21},{... | collective-permute-start | bytes 2371592 | tf_op jit(solution)/shard_map/ppermute | solution.py:141
  30.3 56.7 %collective-permute-start.5 = (bf16[3088,128]{1,0:T(8,128)(2,1)S(1)}, bf16[3088,128]{1,0:T(8,128)(2,1)}, u32[]{:S(2)}, u32[]{:S(2)}) collective-permute-start(bf16[3088,128]{1,0:T(8,128)(2,1)S(1)} %fusion.1.refs_0_.rest_0_), channel_id=1, source_target_pairs={{0,24},{4,28},{8,16},{12,20},{16,8},{20,12},{24,0},{28,4},{1,25},{... | collective-permute-start | bytes 2371592 | tf_op jit(solution)/shard_map/ppermute | solution.py:141
  36.4 59.0 %collective-permute-start.6 = (bf16[3088,128]{1,0:T(8,128)(2,1)S(1)}, bf16[3088,128]{1,0:T(8,128)(2,1)}, u32[]{:S(2)}, u32[]{:S(2)}) collective-permute-start(bf16[3088,128]{1,0:T(8,128)(2,1)S(1)} %fusion.1.refs_0_.rest_0_), channel_id=1, source_target_pairs={{0,28},{4,16},{8,20},{12,24},{16,12},{20,0},{24,4},{28,8},{1,29},{... | collective-permute-start | bytes 2371592 | tf_op jit(solution)/shard_map/ppermute | solution.py:141
  45.6 67.2 %copy-start.1 = (bf16[3088,128]{1,0:T(8,128)(2,1)}, bf16[3088,128]{1,0:T(8,128)(2,1)S(1)}, u32[]{:S(2)}) copy-start(bf16[3088,128]{1,0:T(8,128)(2,1)S(1)} %collective-permute-done.refs_4_.rest_4_) | copy-start | bytes 2371588
  71.7 28.2 %collective-permute-start.1 = (bf16[3088,128]{1,0:T(8,128)(2,1)S(1)}, bf16[3088,128]{1,0:T(8,128)(2,1)}, u32[]{:S(2)}, u32[]{:S(2)}) collective-permute-start(bf16[3088,128]{1,0:T(8,128)(2,1)S(1)} %fusion.1.refs_0_.rest_0_), channel_id=1, source_target_pairs={{0,4},{4,8},{8,12},{12,0},{16,20},{20,24},{24,28},{28,16},{1,5},{5... | collective-permute-start | bytes 2371592 | tf_op jit(solution)/shard_map/ppermute | solution.py:141
  82.8 29.9 %copy-start.2 = (bf16[3088,128]{1,0:T(8,128)(2,1)}, bf16[3088,128]{1,0:T(8,128)(2,1)S(1)}, u32[]{:S(2)}) copy-start(bf16[3088,128]{1,0:T(8,128)(2,1)S(1)} %collective-permute-done.2.refs_2_.rest_2_) | copy-start | bytes 2371588
  82.8 29.9 %collective-permute-start.3 = (bf16[3088,128]{1,0:T(8,128)(2,1)S(1)}, bf16[3088,128]{1,0:T(8,128)(2,1)}, u32[]{:S(2)}, u32[]{:S(2)}) collective-permute-start(bf16[3088,128]{1,0:T(8,128)(2,1)S(1)} %fusion.1.refs_0_.rest_0_), channel_id=1, source_target_pairs={{0,12},{4,0},{8,4},{12,8},{16,28},{20,16},{24,20},{28,24},{1,13},{... | collective-permute-start | bytes 2371592 | tf_op jit(solution)/shard_map/ppermute | solution.py:141
  87.0 25.8 %copy-start.3 = (bf16[3088,128]{1,0:T(8,128)(2,1)}, bf16[3088,128]{1,0:T(8,128)(2,1)S(1)}, u32[]{:S(2)}) copy-start(bf16[3088,128]{1,0:T(8,128)(2,1)S(1)} %collective-permute-done.4.refs_5_.rest_5_) | copy-start | bytes 2371588
  121.1 14.1 %copy-start.5 = (s32[1,1,1,8,2]{3,4,2,1,0:T(2,128)S(1)}, s32[1,1,1,8,2]{3,4,2,1,0:T(2,128)}, u32[]{:S(2)}) copy-start(s32[1,1,1,8,2]{3,4,2,1,0:T(2,128)} %param.14) | copy-start | bytes 196
  123.9 11.4 %copy-start.4 = (bf16[1,1,1,8,2,128,128]{6,5,4,3,2,1,0:T(8,128)(2,1)S(1)}, bf16[1,1,1,8,2,128,128]{6,5,4,3,2,1,0:T(8,128)(2,1)}, u32[]{:S(2)}) copy-start(bf16[1,1,1,8,2,128,128]{6,5,4,3,2,1,0:T(8,128)(2,1)} %param.15) | copy-start | bytes 1572868
  123.9 5.4 %collective-permute-start.7 = (bf16[2,16,128,128]{3,2,1,0:T(8,128)(2,1)S(1)}, bf16[2,16,128,128]{3,2,1,0:T(8,128)(2,1)S(1)}, u32[]{:S(2)}, u32[]{:S(2)}) collective-permute-start(bf16[2,16,128,128]{3,2,1,0:T(8,128)(2,1)S(1)} %get-tuple-element.20), channel_id=1, source_target_pairs={{0,1},{1,0},{2,3},{3,2},{4,5},{5,4},{6,7},{7,6},{8,9},{9,8},{10,11... | collective-permute-start | bytes 3145736 | tf_op jit(solution)/shard_map/ppermute | solution.py:189
  130.3 16.8 %collective-permute-start.8 = (bf16[16,128,128]{2,1,0:T(8,128)(2,1)}, bf16[16,128,128]{2,1,0:T(8,128)(2,1)S(1)}, u32[]{:S(2)}, u32[]{:S(2)}) collective-permute-start(bf16[16,128,128]{2,1,0:T(8,128)(2,1)} %fusion.2), channel_id=1, source_target_pairs={{0,2},{1,3},{2,0},{3,1},{4,6},{5,7},{6,4},{7,5},{8,10},{9,11},{10,... | collective-permute-start | bytes 1572872 | tf_op jit(solution)/shard_map/ppermute | solution.py:191
Sparse Core Ops, SparseCore 0:
  9.4 111.5 all-gather.2

commit v6 on v5

v6 whole, which is shorter than its diff:
```python
import jax
import jax.numpy as jnp
from jax import lax
from jax.experimental import pallas as pl
from jax.experimental.pallas import tpu as pltpu
from jax.sharding import PartitionSpec as P

WINDOW = 16
SLOTS = 12


def by_offset(lines):
    both, ahead, back, across, across_beside = lines
    return [both.at[0], ahead.at[0], across, back.at[0], both.at[1], ahead.at[1], across_beside, back.at[1]]


def key_kernel(*refs):
    lines, shards, (ham_keys, it_keys, ham_slab, it_slab, sem) = refs[:5], refs[5:-5], refs[-5:]
    tail = ham_slab.shape[1]
    n_ham = ham_slab.shape[0]
    shards = by_offset(lines) + list(shards)
    copies = []
    for k, shard in enumerate(shards):
        slab = ham_slab.at[k] if k < n_ham else it_slab.at[k - n_ham]
        copies.append(pltpu.make_async_copy(shard.at[pl.ds(shard.shape[0] - tail, tail)], slab, sem.at[k]))
    for copy in copies:
        copy.start()
    for k, copy in enumerate(copies):
        copy.wait()
        if k < n_ham:
            held = ham_slab[k].astype(jnp.float32)
            for t in range(2):
                row, col, flag = (held[3 * t + i : 3 * t + i + 1] for i in range(3))
                place = jnp.where(flag > 0, row * 8 + col, -1.0)
                ham_keys[2 * k + t : 2 * k + t + 1] = place.astype(jnp.int32)
        else:
            held = it_slab[k - n_ham].astype(jnp.float32)
            place = jnp.where(held[1:2] > 0, held[0:1], -1.0)
            it_keys[k - n_ham : k - n_ham + 1] = place.astype(jnp.int32)


def list_tile(tile, hop, count, ham, own_keys, aim, pairs, slots):
    base = tile * slots + hop * 16 * 256

    def live(state):
        slot, _ = state
        return (slot < slots) & (ham[tile, slot] >= 0)

    def one_slot(state):
        slot, count = state
        key = ham[tile, slot]
        row = key // 8
        inner = key % 8
        for w in range(2):
            there = own_keys(inner * 2 + w)
            for v in range(2):
                pairs[count] = base + slot + (inner * 2 + w) * 256 + (row * 2 + v) * 65536
                count = count + (aim[row * 2 + v] == there).astype(jnp.int32)
        return slot + 1, count

    return lax.while_loop(live, one_slot, (jnp.int32(0), count))[1]


def pair_kernel(where, ham, iterate, aim, pairs):
    tiles = ham.shape[0]
    pieces = iterate.shape[0] + 1
    last = pieces // 2
    near = where[0] // 4
    step = where[0] % 4

    def one_tile(tile, count):
        array = tile // 2
        col = ((array // 4) ^ near) * 4 + (step - array % 4 + 4) % 4
        piece = col * 2 + tile % 2
        hop = (where[2] - piece + pieces) % pieces
        at = jnp.minimum(jnp.where(hop > last, hop - 1, hop), pieces - 2)
        keys = lambda spot: iterate[at, spot]
        listed = list_tile(tile, hop, count, ham, keys, aim, pairs, SLOTS)
        return jnp.where(hop == last, count, listed)

    end = pairs.shape[0]
    pairs[end - 1] = lax.fori_loop(0, tiles, one_tile, jnp.int32(0))
    pairs[end - 2] = where[1]
    piece = (where[2] + last) % pieces
    col = piece // 2
    array = ((col // 4) ^ near) * 4 + (step - col % 4 + 4) % 4
    pairs[end - 3] = array * 2 + piece % 2


def product_kernel(pairs, ham_keys, aim, *rest):
    lines, shards, rest = rest[:5], rest[5:22], rest[22:]
    hams = by_offset(lines)
    sent, kept, total, ham_buf, it_buf, slab, key_row, late_keys, late_pairs, ham_sem, it_sem, late_sem = rest
    size = ham_buf.shape[1]
    end = pairs.shape[0]
    count = pairs[end - 1]
    last = 8
    tail = slab.shape[0]
    slab_copy = pltpu.make_async_copy(shards[last].at[pl.ds(shards[last].shape[0] - tail, tail)], slab, late_sem.at[0])
    slab_copy.start()

    def start(codes, at):
        code = codes[at]
        ham_at = code % 256
        spot = (code // 256) % 16
        hop = (code // 4096) % 16
        slot = at % WINDOW
        rows = pl.ds(pl.multiple_of((ham_at % (2 * SLOTS)) * size, size), size)
        for k, ham in enumerate(hams):

            @pl.when(ham_at // (2 * SLOTS) == k)
            def _():
                pltpu.make_async_copy(ham.at[rows], ham_buf.at[slot], ham_sem.at[slot]).start()

        source = jnp.where((hop == last) & (spot < 8), 16, hop)
        rows = pl.ds(pl.multiple_of(jnp.where(hop == last, spot % 8, spot) * size, size), size)
        for k, shard in enumerate(shards):

            @pl.when(source == k)
            def _():
                pltpu.make_async_copy(shard.at[rows], it_buf.at[slot], it_sem.at[slot]).start()

    def prime(codes, count):
        def first(at, carry):
            start(codes, at)
            return carry

        lax.fori_loop(0, jnp.minimum(count, WINDOW), first, 0)

    def drain(codes, count):
        def multiply(at, carry):
            slot = at % WINDOW
            pltpu.make_async_copy(hams[0].at[pl.ds(0, size)], ham_buf.at[slot], ham_sem.at[slot]).wait()
            pltpu.make_async_copy(shards[0].at[pl.ds(0, size)], it_buf.at[slot], it_sem.at[slot]).wait()
            goal = codes[at] // 65536
            total[goal] += jnp.dot(ham_buf[slot], it_buf[slot], preferred_element_type=jnp.float32)

            @pl.when(at + WINDOW < count)
            def _():
                start(codes, at + WINDOW)

            return carry

        lax.fori_loop(0, count, multiply, 0)

    prime(pairs, count)

    def clear(at, carry):
        total[at] = jnp.zeros(total.shape[1:], total.dtype)
        return carry

    lax.fori_loop(0, total.shape[0], clear, 0, unroll=4)
    slab_copy.wait()
    held = slab[...].astype(jnp.float32)
    key_row[...] = jnp.where(held[1:2] > 0, held[0:1], -1.0).astype(jnp.int32)
    key_copy = pltpu.make_async_copy(key_row, late_keys, late_sem.at[1])
    key_copy.start()
    drain(pairs, count)
    key_copy.wait()
    late = list_tile(pairs[end - 3], last, jnp.int32(0), ham_keys, lambda spot: late_keys[0, spot], aim, late_pairs, SLOTS)
    prime(late_pairs, late)
    drain(late_pairs, late)
    half = sent.shape[1]
    depth = pairs[end - 2]
    core = depth % 2
    high = depth // 2

    def finish(at, carry):
        for part, far in enumerate((1 - high, high)):
            sent[part, at] = total[(far * 2 + 1 - core) * half + at].astype(sent.dtype)
            kept[part, at] = total[(far * 2 + core) * half + at].astype(kept.dtype)
        return carry

    lax.fori_loop(0, half, finish, 0, unroll=2)


def with_tail(blocks, ints):
    width = blocks.shape[-1]
    ints = ints.astype(blocks.dtype)
    ints = jnp.pad(ints, ((0, 16 - ints.shape[0]), (0, width - ints.shape[1])))
    return jnp.concatenate([blocks.reshape(-1, width), ints], axis=0)


def body(h_blocks, h_rows, h_cols, h_flags, x_blocks, x_cols, x_flags, previous):
    block = x_blocks.shape[-1]
    n_row, n_col, n_depth = lax.axis_size("row"), lax.axis_size("col"), lax.axis_size("depth")
    results = x_cols.shape[3] * x_cols.shape[4]
    where = jnp.stack([lax.axis_index("col"), lax.axis_index("depth"), lax.axis_index("row")]).astype(jnp.int32)
    x_ints = jnp.concatenate([x_cols.reshape(1, -1), x_flags.reshape(1, -1)], axis=0)
    own = with_tail(x_blocks, x_ints)
    h_ints = jnp.concatenate([h_rows, h_cols, h_flags], axis=2).reshape(-1, SLOTS)
    mine = with_tail(h_blocks, h_ints)

    up = [(i, (i + 1) % n_row) for i in range(n_row)]
    down = [(i, (i - 1) % n_row) for i in range(n_row)]
    last = n_row // 2
    cut = (results // 2) * block
    shards = [own] + [None] * n_row
    shards[1] = lax.ppermute(own, "row", up)
    shards[n_row - 1] = lax.ppermute(own, "row", down)
    beside = lax.ppermute(mine, "col", [(c, c ^ 4) for c in range(n_col)])
    pattern = jnp.concatenate([x_cols, x_flags], axis=2)
    beside, pattern = lax.optimization_barrier((beside, pattern))
    aim_ints = lax.all_gather(pattern, "depth", axis=1, tiled=True)
    both = jnp.stack([mine, beside])
    ahead = [(c, (c // 4) * 4 + (c + 1) % 4) for c in range(n_col)]
    back = [(c, (c // 4) * 4 + (c + 3) % 4) for c in range(n_col)]
    line_ahead = lax.ppermute(both, "col", ahead)
    line_back = lax.ppermute(both, "col", back)
    across = lax.ppermute(line_ahead[0], "col", ahead)
    across_beside = lax.ppermute(line_back[1], "col", back)
    lines = [both, line_ahead, line_back, across, across_beside]
    for hop in range(2, last):
        if hop == 5:
            shards[hop - 1], aim_ints = lax.optimization_barrier((shards[hop - 1], aim_ints))
        shards[hop] = lax.ppermute(shards[hop - 1], "row", up)
        shards[n_row - hop] = lax.ppermute(shards[n_row - hop + 1], "row", down)
    shards[last - 1], shards[last + 1], lines[3], lines[4] = lax.optimization_barrier(
        (shards[last - 1], shards[last + 1], lines[3], lines[4])
    )
    shards[last] = lax.ppermute(shards[last - 1][cut:], "row", up)
    shards[n_row] = lax.ppermute(shards[last + 1][:cut], "row", down)
    lines, shards = ([pltpu.with_memory_space_constraint(x, pltpu.HBM) for x in xs] for xs in (lines, shards))

    aim_keys = jnp.where(aim_ints[0, :, 1] > 0, aim_ints[0, :, 0], -2).reshape(-1)
    smem = pl.BlockSpec(memory_space=pltpu.SMEM)
    anywhere = pl.BlockSpec(memory_space=pl.ANY)
    vmem = pl.BlockSpec(memory_space=pltpu.VMEM)
    early = shards[:last] + shards[last + 1 : n_row]
    ham_keys, it_keys = pl.pallas_call(
        key_kernel,
        out_shape=(
            jax.ShapeDtypeStruct((2 * n_col, block), jnp.int32),
            jax.ShapeDtypeStruct((len(early), block), jnp.int32),
        ),
        in_specs=[anywhere] * (len(lines) + len(early)),
        out_specs=(vmem, vmem),
        scratch_shapes=[
            pltpu.VMEM((n_col, 16, block), jnp.bfloat16),
            pltpu.VMEM((len(early), 16, block), jnp.bfloat16),
            pltpu.SemaphoreType.DMA((n_col + len(early),)),
        ],
        name="keys",
    )(*lines, *early)
    pairs = pl.pallas_call(
        pair_kernel,
        out_shape=jax.ShapeDtypeStruct((512,), jnp.int32),
        in_specs=[smem] * 4,
        out_specs=smem,
        name="pairs",
    )(where, ham_keys, it_keys, aim_keys)
    halves = jax.ShapeDtypeStruct((2, results, block, block), jnp.bfloat16)
    sent, kept = pl.pallas_call(
        product_kernel,
        out_shape=(halves,) * 2,
        in_specs=[smem] * 3 + [anywhere] * (len(lines) + n_row + 1),
        out_specs=(vmem,) * 2,
        scratch_shapes=[
            pltpu.VMEM((n_depth * results, block, block), jnp.float32),
            pltpu.VMEM((WINDOW, block, block), jnp.bfloat16),
            pltpu.VMEM((WINDOW, block, block), jnp.bfloat16),
            pltpu.VMEM((16, block), jnp.bfloat16),
            pltpu.VMEM((1, block), jnp.int32),
            pltpu.SMEM((1, block), jnp.int32),
            pltpu.SMEM((64,), jnp.int32),
            pltpu.SemaphoreType.DMA((WINDOW,)),
            pltpu.SemaphoreType.DMA((WINDOW,)),
            pltpu.SemaphoreType.DMA((2,)),
        ],
        compiler_params=pltpu.CompilerParams(vmem_limit_bytes=24 << 20),
        name="products",
    )(*[pltpu.with_memory_space_constraint(x, pltpu.HBM) for x in (pairs, ham_keys, aim_keys)], *lines, *shards)
    near = lax.ppermute(sent, "depth", [(d, d ^ 1) for d in range(n_depth)])
    onward = (kept[0].astype(jnp.float32) + near[0].astype(jnp.float32)).astype(jnp.bfloat16)
    far = lax.ppermute(onward, "depth", [(d, d ^ 2) for d in range(n_depth)])
    prior = previous.reshape(results, block, block).astype(jnp.float32)
    live = x_flags.reshape(results, 1, 1).astype(jnp.float32)
    base = 2.0 * (kept[1].astype(jnp.float32) + near[1].astype(jnp.float32)) - prior
    base = lax.optimization_barrier(base)
    result = (base + 2.0 * far.astype(jnp.float32)) * live
    return result.astype(jnp.bfloat16).reshape(previous.shape)


def solution(mesh):
    placed = (
        P("row", "col", "depth", None, None, None),
        P("row", "col", "depth", None),
        P("row", "col", "depth", None),
        P("row", "col", "depth", None),
        P("row", "depth", "col", None, None, None, None),
        P("row", "depth", "col", None, None),
        P("row", "depth", "col", None, None),
        P("row", "depth", "col", None, None, None, None),
    )
    return jax.shard_map(
        body,
        mesh=mesh,
        in_specs=placed,
        out_specs=P("row", "depth", "col", None, None, None, None),
        check_vma=False,
    )
```

time: 156 us -> 178 us (1.14)
  starting transfers between devices: 29.9 us -> 89.5 us
  blocking collectives: 39.4 us -> 11 us
  between operations: 13.6 us -> 0.62 us
  local copies, waits for them, and re-layouts: 1.75 us -> 4.62 us
    ppermute x7 -> x21, starting transfers between devices: 21.8 us -> 79.2 us  [the longest x6 29.7 us: body(): shards[n_row - hop] = lax.ppermute(shards[n_row - hop + 1], 'row', down)]
    all_gather x2 -> x1, blocking collectives: 39.4 us -> 11 us  [body(): aim_ints = lax.all_gather(pattern, 'depth', axis=1, tiled=True)]
    ppermute x7 -> x21, waiting for transfers between devices: 37.9 us -> 42.1 us  [the longest x6 16.5 us: body(): shards[hop] = lax.ppermute(shards[hop - 1], 'row', up)]
    all_gather x1 -> x0, waiting for transfers between devices: 3.95 us -> none  [body(): iterate = lax.all_gather(x_blocks[0, 0, 0], 'row', axis=0)]
    ppermute x1, starting transfers between devices: 3.14 us -> 5.47 us  [body(): near = lax.ppermute(sent, 'depth', [(d, d ^ 1) for d in range(n_depth)])]
    concatenate x3 -> x4, other arithmetic: 1.9 us -> 0.07 us  [the longest x1 0.04 us: with_tail(): return jnp.concatenate([blocks.reshape(-1, width), ints], axis=0)]
    another operation x4 -> x7, other arithmetic: 2.71 us -> 4.24 us
  transfers between devices with their start and end apart: 10 -> 23, of which waited for: 8 -> 10; matrix products, arithmetic and copies ran while one was open for 4% -> 2% of each run, Pallas kernels for 3% -> 3%
where the time goes in v6:
time: 178 us; the launch traced here: 177 us
  starting transfers between devices  89.5 us (50%)
  waiting for transfers between devices  55.8 us (31%)
  blocking collectives  11 us (6%)
  Pallas kernels  8.81 us (5%)
  other arithmetic  6.49 us (4%)
  local copies, waits for them, and re-layouts  4.62 us (3%)
    ppermute x6, starting transfers between devices, body(): shards[n_row - hop] = lax.ppermute(shards[n_row - hop + 1], 'row', down)  29.7 us
    ppermute x6, waiting for transfers between devices, body(): shards[hop] = lax.ppermute(shards[hop - 1], 'row', up)  16.5 us
    ppermute x6, waiting for transfers between devices, body(): shards[n_row - hop] = lax.ppermute(shards[n_row - hop + 1], 'row', down)  11.8 us
    ppermute x6, starting transfers between devices, body(): shards[hop] = lax.ppermute(shards[hop - 1], 'row', up)  11.5 us
    ppermute x1, waiting for transfers between devices, body(): far = lax.ppermute(onward, 'depth', [(d, d ^ 2) for d in range(n_depth)])  11.5 us
    ppermute x1, starting transfers between devices, body(): shards[n_row - 1] = lax.ppermute(own, 'row', down)  11.1 us
    all_gather x1, blocking collectives, body(): aim_ints = lax.all_gather(pattern, 'depth', axis=1, tiled=True)  11 us
    ppermute x1, waiting for transfers between devices, body(): shards[n_row - 1] = lax.ppermute(own, 'row', down)  8.4 us
  transfers between devices with their start and end apart: 23, of which 10 were waited for; matrix products, arithmetic and copies ran while one was open for 2% of the time, Pallas kernels for 3%

profile of v6, /device:TPU:1, one launch (start us, length us, event | category | flops | bytes accessed | tf_op | source)
XLA Modules:
  0.0 176.8 jit_solution(9182680008215234181)
XLA Ops:
  3.5 3.9 %collective-permute-start = (bf16[3088,128]{1,0:T(8,128)(2,1)S(1)}, bf16[3088,128]{1,0:T(8,128)(2,1)S(1)}, u32[]{:S(2)}, u32[]{:S(2)}) collective-permute-start(bf16[3088,128]{1,0:T(8,128)(2,1)S(1)} %get-tuple-element.30), channel_id=1, source_target_pairs={{0,16},{4,20},{8,24},{12,28},{16,0},{20,4},{24,8},{28,12},{1,17},{... | collective-permute-start | bytes 2371592 | tf_op jit(solution)/shard_map/ppermute | solution.py:201
  7.9 11.1 %collective-permute-start.10 = (bf16[2064,128]{1,0:T(8,128)(2,1)S(1)}, bf16[2064,128]{1,0:T(8,128)(2,1)S(1)}, u32[]{:S(2)}, u32[]{:S(2)}) collective-permute-start(bf16[2064,128]{1,0:T(8,128)(2,1)S(1)} %pad_maximum_fusion.1.refs_5_.rest_5_), channel_id=1, source_target_pairs={{0,480},{32,0},{64,32},{96,64},{128,96},{160,128},{192,160},{224,1... | collective-permute-start | bytes 1585160 | tf_op jit(solution)/shard_map/ppermute | solution.py:200
  21.0 8.4 %collective-permute-done.10.refs_19_.rest_20_ = bf16[2064,128]{1,0:T(8,128)(2,1)S(1)} collective-permute-done((bf16[2064,128]{1,0:T(8,128)(2,1)S(1)}, bf16[2064,128]{1,0:T(8,128)(2,1)S(1)}, u32[]{:S(2)}, u32[]{:S(2)}) %collective-permute-start.10) | collective-permute-done | bytes 528416 | tf_op jit(solution)/shard_map/ppermute | solution.py:200
  29.4 5.3 %collective-permute-start.11 = (bf16[2064,128]{1,0:T(8,128)(2,1)S(1)}, bf16[2064,128]{1,0:T(8,128)(2,1)S(1)}, u32[]{:S(2)}, u32[]{:S(2)}) collective-permute-start(bf16[2064,128]{1,0:T(8,128)(2,1)S(1)} %collective-permute-done.10.refs_19_.rest_20_), channel_id=1, source_target_pairs={{0,480},{32,0},{64,32},{96,64},{128,96},{160,128},{192,160},{224,1... | collective-permute-start | bytes 1585160 | tf_op jit(solution)/shard_map/ppermute | solution.py:217
  36.9 4.6 %collective-permute-start.2 = (bf16[2,3088,128]{2,1,0:T(8,128)(2,1)S(1)}, bf16[2,3088,128]{2,1,0:T(8,128)(2,1)S(1)}, u32[]{:S(2)}, u32[]{:S(2)}) collective-permute-start(bf16[2,3088,128]{2,1,0:T(8,128)(2,1)S(1)} %pad_maximum_fusion.refs_0_.rest_0_), channel_id=1, source_target_pairs={{0,12},{4,0},{8,4},{12,8},{16,28},{20,16},{24,20},{28,24},{1,13},{... | collective-permute-start | bytes 4743176 | tf_op jit(solution)/shard_map/ppermute | solution.py:209
  41.5 7.7 %collective-permute-done.4.refs_7_.rest_7_ = bf16[2064,128]{1,0:T(8,128)(2,1)S(1)} collective-permute-done((bf16[2064,128]{1,0:T(8,128)(2,1)S(1)}, bf16[2064,128]{1,0:T(8,128)(2,1)S(1)}, u32[]{:S(2)}, u32[]{:S(2)}) %collective-permute-start.4) | collective-permute-done | bytes 528416 | tf_op jit(solution)/shard_map/ppermute | solution.py:216
  51.1 4.6 %collective-permute-start.12 = (bf16[2064,128]{1,0:T(8,128)(2,1)S(1)}, bf16[2064,128]{1,0:T(8,128)(2,1)S(1)}, u32[]{:S(2)}, u32[]{:S(2)}) collective-permute-start(bf16[2064,128]{1,0:T(8,128)(2,1)S(1)} %collective-permute-done.11.refs_18_.rest_19_), channel_id=1, source_target_pairs={{0,480},{32,0},{64,32},{96,64},{128,96},{160,128},{192,160},{224,1... | collective-permute-start | bytes 1585160 | tf_op jit(solution)/shard_map/ppermute | solution.py:217
  58.9 3.8 %collective-permute-done.5.refs_8_.rest_8_ = bf16[2064,128]{1,0:T(8,128)(2,1)S(1)} collective-permute-done((bf16[2064,128]{1,0:T(8,128)(2,1)S(1)}, bf16[2064,128]{1,0:T(8,128)(2,1)S(1)}, u32[]{:S(2)}, u32[]{:S(2)}) %collective-permute-start.5) | collective-permute-done | bytes 528416 | tf_op jit(solution)/shard_map/ppermute | solution.py:216
  64.7 4.6 %collective-permute-start.13 = (bf16[2064,128]{1,0:T(8,128)(2,1)S(1)}, bf16[2064,128]{1,0:T(8,128)(2,1)S(1)}, u32[]{:S(2)}, u32[]{:S(2)}) collective-permute-start(bf16[2064,128]{1,0:T(8,128)(2,1)S(1)} %collective-permute-done.12.refs_17_.rest_18_), channel_id=1, source_target_pairs={{0,480},{32,0},{64,32},{96,64},{128,96},{160,128},{192,160},{224,1... | collective-permute-start | bytes 1585160 | tf_op jit(solution)/shard_map/ppermute | solution.py:217
  69.3 11.0 %all_gather.3 = s32[1,4,2,8,2]{3,4,2,0,1:T(2,128)S(1)} all-gather(s32[1,1,2,8,2]{3,4,2,0,1:T(2,128)S(1)} %pad_add_fusion), channel_id=1, replica_groups=mesh['row'=16,'col'=8,'depth'=4] {'depth'}, dimensions={1}, use_global_device_ids=true | all-gather | bytes 640 | tf_op jit(solution)/shard_map/all_gather | solution.py:204
  82.2 4.6 %collective-permute-start.14 = (bf16[2064,128]{1,0:T(8,128)(2,1)S(1)}, bf16[2064,128]{1,0:T(8,128)(2,1)S(1)}, u32[]{:S(2)}, u32[]{:S(2)}) collective-permute-start(bf16[2064,128]{1,0:T(8,128)(2,1)S(1)} %collective-permute-done.13.refs_16_.rest_17_), channel_id=1, source_target_pairs={{0,480},{32,0},{64,32},{96,64},{128,96},{160,128},{192,160},{224,1... | collective-permute-start | bytes 1585160 | tf_op jit(solution)/shard_map/ppermute | solution.py:217
  87.8 4.6 %collective-permute-start.18 = (bf16[3088,128]{1,0:T(8,128)(2,1)}, bf16[3088,128]{1,0:T(8,128)(2,1)S(1)}, u32[]{:S(2)}, u32[]{:S(2)}) collective-permute-start(bf16[3088,128]{1,0:T(8,128)(2,1)} %slice_bitcast_fusion), channel_id=1, source_target_pairs={{0,12},{4,0},{8,4},{12,8},{16,28},{20,16},{24,20},{28,24},{1,13},{... | collective-permute-start | bytes 2371592 | tf_op jit(solution)/shard_map/ppermute | solution.py:211
  92.5 5.2 %collective-permute-done.14.refs_15_.rest_16_ = bf16[2064,128]{1,0:T(8,128)(2,1)S(1)} collective-permute-done((bf16[2064,128]{1,0:T(8,128)(2,1)S(1)}, bf16[2064,128]{1,0:T(8,128)(2,1)S(1)}, u32[]{:S(2)}, u32[]{:S(2)}) %collective-permute-start.14) | collective-permute-done | bytes 528416 | tf_op jit(solution)/shard_map/ppermute | solution.py:217
  97.7 5.3 %collective-permute-start.15 = (bf16[2064,128]{1,0:T(8,128)(2,1)S(1)}, bf16[2064,128]{1,0:T(8,128)(2,1)}, u32[]{:S(2)}, u32[]{:S(2)}) collective-permute-start(bf16[2064,128]{1,0:T(8,128)(2,1)S(1)} %collective-permute-done.14.refs_15_.rest_16_), channel_id=1, source_target_pairs={{0,480},{32,0},{64,32},{96,64},{128,96},{160,128},{192,160},{224,1... | collective-permute-start | bytes 1585160 | tf_op jit(solution)/shard_map/ppermute | solution.py:217
  108.3 4.7 %collective-permute-done.15.refs_14_.rest_15_ = bf16[2064,128]{1,0:T(8,128)(2,1)} collective-permute-done((bf16[2064,128]{1,0:T(8,128)(2,1)S(1)}, bf16[2064,128]{1,0:T(8,128)(2,1)}, u32[]{:S(2)}, u32[]{:S(2)}) %collective-permute-start.15) | collective-permute-done | bytes 528416 | tf_op jit(solution)/shard_map/ppermute | solution.py:217
  113.0 5.4 %collective-permute-start.16 = (bf16[2064,128]{1,0:T(8,128)(2,1)}, bf16[2064,128]{1,0:T(8,128)(2,1)S(1)}, u32[]{:S(2)}, u32[]{:S(2)}) collective-permute-start(bf16[2064,128]{1,0:T(8,128)(2,1)} %collective-permute-done.15.refs_14_.rest_15_), channel_id=1, source_target_pairs={{0,480},{32,0},{64,32},{96,64},{128,96},{160,128},{192,160},{224,1... | collective-permute-start | bytes 1585160 | tf_op jit(solution)/shard_map/ppermute | solution.py:217
  120.4 5.4 %collective-permute-done.17.refs_3_.rest_3_ = bf16[3088,128]{1,0:T(8,128)(2,1)S(1)} collective-permute-done((bf16[3088,128]{1,0:T(8,128)(2,1)S(1)}, bf16[3088,128]{1,0:T(8,128)(2,1)S(1)}, u32[]{:S(2)}, u32[]{:S(2)}) %collective-permute-start.17) | collective-permute-done | bytes 790560 | tf_op jit(solution)/shard_map/ppermute | solution.py:210
  127.7 5.0 %collective-permute-done.9.refs_12_.rest_12_ = bf16[2064,128]{1,0:T(8,128)(2,1)S(1)} collective-permute-done((bf16[2064,128]{1,0:T(8,128)(2,1)}, bf16[2064,128]{1,0:T(8,128)(2,1)S(1)}, u32[]{:S(2)}, u32[]{:S(2)}) %collective-permute-start.9) | collective-permute-done | bytes 528416 | tf_op jit(solution)/shard_map/ppermute | solution.py:216
  135.4 3.4 %collective-permute-start.19 = (bf16[1040,128]{1,0:T(8,128)(2,1)S(1)}, bf16[1040,128]{1,0:T(8,128)(2,1)S(1)}, u32[]{:S(2)}, u32[]{:S(2)}) collective-permute-start(bf16[1040,128]{1,0:T(8,128)(2,1)S(1)} %slice.34), channel_id=1, source_target_pairs={{0,32},{32,64},{64,96},{96,128},{128,160},{160,192},{192,224},{224... | collective-permute-start | bytes 798728 | tf_op jit(solution)/shard_map/ppermute | solution.py:221
  141.9 3.5 %pairs.1 = s32[512]{0:T(512)} custom-call(s32[3]{0:T(128)} %pad_add_fusion.1.where, s32[16,128]{1,0:T(8,128)} %get-tuple-element.24.ham.ham_keys, s32[15,128]{1,0:T(8,128)} %get-tuple-element.25.iterate, s32[64]{0:T(128)} %select_n.9.aim), custom_call_target="tpu_custom_call" | custom-call | tf_op jit(solution)/shard_map/pairs/pallas_call | solution.py:245
  146.8 3.6 %products.1 = (bf16[2,16,128,128]{3,2,1,0:T(8,128)(2,1)S(1)}, bf16[2,16,128,128]{3,2,1,0:T(8,128)(2,1)S(1)}) custom-call(s32[512]{0:T(512)} %pairs.1, s32[16,128]{1,0:T(8,128)} %get-tuple-element.24.ham.ham_keys, s32[64]{0:T(128)} %select_n.9.aim, bf16[2,3088,128]{2,1,0:T(8,128)(2,1)} %copy-done, bf16[2,3088,128]{2,1,0:T(8,128)(2,1)} %copy-done.2, ...), custom_call_target="tpu_custom_call" | custom-call | tf_op jit(solution)/shard_map/products/pallas_call | solution.py:253
  150.5 5.5 %collective-permute-start.21 = (bf16[2,16,128,128]{3,2,1,0:T(8,128)(2,1)S(1)}, bf16[2,16,128,128]{3,2,1,0:T(8,128)(2,1)S(1)}, u32[]{:S(2)}, u32[]{:S(2)}) collective-permute-start(bf16[2,16,128,128]{3,2,1,0:T(8,128)(2,1)S(1)} %get-tuple-element.28), channel_id=1, source_target_pairs={{0,1},{1,0},{2,3},{3,2},{4,5},{5,4},{6,7},{7,6},{8,9},{9,8},{10,11... | collective-permute-start | bytes 3145736 | tf_op jit(solution)/shard_map/ppermute | solution.py:273
  159.1 4.8 %collective-permute-start.22 = (bf16[16,128,128]{2,1,0:T(8,128)(2,1)}, bf16[16,128,128]{2,1,0:T(8,128)(2,1)S(1)}, u32[]{:S(2)}, u32[]{:S(2)}) collective-permute-start(bf16[16,128,128]{2,1,0:T(8,128)(2,1)} %fusion.2), channel_id=1, source_target_pairs={{0,2},{1,3},{2,0},{3,1},{4,6},{5,7},{6,4},{7,5},{8,10},{9,11},{10,... | collective-permute-start | bytes 1572872 | tf_op jit(solution)/shard_map/ppermute | solution.py:275
  164.4 11.5 %collective-permute-done.22 = bf16[16,128,128]{2,1,0:T(8,128)(2,1)S(1)} collective-permute-done((bf16[16,128,128]{2,1,0:T(8,128)(2,1)}, bf16[16,128,128]{2,1,0:T(8,128)(2,1)S(1)}, u32[]{:S(2)}, u32[]{:S(2)}) %collective-permute-start.22) | collective-permute-done | bytes 524320 | tf_op jit(solution)/shard_map/ppermute | solution.py:275
  (103 shorter events, 38.8 us)
Async XLA Ops:
  3.5 33.2 %collective-permute-start = (bf16[3088,128]{1,0:T(8,128)(2,1)S(1)}, bf16[3088,128]{1,0:T(8,128)(2,1)S(1)}, u32[]{:S(2)}, u32[]{:S(2)}) collective-permute-start(bf16[3088,128]{1,0:T(8,128)(2,1)S(1)} %get-tuple-element.30), channel_id=1, source_target_pairs={{0,16},{4,20},{8,24},{12,28},{16,0},{20,4},{24,8},{28,12},{1,17},{... | collective-permute-start | bytes 2371592 | tf_op jit(solution)/shard_map/ppermute | solution.py:201
  7.9 21.5 %collective-permute-start.10 = (bf16[2064,128]{1,0:T(8,128)(2,1)S(1)}, bf16[2064,128]{1,0:T(8,128)(2,1)S(1)}, u32[]{:S(2)}, u32[]{:S(2)}) collective-permute-start(bf16[2064,128]{1,0:T(8,128)(2,1)S(1)} %pad_maximum_fusion.1.refs_5_.rest_5_), channel_id=1, source_target_pairs={{0,480},{32,0},{64,32},{96,64},{128,96},{160,128},{192,160},{224,1... | collective-permute-start | bytes 1585160 | tf_op jit(solution)/shard_map/ppermute | solution.py:200
  19.1 15.7 %collective-permute-start.3 = (bf16[2064,128]{1,0:T(8,128)(2,1)S(1)}, bf16[2064,128]{1,0:T(8,128)(2,1)S(1)}, u32[]{:S(2)}, u32[]{:S(2)}) collective-permute-start(bf16[2064,128]{1,0:T(8,128)(2,1)S(1)} %pad_maximum_fusion.1.refs_5_.rest_5_), channel_id=1, source_target_pairs={{0,32},{32,64},{64,96},{96,128},{128,160},{160,192},{192,224},{224... | collective-permute-start | bytes 1585160 | tf_op jit(solution)/shard_map/ppermute | solution.py:199
  29.4 21.7 %collective-permute-start.11 = (bf16[2064,128]{1,0:T(8,128)(2,1)S(1)}, bf16[2064,128]{1,0:T(8,128)(2,1)S(1)}, u32[]{:S(2)}, u32[]{:S(2)}) collective-permute-start(bf16[2064,128]{1,0:T(8,128)(2,1)S(1)} %collective-permute-done.10.refs_19_.rest_20_), channel_id=1, source_target_pairs={{0,480},{32,0},{64,32},{96,64},{128,96},{160,128},{192,160},{224,1... | collective-permute-start | bytes 1585160 | tf_op jit(solution)/shard_map/ppermute | solution.py:217
  34.7 14.5 %collective-permute-start.4 = (bf16[2064,128]{1,0:T(8,128)(2,1)S(1)}, bf16[2064,128]{1,0:T(8,128)(2,1)S(1)}, u32[]{:S(2)}, u32[]{:S(2)}) collective-permute-start(bf16[2064,128]{1,0:T(8,128)(2,1)S(1)} %collective-permute-done.3.refs_6_.rest_6_), channel_id=1, source_target_pairs={{0,32},{32,64},{64,96},{96,128},{128,160},{160,192},{192,224},{224... | collective-permute-start | bytes 1585160 | tf_op jit(solution)/shard_map/ppermute | solution.py:216
  36.9 49.9 %collective-permute-start.2 = (bf16[2,3088,128]{2,1,0:T(8,128)(2,1)S(1)}, bf16[2,3088,128]{2,1,0:T(8,128)(2,1)S(1)}, u32[]{:S(2)}, u32[]{:S(2)}) collective-permute-start(bf16[2,3088,128]{2,1,0:T(8,128)(2,1)S(1)} %pad_maximum_fusion.refs_0_.rest_0_), channel_id=1, source_target_pairs={{0,12},{4,0},{8,4},{12,8},{16,28},{20,16},{24,20},{28,24},{1,13},{... | collective-permute-start | bytes 4743176 | tf_op jit(solution)/shard_map/ppermute | solution.py:209
  49.2 69.2 %copy-start.11 = (bf16[2064,128]{1,0:T(8,128)(2,1)}, bf16[2064,128]{1,0:T(8,128)(2,1)S(1)}, u32[]{:S(2)}) copy-start(bf16[2064,128]{1,0:T(8,128)(2,1)S(1)} %collective-permute-done.4.refs_7_.rest_7_) | copy-start | bytes 1585156
  49.2 13.5 %collective-permute-start.5 = (bf16[2064,128]{1,0:T(8,128)(2,1)S(1)}, bf16[2064,128]{1,0:T(8,128)(2,1)S(1)}, u32[]{:S(2)}, u32[]{:S(2)}) collective-permute-start(bf16[2064,128]{1,0:T(8,128)(2,1)S(1)} %collective-permute-done.4.refs_7_.rest_7_), channel_id=1, source_target_pairs={{0,32},{32,64},{64,96},{96,128},{128,160},{160,192},{192,224},{224... | collective-permute-start | bytes 1585160 | tf_op jit(solution)/shard_map/ppermute | solution.py:216
  51.1 13.5 %collective-permute-start.12 = (bf16[2064,128]{1,0:T(8,128)(2,1)S(1)}, bf16[2064,128]{1,0:T(8,128)(2,1)S(1)}, u32[]{:S(2)}, u32[]{:S(2)}) collective-permute-start(bf16[2064,128]{1,0:T(8,128)(2,1)S(1)} %collective-permute-done.11.refs_18_.rest_19_), channel_id=1, source_target_pairs={{0,480},{32,0},{64,32},{96,64},{128,96},{160,128},{192,160},{224,1... | collective-permute-start | bytes 1585160 | tf_op jit(solution)/shard_map/ppermute | solution.py:217
  55.7 49.2 %collective-permute-start.1 = (bf16[2,3088,128]{2,1,0:T(8,128)(2,1)S(1)}, bf16[2,3088,128]{2,1,0:T(8,128)(2,1)S(1)}, u32[]{:S(2)}, u32[]{:S(2)}) collective-permute-start(bf16[2,3088,128]{2,1,0:T(8,128)(2,1)S(1)} %pad_maximum_fusion.refs_0_.rest_0_), channel_id=1, source_target_pairs={{0,4},{4,8},{8,12},{12,0},{16,20},{20,24},{24,28},{28,16},{1,5},{5... | collective-permute-start | bytes 4743176 | tf_op jit(solution)/shard_map/ppermute | solution.py:208
  62.7 17.5 %collective-permute-start.6 = (bf16[2064,128]{1,0:T(8,128)(2,1)S(1)}, bf16[2064,128]{1,0:T(8,128)(2,1)S(1)}, u32[]{:S(2)}, u32[]{:S(2)}) collective-permute-start(bf16[2064,128]{1,0:T(8,128)(2,1)S(1)} %collective-permute-done.5.refs_8_.rest_8_), channel_id=1, source_target_pairs={{0,32},{32,64},{64,96},{96,128},{128,160},{160,192},{192,224},{224... | collective-permute-start | bytes 1585160 | tf_op jit(solution)/shard_map/ppermute | solution.py:216
  64.7 17.5 %collective-permute-start.13 = (bf16[2064,128]{1,0:T(8,128)(2,1)S(1)}, bf16[2064,128]{1,0:T(8,128)(2,1)S(1)}, u32[]{:S(2)}, u32[]{:S(2)}) collective-permute-start(bf16[2064,128]{1,0:T(8,128)(2,1)S(1)} %collective-permute-done.12.refs_17_.rest_18_), channel_id=1, source_target_pairs={{0,480},{32,0},{64,32},{96,64},{128,96},{160,128},{192,160},{224,1... | collective-permute-start | bytes 1585160 | tf_op jit(solution)/shard_map/ppermute | solution.py:217
  80.3 22.7 %collective-permute-start.7 = (bf16[2064,128]{1,0:T(8,128)(2,1)S(1)}, bf16[2064,128]{1,0:T(8,128)(2,1)S(1)}, u32[]{:S(2)}, u32[]{:S(2)}) collective-permute-start(bf16[2064,128]{1,0:T(8,128)(2,1)S(1)} %collective-permute-done.6.refs_9_.rest_9_), channel_id=1, source_target_pairs={{0,32},{32,64},{64,96},{96,128},{128,160},{160,192},{192,224},{224... | collective-permute-start | bytes 1585160 | tf_op jit(solution)/shard_map/ppermute | solution.py:216
  82.2 15.5 %collective-permute-start.14 = (bf16[2064,128]{1,0:T(8,128)(2,1)S(1)}, bf16[2064,128]{1,0:T(8,128)(2,1)S(1)}, u32[]{:S(2)}, u32[]{:S(2)}) collective-permute-start(bf16[2064,128]{1,0:T(8,128)(2,1)S(1)} %collective-permute-done.13.refs_16_.rest_17_), channel_id=1, source_target_pairs={{0,480},{32,0},{64,32},{96,64},{128,96},{160,128},{192,160},{224,1... | collective-permute-start | bytes 1585160 | tf_op jit(solution)/shard_map/ppermute | solution.py:217
  87.8 32.6 %collective-permute-start.18 = (bf16[3088,128]{1,0:T(8,128)(2,1)}, bf16[3088,128]{1,0:T(8,128)(2,1)S(1)}, u32[]{:S(2)}, u32[]{:S(2)}) collective-permute-start(bf16[3088,128]{1,0:T(8,128)(2,1)} %slice_bitcast_fusion), channel_id=1, source_target_pairs={{0,12},{4,0},{8,4},{12,8},{16,28},{20,16},{24,20},{28,24},{1,13},{... | collective-permute-start | bytes 2371592 | tf_op jit(solution)/shard_map/ppermute | solution.py:211
  97.7 15.3 %collective-permute-start.15 = (bf16[2064,128]{1,0:T(8,128)(2,1)S(1)}, bf16[2064,128]{1,0:T(8,128)(2,1)}, u32[]{:S(2)}, u32[]{:S(2)}) collective-permute-start(bf16[2064,128]{1,0:T(8,128)(2,1)S(1)} %collective-permute-done.14.refs_15_.rest_16_), channel_id=1, source_target_pairs={{0,480},{32,0},{64,32},{96,64},{128,96},{160,128},{192,160},{224,1... | collective-permute-start | bytes 1585160 | tf_op jit(solution)/shard_map/ppermute | solution.py:217
  103.0 15.4 %collective-permute-start.8 = (bf16[2064,128]{1,0:T(8,128)(2,1)S(1)}, bf16[2064,128]{1,0:T(8,128)(2,1)}, u32[]{:S(2)}, u32[]{:S(2)}) collective-permute-start(bf16[2064,128]{1,0:T(8,128)(2,1)S(1)} %collective-permute-done.7.refs_10_.rest_10_), channel_id=1, source_target_pairs={{0,32},{32,64},{64,96},{96,128},{128,160},{160,192},{192,224},{224... | collective-permute-start | bytes 1585160 | tf_op jit(solution)/shard_map/ppermute | solution.py:216
  105.0 20.8 %collective-permute-start.17 = (bf16[3088,128]{1,0:T(8,128)(2,1)S(1)}, bf16[3088,128]{1,0:T(8,128)(2,1)S(1)}, u32[]{:S(2)}, u32[]{:S(2)}) collective-permute-start(bf16[3088,128]{1,0:T(8,128)(2,1)S(1)} %slice_bitcast_fusion.1), channel_id=1, source_target_pairs={{0,4},{4,8},{8,12},{12,0},{16,20},{20,24},{24,28},{28,16},{1,5},{5... | collective-permute-start | bytes 2371592 | tf_op jit(solution)/shard_map/ppermute | solution.py:210
  113.0 14.8 %collective-permute-start.16 = (bf16[2064,128]{1,0:T(8,128)(2,1)}, bf16[2064,128]{1,0:T(8,128)(2,1)S(1)}, u32[]{:S(2)}, u32[]{:S(2)}) collective-permute-start(bf16[2064,128]{1,0:T(8,128)(2,1)} %collective-permute-done.15.refs_14_.rest_15_), channel_id=1, source_target_pairs={{0,480},{32,0},{64,32},{96,64},{128,96},{160,128},{192,160},{224,1... | collective-permute-start | bytes 1585160 | tf_op jit(solution)/shard_map/ppermute | solution.py:217
  118.4 14.3 %collective-permute-start.9 = (bf16[2064,128]{1,0:T(8,128)(2,1)}, bf16[2064,128]{1,0:T(8,128)(2,1)S(1)}, u32[]{:S(2)}, u32[]{:S(2)}) collective-permute-start(bf16[2064,128]{1,0:T(8,128)(2,1)} %collective-permute-done.8.refs_11_.rest_11_), channel_id=1, source_target_pairs={{0,32},{32,64},{64,96},{96,128},{128,160},{160,192},{192,224},{224... | collective-permute-start | bytes 1585160 | tf_op jit(solution)/shard_map/ppermute | solution.py:216
  133.5 11.9 %collective-permute-start.20 = (bf16[1024,128]{1,0:T(8,128)(2,1)}, bf16[1024,128]{1,0:T(8,128)(2,1)S(1)}, u32[]{:S(2)}, u32[]{:S(2)}) collective-permute-start(bf16[1024,128]{1,0:T(8,128)(2,1)} %slice.35), channel_id=1, source_target_pairs={{0,480},{32,0},{64,32},{96,64},{128,96},{160,128},{192,160},{224,1... | collective-permute-start | bytes 786440 | tf_op jit(solution)/shard_map/ppermute | solution.py:222
  135.4 10.0 %collective-permute-start.19 = (bf16[1040,128]{1,0:T(8,128)(2,1)S(1)}, bf16[1040,128]{1,0:T(8,128)(2,1)S(1)}, u32[]{:S(2)}, u32[]{:S(2)}) collective-permute-start(bf16[1040,128]{1,0:T(8,128)(2,1)S(1)} %slice.34), channel_id=1, source_target_pairs={{0,32},{32,64},{64,96},{96,128},{128,160},{160,192},{192,224},{224... | collective-permute-start | bytes 798728 | tf_op jit(solution)/shard_map/ppermute | solution.py:221
  150.5 7.7 %collective-permute-start.21 = (bf16[2,16,128,128]{3,2,1,0:T(8,128)(2,1)S(1)}, bf16[2,16,128,128]{3,2,1,0:T(8,128)(2,1)S(1)}, u32[]{:S(2)}, u32[]{:S(2)}) collective-permute-start(bf16[2,16,128,128]{3,2,1,0:T(8,128)(2,1)S(1)} %get-tuple-element.28), channel_id=1, source_target_pairs={{0,1},{1,0},{2,3},{3,2},{4,5},{5,4},{6,7},{7,6},{8,9},{9,8},{10,11... | collective-permute-start | bytes 3145736 | tf_op jit(solution)/shard_map/ppermute | solution.py:273
  159.1 16.7 %collective-permute-start.22 = (bf16[16,128,128]{2,1,0:T(8,128)(2,1)}, bf16[16,128,128]{2,1,0:T(8,128)(2,1)S(1)}, u32[]{:S(2)}, u32[]{:S(2)}) collective-permute-start(bf16[16,128,128]{2,1,0:T(8,128)(2,1)} %fusion.2), channel_id=1, source_target_pairs={{0,2},{1,3},{2,0},{3,1},{4,6},{5,7},{6,4},{7,5},{8,10},{9,11},{10,... | collective-permute-start | bytes 1572872 | tf_op jit(solution)/shard_map/ppermute | solution.py:275
  (23 other events, 519.2 us)

commit v7 on v5

--- a/solution.py
+++ b/solution.py
@@ -26,7 +26,12 @@
             keys[2 * k + t : 2 * k + t + 1] = place.astype(jnp.int32)
 
 
-def pair_kernel(where, ham, iterate, aim, pairs):
+def pair_kernel(where, ham, iterate, aim, pairs, touched):
+    def untouch(at, carry):
+        touched[at] = 0
+        return carry
+
+    lax.fori_loop(0, aim.shape[0], untouch, 0)
     pieces = ham.shape[0]
     slots = 12
     per_col = pieces // 8
@@ -52,8 +57,12 @@
             for w in range(2):
                 there = iterate[piece, inner * 2 + w]
                 for v in range(2):
-                    pairs[count] = base + slot + (inner * 2 + w) * 256 + (row * 2 + v) * 65536
-                    count = count + (aim[row * 2 + v] == there).astype(jnp.int32)
+                    goal = row * 2 + v
+                    match = (aim[goal] == there).astype(jnp.int32)
+                    seen = touched[goal]
+                    pairs[count] = base + slot + (inner * 2 + w) * 256 + (goal + 64 * seen) * 65536
+                    touched[goal] = seen | match
+                    count = count + match
             return slot + 1, count
 
         return lax.while_loop(live, one_slot, (jnp.int32(0), count))[1]
@@ -87,18 +96,39 @@
 
     lax.fori_loop(0, jnp.minimum(count, WINDOW), first, 0)
 
+    half = sent.shape[1]
+    depth = pairs[pairs.shape[0] - 2]
+    core = depth % 2
+    high = depth // 2
+
     def clear(at, carry):
-        total[at] = jnp.zeros(total.shape[1:], total.dtype)
-        return carry
-
-    lax.fori_loop(0, total.shape[0], clear, 0, unroll=4)
+        for part in range(2):
+            sent[part, at] = jnp.zeros(sent.shape[2:], sent.dtype)
+            kept[part, at] = jnp.zeros(kept.shape[2:], kept.dtype)
+        return carry
+
+    lax.fori_loop(0, half, clear, 0, unroll=4)
 
     def multiply(at, carry):
         slot = at % WINDOW
         pltpu.make_async_copy(hams[0].at[pl.ds(0, size)], ham_buf.at[slot], ham_sem.at[slot]).wait()
         pltpu.make_async_copy(iterate.at[0], it_buf.at[slot], it_sem.at[slot]).wait()
         goal = pairs[at] // 65536
-        total[goal] += jnp.dot(ham_buf[slot], it_buf[slot], preferred_element_type=jnp.float32)
+        seen = goal >= 64
+        goal = goal % 64
+        product = jnp.dot(ham_buf[slot], it_buf[slot], preferred_element_type=jnp.float32)
+        product = jnp.where(seen, total[goal], 0.0) + product
+        total[goal] = product
+        owner = goal // half
+        part = (owner // 2 == high).astype(jnp.int32)
+
+        @pl.when(owner % 2 == core)
+        def _():
+            kept[part, goal % half] = product.astype(kept.dtype)
+
+        @pl.when(owner % 2 != core)
+        def _():
+            sent[part, goal % half] = product.astype(sent.dtype)
 
         @pl.when(at + WINDOW < count)
         def _():
@@ -107,18 +137,6 @@
         return carry
 
     lax.fori_loop(0, count, multiply, 0)
-    half = sent.shape[1]
-    depth = pairs[pairs.shape[0] - 2]
-    core = depth % 2
-    high = depth // 2
-
-    def finish(at, carry):
-        for part, far in enumerate((1 - high, high)):
-            sent[part, at] = total[(far * 2 + 1 - core) * half + at].astype(sent.dtype)
-            kept[part, at] = total[(far * 2 + core) * half + at].astype(kept.dtype)
-        return carry
-
-    lax.fori_loop(0, half, finish, 0, unroll=2)
 
 
 def body(h_blocks, h_rows, h_cols, h_flags, x_blocks, x_cols, x_flags, previous):
@@ -162,15 +180,16 @@
         scratch_shapes=[pltpu.VMEM((n_col, 16, block), jnp.bfloat16), pltpu.SemaphoreType.DMA((n_col,))],
         name="keys",
     )(*hams)
+    results = x_cols.shape[3] * x_cols.shape[4]
+    halves = jax.ShapeDtypeStruct((2, results, block, block), jnp.bfloat16)
     pairs = pl.pallas_call(
         pair_kernel,
         out_shape=jax.ShapeDtypeStruct((512,), jnp.int32),
         in_specs=[smem] * 4,
         out_specs=smem,
+        scratch_shapes=[pltpu.SMEM((n_depth * results,), jnp.int32)],
         name="pairs",
     )(where, ham_keys, it_keys, aim_keys)
-    results = x_cols.shape[3] * x_cols.shape[4]
-    halves = jax.ShapeDtypeStruct((2, results, block, block), jnp.bfloat16)
     sent, kept = pl.pallas_call(
         product_kernel,
         out_shape=(halves,) * 2,

time: 156 us -> 157 us (level)
  transfers between devices with their start and end apart: 10 -> 10, of which waited for: 8 -> 8; matrix products, arithmetic and copies ran while one was open for 4% -> 4% of each run, Pallas kernels for 3% -> 4%
where the time goes in v7:
time: 157 us; the launch traced here: 156 us
  waiting for transfers between devices  55.4 us (35%)
  blocking collectives  39.4 us (25%)
  starting transfers between devices  31.1 us (20%)
  between operations  13.6 us (9%)
  Pallas kernels  7.81 us (5%)
  other arithmetic  6.8 us (4%)
  local copies, waits for them, and re-layouts  1.75 us (1%)
    ppermute x7, waiting for transfers between devices, send(): return lax.ppermute(source, 'col', route)  37.9 us
    all_gather x1, blocking collectives, body(): it_ints = lax.all_gather(it_ints, 'row', axis=0, tiled=True)  26.1 us
    ppermute x7, starting transfers between devices, send(): return lax.ppermute(source, 'col', route)  21.8 us
    all_gather x1, blocking collectives, body(): aim_ints = lax.all_gather(it_ints, 'depth', axis=1, tiled=True)  13.3 us
    ppermute x1, waiting for transfers between devices, body(): far = lax.ppermute(onward, 'depth', [(d, d ^ 2) for d in range(n_depth)])  11.7 us
    ppermute x1, starting transfers between devices, body(): far = lax.ppermute(onward, 'depth', [(d, d ^ 2) for d in range(n_depth)])  5.34 us
    pallas_call x1, Pallas kernels, body(): pl.pallas_call(pair_kernel, out_shape=jax.ShapeDtypeStruct((512,), jnp.in...  4.04 us
    ppermute x1, starting transfers between devices, body(): near = lax.ppermute(sent, 'depth', [(d, d ^ 1) for d in range(n_depth)])  3.91 us
  transfers between devices with their start and end apart: 10, of which 8 were waited for; matrix products, arithmetic and copies ran while one was open for 4% of the time, Pallas kernels for 4%

profile of v7, /device:TPU:1, one launch (start us, length us, event | category | flops | bytes accessed | tf_op | source)
XLA Modules:
  0.0 155.9 jit_solution(15513486346683374406)
XLA Ops:
  10.0 13.3 %all_gather.9 = s32[1,4,2,8,2]{3,4,2,0,1:T(2,128)S(1)} all-gather(s32[1,1,2,8,2]{3,4,2,0,1:T(2,128)S(1)} %pad_add_fusion), channel_id=1, replica_groups=mesh['row'=16,'col'=8,'depth'=4] {'depth'}, dimensions={1}, use_global_device_ids=true | all-gather | bytes 640 | tf_op jit(solution)/shard_map/all_gather | solution.py:149
  23.4 1.2 fusion.1.refs_0_.rest_0_
  24.6 1.9 %collective-permute-start = (bf16[3088,128]{1,0:T(8,128)(2,1)S(1)}, bf16[3088,128]{1,0:T(8,128)(2,1)S(1)}, u32[]{:S(2)}, u32[]{:S(2)}) collective-permute-start(bf16[3088,128]{1,0:T(8,128)(2,1)S(1)} %fusion.1.refs_0_.rest_0_), channel_id=1, source_target_pairs={{0,16},{4,20},{8,24},{12,28},{16,0},{20,4},{24,8},{28,12},{1,17},{... | collective-permute-start | bytes 2371592 | tf_op jit(solution)/shard_map/ppermute | solution.py:159
  26.5 1.9 %collective-permute-start.2 = (bf16[3088,128]{1,0:T(8,128)(2,1)S(1)}, bf16[3088,128]{1,0:T(8,128)(2,1)S(1)}, u32[]{:S(2)}, u32[]{:S(2)}) collective-permute-start(bf16[3088,128]{1,0:T(8,128)(2,1)S(1)} %fusion.1.refs_0_.rest_0_), channel_id=1, source_target_pairs={{0,8},{4,12},{8,0},{12,4},{16,24},{20,28},{24,16},{28,20},{1,9},{5... | collective-permute-start | bytes 2371592 | tf_op jit(solution)/shard_map/ppermute | solution.py:159
  28.4 1.9 %collective-permute-start.4 = (bf16[3088,128]{1,0:T(8,128)(2,1)S(1)}, bf16[3088,128]{1,0:T(8,128)(2,1)S(1)}, u32[]{:S(2)}, u32[]{:S(2)}) collective-permute-start(bf16[3088,128]{1,0:T(8,128)(2,1)S(1)} %fusion.1.refs_0_.rest_0_), channel_id=1, source_target_pairs={{0,20},{4,24},{8,28},{12,16},{16,4},{20,8},{24,12},{28,0},{1,21},{... | collective-permute-start | bytes 2371592 | tf_op jit(solution)/shard_map/ppermute | solution.py:159
  30.3 6.0 %collective-permute-start.5 = (bf16[3088,128]{1,0:T(8,128)(2,1)S(1)}, bf16[3088,128]{1,0:T(8,128)(2,1)}, u32[]{:S(2)}, u32[]{:S(2)}) collective-permute-start(bf16[3088,128]{1,0:T(8,128)(2,1)S(1)} %fusion.1.refs_0_.rest_0_), channel_id=1, source_target_pairs={{0,24},{4,28},{8,16},{12,20},{16,8},{20,12},{24,0},{28,4},{1,25},{... | collective-permute-start | bytes 2371592 | tf_op jit(solution)/shard_map/ppermute | solution.py:159
  36.4 4.9 %collective-permute-start.6 = (bf16[3088,128]{1,0:T(8,128)(2,1)S(1)}, bf16[3088,128]{1,0:T(8,128)(2,1)}, u32[]{:S(2)}, u32[]{:S(2)}) collective-permute-start(bf16[3088,128]{1,0:T(8,128)(2,1)S(1)} %fusion.1.refs_0_.rest_0_), channel_id=1, source_target_pairs={{0,28},{4,16},{8,20},{12,24},{16,12},{20,0},{24,4},{28,8},{1,29},{... | collective-permute-start | bytes 2371592 | tf_op jit(solution)/shard_map/ppermute | solution.py:159
  41.3 4.3 %collective-permute-done.refs_4_.rest_4_ = bf16[3088,128]{1,0:T(8,128)(2,1)S(1)} collective-permute-done((bf16[3088,128]{1,0:T(8,128)(2,1)S(1)}, bf16[3088,128]{1,0:T(8,128)(2,1)S(1)}, u32[]{:S(2)}, u32[]{:S(2)}) %collective-permute-start) | collective-permute-done | bytes 790560 | tf_op jit(solution)/shard_map/ppermute | solution.py:159
  45.6 26.1 %all_gather.10 = s32[16,1,2,8,2]{3,4,2,1,0:T(2,128)S(1)} all-gather(s32[1,1,2,8,2]{3,4,2,1,0:T(2,128)S(1)} %bitcast.25), channel_id=1, replica_groups=mesh['row'=16,'col'=8,'depth'=4] {'row'}, dimensions={0}, use_global_device_ids=true | all-gather | bytes 2176 | tf_op jit(solution)/shard_map/all_gather | solution.py:165
  71.7 3.3 %collective-permute-start.1 = (bf16[3088,128]{1,0:T(8,128)(2,1)S(1)}, bf16[3088,128]{1,0:T(8,128)(2,1)}, u32[]{:S(2)}, u32[]{:S(2)}) collective-permute-start(bf16[3088,128]{1,0:T(8,128)(2,1)S(1)} %fusion.1.refs_0_.rest_0_), channel_id=1, source_target_pairs={{0,4},{4,8},{8,12},{12,0},{16,20},{20,24},{24,28},{28,16},{1,5},{5... | collective-permute-start | bytes 2371592 | tf_op jit(solution)/shard_map/ppermute | solution.py:159
  75.0 7.9 %collective-permute-done.2.refs_2_.rest_2_ = bf16[3088,128]{1,0:T(8,128)(2,1)S(1)} collective-permute-done((bf16[3088,128]{1,0:T(8,128)(2,1)S(1)}, bf16[3088,128]{1,0:T(8,128)(2,1)S(1)}, u32[]{:S(2)}, u32[]{:S(2)}) %collective-permute-start.2) | collective-permute-done | bytes 790560 | tf_op jit(solution)/shard_map/ppermute | solution.py:159
  82.8 1.9 %collective-permute-start.3 = (bf16[3088,128]{1,0:T(8,128)(2,1)S(1)}, bf16[3088,128]{1,0:T(8,128)(2,1)}, u32[]{:S(2)}, u32[]{:S(2)}) collective-permute-start(bf16[3088,128]{1,0:T(8,128)(2,1)S(1)} %fusion.1.refs_0_.rest_0_), channel_id=1, source_target_pairs={{0,12},{4,0},{8,4},{12,8},{16,28},{20,16},{24,20},{28,24},{1,13},{... | collective-permute-start | bytes 2371592 | tf_op jit(solution)/shard_map/ppermute | solution.py:159
  87.0 8.3 %collective-permute-done.6.refs_7_.rest_7_ = bf16[3088,128]{1,0:T(8,128)(2,1)} collective-permute-done((bf16[3088,128]{1,0:T(8,128)(2,1)S(1)}, bf16[3088,128]{1,0:T(8,128)(2,1)}, u32[]{:S(2)}, u32[]{:S(2)}) %collective-permute-start.6) | collective-permute-done | bytes 790560 | tf_op jit(solution)/shard_map/ppermute | solution.py:159
  95.3 4.6 %collective-permute-done.1.refs_1_.rest_1_ = bf16[3088,128]{1,0:T(8,128)(2,1)} collective-permute-done((bf16[3088,128]{1,0:T(8,128)(2,1)S(1)}, bf16[3088,128]{1,0:T(8,128)(2,1)}, u32[]{:S(2)}, u32[]{:S(2)}) %collective-permute-start.1) | collective-permute-done | bytes 790560 | tf_op jit(solution)/shard_map/ppermute | solution.py:159
  100.0 12.8 %collective-permute-done.3.refs_3_.rest_3_ = bf16[3088,128]{1,0:T(8,128)(2,1)} collective-permute-done((bf16[3088,128]{1,0:T(8,128)(2,1)S(1)}, bf16[3088,128]{1,0:T(8,128)(2,1)}, u32[]{:S(2)}, u32[]{:S(2)}) %collective-permute-start.3) | collective-permute-done | bytes 790560 | tf_op jit(solution)/shard_map/ppermute | solution.py:159
  112.8 1.4 keys.1.ham
  114.2 4.0 %pairs.1 = s32[512]{0:T(512)} custom-call(s32[2]{0:T(128)} %pad_add_fusion.1.where, s32[16,128]{1,0:T(8,128)} %keys.1.ham, s32[16,16]{1,0:T(8,128)} %copy.21.iterate, s32[64]{0:T(128)} %select_n.19.aim), custom_call_target="tpu_custom_call" | custom-call | tf_op jit(solution)/shard_map/pairs/pallas_call | solution.py:185
  118.3 2.8 %all-gather.3.cloned.1.call-done = bf16[16,1,1,8,2,128,128]{6,5,4,3,2,1,0:T(8,128)(2,1)} async-done(((bf16[1,1,1,8,2,128,128]{6,5,4,3,2,1,0:T(8,128)(2,1)}), bf16[16,1,1,8,2,128,128]{6,5,4,3,2,1,0:T(8,128)(2,1)}) %all-gather.3.cloned.1.call-update) | async-done | bytes 8388624 | tf_op jit(solution)/shard_map/all_gather | solution.py:146
  121.1 2.3 %products.1 = (bf16[2,16,128,128]{3,2,1,0:T(8,128)(2,1)S(1)}, bf16[2,16,128,128]{3,2,1,0:T(8,128)(2,1)S(1)}) custom-call(s32[512]{0:T(512)} %pairs.1, bf16[256,128,128]{2,1,0:T(8,128)(2,1)} %bitcast.22, bf16[3088,128]{1,0:T(8,128)(2,1)} %copy-done, bf16[3088,128]{1,0:T(8,128)(2,1)} %collective-permute-done.1.refs_1_.rest_1_, bf16[3088,128]{1,0:T(8,128)(2,1)} %copy-done.2, ...), custom_call_target="tpu_custom_call" | custom-call | tf_op jit(solution)/shard_map/products/pallas_call | solution.py:193
  123.4 3.9 %collective-permute-start.7 = (bf16[2,16,128,128]{3,2,1,0:T(8,128)(2,1)S(1)}, bf16[2,16,128,128]{3,2,1,0:T(8,128)(2,1)S(1)}, u32[]{:S(2)}, u32[]{:S(2)}) collective-permute-start(bf16[2,16,128,128]{3,2,1,0:T(8,128)(2,1)S(1)} %get-tuple-element.20), channel_id=1, source_target_pairs={{0,1},{1,0},{2,3},{3,2},{4,5},{5,4},{6,7},{7,6},{8,9},{9,8},{10,11... | collective-permute-start | bytes 3145736 | tf_op jit(solution)/shard_map/ppermute | solution.py:208
  127.3 2.3 %collective-permute-done.7 = bf16[2,16,128,128]{3,2,1,0:T(8,128)(2,1)S(1)} collective-permute-done((bf16[2,16,128,128]{3,2,1,0:T(8,128)(2,1)S(1)}, bf16[2,16,128,128]{3,2,1,0:T(8,128)(2,1)S(1)}, u32[]{:S(2)}, u32[]{:S(2)}) %collective-permute-start.7) | collective-permute-done | bytes 1048608 | tf_op jit(solution)/shard_map/ppermute | solution.py:208
  130.5 5.3 %collective-permute-start.8 = (bf16[16,128,128]{2,1,0:T(8,128)(2,1)}, bf16[16,128,128]{2,1,0:T(8,128)(2,1)S(1)}, u32[]{:S(2)}, u32[]{:S(2)}) collective-permute-start(bf16[16,128,128]{2,1,0:T(8,128)(2,1)} %fusion.2), channel_id=1, source_target_pairs={{0,2},{1,3},{2,0},{3,1},{4,6},{5,7},{6,4},{7,5},{8,10},{9,11},{10,... | collective-permute-start | bytes 1572872 | tf_op jit(solution)/shard_map/ppermute | solution.py:210
  136.3 11.7 %collective-permute-done.8 = bf16[16,128,128]{2,1,0:T(8,128)(2,1)S(1)} collective-permute-done((bf16[16,128,128]{2,1,0:T(8,128)(2,1)}, bf16[16,128,128]{2,1,0:T(8,128)(2,1)S(1)}, u32[]{:S(2)}, u32[]{:S(2)}) %collective-permute-start.8) | collective-permute-done | bytes 524320 | tf_op jit(solution)/shard_map/ppermute | solution.py:210
  148.1 1.0 multiply_convert_fusion
  (34 shorter events, 7.1 us)
Async XLA Ops:
  6.5 114.5 %all-gather.3.cloned.1.call-start = ((), (), s32[]{:S(2)}) async-start(), calls=%async_computation | async-start | bytes 8912896 | tf_op jit(solution)/shard_map/all_gather | solution.py:146
  24.5 88.2 %copy-start = (bf16[3088,128]{1,0:T(8,128)(2,1)}, bf16[3088,128]{1,0:T(8,128)(2,1)S(1)}, u32[]{:S(2)}) copy-start(bf16[3088,128]{1,0:T(8,128)(2,1)S(1)} %fusion.1.refs_0_.rest_0_) | copy-start | bytes 2371588
  24.6 21.0 %collective-permute-start = (bf16[3088,128]{1,0:T(8,128)(2,1)S(1)}, bf16[3088,128]{1,0:T(8,128)(2,1)S(1)}, u32[]{:S(2)}, u32[]{:S(2)}) collective-permute-start(bf16[3088,128]{1,0:T(8,128)(2,1)S(1)} %fusion.1.refs_0_.rest_0_), channel_id=1, source_target_pairs={{0,16},{4,20},{8,24},{12,28},{16,0},{20,4},{24,8},{28,12},{1,17},{... | collective-permute-start | bytes 2371592 | tf_op jit(solution)/shard_map/ppermute | solution.py:159
  26.5 56.4 %collective-permute-start.2 = (bf16[3088,128]{1,0:T(8,128)(2,1)S(1)}, bf16[3088,128]{1,0:T(8,128)(2,1)S(1)}, u32[]{:S(2)}, u32[]{:S(2)}) collective-permute-start(bf16[3088,128]{1,0:T(8,128)(2,1)S(1)} %fusion.1.refs_0_.rest_0_), channel_id=1, source_target_pairs={{0,8},{4,12},{8,0},{12,4},{16,24},{20,28},{24,16},{28,20},{1,9},{5... | collective-permute-start | bytes 2371592 | tf_op jit(solution)/shard_map/ppermute | solution.py:159
  28.4 58.6 %collective-permute-start.4 = (bf16[3088,128]{1,0:T(8,128)(2,1)S(1)}, bf16[3088,128]{1,0:T(8,128)(2,1)S(1)}, u32[]{:S(2)}, u32[]{:S(2)}) collective-permute-start(bf16[3088,128]{1,0:T(8,128)(2,1)S(1)} %fusion.1.refs_0_.rest_0_), channel_id=1, source_target_pairs={{0,20},{4,24},{8,28},{12,16},{16,4},{20,8},{24,12},{28,0},{1,21},{... | collective-permute-start | bytes 2371592 | tf_op jit(solution)/shard_map/ppermute | solution.py:159
  30.3 56.7 %collective-permute-start.5 = (bf16[3088,128]{1,0:T(8,128)(2,1)S(1)}, bf16[3088,128]{1,0:T(8,128)(2,1)}, u32[]{:S(2)}, u32[]{:S(2)}) collective-permute-start(bf16[3088,128]{1,0:T(8,128)(2,1)S(1)} %fusion.1.refs_0_.rest_0_), channel_id=1, source_target_pairs={{0,24},{4,28},{8,16},{12,20},{16,8},{20,12},{24,0},{28,4},{1,25},{... | collective-permute-start | bytes 2371592 | tf_op jit(solution)/shard_map/ppermute | solution.py:159
  36.4 59.0 %collective-permute-start.6 = (bf16[3088,128]{1,0:T(8,128)(2,1)S(1)}, bf16[3088,128]{1,0:T(8,128)(2,1)}, u32[]{:S(2)}, u32[]{:S(2)}) collective-permute-start(bf16[3088,128]{1,0:T(8,128)(2,1)S(1)} %fusion.1.refs_0_.rest_0_), channel_id=1, source_target_pairs={{0,28},{4,16},{8,20},{12,24},{16,12},{20,0},{24,4},{28,8},{1,29},{... | collective-permute-start | bytes 2371592 | tf_op jit(solution)/shard_map/ppermute | solution.py:159
  45.6 67.2 %copy-start.1 = (bf16[3088,128]{1,0:T(8,128)(2,1)}, bf16[3088,128]{1,0:T(8,128)(2,1)S(1)}, u32[]{:S(2)}) copy-start(bf16[3088,128]{1,0:T(8,128)(2,1)S(1)} %collective-permute-done.refs_4_.rest_4_) | copy-start | bytes 2371588
  71.7 28.2 %collective-permute-start.1 = (bf16[3088,128]{1,0:T(8,128)(2,1)S(1)}, bf16[3088,128]{1,0:T(8,128)(2,1)}, u32[]{:S(2)}, u32[]{:S(2)}) collective-permute-start(bf16[3088,128]{1,0:T(8,128)(2,1)S(1)} %fusion.1.refs_0_.rest_0_), channel_id=1, source_target_pairs={{0,4},{4,8},{8,12},{12,0},{16,20},{20,24},{24,28},{28,16},{1,5},{5... | collective-permute-start | bytes 2371592 | tf_op jit(solution)/shard_map/ppermute | solution.py:159
  82.8 29.9 %copy-start.2 = (bf16[3088,128]{1,0:T(8,128)(2,1)}, bf16[3088,128]{1,0:T(8,128)(2,1)S(1)}, u32[]{:S(2)}) copy-start(bf16[3088,128]{1,0:T(8,128)(2,1)S(1)} %collective-permute-done.2.refs_2_.rest_2_) | copy-start | bytes 2371588
  82.8 29.9 %collective-permute-start.3 = (bf16[3088,128]{1,0:T(8,128)(2,1)S(1)}, bf16[3088,128]{1,0:T(8,128)(2,1)}, u32[]{:S(2)}, u32[]{:S(2)}) collective-permute-start(bf16[3088,128]{1,0:T(8,128)(2,1)S(1)} %fusion.1.refs_0_.rest_0_), channel_id=1, source_target_pairs={{0,12},{4,0},{8,4},{12,8},{16,28},{20,16},{24,20},{28,24},{1,13},{... | collective-permute-start | bytes 2371592 | tf_op jit(solution)/shard_map/ppermute | solution.py:159
  87.0 25.8 %copy-start.3 = (bf16[3088,128]{1,0:T(8,128)(2,1)}, bf16[3088,128]{1,0:T(8,128)(2,1)S(1)}, u32[]{:S(2)}) copy-start(bf16[3088,128]{1,0:T(8,128)(2,1)S(1)} %collective-permute-done.4.refs_5_.rest_5_) | copy-start | bytes 2371588
  121.1 14.8 %copy-start.5 = (s32[1,1,1,8,2]{3,4,2,1,0:T(2,128)S(1)}, s32[1,1,1,8,2]{3,4,2,1,0:T(2,128)}, u32[]{:S(2)}) copy-start(s32[1,1,1,8,2]{3,4,2,1,0:T(2,128)} %param.14) | copy-start | bytes 196
  123.4 12.7 %copy-start.4 = (bf16[1,1,1,8,2,128,128]{6,5,4,3,2,1,0:T(8,128)(2,1)S(1)}, bf16[1,1,1,8,2,128,128]{6,5,4,3,2,1,0:T(8,128)(2,1)}, u32[]{:S(2)}) copy-start(bf16[1,1,1,8,2,128,128]{6,5,4,3,2,1,0:T(8,128)(2,1)} %param.15) | copy-start | bytes 1572868
  123.4 6.2 %collective-permute-start.7 = (bf16[2,16,128,128]{3,2,1,0:T(8,128)(2,1)S(1)}, bf16[2,16,128,128]{3,2,1,0:T(8,128)(2,1)S(1)}, u32[]{:S(2)}, u32[]{:S(2)}) collective-permute-start(bf16[2,16,128,128]{3,2,1,0:T(8,128)(2,1)S(1)} %get-tuple-element.20), channel_id=1, source_target_pairs={{0,1},{1,0},{2,3},{3,2},{4,5},{5,4},{6,7},{7,6},{8,9},{9,8},{10,11... | collective-permute-start | bytes 3145736 | tf_op jit(solution)/shard_map/ppermute | solution.py:208
  130.5 17.5 %collective-permute-start.8 = (bf16[16,128,128]{2,1,0:T(8,128)(2,1)}, bf16[16,128,128]{2,1,0:T(8,128)(2,1)S(1)}, u32[]{:S(2)}, u32[]{:S(2)}) collective-permute-start(bf16[16,128,128]{2,1,0:T(8,128)(2,1)} %fusion.2), channel_id=1, source_target_pairs={{0,2},{1,3},{2,0},{3,1},{4,6},{5,7},{6,4},{7,5},{8,10},{9,11},{10,... | collective-permute-start | bytes 1572872 | tf_op jit(solution)/shard_map/ppermute | solution.py:210
Sparse Core Ops, SparseCore 0:
  9.4 111.5 all-gather.2

commit v8 on v7

--- a/solution.py
+++ b/solution.py
@@ -152,20 +152,22 @@
     ham_ints = ham_ints.astype(jnp.bfloat16)
     ham_ints = jnp.pad(ham_ints, ((0, 16 - ham_ints.shape[0]), (0, block - slots)))
     mine = jnp.concatenate([h_blocks.reshape(-1, block), ham_ints], axis=0)
-    mine, aim_ints = lax.optimization_barrier((mine, aim_ints))
 
     def send(source, flip, step):
         route = [(c, ((c // 4) ^ flip) * 4 + (c % 4 + step) % 4) for c in range(n_col)]
         return lax.ppermute(source, "col", route)
 
     hams = [mine] + [None] * (n_col - 1)
-    for flip, step in ((1, 0), (1, 2), (0, 2), (1, 1), (1, 3)):
+    for flip, step in ((0, 1), (0, 3)):
         hams[flip * 4 + step] = send(mine, flip, step)
-    hams[4], it_ints = lax.optimization_barrier((hams[4], it_ints))
+    crossing, aim_ints = lax.optimization_barrier((mine, aim_ints))
+    for flip, step in ((1, 0), (1, 2), (1, 1)):
+        hams[flip * 4 + step] = send(crossing, flip, step)
+    hams[1], crossing = lax.optimization_barrier((hams[1], crossing))
+    hams[7] = send(crossing, 1, 3)
+    hams[3], crossing, it_ints = lax.optimization_barrier((hams[3], crossing, it_ints))
+    hams[2] = send(crossing, 0, 2)
     it_ints = lax.all_gather(it_ints, "row", axis=0, tiled=True)
-    late, it_ints = lax.optimization_barrier((mine, it_ints))
-    for flip, step in ((0, 1), (0, 3)):
-        hams[flip * 4 + step] = send(late, flip, step)
     hams = [pltpu.with_memory_space_constraint(ham, pltpu.HBM) for ham in hams]
     it_keys = jnp.where(it_ints[:, 0, 1] > 0, it_ints[:, 0, 0], -1).reshape(n_row, -1)
     aim_keys = jnp.where(aim_ints[0, :, 1] > 0, aim_ints[0, :, 0], -2).reshape(-1)

time: 157 us -> 156 us (level)
  waiting for transfers between devices: 55.4 us -> 52.9 us
    ppermute x7, waiting for transfers between devices: 37.9 us -> 26 us  [send(): return lax.ppermute(source, 'col', route)]
    all_gather x1, waiting for transfers between devices: 2.79 us -> 12.4 us  [body(): iterate = lax.all_gather(x_blocks[0, 0, 0], 'row', axis=0)]
    ppermute x7, starting transfers between devices: 21.8 us -> 24.7 us  [send(): return lax.ppermute(source, 'col', route)]
  transfers between devices with their start and end apart: 10 -> 10, of which waited for: 8 -> 6; matrix products, arithmetic and copies ran while one was open for 4% -> 4% of each run, Pallas kernels for 4% -> 4%
where the time goes in v8:
time: 156 us; the launch traced here: 154 us
  waiting for transfers between devices  52.9 us (34%)
  blocking collectives  39.5 us (25%)
  starting transfers between devices  32.3 us (21%)
  between operations  13.6 us (9%)
  Pallas kernels  8.03 us (5%)
  other arithmetic  6.06 us (4%)
  local copies, waits for them, and re-layouts  1.76 us (1%)
    all_gather x1, blocking collectives, body(): it_ints = lax.all_gather(it_ints, 'row', axis=0, tiled=True)  26.5 us
    ppermute x7, waiting for transfers between devices, send(): return lax.ppermute(source, 'col', route)  26 us
    ppermute x7, starting transfers between devices, send(): return lax.ppermute(source, 'col', route)  24.7 us
    all_gather x1, blocking collectives, body(): aim_ints = lax.all_gather(it_ints, 'depth', axis=1, tiled=True)  13 us
    all_gather x1, waiting for transfers between devices, body(): iterate = lax.all_gather(x_blocks[0, 0, 0], 'row', axis=0)  12.4 us
    ppermute x1, waiting for transfers between devices, body(): far = lax.ppermute(onward, 'depth', [(d, d ^ 2) for d in range(n_depth)])  11.5 us
    ppermute x1, starting transfers between devices, body(): far = lax.ppermute(onward, 'depth', [(d, d ^ 2) for d in range(n_depth)])  4.74 us
    pallas_call x1, Pallas kernels, body(): pl.pallas_call(pair_kernel, out_shape=jax.ShapeDtypeStruct((512,), jnp.in...  4.25 us
  transfers between devices with their start and end apart: 10, of which 6 were waited for; matrix products, arithmetic and copies ran while one was open for 4% of the time, Pallas kernels for 4%

profile of v8, /device:TPU:1, one launch (start us, length us, event | category | flops | bytes accessed | tf_op | source)
XLA Modules:
  0.0 154.1 jit_solution(8907890940964269417)
XLA Ops:
  6.5 0.7 all-gather.3.cloned.1.call-update
  9.3 1.2 fusion.1.refs_0_.rest_0_
  10.5 4.0 %collective-permute-start = (bf16[3088,128]{1,0:T(8,128)(2,1)S(1)}, bf16[3088,128]{1,0:T(8,128)(2,1)S(1)}, u32[]{:S(2)}, u32[]{:S(2)}) collective-permute-start(bf16[3088,128]{1,0:T(8,128)(2,1)S(1)} %fusion.1.refs_0_.rest_0_), channel_id=1, source_target_pairs={{0,4},{4,8},{8,12},{12,0},{16,20},{20,24},{24,28},{28,16},{1,5},{5... | collective-permute-start | bytes 2371592 | tf_op jit(solution)/shard_map/ppermute | solution.py:158
  14.6 3.4 %collective-permute-start.1 = (bf16[3088,128]{1,0:T(8,128)(2,1)S(1)}, bf16[3088,128]{1,0:T(8,128)(2,1)S(1)}, u32[]{:S(2)}, u32[]{:S(2)}) collective-permute-start(bf16[3088,128]{1,0:T(8,128)(2,1)S(1)} %fusion.1.refs_0_.rest_0_), channel_id=1, source_target_pairs={{0,12},{4,0},{8,4},{12,8},{16,28},{20,16},{24,20},{28,24},{1,13},{... | collective-permute-start | bytes 2371592 | tf_op jit(solution)/shard_map/ppermute | solution.py:158
  18.0 13.0 %all_gather.9 = s32[1,4,2,8,2]{3,4,2,0,1:T(2,128)S(1)} all-gather(s32[1,1,2,8,2]{3,4,2,0,1:T(2,128)S(1)} %pad_add_fusion), channel_id=1, replica_groups=mesh['row'=16,'col'=8,'depth'=4] {'depth'}, dimensions={1}, use_global_device_ids=true | all-gather | bytes 640 | tf_op jit(solution)/shard_map/all_gather | solution.py:149
  31.0 1.9 %collective-permute-start.3 = (bf16[3088,128]{1,0:T(8,128)(2,1)S(1)}, bf16[3088,128]{1,0:T(8,128)(2,1)S(1)}, u32[]{:S(2)}, u32[]{:S(2)}) collective-permute-start(bf16[3088,128]{1,0:T(8,128)(2,1)S(1)} %fusion.1.refs_0_.rest_0_), channel_id=1, source_target_pairs={{0,16},{4,20},{8,24},{12,28},{16,0},{20,4},{24,8},{28,12},{1,17},{... | collective-permute-start | bytes 2371592 | tf_op jit(solution)/shard_map/ppermute | solution.py:158
  32.9 1.9 %collective-permute-start.4 = (bf16[3088,128]{1,0:T(8,128)(2,1)S(1)}, bf16[3088,128]{1,0:T(8,128)(2,1)}, u32[]{:S(2)}, u32[]{:S(2)}) collective-permute-start(bf16[3088,128]{1,0:T(8,128)(2,1)S(1)} %fusion.1.refs_0_.rest_0_), channel_id=1, source_target_pairs={{0,20},{4,24},{8,28},{12,16},{16,4},{20,8},{24,12},{28,0},{1,21},{... | collective-permute-start | bytes 2371592 | tf_op jit(solution)/shard_map/ppermute | solution.py:158
  34.8 3.7 %collective-permute-start.5 = (bf16[3088,128]{1,0:T(8,128)(2,1)S(1)}, bf16[3088,128]{1,0:T(8,128)(2,1)}, u32[]{:S(2)}, u32[]{:S(2)}) collective-permute-start(bf16[3088,128]{1,0:T(8,128)(2,1)S(1)} %fusion.1.refs_0_.rest_0_), channel_id=1, source_target_pairs={{0,24},{4,28},{8,16},{12,20},{16,8},{20,12},{24,0},{28,4},{1,25},{... | collective-permute-start | bytes 2371592 | tf_op jit(solution)/shard_map/ppermute | solution.py:158
  38.6 4.2 %collective-permute-start.2 = (bf16[3088,128]{1,0:T(8,128)(2,1)S(1)}, bf16[3088,128]{1,0:T(8,128)(2,1)}, u32[]{:S(2)}, u32[]{:S(2)}) collective-permute-start(bf16[3088,128]{1,0:T(8,128)(2,1)S(1)} %fusion.1.refs_0_.rest_0_), channel_id=1, source_target_pairs={{0,8},{4,12},{8,0},{12,4},{16,24},{20,28},{24,16},{28,20},{1,9},{5... | collective-permute-start | bytes 2371592 | tf_op jit(solution)/shard_map/ppermute | solution.py:158
  42.8 5.5 %collective-permute-start.6 = (bf16[3088,128]{1,0:T(8,128)(2,1)S(1)}, bf16[3088,128]{1,0:T(8,128)(2,1)}, u32[]{:S(2)}, u32[]{:S(2)}) collective-permute-start(bf16[3088,128]{1,0:T(8,128)(2,1)S(1)} %fusion.1.refs_0_.rest_0_), channel_id=1, source_target_pairs={{0,28},{4,16},{8,20},{12,24},{16,12},{20,0},{24,4},{28,8},{1,29},{... | collective-permute-start | bytes 2371592 | tf_op jit(solution)/shard_map/ppermute | solution.py:158
  49.8 26.5 %all_gather.10 = s32[16,1,2,8,2]{3,4,2,1,0:T(2,128)S(1)} all-gather(s32[1,1,2,8,2]{3,4,2,1,0:T(2,128)S(1)} %bitcast.25), channel_id=1, replica_groups=mesh['row'=16,'col'=8,'depth'=4] {'row'}, dimensions={0}, use_global_device_ids=true | all-gather | bytes 2176 | tf_op jit(solution)/shard_map/all_gather | solution.py:170
  77.0 8.2 %collective-permute-done.5.refs_6_.rest_6_ = bf16[3088,128]{1,0:T(8,128)(2,1)} collective-permute-done((bf16[3088,128]{1,0:T(8,128)(2,1)S(1)}, bf16[3088,128]{1,0:T(8,128)(2,1)}, u32[]{:S(2)}, u32[]{:S(2)}) %collective-permute-start.5) | collective-permute-done | bytes 790560 | tf_op jit(solution)/shard_map/ppermute | solution.py:158
  85.2 12.4 %collective-permute-done.2.refs_2_.rest_2_ = bf16[3088,128]{1,0:T(8,128)(2,1)} collective-permute-done((bf16[3088,128]{1,0:T(8,128)(2,1)S(1)}, bf16[3088,128]{1,0:T(8,128)(2,1)}, u32[]{:S(2)}, u32[]{:S(2)}) %collective-permute-start.2) | collective-permute-done | bytes 790560 | tf_op jit(solution)/shard_map/ppermute | solution.py:158
  97.6 5.4 %collective-permute-done.6.refs_7_.rest_7_ = bf16[3088,128]{1,0:T(8,128)(2,1)} collective-permute-done((bf16[3088,128]{1,0:T(8,128)(2,1)S(1)}, bf16[3088,128]{1,0:T(8,128)(2,1)}, u32[]{:S(2)}, u32[]{:S(2)}) %collective-permute-start.6) | collective-permute-done | bytes 790560 | tf_op jit(solution)/shard_map/ppermute | solution.py:158
  103.0 1.4 keys.1.ham
  104.5 4.2 %pairs.1 = s32[512]{0:T(512)} custom-call(s32[2]{0:T(128)} %pad_add_fusion.1.where, s32[16,128]{1,0:T(8,128)} %keys.1.ham, s32[16,16]{1,0:T(8,128)} %copy.21.iterate, s32[64]{0:T(128)} %select_n.19.aim), custom_call_target="tpu_custom_call" | custom-call | tf_op jit(solution)/shard_map/pairs/pallas_call | solution.py:187
  108.7 12.4 %all-gather.3.cloned.1.call-done = bf16[16,1,1,8,2,128,128]{6,5,4,3,2,1,0:T(8,128)(2,1)} async-done(((bf16[1,1,1,8,2,128,128]{6,5,4,3,2,1,0:T(8,128)(2,1)}), bf16[16,1,1,8,2,128,128]{6,5,4,3,2,1,0:T(8,128)(2,1)}) %all-gather.3.cloned.1.call-update) | async-done | bytes 8388624 | tf_op jit(solution)/shard_map/all_gather | solution.py:146
  121.1 2.4 %products.1 = (bf16[2,16,128,128]{3,2,1,0:T(8,128)(2,1)S(1)}, bf16[2,16,128,128]{3,2,1,0:T(8,128)(2,1)S(1)}) custom-call(s32[512]{0:T(512)} %pairs.1, bf16[256,128,128]{2,1,0:T(8,128)(2,1)} %bitcast.22, bf16[3088,128]{1,0:T(8,128)(2,1)} %copy-done, bf16[3088,128]{1,0:T(8,128)(2,1)} %copy-done.1, bf16[3088,128]{1,0:T(8,128)(2,1)} %collective-permute-done.2.refs_2_.rest_2_, ...), custom_call_target="tpu_custom_call" | custom-call | tf_op jit(solution)/shard_map/products/pallas_call | solution.py:195
  123.4 2.9 %collective-permute-start.7 = (bf16[2,16,128,128]{3,2,1,0:T(8,128)(2,1)S(1)}, bf16[2,16,128,128]{3,2,1,0:T(8,128)(2,1)S(1)}, u32[]{:S(2)}, u32[]{:S(2)}) collective-permute-start(bf16[2,16,128,128]{3,2,1,0:T(8,128)(2,1)S(1)} %get-tuple-element.22), channel_id=1, source_target_pairs={{0,1},{1,0},{2,3},{3,2},{4,5},{5,4},{6,7},{7,6},{8,9},{9,8},{10,11... | collective-permute-start | bytes 3145736 | tf_op jit(solution)/shard_map/ppermute | solution.py:210
  126.3 2.3 %collective-permute-done.7 = bf16[2,16,128,128]{3,2,1,0:T(8,128)(2,1)S(1)} collective-permute-done((bf16[2,16,128,128]{3,2,1,0:T(8,128)(2,1)S(1)}, bf16[2,16,128,128]{3,2,1,0:T(8,128)(2,1)S(1)}, u32[]{:S(2)}, u32[]{:S(2)}) %collective-permute-start.7) | collective-permute-done | bytes 1048608 | tf_op jit(solution)/shard_map/ppermute | solution.py:210
  128.6 0.9 fusion.2
  129.5 4.7 %collective-permute-start.8 = (bf16[16,128,128]{2,1,0:T(8,128)(2,1)}, bf16[16,128,128]{2,1,0:T(8,128)(2,1)S(1)}, u32[]{:S(2)}, u32[]{:S(2)}) collective-permute-start(bf16[16,128,128]{2,1,0:T(8,128)(2,1)} %fusion.2), channel_id=1, source_target_pairs={{0,2},{1,3},{2,0},{3,1},{4,6},{5,7},{6,4},{7,5},{8,10},{9,11},{10,... | collective-permute-start | bytes 1572872 | tf_op jit(solution)/shard_map/ppermute | solution.py:212
  134.7 11.5 %collective-permute-done.8 = bf16[16,128,128]{2,1,0:T(8,128)(2,1)S(1)} collective-permute-done((bf16[16,128,128]{2,1,0:T(8,128)(2,1)}, bf16[16,128,128]{2,1,0:T(8,128)(2,1)S(1)}, u32[]{:S(2)}, u32[]{:S(2)}) %collective-permute-start.8) | collective-permute-done | bytes 524320 | tf_op jit(solution)/shard_map/ppermute | solution.py:212
  146.2 1.0 multiply_convert_fusion
  (36 shorter events, 4.7 us)
Async XLA Ops:
  6.5 11.4 %copy-start.6 = (s32[1,1,1,8,2]{3,4,2,1,0:T(2,128)S(1)}, s32[1,1,1,8,2]{3,4,2,1,0:T(2,128)}, u32[]{:S(2)}) copy-start(s32[1,1,1,8,2]{3,4,2,1,0:T(2,128)} %param.13) | copy-start | bytes 196
  6.5 11.4 %copy-start.5 = (s32[1,1,1,8,2]{3,4,2,1,0:T(2,128)S(1)}, s32[1,1,1,8,2]{3,4,2,1,0:T(2,128)}, u32[]{:S(2)}) copy-start(s32[1,1,1,8,2]{3,4,2,1,0:T(2,128)} %param.14) | copy-start | bytes 196
  6.5 114.5 %all-gather.3.cloned.1.call-start = ((), (), s32[]{:S(2)}) async-start(), calls=%async_computation | async-start | bytes 8912896 | tf_op jit(solution)/shard_map/all_gather | solution.py:146
  10.5 92.5 %copy-start = (bf16[3088,128]{1,0:T(8,128)(2,1)}, bf16[3088,128]{1,0:T(8,128)(2,1)S(1)}, u32[]{:S(2)}) copy-start(bf16[3088,128]{1,0:T(8,128)(2,1)S(1)} %fusion.1.refs_0_.rest_0_) | copy-start | bytes 2371588
  10.5 28.0 %collective-permute-start = (bf16[3088,128]{1,0:T(8,128)(2,1)S(1)}, bf16[3088,128]{1,0:T(8,128)(2,1)S(1)}, u32[]{:S(2)}, u32[]{:S(2)}) collective-permute-start(bf16[3088,128]{1,0:T(8,128)(2,1)S(1)} %fusion.1.refs_0_.rest_0_), channel_id=1, source_target_pairs={{0,4},{4,8},{8,12},{12,0},{16,20},{20,24},{24,28},{28,16},{1,5},{5... | collective-permute-start | bytes 2371592 | tf_op jit(solution)/shard_map/ppermute | solution.py:158
  14.6 24.0 %collective-permute-start.1 = (bf16[3088,128]{1,0:T(8,128)(2,1)S(1)}, bf16[3088,128]{1,0:T(8,128)(2,1)S(1)}, u32[]{:S(2)}, u32[]{:S(2)}) collective-permute-start(bf16[3088,128]{1,0:T(8,128)(2,1)S(1)} %fusion.1.refs_0_.rest_0_), channel_id=1, source_target_pairs={{0,12},{4,0},{8,4},{12,8},{16,28},{20,16},{24,20},{28,24},{1,13},{... | collective-permute-start | bytes 2371592 | tf_op jit(solution)/shard_map/ppermute | solution.py:158
  31.0 46.0 %collective-permute-start.3 = (bf16[3088,128]{1,0:T(8,128)(2,1)S(1)}, bf16[3088,128]{1,0:T(8,128)(2,1)S(1)}, u32[]{:S(2)}, u32[]{:S(2)}) collective-permute-start(bf16[3088,128]{1,0:T(8,128)(2,1)S(1)} %fusion.1.refs_0_.rest_0_), channel_id=1, source_target_pairs={{0,16},{4,20},{8,24},{12,28},{16,0},{20,4},{24,8},{28,12},{1,17},{... | collective-permute-start | bytes 2371592 | tf_op jit(solution)/shard_map/ppermute | solution.py:158
  32.9 44.1 %collective-permute-start.4 = (bf16[3088,128]{1,0:T(8,128)(2,1)S(1)}, bf16[3088,128]{1,0:T(8,128)(2,1)}, u32[]{:S(2)}, u32[]{:S(2)}) collective-permute-start(bf16[3088,128]{1,0:T(8,128)(2,1)S(1)} %fusion.1.refs_0_.rest_0_), channel_id=1, source_target_pairs={{0,20},{4,24},{8,28},{12,16},{16,4},{20,8},{24,12},{28,0},{1,21},{... | collective-permute-start | bytes 2371592 | tf_op jit(solution)/shard_map/ppermute | solution.py:158
  34.8 50.4 %collective-permute-start.5 = (bf16[3088,128]{1,0:T(8,128)(2,1)S(1)}, bf16[3088,128]{1,0:T(8,128)(2,1)}, u32[]{:S(2)}, u32[]{:S(2)}) collective-permute-start(bf16[3088,128]{1,0:T(8,128)(2,1)S(1)} %fusion.1.refs_0_.rest_0_), channel_id=1, source_target_pairs={{0,24},{4,28},{8,16},{12,20},{16,8},{20,12},{24,0},{28,4},{1,25},{... | collective-permute-start | bytes 2371592 | tf_op jit(solution)/shard_map/ppermute | solution.py:158
  38.6 64.5 %copy-start.1 = (bf16[3088,128]{1,0:T(8,128)(2,1)}, bf16[3088,128]{1,0:T(8,128)(2,1)S(1)}, u32[]{:S(2)}) copy-start(bf16[3088,128]{1,0:T(8,128)(2,1)S(1)} %collective-permute-done.refs_1_.rest_1_) | copy-start | bytes 2371588
  38.6 64.4 %copy-start.2 = (bf16[3088,128]{1,0:T(8,128)(2,1)}, bf16[3088,128]{1,0:T(8,128)(2,1)S(1)}, u32[]{:S(2)}) copy-start(bf16[3088,128]{1,0:T(8,128)(2,1)S(1)} %collective-permute-done.1.refs_3_.rest_3_) | copy-start | bytes 2371588
  38.6 59.0 %collective-permute-start.2 = (bf16[3088,128]{1,0:T(8,128)(2,1)S(1)}, bf16[3088,128]{1,0:T(8,128)(2,1)}, u32[]{:S(2)}, u32[]{:S(2)}) collective-permute-start(bf16[3088,128]{1,0:T(8,128)(2,1)S(1)} %fusion.1.refs_0_.rest_0_), channel_id=1, source_target_pairs={{0,8},{4,12},{8,0},{12,4},{16,24},{20,28},{24,16},{28,20},{1,9},{5... | collective-permute-start | bytes 2371592 | tf_op jit(solution)/shard_map/ppermute | solution.py:158
  42.8 60.2 %collective-permute-start.6 = (bf16[3088,128]{1,0:T(8,128)(2,1)S(1)}, bf16[3088,128]{1,0:T(8,128)(2,1)}, u32[]{:S(2)}, u32[]{:S(2)}) collective-permute-start(bf16[3088,128]{1,0:T(8,128)(2,1)S(1)} %fusion.1.refs_0_.rest_0_), channel_id=1, source_target_pairs={{0,28},{4,16},{8,20},{12,24},{16,12},{20,0},{24,4},{28,8},{1,29},{... | collective-permute-start | bytes 2371592 | tf_op jit(solution)/shard_map/ppermute | solution.py:158
  77.0 26.0 %copy-start.3 = (bf16[3088,128]{1,0:T(8,128)(2,1)}, bf16[3088,128]{1,0:T(8,128)(2,1)S(1)}, u32[]{:S(2)}) copy-start(bf16[3088,128]{1,0:T(8,128)(2,1)S(1)} %collective-permute-done.3.refs_4_.rest_4_) | copy-start | bytes 2371588
  123.4 11.0 %copy-start.4 = (bf16[1,1,1,8,2,128,128]{6,5,4,3,2,1,0:T(8,128)(2,1)S(1)}, bf16[1,1,1,8,2,128,128]{6,5,4,3,2,1,0:T(8,128)(2,1)}, u32[]{:S(2)}) copy-start(bf16[1,1,1,8,2,128,128]{6,5,4,3,2,1,0:T(8,128)(2,1)} %param.15) | copy-start | bytes 1572868
  123.4 5.1 %collective-permute-start.7 = (bf16[2,16,128,128]{3,2,1,0:T(8,128)(2,1)S(1)}, bf16[2,16,128,128]{3,2,1,0:T(8,128)(2,1)S(1)}, u32[]{:S(2)}, u32[]{:S(2)}) collective-permute-start(bf16[2,16,128,128]{3,2,1,0:T(8,128)(2,1)S(1)} %get-tuple-element.22), channel_id=1, source_target_pairs={{0,1},{1,0},{2,3},{3,2},{4,5},{5,4},{6,7},{7,6},{8,9},{9,8},{10,11... | collective-permute-start | bytes 3145736 | tf_op jit(solution)/shard_map/ppermute | solution.py:210
  129.5 16.7 %collective-permute-start.8 = (bf16[16,128,128]{2,1,0:T(8,128)(2,1)}, bf16[16,128,128]{2,1,0:T(8,128)(2,1)S(1)}, u32[]{:S(2)}, u32[]{:S(2)}) collective-permute-start(bf16[16,128,128]{2,1,0:T(8,128)(2,1)} %fusion.2), channel_id=1, source_target_pairs={{0,2},{1,3},{2,0},{3,1},{4,6},{5,7},{6,4},{7,5},{8,10},{9,11},{10,... | collective-permute-start | bytes 1572872 | tf_op jit(solution)/shard_map/ppermute | solution.py:212
Sparse Core Ops, SparseCore 0:
  9.4 111.5 all-gather.2

commit v9 on v6

v9 whole, which is shorter than its diff:
```python
import jax
import jax.numpy as jnp
from jax import lax
from jax.experimental import pallas as pl
from jax.experimental.pallas import tpu as pltpu
from jax.sharding import PartitionSpec as P

WINDOW = 16
SLOTS = 12


def key_kernel(*refs):
    hams, shards, (ham_keys, it_keys, ham_slab, it_slab, sem) = refs[:8], refs[8:-5], refs[-5:]
    tail = ham_slab.shape[1]
    n_ham = ham_slab.shape[0]
    copies = []
    for k, ham in enumerate(hams):
        copies.append(pltpu.make_async_copy(ham.at[pl.ds(ham.shape[0] - tail, tail)], ham_slab.at[k], sem.at[k]))
    for k, shard in enumerate(shards):
        shard = shard.at[0] if len(shard.shape) == 3 else shard
        middle = pl.ds((shard.shape[0] - tail) // 2, tail)
        copies.append(pltpu.make_async_copy(shard.at[middle], it_slab.at[k], sem.at[n_ham + k]))
    for copy in copies:
        copy.start()
    for k, copy in enumerate(copies):
        copy.wait()
        if k < n_ham:
            held = ham_slab[k].astype(jnp.float32)
            for t in range(2):
                row, col, flag = (held[3 * t + i : 3 * t + i + 1] for i in range(3))
                place = jnp.where(flag > 0, row * 8 + col, -1.0)
                ham_keys[2 * k + t : 2 * k + t + 1] = place.astype(jnp.int32)
        else:
            held = it_slab[k - n_ham].astype(jnp.float32)
            place = jnp.where(held[1:2] > 0, held[0:1], -1.0)
            it_keys[k - n_ham : k - n_ham + 1] = place.astype(jnp.int32)


def list_tile(tile, hop, count, ham, own_keys, aim, pairs, touched, slots):
    base = tile * SLOTS + hop * 16 * 256

    def live(state):
        slot, _ = state
        return (slot < slots) & (ham[tile, slot] >= 0)

    def one_slot(state):
        slot, count = state
        key = ham[tile, slot]
        row = key // 8
        inner = key % 8
        for w in range(2):
            there = own_keys(inner * 2 + w)
            for v in range(2):
                goal = row * 2 + v
                match = (aim[goal] == there).astype(jnp.int32)
                seen = touched[goal]
                pairs[count] = base + slot + (inner * 2 + w) * 256 + (goal + 64 * seen) * 65536
                touched[goal] = seen | match
                count = count + match
        return slot + 1, count

    return lax.while_loop(live, one_slot, (jnp.int32(0), count))[1]


def pair_kernel(where, ham, iterate, aim, pairs, touched):
    tiles = ham.shape[0]
    pieces = iterate.shape[0] + 1
    last = pieces // 2
    near = where[0] // 4
    step = where[0] % 4
    sign = 1 - 2 * (where[1] % 2)

    def untouch(at, carry):
        touched[at] = 0
        return carry

    lax.fori_loop(0, aim.shape[0], untouch, 0)

    def one_tile(tile, count):
        array = tile // 2
        col = ((array // 4) ^ near) * 4 + (step - array % 4 + 4) % 4
        piece = col * 2 + tile % 2
        hop = (sign * (where[2] - piece) + pieces) % pieces
        at = jnp.minimum(jnp.where(hop > last, hop - 1, hop), pieces - 2)
        keys = lambda spot: iterate[at, spot]
        late = hop == last
        return list_tile(tile, hop, count, ham, keys, aim, pairs, touched, jnp.where(late, 0, SLOTS))

    end = pairs.shape[0]
    pairs[end - 1] = lax.fori_loop(0, tiles, one_tile, jnp.int32(0))
    pairs[end - 2] = where[1]
    piece = (where[2] + last) % pieces
    col = piece // 2
    array = ((col // 4) ^ near) * 4 + (step - col % 4 + 4) % 4
    pairs[end - 3] = array * 2 + piece % 2

    def keep(at, carry):
        pairs[end - 96 + at] = touched[at]
        return carry

    lax.fori_loop(0, aim.shape[0], keep, 0)


def product_kernel(pairs, ham_keys, aim, *rest):
    hams, shards, rest = rest[:8], rest[8:25], rest[25:]
    sent, kept, total, ham_buf, it_buf, slab, key_row, late_keys, late_pairs, touched, ham_sem, it_sem, late_sem = rest
    shards = [shard.at[0] if len(shard.shape) == 3 else shard for shard in shards]
    size = ham_buf.shape[1]
    end = pairs.shape[0]
    count = pairs[end - 1]
    depth = pairs[end - 2]
    core = depth % 2
    high = depth // 2
    last = 8
    tail = slab.shape[0]
    half = sent.shape[1]
    cut = last * size
    slab_at = pl.ds(pl.multiple_of(core * cut, tail), tail)
    slab_copy = pltpu.make_async_copy(shards[last].at[slab_at], slab, late_sem.at[0])
    slab_copy.start()

    def start(codes, at):
        code = codes[at]
        ham_at = code % 256
        spot = (code // 256) % 16
        hop = (code // 4096) % 16
        slot = at % WINDOW
        rows = pl.ds(pl.multiple_of((ham_at % (2 * SLOTS)) * size, size), size)
        for k, ham in enumerate(hams):

            @pl.when(ham_at // (2 * SLOTS) == k)
            def _():
                pltpu.make_async_copy(ham.at[rows], ham_buf.at[slot], ham_sem.at[slot]).start()

        upper = (spot >= 8).astype(jnp.int32)
        split = hop == last
        source = jnp.where(split & (upper == core), 16, hop)
        row = spot * size + tail * upper - jnp.where(split, cut * upper, 0)
        rows = pl.ds(pl.multiple_of(row, tail), size)
        for k, shard in enumerate(shards):

            @pl.when(source == k)
            def _():
                pltpu.make_async_copy(shard.at[rows], it_buf.at[slot], it_sem.at[slot]).start()

    def prime(codes, count):
        def first(at, carry):
            start(codes, at)
            return carry

        lax.fori_loop(0, jnp.minimum(count, WINDOW), first, 0)

    def drain(codes, count):
        def multiply(at, carry):
            slot = at % WINDOW
            pltpu.make_async_copy(hams[0].at[pl.ds(0, size)], ham_buf.at[slot], ham_sem.at[slot]).wait()
            pltpu.make_async_copy(shards[0].at[pl.ds(0, size)], it_buf.at[slot], it_sem.at[slot]).wait()
            goal = codes[at] // 65536
            seen = goal >= 64
            goal = goal % 64
            product = jnp.dot(ham_buf[slot], it_buf[slot], preferred_element_type=jnp.float32)
            product = jnp.where(seen, total[goal], 0.0) + product
            total[goal] = product
            owner = goal // half
            part = (owner // 2 == high).astype(jnp.int32)

            @pl.when(owner % 2 == core)
            def _():
                kept[part, goal % half] = product.astype(kept.dtype)

            @pl.when(owner % 2 != core)
            def _():
                sent[part, goal % half] = product.astype(sent.dtype)

            @pl.when(at + WINDOW < count)
            def _():
                start(codes, at + WINDOW)

            return carry

        lax.fori_loop(0, count, multiply, 0)

    prime(pairs, count)

    def clear(at, carry):
        for part in range(2):
            sent[part, at] = jnp.zeros(sent.shape[2:], sent.dtype)
            kept[part, at] = jnp.zeros(kept.shape[2:], kept.dtype)
        return carry

    lax.fori_loop(0, half, clear, 0, unroll=4)

    def recall(at, carry):
        touched[at] = pairs[end - 96 + at]
        return carry

    slab_copy.wait()
    held = slab[...].astype(jnp.float32)
    key_row[...] = jnp.where(held[1:2] > 0, held[0:1], -1.0).astype(jnp.int32)
    key_copy = pltpu.make_async_copy(key_row, late_keys, late_sem.at[1])
    key_copy.start()
    lax.fori_loop(0, aim.shape[0], recall, 0)
    drain(pairs, count)
    key_copy.wait()
    keys = lambda spot: late_keys[0, spot]
    late = list_tile(pairs[end - 3], last, jnp.int32(0), ham_keys, keys, aim, late_pairs, touched, SLOTS)
    prime(late_pairs, late)
    drain(late_pairs, late)


def with_slab(blocks, ints, at):
    width = blocks.shape[-1]
    ints = ints.astype(blocks.dtype)
    ints = jnp.pad(ints, ((0, 16 - ints.shape[0]), (0, width - ints.shape[1])))
    rows = blocks.reshape(-1, width)
    return jnp.concatenate([rows[: at * width], ints, rows[at * width :]], axis=0)


def body(h_blocks, h_rows, h_cols, h_flags, x_blocks, x_cols, x_flags, previous):
    block = x_blocks.shape[-1]
    n_row, n_col, n_depth = lax.axis_size("row"), lax.axis_size("col"), lax.axis_size("depth")
    results = x_cols.shape[3] * x_cols.shape[4]
    where = jnp.stack([lax.axis_index("col"), lax.axis_index("depth"), lax.axis_index("row")]).astype(jnp.int32)
    x_ints = jnp.concatenate([x_cols.reshape(1, -1), x_flags.reshape(1, -1)], axis=0)
    own = with_slab(x_blocks, x_ints, results // 2)
    h_ints = jnp.concatenate([h_rows, h_cols, h_flags], axis=2).reshape(-1, SLOTS)
    mine = with_slab(h_blocks, h_ints, 2 * SLOTS)

    last = n_row // 2
    cut = results // 2 * block
    core = lax.axis_index("depth") % 2
    swap = [(d, d ^ 1) for d in range(n_depth)]
    ring = []
    for r in range(n_row):
        for d in range(n_depth):
            ring.append((r * n_depth + d, (r + 1 - 2 * (d % 2)) % n_row * n_depth + d))

    beside = lax.ppermute(mine, "col", [(c, c ^ 4) for c in range(n_col)])
    pattern = jnp.concatenate([x_cols, x_flags], axis=2)
    beside, pattern = lax.optimization_barrier((beside, pattern))
    aim_ints = lax.all_gather(pattern, "depth", axis=1, tiled=True)
    ahead = [(c, (c // 4) * 4 + (c + 1) % 4) for c in range(n_col)]
    back = [(c, (c // 4) * 4 + (c + 3) % 4) for c in range(n_col)]
    hams = [mine, None, None, None, beside, None, None, None]
    hams[1] = lax.ppermute(mine, "col", ahead)
    hams[3] = lax.ppermute(mine, "col", back)
    hams[5] = lax.ppermute(beside, "col", ahead)
    hams[7] = lax.ppermute(beside, "col", back)

    pair = jnp.stack([own, lax.ppermute(own, "depth", swap)])
    shards = [own] + [None] * n_row
    for hop in range(1, last):
        pair = lax.ppermute(pair, ("row", "depth"), ring)
        if hop == 1:
            pair, hams[4] = lax.optimization_barrier((pair, hams[4]))
        if hop == 2:
            pair, aim_ints, hams[1], hams[3] = lax.optimization_barrier((pair, aim_ints, hams[1], hams[3]))
            hams[2] = lax.ppermute(hams[1], "col", ahead)
        if hop == 4:
            pair, hams[5], hams[7] = lax.optimization_barrier((pair, hams[5], hams[7]))
            hams[6] = lax.ppermute(hams[7], "col", back)
        if hop == last - 2:
            pair, hams[2], hams[6] = lax.optimization_barrier((pair, hams[2], hams[6]))
        if hop > 2:
            before = n_row - hop + 2
            pair, shards[before] = lax.optimization_barrier((pair, shards[before]))
        shards[hop] = pair
        shards[n_row - hop] = lax.ppermute(pair[1], "depth", swap)
    portion = lax.dynamic_slice_in_dim(pair, (1 - core) * cut, cut + 16, axis=1)
    shards[last] = lax.ppermute(portion, ("row", "depth"), ring)
    shards[last], *_ = lax.optimization_barrier((shards[last], shards[last + 1], shards[last + 2]))
    shards[n_row] = lax.ppermute(shards[last][1], "depth", swap)
    hams, shards = ([pltpu.with_memory_space_constraint(x, pltpu.HBM) for x in xs] for xs in (hams, shards))

    aim_keys = jnp.where(aim_ints[0, :, 1] > 0, aim_ints[0, :, 0], -2).reshape(-1)
    smem = pl.BlockSpec(memory_space=pltpu.SMEM)
    anywhere = pl.BlockSpec(memory_space=pl.ANY)
    vmem = pl.BlockSpec(memory_space=pltpu.VMEM)
    early = shards[:last] + shards[last + 1 : n_row]
    ham_keys, it_keys = pl.pallas_call(
        key_kernel,
        out_shape=(
            jax.ShapeDtypeStruct((2 * n_col, block), jnp.int32),
            jax.ShapeDtypeStruct((len(early), block), jnp.int32),
        ),
        in_specs=[anywhere] * (len(hams) + len(early)),
        out_specs=(vmem, vmem),
        scratch_shapes=[
            pltpu.VMEM((n_col, 16, block), jnp.bfloat16),
            pltpu.VMEM((len(early), 16, block), jnp.bfloat16),
            pltpu.SemaphoreType.DMA((n_col + len(early),)),
        ],
        name="keys",
    )(*hams, *early)
    pairs = pl.pallas_call(
        pair_kernel,
        out_shape=jax.ShapeDtypeStruct((512,), jnp.int32),
        in_specs=[smem] * 4,
        out_specs=smem,
        scratch_shapes=[pltpu.SMEM((n_depth * results,), jnp.int32)],
        name="pairs",
    )(where, ham_keys, it_keys, aim_keys)
    halves = jax.ShapeDtypeStruct((2, results, block, block), jnp.bfloat16)
    sent, kept = pl.pallas_call(
        product_kernel,
        out_shape=(halves,) * 2,
        in_specs=[smem] * 3 + [anywhere] * (len(hams) + n_row + 1),
        out_specs=(vmem,) * 2,
        scratch_shapes=[
            pltpu.VMEM((n_depth * results, block, block), jnp.float32),
            pltpu.VMEM((WINDOW, block, block), jnp.bfloat16),
            pltpu.VMEM((WINDOW, block, block), jnp.bfloat16),
            pltpu.VMEM((16, block), jnp.bfloat16),
            pltpu.VMEM((1, block), jnp.int32),
            pltpu.SMEM((1, block), jnp.int32),
            pltpu.SMEM((64,), jnp.int32),
            pltpu.SMEM((64,), jnp.int32),
            pltpu.SemaphoreType.DMA((WINDOW,)),
            pltpu.SemaphoreType.DMA((WINDOW,)),
            pltpu.SemaphoreType.DMA((2,)),
        ],
        compiler_params=pltpu.CompilerParams(vmem_limit_bytes=24 << 20),
        name="products",
    )(*[pltpu.with_memory_space_constraint(x, pltpu.HBM) for x in (pairs, ham_keys, aim_keys)], *hams, *shards)
    near = lax.ppermute(sent, "depth", [(d, d ^ 1) for d in range(n_depth)])
    onward = (kept[0].astype(jnp.float32) + near[0].astype(jnp.float32)).astype(jnp.bfloat16)
    far = lax.ppermute(onward, "depth", [(d, d ^ 2) for d in range(n_depth)])
    prior = previous.reshape(results, block, block).astype(jnp.float32)
    live = x_flags.reshape(results, 1, 1).astype(jnp.float32)
    base = 2.0 * (kept[1].astype(jnp.float32) + near[1].astype(jnp.float32)) - prior
    base = lax.optimization_barrier(base)
    result = (base + 2.0 * far.astype(jnp.float32)) * live
    return result.astype(jnp.bfloat16).reshape(previous.shape)


def solution(mesh):
    placed = (
        P("row", "col", "depth", None, None, None),
        P("row", "col", "depth", None),
        P("row", "col", "depth", None),
        P("row", "col", "depth", None),
        P("row", "depth", "col", None, None, None, None),
        P("row", "depth", "col", None, None),
        P("row", "depth", "col", None, None),
        P("row", "depth", "col", None, None, None, None),
    )
    return jax.shard_map(
        body,
        mesh=mesh,
        in_specs=placed,
        out_specs=P("row", "depth", "col", None, None, None, None),
        check_vma=False,
    )
```

time: 178 us -> 212 us (1.19)
  starting transfers between devices: 89.5 us -> 112 us
  waiting for transfers between devices: 55.8 us -> 69.5 us
  blocking collectives: 11 us -> 6.44 us
  local copies, waits for them, and re-layouts: 4.62 us -> 7.07 us
    ppermute x20 -> x23, starting transfers between devices: 75.2 us -> 103 us  [the longest x7 40.1 us: body(): pair = lax.ppermute(pair, ('row', 'depth'), ring)]
    ppermute x1, waiting for transfers between devices: 0.01 us -> 15.1 us  [body(): beside = lax.ppermute(mine, 'col', [(c, c ^ 4) for c in range(n_col)])]
    all_gather x1, blocking collectives: 11 us -> 6.44 us  [body(): aim_ints = lax.all_gather(pattern, 'depth', axis=1, tiled=True)]
    ppermute x1, starting transfers between devices: 5.47 us -> 2.05 us  [body(): near = lax.ppermute(sent, 'depth', [(d, d ^ 1) for d in range(n_depth)])]
    ppermute x20 -> x23, waiting for transfers between devices: 42.1 us -> 39.2 us  [the longest x7 17.5 us: body(): pair = lax.ppermute(pair, ('row', 'depth'), ring)]
    another operation x6, other arithmetic: 3.59 us -> 0.87 us
  transfers between devices with their start and end apart: 23 -> 26, of which waited for: 10 -> 16; matrix products, arithmetic and copies ran while one was open for 2% -> 2% of each run, Pallas kernels for 3% -> 3%
where the time goes in v9:
time: 212 us; the launch traced here: 211 us
  starting transfers between devices  112 us (53%)
  waiting for transfers between devices  69.5 us (33%)
  Pallas kernels  10.3 us (5%)
  local copies, waits for them, and re-layouts  7.07 us (3%)
  blocking collectives  6.44 us (3%)
  other arithmetic  4.56 us (2%)
    ppermute x7, starting transfers between devices, body(): pair = lax.ppermute(pair, ('row', 'depth'), ring)  40.1 us
    ppermute x7, starting transfers between devices, body(): shards[n_row - hop] = lax.ppermute(pair[1], 'depth', swap)  22.1 us
    ppermute x7, waiting for transfers between devices, body(): pair = lax.ppermute(pair, ('row', 'depth'), ring)  17.5 us
    ppermute x1, waiting for transfers between devices, body(): beside = lax.ppermute(mine, 'col', [(c, c ^ 4) for c in range(n_col)])  15.1 us
    ppermute x1, waiting for transfers between devices, body(): far = lax.ppermute(onward, 'depth', [(d, d ^ 2) for d in range(n_depth)])  12.7 us
    ppermute x1, starting transfers between devices, body(): shards[n_row] = lax.ppermute(shards[last][1], 'depth', swap)  9.01 us
    ppermute x1, starting transfers between devices, body(): pair = jnp.stack([own, lax.ppermute(own, 'depth', swap)])  8.79 us
    all_gather x1, blocking collectives, body(): aim_ints = lax.all_gather(pattern, 'depth', axis=1, tiled=True)  6.44 us
  transfers between devices with their start and end apart: 26, of which 16 were waited for; matrix products, arithmetic and copies ran while one was open for 2% of the time, Pallas kernels for 3%

profile of v9, /device:TPU:1, one launch (start us, length us, event | category | flops | bytes accessed | tf_op | source)
XLA Modules:
  0.0 211.0 jit_solution(349394122734078950)
XLA Ops:
  3.0 8.8 %collective-permute-start = (bf16[2064,128]{1,0:T(8,128)(2,1)S(1)}, bf16[2064,128]{1,0:T(8,128)(2,1)S(1)}, u32[]{:S(2)}, u32[]{:S(2)}) collective-permute-start(bf16[2064,128]{1,0:T(8,128)(2,1)S(1)} %get-tuple-element.64.refs_8_.rest_8_), channel_id=1, source_target_pairs={{0,1},{1,0},{2,3},{3,2},{4,5},{5,4},{6,7},{7,6},{8,9},{9,8},{10,11... | collective-permute-start | bytes 1585160 | tf_op jit(solution)/shard_map/ppermute | solution.py:250
  13.5 5.9 %collective-permute-start.1 = (bf16[2,2064,128]{2,1,0:T(8,128)(2,1)S(1)}, bf16[2,2064,128]{2,1,0:T(8,128)(2,1)S(1)}, u32[]{:S(2)}, u32[]{:S(2)}) collective-permute-start(bf16[2,2064,128]{2,1,0:T(8,128)(2,1)S(1)} %pad_maximum_fusion), channel_id=1, source_target_pairs={{0,32},{1,481},{2,34},{3,483},{32,64},{33,1},{34,66},{35,3},{64,96... | collective-permute-start | bytes 3170312 | tf_op jit(solution)/shard_map/ppermute | solution.py:253
  22.6 15.1 %collective-permute-done.2.refs_4_.rest_4_ = bf16[3088,128]{1,0:T(8,128)(2,1)S(1)} collective-permute-done((bf16[3088,128]{1,0:T(8,128)(2,1)S(1)}, bf16[3088,128]{1,0:T(8,128)(2,1)S(1)}, u32[]{:S(2)}, u32[]{:S(2)}) %collective-permute-start.2) | collective-permute-done | bytes 790560 | tf_op jit(solution)/shard_map/ppermute | solution.py:238
  37.7 5.8 %collective-permute-start.3 = (bf16[2,2064,128]{2,1,0:T(8,128)(2,1)S(1)}, bf16[2,2064,128]{2,1,0:T(8,128)(2,1)S(1)}, u32[]{:S(2)}, u32[]{:S(2)}) collective-permute-start(bf16[2,2064,128]{2,1,0:T(8,128)(2,1)S(1)} %collective-permute-done.1.refs_9_.rest_9_), channel_id=1, source_target_pairs={{0,32},{1,481},{2,34},{3,483},{32,64},{33,1},{34,66},{35,3},{64,96... | collective-permute-start | bytes 3170312 | tf_op jit(solution)/shard_map/ppermute | solution.py:253
  43.5 4.6 %collective-permute-start.5 = (bf16[3088,128]{1,0:T(8,128)(2,1)S(1)}, bf16[3088,128]{1,0:T(8,128)(2,1)S(1)}, u32[]{:S(2)}, u32[]{:S(2)}) collective-permute-start(bf16[3088,128]{1,0:T(8,128)(2,1)S(1)} %fusion.1.refs_0_.rest_0_), channel_id=1, source_target_pairs={{0,12},{4,0},{8,4},{12,8},{16,28},{20,16},{24,20},{28,24},{1,13},{... | collective-permute-start | bytes 2371592 | tf_op jit(solution)/shard_map/ppermute | solution.py:246
  50.1 6.4 %all_gather.3 = s32[1,4,2,8,2]{3,4,2,0,1:T(2,128)S(1)} all-gather(s32[1,1,2,8,2]{3,4,2,0,1:T(2,128)S(1)} %pad_add_fusion), channel_id=1, replica_groups=mesh['row'=16,'col'=8,'depth'=4] {'depth'}, dimensions={1}, use_global_device_ids=true | all-gather | bytes 640 | tf_op jit(solution)/shard_map/all_gather | solution.py:241
  59.0 5.0 %collective-permute-done.4.refs_1_.rest_1_ = bf16[3088,128]{1,0:T(8,128)(2,1)} collective-permute-done((bf16[3088,128]{1,0:T(8,128)(2,1)S(1)}, bf16[3088,128]{1,0:T(8,128)(2,1)}, u32[]{:S(2)}, u32[]{:S(2)}) %collective-permute-start.4) | collective-permute-done | bytes 790560 | tf_op jit(solution)/shard_map/ppermute | solution.py:245
  64.0 7.7 %collective-permute-start.6 = (bf16[2,2064,128]{2,1,0:T(8,128)(2,1)S(1)}, bf16[2,2064,128]{2,1,0:T(8,128)(2,1)S(1)}, u32[]{:S(2)}, u32[]{:S(2)}) collective-permute-start(bf16[2,2064,128]{2,1,0:T(8,128)(2,1)S(1)} %collective-permute-done.3.refs_10_.rest_10_), channel_id=1, source_target_pairs={{0,32},{1,481},{2,34},{3,483},{32,64},{33,1},{34,66},{35,3},{64,96... | collective-permute-start | bytes 3170312 | tf_op jit(solution)/shard_map/ppermute | solution.py:253
  79.0 4.5 %collective-permute-done.6.refs_11_.rest_11_ = bf16[2,2064,128]{2,1,0:T(8,128)(2,1)S(1)} collective-permute-done((bf16[2,2064,128]{2,1,0:T(8,128)(2,1)S(1)}, bf16[2,2064,128]{2,1,0:T(8,128)(2,1)S(1)}, u32[]{:S(2)}, u32[]{:S(2)}) %collective-permute-start.6) | collective-permute-done | bytes 1056800 | tf_op jit(solution)/shard_map/ppermute | solution.py:253
  83.5 5.3 %collective-permute-start.8 = (bf16[2,2064,128]{2,1,0:T(8,128)(2,1)S(1)}, bf16[2,2064,128]{2,1,0:T(8,128)(2,1)S(1)}, u32[]{:S(2)}, u32[]{:S(2)}) collective-permute-start(bf16[2,2064,128]{2,1,0:T(8,128)(2,1)S(1)} %collective-permute-done.6.refs_11_.rest_11_), channel_id=1, source_target_pairs={{0,32},{1,481},{2,34},{3,483},{32,64},{33,1},{34,66},{35,3},{64,96... | collective-permute-start | bytes 3170312 | tf_op jit(solution)/shard_map/ppermute | solution.py:253
  100.6 5.0 %collective-permute-start.12 = (bf16[2,2064,128]{2,1,0:T(8,128)(2,1)S(1)}, bf16[2,2064,128]{2,1,0:T(8,128)(2,1)S(1)}, u32[]{:S(2)}, u32[]{:S(2)}) collective-permute-start(bf16[2,2064,128]{2,1,0:T(8,128)(2,1)S(1)} %collective-permute-done.8.refs_12_.rest_12_), channel_id=1, source_target_pairs={{0,32},{1,481},{2,34},{3,483},{32,64},{33,1},{34,66},{35,3},{64,96... | collective-permute-start | bytes 3170312 | tf_op jit(solution)/shard_map/ppermute | solution.py:253
  110.3 4.6 %collective-permute-start.16 = (bf16[3088,128]{1,0:T(8,128)(2,1)}, bf16[3088,128]{1,0:T(8,128)(2,1)}, u32[]{:S(2)}, u32[]{:S(2)}) collective-permute-start(bf16[3088,128]{1,0:T(8,128)(2,1)} %collective-permute-done.10.refs_7_.rest_7_), channel_id=1, source_target_pairs={{0,12},{4,0},{8,4},{12,8},{16,28},{20,16},{24,20},{28,24},{1,13},{... | collective-permute-start | bytes 2371592 | tf_op jit(solution)/shard_map/ppermute | solution.py:261
  117.5 5.4 %collective-permute-start.14 = (bf16[2,2064,128]{2,1,0:T(8,128)(2,1)S(1)}, bf16[2,2064,128]{2,1,0:T(8,128)(2,1)S(1)}, u32[]{:S(2)}, u32[]{:S(2)}) collective-permute-start(bf16[2,2064,128]{2,1,0:T(8,128)(2,1)S(1)} %collective-permute-done.12.refs_13_.rest_13_), channel_id=1, source_target_pairs={{0,32},{1,481},{2,34},{3,483},{32,64},{33,1},{34,66},{35,3},{64,96... | collective-permute-start | bytes 3170312 | tf_op jit(solution)/shard_map/ppermute | solution.py:253
  127.2 3.9 %collective-permute-done.15.refs_2_.rest_2_ = bf16[3088,128]{1,0:T(8,128)(2,1)} collective-permute-done((bf16[3088,128]{1,0:T(8,128)(2,1)}, bf16[3088,128]{1,0:T(8,128)(2,1)}, u32[]{:S(2)}, u32[]{:S(2)}) %collective-permute-start.15) | collective-permute-done | bytes 790560 | tf_op jit(solution)/shard_map/ppermute | solution.py:258
  134.7 5.0 %collective-permute-start.18 = (bf16[2,2064,128]{2,1,0:T(8,128)(2,1)S(1)}, bf16[2,2064,128]{2,1,0:T(8,128)(2,1)S(1)}, u32[]{:S(2)}, u32[]{:S(2)}) collective-permute-start(bf16[2,2064,128]{2,1,0:T(8,128)(2,1)S(1)} %collective-permute-done.14.refs_14_.rest_14_), channel_id=1, source_target_pairs={{0,32},{1,481},{2,34},{3,483},{32,64},{33,1},{34,66},{35,3},{64,96... | collective-permute-start | bytes 3170312 | tf_op jit(solution)/shard_map/ppermute | solution.py:253
  139.8 4.6 %collective-permute-start.19 = (bf16[2064,128]{1,0:T(8,128)(2,1)S(1)}, bf16[2064,128]{1,0:T(8,128)(2,1)}, u32[]{:S(2)}, u32[]{:S(2)}) collective-permute-start(bf16[2064,128]{1,0:T(8,128)(2,1)S(1)} %slice_bitcast_fusion.2), channel_id=1, source_target_pairs={{0,1},{1,0},{2,3},{3,2},{4,5},{5,4},{6,7},{7,6},{8,9},{9,8},{10,11... | collective-permute-start | bytes 1585160 | tf_op jit(solution)/shard_map/ppermute | solution.py:268
  146.3 5.2 %collective-permute-done.18.refs_15_.rest_15_ = bf16[2,2064,128]{2,1,0:T(8,128)(2,1)S(1)} collective-permute-done((bf16[2,2064,128]{2,1,0:T(8,128)(2,1)S(1)}, bf16[2,2064,128]{2,1,0:T(8,128)(2,1)S(1)}, u32[]{:S(2)}, u32[]{:S(2)}) %collective-permute-start.18) | collective-permute-done | bytes 1056800 | tf_op jit(solution)/shard_map/ppermute | solution.py:253
  152.4 5.0 %collective-permute-start.22 = (bf16[2,1040,128]{2,1,0:T(8,128)(2,1)}, bf16[2,1040,128]{2,1,0:T(8,128)(2,1)}, u32[]{:S(2)}, u32[]{:S(2)}) collective-permute-start(bf16[2,1040,128]{2,1,0:T(8,128)(2,1)} %constant_dynamic-slice_fusion), channel_id=1, source_target_pairs={{0,32},{1,481},{2,34},{3,483},{32,64},{33,1},{34,66},{35,3},{64,96... | collective-permute-start | bytes 1597448 | tf_op jit(solution)/shard_map/ppermute | solution.py:270
  157.5 5.7 %collective-permute-start.20 = (bf16[2064,128]{1,0:T(8,128)(2,1)S(1)}, bf16[2064,128]{1,0:T(8,128)(2,1)S(1)}, u32[]{:S(2)}, u32[]{:S(2)}) collective-permute-start(bf16[2064,128]{1,0:T(8,128)(2,1)S(1)} %slice_bitcast_fusion.1), channel_id=1, source_target_pairs={{0,1},{1,0},{2,3},{3,2},{4,5},{5,4},{6,7},{7,6},{8,9},{9,8},{10,11... | collective-permute-start | bytes 1585160 | tf_op jit(solution)/shard_map/ppermute | solution.py:268
  165.9 9.0 %collective-permute-start.23 = (bf16[1040,128]{1,0:T(8,128)(2,1)S(1)}, bf16[1040,128]{1,0:T(8,128)(2,1)S(1)}, u32[]{:S(2)}, u32[]{:S(2)}) collective-permute-start(bf16[1040,128]{1,0:T(8,128)(2,1)S(1)} %slice_bitcast_fusion.7), channel_id=1, source_target_pairs={{0,1},{1,0},{2,3},{3,2},{4,5},{5,4},{6,7},{7,6},{8,9},{9,8},{10,11... | collective-permute-start | bytes 798728 | tf_op jit(solution)/shard_map/ppermute | solution.py:272
  178.0 4.9 %pairs.1 = s32[512]{0:T(512)} custom-call(s32[3]{0:T(128)} %pad_add_fusion.1.where, s32[16,128]{1,0:T(8,128)} %get-tuple-element.57.ham.ham_keys, s32[15,128]{1,0:T(8,128)} %get-tuple-element.58.iterate, s32[64]{0:T(128)} %select_n.19.aim), custom_call_target="tpu_custom_call" | custom-call | tf_op jit(solution)/shard_map/pairs/pallas_call | solution.py:295
  183.7 3.8 %products.1 = (bf16[2,16,128,128]{3,2,1,0:T(8,128)(2,1)S(1)}, bf16[2,16,128,128]{3,2,1,0:T(8,128)(2,1)S(1)}) custom-call(s32[512]{0:T(512)} %pairs.1, s32[16,128]{1,0:T(8,128)} %get-tuple-element.57.ham.ham_keys, s32[64]{0:T(128)} %select_n.19.aim, bf16[3088,128]{1,0:T(8,128)(2,1)} %copy-done.1, bf16[3088,128]{1,0:T(8,128)(2,1)} %collective-permute-done.4.refs_1_.rest_1_, ...), custom_call_target="tpu_custom_call" | custom-call | tf_op jit(solution)/shard_map/products/pallas_call | solution.py:304
  193.1 3.9 %collective-permute-start.25 = (bf16[16,128,128]{2,1,0:T(8,128)(2,1)}, bf16[16,128,128]{2,1,0:T(8,128)(2,1)S(1)}, u32[]{:S(2)}, u32[]{:S(2)}) collective-permute-start(bf16[16,128,128]{2,1,0:T(8,128)(2,1)} %fusion.2), channel_id=1, source_target_pairs={{0,2},{1,3},{2,0},{3,1},{4,6},{5,7},{6,4},{7,5},{8,10},{9,11},{10,... | collective-permute-start | bytes 1572872 | tf_op jit(solution)/shard_map/ppermute | solution.py:327
  197.4 12.7 %collective-permute-done.25 = bf16[16,128,128]{2,1,0:T(8,128)(2,1)S(1)} collective-permute-done((bf16[16,128,128]{2,1,0:T(8,128)(2,1)}, bf16[16,128,128]{2,1,0:T(8,128)(2,1)S(1)}, u32[]{:S(2)}, u32[]{:S(2)}) %collective-permute-start.25) | collective-permute-done | bytes 524320 | tf_op jit(solution)/shard_map/ppermute | solution.py:327
  (117 shorter events, 62.6 us)
Async XLA Ops:
  3.0 10.3 %collective-permute-start = (bf16[2064,128]{1,0:T(8,128)(2,1)S(1)}, bf16[2064,128]{1,0:T(8,128)(2,1)S(1)}, u32[]{:S(2)}, u32[]{:S(2)}) collective-permute-start(bf16[2064,128]{1,0:T(8,128)(2,1)S(1)} %get-tuple-element.64.refs_8_.rest_8_), channel_id=1, source_target_pairs={{0,1},{1,0},{2,3},{3,2},{4,5},{5,4},{6,7},{7,6},{8,9},{9,8},{10,11... | collective-permute-start | bytes 1585160 | tf_op jit(solution)/shard_map/ppermute | solution.py:250
  13.5 24.2 %collective-permute-start.1 = (bf16[2,2064,128]{2,1,0:T(8,128)(2,1)S(1)}, bf16[2,2064,128]{2,1,0:T(8,128)(2,1)S(1)}, u32[]{:S(2)}, u32[]{:S(2)}) collective-permute-start(bf16[2,2064,128]{2,1,0:T(8,128)(2,1)S(1)} %pad_maximum_fusion), channel_id=1, source_target_pairs={{0,32},{1,481},{2,34},{3,483},{32,64},{33,1},{34,66},{35,3},{64,96... | collective-permute-start | bytes 3170312 | tf_op jit(solution)/shard_map/ppermute | solution.py:253
  19.5 18.3 %collective-permute-start.2 = (bf16[3088,128]{1,0:T(8,128)(2,1)S(1)}, bf16[3088,128]{1,0:T(8,128)(2,1)S(1)}, u32[]{:S(2)}, u32[]{:S(2)}) collective-permute-start(bf16[3088,128]{1,0:T(8,128)(2,1)S(1)} %fusion.1.refs_0_.rest_0_), channel_id=1, source_target_pairs={{0,16},{4,20},{8,24},{12,28},{16,0},{20,4},{24,8},{28,12},{1,17},{... | collective-permute-start | bytes 2371592 | tf_op jit(solution)/shard_map/ppermute | solution.py:238
  37.7 26.3 %collective-permute-start.3 = (bf16[2,2064,128]{2,1,0:T(8,128)(2,1)S(1)}, bf16[2,2064,128]{2,1,0:T(8,128)(2,1)S(1)}, u32[]{:S(2)}, u32[]{:S(2)}) collective-permute-start(bf16[2,2064,128]{2,1,0:T(8,128)(2,1)S(1)} %collective-permute-done.1.refs_9_.rest_9_), channel_id=1, source_target_pairs={{0,32},{1,481},{2,34},{3,483},{32,64},{33,1},{34,66},{35,3},{64,96... | collective-permute-start | bytes 3170312 | tf_op jit(solution)/shard_map/ppermute | solution.py:253
  43.5 15.5 %collective-permute-start.5 = (bf16[3088,128]{1,0:T(8,128)(2,1)S(1)}, bf16[3088,128]{1,0:T(8,128)(2,1)S(1)}, u32[]{:S(2)}, u32[]{:S(2)}) collective-permute-start(bf16[3088,128]{1,0:T(8,128)(2,1)S(1)} %fusion.1.refs_0_.rest_0_), channel_id=1, source_target_pairs={{0,12},{4,0},{8,4},{12,8},{16,28},{20,16},{24,20},{28,24},{1,13},{... | collective-permute-start | bytes 2371592 | tf_op jit(solution)/shard_map/ppermute | solution.py:246
  48.2 15.8 %collective-permute-start.4 = (bf16[3088,128]{1,0:T(8,128)(2,1)S(1)}, bf16[3088,128]{1,0:T(8,128)(2,1)}, u32[]{:S(2)}, u32[]{:S(2)}) collective-permute-start(bf16[3088,128]{1,0:T(8,128)(2,1)S(1)} %fusion.1.refs_0_.rest_0_), channel_id=1, source_target_pairs={{0,4},{4,8},{8,12},{12,0},{16,20},{20,24},{24,28},{28,16},{1,5},{5... | collective-permute-start | bytes 2371592 | tf_op jit(solution)/shard_map/ppermute | solution.py:245
  64.0 19.5 %collective-permute-start.6 = (bf16[2,2064,128]{2,1,0:T(8,128)(2,1)S(1)}, bf16[2,2064,128]{2,1,0:T(8,128)(2,1)S(1)}, u32[]{:S(2)}, u32[]{:S(2)}) collective-permute-start(bf16[2,2064,128]{2,1,0:T(8,128)(2,1)S(1)} %collective-permute-done.3.refs_10_.rest_10_), channel_id=1, source_target_pairs={{0,32},{1,481},{2,34},{3,483},{32,64},{33,1},{34,66},{35,3},{64,96... | collective-permute-start | bytes 3170312 | tf_op jit(solution)/shard_map/ppermute | solution.py:253
  71.7 7.2 %collective-permute-start.7 = (bf16[2064,128]{1,0:T(8,128)(2,1)S(1)}, bf16[2064,128]{1,0:T(8,128)(2,1)S(1)}, u32[]{:S(2)}, u32[]{:S(2)}) collective-permute-start(bf16[2064,128]{1,0:T(8,128)(2,1)S(1)} %slice_bitcast_fusion.6), channel_id=1, source_target_pairs={{0,1},{1,0},{2,3},{3,2},{4,5},{5,4},{6,7},{7,6},{8,9},{9,8},{10,11... | collective-permute-start | bytes 1585160 | tf_op jit(solution)/shard_map/ppermute | solution.py:268
  73.7 20.7 %collective-permute-start.10 = (bf16[3088,128]{1,0:T(8,128)(2,1)S(1)}, bf16[3088,128]{1,0:T(8,128)(2,1)}, u32[]{:S(2)}, u32[]{:S(2)}) collective-permute-start(bf16[3088,128]{1,0:T(8,128)(2,1)S(1)} %collective-permute-done.2.refs_4_.rest_4_), channel_id=1, source_target_pairs={{0,12},{4,0},{8,4},{12,8},{16,28},{20,16},{24,20},{28,24},{1,13},{... | collective-permute-start | bytes 2371592 | tf_op jit(solution)/shard_map/ppermute | solution.py:248
  75.6 21.8 %collective-permute-start.9 = (bf16[3088,128]{1,0:T(8,128)(2,1)S(1)}, bf16[3088,128]{1,0:T(8,128)(2,1)S(1)}, u32[]{:S(2)}, u32[]{:S(2)}) collective-permute-start(bf16[3088,128]{1,0:T(8,128)(2,1)S(1)} %collective-permute-done.2.refs_4_.rest_4_), channel_id=1, source_target_pairs={{0,4},{4,8},{8,12},{12,0},{16,20},{20,24},{24,28},{28,16},{1,5},{5... | collective-permute-start | bytes 2371592 | tf_op jit(solution)/shard_map/ppermute | solution.py:247
  83.5 17.1 %collective-permute-start.8 = (bf16[2,2064,128]{2,1,0:T(8,128)(2,1)S(1)}, bf16[2,2064,128]{2,1,0:T(8,128)(2,1)S(1)}, u32[]{:S(2)}, u32[]{:S(2)}) collective-permute-start(bf16[2,2064,128]{2,1,0:T(8,128)(2,1)S(1)} %collective-permute-done.6.refs_11_.rest_11_), channel_id=1, source_target_pairs={{0,32},{1,481},{2,34},{3,483},{32,64},{33,1},{34,66},{35,3},{64,96... | collective-permute-start | bytes 3170312 | tf_op jit(solution)/shard_map/ppermute | solution.py:253
  88.9 11.8 %collective-permute-start.11 = (bf16[2064,128]{1,0:T(8,128)(2,1)S(1)}, bf16[2064,128]{1,0:T(8,128)(2,1)S(1)}, u32[]{:S(2)}, u32[]{:S(2)}) collective-permute-start(bf16[2064,128]{1,0:T(8,128)(2,1)S(1)} %slice_bitcast_fusion.5), channel_id=1, source_target_pairs={{0,1},{1,0},{2,3},{3,2},{4,5},{5,4},{6,7},{7,6},{8,9},{9,8},{10,11... | collective-permute-start | bytes 1585160 | tf_op jit(solution)/shard_map/ppermute | solution.py:268
  100.6 16.8 %collective-permute-start.12 = (bf16[2,2064,128]{2,1,0:T(8,128)(2,1)S(1)}, bf16[2,2064,128]{2,1,0:T(8,128)(2,1)S(1)}, u32[]{:S(2)}, u32[]{:S(2)}) collective-permute-start(bf16[2,2064,128]{2,1,0:T(8,128)(2,1)S(1)} %collective-permute-done.8.refs_12_.rest_12_), channel_id=1, source_target_pairs={{0,32},{1,481},{2,34},{3,483},{32,64},{33,1},{34,66},{35,3},{64,96... | collective-permute-start | bytes 3170312 | tf_op jit(solution)/shard_map/ppermute | solution.py:253
  105.7 9.2 %collective-permute-start.13 = (bf16[2064,128]{1,0:T(8,128)(2,1)S(1)}, bf16[2064,128]{1,0:T(8,128)(2,1)S(1)}, u32[]{:S(2)}, u32[]{:S(2)}) collective-permute-start(bf16[2064,128]{1,0:T(8,128)(2,1)S(1)} %slice_bitcast_fusion.4), channel_id=1, source_target_pairs={{0,1},{1,0},{2,3},{3,2},{4,5},{5,4},{6,7},{7,6},{8,9},{9,8},{10,11... | collective-permute-start | bytes 1585160 | tf_op jit(solution)/shard_map/ppermute | solution.py:268
  108.4 22.7 %collective-permute-start.15 = (bf16[3088,128]{1,0:T(8,128)(2,1)}, bf16[3088,128]{1,0:T(8,128)(2,1)}, u32[]{:S(2)}, u32[]{:S(2)}) collective-permute-start(bf16[3088,128]{1,0:T(8,128)(2,1)} %collective-permute-done.4.refs_1_.rest_1_), channel_id=1, source_target_pairs={{0,4},{4,8},{8,12},{12,0},{16,20},{20,24},{24,28},{28,16},{1,5},{5... | collective-permute-start | bytes 2371592 | tf_op jit(solution)/shard_map/ppermute | solution.py:258
  110.3 21.6 %collective-permute-start.16 = (bf16[3088,128]{1,0:T(8,128)(2,1)}, bf16[3088,128]{1,0:T(8,128)(2,1)}, u32[]{:S(2)}, u32[]{:S(2)}) collective-permute-start(bf16[3088,128]{1,0:T(8,128)(2,1)} %collective-permute-done.10.refs_7_.rest_7_), channel_id=1, source_target_pairs={{0,12},{4,0},{8,4},{12,8},{16,28},{20,16},{24,20},{28,24},{1,13},{... | collective-permute-start | bytes 2371592 | tf_op jit(solution)/shard_map/ppermute | solution.py:261
  117.5 17.2 %collective-permute-start.14 = (bf16[2,2064,128]{2,1,0:T(8,128)(2,1)S(1)}, bf16[2,2064,128]{2,1,0:T(8,128)(2,1)S(1)}, u32[]{:S(2)}, u32[]{:S(2)}) collective-permute-start(bf16[2,2064,128]{2,1,0:T(8,128)(2,1)S(1)} %collective-permute-done.12.refs_13_.rest_13_), channel_id=1, source_target_pairs={{0,32},{1,481},{2,34},{3,483},{32,64},{33,1},{34,66},{35,3},{64,96... | collective-permute-start | bytes 3170312 | tf_op jit(solution)/shard_map/ppermute | solution.py:253
  123.7 11.0 %collective-permute-start.17 = (bf16[2064,128]{1,0:T(8,128)(2,1)}, bf16[2064,128]{1,0:T(8,128)(2,1)}, u32[]{:S(2)}, u32[]{:S(2)}) collective-permute-start(bf16[2064,128]{1,0:T(8,128)(2,1)} %slice_bitcast_fusion.3), channel_id=1, source_target_pairs={{0,1},{1,0},{2,3},{3,2},{4,5},{5,4},{6,7},{7,6},{8,9},{9,8},{10,11... | collective-permute-start | bytes 1585160 | tf_op jit(solution)/shard_map/ppermute | solution.py:268
  134.7 16.8 %collective-permute-start.18 = (bf16[2,2064,128]{2,1,0:T(8,128)(2,1)S(1)}, bf16[2,2064,128]{2,1,0:T(8,128)(2,1)S(1)}, u32[]{:S(2)}, u32[]{:S(2)}) collective-permute-start(bf16[2,2064,128]{2,1,0:T(8,128)(2,1)S(1)} %collective-permute-done.14.refs_14_.rest_14_), channel_id=1, source_target_pairs={{0,32},{1,481},{2,34},{3,483},{32,64},{33,1},{34,66},{35,3},{64,96... | collective-permute-start | bytes 3170312 | tf_op jit(solution)/shard_map/ppermute | solution.py:253
  144.4 18.8 %collective-permute-start.21 = (bf16[2064,128]{1,0:T(8,128)(2,1)S(1)}, bf16[2064,128]{1,0:T(8,128)(2,1)S(1)}, u32[]{:S(2)}, u32[]{:S(2)}) collective-permute-start(bf16[2064,128]{1,0:T(8,128)(2,1)S(1)} %slice_bitcast_fusion), channel_id=1, source_target_pairs={{0,1},{1,0},{2,3},{3,2},{4,5},{5,4},{6,7},{7,6},{8,9},{9,8},{10,11... | collective-permute-start | bytes 1585160 | tf_op jit(solution)/shard_map/ppermute | solution.py:268
  152.4 12.3 %collective-permute-start.22 = (bf16[2,1040,128]{2,1,0:T(8,128)(2,1)}, bf16[2,1040,128]{2,1,0:T(8,128)(2,1)}, u32[]{:S(2)}, u32[]{:S(2)}) collective-permute-start(bf16[2,1040,128]{2,1,0:T(8,128)(2,1)} %constant_dynamic-slice_fusion), channel_id=1, source_target_pairs={{0,32},{1,481},{2,34},{3,483},{32,64},{33,1},{34,66},{35,3},{64,96... | collective-permute-start | bytes 1597448 | tf_op jit(solution)/shard_map/ppermute | solution.py:270
  157.5 7.2 %collective-permute-start.20 = (bf16[2064,128]{1,0:T(8,128)(2,1)S(1)}, bf16[2064,128]{1,0:T(8,128)(2,1)S(1)}, u32[]{:S(2)}, u32[]{:S(2)}) collective-permute-start(bf16[2064,128]{1,0:T(8,128)(2,1)S(1)} %slice_bitcast_fusion.1), channel_id=1, source_target_pairs={{0,1},{1,0},{2,3},{3,2},{4,5},{5,4},{6,7},{7,6},{8,9},{9,8},{10,11... | collective-permute-start | bytes 1585160 | tf_op jit(solution)/shard_map/ppermute | solution.py:268
  165.9 17.1 %collective-permute-start.23 = (bf16[1040,128]{1,0:T(8,128)(2,1)S(1)}, bf16[1040,128]{1,0:T(8,128)(2,1)S(1)}, u32[]{:S(2)}, u32[]{:S(2)}) collective-permute-start(bf16[1040,128]{1,0:T(8,128)(2,1)S(1)} %slice_bitcast_fusion.7), channel_id=1, source_target_pairs={{0,1},{1,0},{2,3},{3,2},{4,5},{5,4},{6,7},{7,6},{8,9},{9,8},{10,11... | collective-permute-start | bytes 798728 | tf_op jit(solution)/shard_map/ppermute | solution.py:272
  193.1 17.0 %collective-permute-start.25 = (bf16[16,128,128]{2,1,0:T(8,128)(2,1)}, bf16[16,128,128]{2,1,0:T(8,128)(2,1)S(1)}, u32[]{:S(2)}, u32[]{:S(2)}) collective-permute-start(bf16[16,128,128]{2,1,0:T(8,128)(2,1)} %fusion.2), channel_id=1, source_target_pairs={{0,2},{1,3},{2,0},{3,1},{4,6},{5,7},{6,4},{7,5},{8,10},{9,11},{10,... | collective-permute-start | bytes 1572872 | tf_op jit(solution)/shard_map/ppermute | solution.py:327
  (27 other events, 634.2 us)

commit v10 on v8

--- a/solution.py
+++ b/solution.py
@@ -72,7 +72,7 @@
 
 
 def product_kernel(pairs, iterate, *rest):
-    hams, (sent, kept, total, ham_buf, it_buf, ham_sem, it_sem) = rest[:8], rest[8:]
+    hams, (sent_on, sent_keep, kept, total, ham_buf, it_buf, ham_sem, it_sem) = rest[:8], rest[8:]
     size = ham_buf.shape[1]
     slots = hams[0].shape[0] // size
     count = pairs[pairs.shape[0] - 1]
@@ -96,15 +96,14 @@
 
     lax.fori_loop(0, jnp.minimum(count, WINDOW), first, 0)
 
-    half = sent.shape[1]
+    half = kept.shape[1]
     depth = pairs[pairs.shape[0] - 2]
     core = depth % 2
     high = depth // 2
 
     def clear(at, carry):
-        for part in range(2):
-            sent[part, at] = jnp.zeros(sent.shape[2:], sent.dtype)
-            kept[part, at] = jnp.zeros(kept.shape[2:], kept.dtype)
+        for ref in (sent_on.at[at], sent_keep.at[at], kept.at[0, at], kept.at[1, at]):
+            ref[...] = jnp.zeros(ref.shape, ref.dtype)
         return carry
 
     lax.fori_loop(0, half, clear, 0, unroll=4)
@@ -126,9 +125,13 @@
         def _():
             kept[part, goal % half] = product.astype(kept.dtype)
 
-        @pl.when(owner % 2 != core)
-        def _():
-            sent[part, goal % half] = product.astype(sent.dtype)
+        @pl.when((owner % 2 != core) & (part == 0))
+        def _():
+            sent_on[goal % half] = product.astype(sent_on.dtype)
+
+        @pl.when((owner % 2 != core) & (part == 1))
+        def _():
+            sent_keep[goal % half] = product.astype(sent_keep.dtype)
 
         @pl.when(at + WINDOW < count)
         def _():
@@ -192,11 +195,12 @@
         scratch_shapes=[pltpu.SMEM((n_depth * results,), jnp.int32)],
         name="pairs",
     )(where, ham_keys, it_keys, aim_keys)
-    sent, kept = pl.pallas_call(
+    whole = jax.ShapeDtypeStruct((results, block, block), jnp.bfloat16)
+    sent_on, sent_keep, kept = pl.pallas_call(
         product_kernel,
-        out_shape=(halves,) * 2,
+        out_shape=(whole, whole, halves),
         in_specs=[smem] + [anywhere] * 9,
-        out_specs=(vmem,) * 2,
+        out_specs=(vmem,) * 3,
         scratch_shapes=[
             pltpu.VMEM((n_depth * results, block, block), jnp.float32),
             pltpu.VMEM((WINDOW, block, block), jnp.bfloat16),
@@ -207,12 +211,17 @@
         compiler_params=pltpu.CompilerParams(vmem_limit_bytes=24 << 20),
         name="products",
     )(*[pltpu.with_memory_space_constraint(x, pltpu.HBM) for x in (pairs, iterate)], *hams)
-    near = lax.ppermute(sent, "depth", [(d, d ^ 1) for d in range(n_depth)])
-    onward = (kept[0].astype(jnp.float32) + near[0].astype(jnp.float32)).astype(jnp.bfloat16)
-    far = lax.ppermute(onward, "depth", [(d, d ^ 2) for d in range(n_depth)])
+    to_core = [(d, d ^ 1) for d in range(n_depth)]
+    near_on = lax.ppermute(sent_on, "depth", to_core)
+    near_keep = lax.ppermute(sent_keep, "depth", to_core)
+    far = []
+    for rows in (slice(0, results // 2), slice(results // 2, results)):
+        onward = kept[0, rows].astype(jnp.float32) + near_on[rows].astype(jnp.float32)
+        far.append(lax.ppermute(onward.astype(jnp.bfloat16), "depth", [(d, d ^ 2) for d in range(n_depth)]))
+    far = jnp.concatenate(far, axis=0)
     prior = previous.reshape(results, block, block).astype(jnp.float32)
     live = x_flags.reshape(results, 1, 1).astype(jnp.float32)
-    base = 2.0 * (kept[1].astype(jnp.float32) + near[1].astype(jnp.float32)) - prior
+    base = 2.0 * (kept[1].astype(jnp.float32) + near_keep.astype(jnp.float32)) - prior
     base = lax.optimization_barrier(base)
     result = (base + 2.0 * far.astype(jnp.float32)) * live
     return result.astype(jnp.bfloat16).reshape(previous.shape)

time: 156 us -> 156 us (level)
  waiting for transfers between devices: 52.9 us -> 48 us
  starting transfers between devices: 32.3 us -> 36.3 us
    ppermute x2 -> x4, waiting for transfers between devices: 13.8 us -> 9.62 us  [the longest x2 9.62 us: body(): lax.ppermute(onward.astype(jnp.bfloat16), 'depth', [(d, d ^ 2) for d in r...]
    ppermute x2 -> x4, starting transfers between devices: 7.6 us -> 11.6 us  [the longest x2 7.09 us: body(): lax.ppermute(onward.astype(jnp.bfloat16), 'depth', [(d, d ^ 2) for d in r...]
  transfers between devices with their start and end apart: 10 -> 12, of which waited for: 6 -> 6; matrix products, arithmetic and copies ran while one was open for 4% -> 5% of each run, Pallas kernels for 4% -> 4%
where the time goes in v10:
time: 156 us; the launch traced here: 154 us
  waiting for transfers between devices  48 us (31%)
  blocking collectives  39.4 us (25%)
  starting transfers between devices  36.3 us (23%)
  between operations  13.6 us (9%)
  Pallas kernels  8.9 us (6%)
  other arithmetic  6.34 us (4%)
  local copies, waits for them, and re-layouts  1.74 us (1%)
    all_gather x1, blocking collectives, body(): it_ints = lax.all_gather(it_ints, 'row', axis=0, tiled=True)  26.4 us
    ppermute x7, waiting for transfers between devices, send(): return lax.ppermute(source, 'col', route)  26 us
    ppermute x7, starting transfers between devices, send(): return lax.ppermute(source, 'col', route)  24.7 us
    all_gather x1, blocking collectives, body(): aim_ints = lax.all_gather(it_ints, 'depth', axis=1, tiled=True)  13 us
    all_gather x1, waiting for transfers between devices, body(): iterate = lax.all_gather(x_blocks[0, 0, 0], 'row', axis=0)  11.7 us
    ppermute x2, waiting for transfers between devices, body(): lax.ppermute(onward.astype(jnp.bfloat16), 'depth', [(d, d ^ 2) for d in r...  9.62 us
    ppermute x2, starting transfers between devices, body(): lax.ppermute(onward.astype(jnp.bfloat16), 'depth', [(d, d ^ 2) for d in r...  7.09 us
    pallas_call x1, Pallas kernels, body(): pl.pallas_call(pair_kernel, out_shape=jax.ShapeDtypeStruct((512,), jnp.in...  4.94 us
  transfers between devices with their start and end apart: 12, of which 6 were waited for; matrix products, arithmetic and copies ran while one was open for 5% of the time, Pallas kernels for 4%

profile of v10, /device:TPU:1, one launch (start us, length us, event | category | flops | bytes accessed | tf_op | source)
XLA Modules:
  0.0 154.3 jit_solution(12530347324563004810)
XLA Ops:
  9.3 1.2 fusion.2.refs_0_.rest_0_
  10.5 4.0 %collective-permute-start = (bf16[3088,128]{1,0:T(8,128)(2,1)S(1)}, bf16[3088,128]{1,0:T(8,128)(2,1)S(1)}, u32[]{:S(2)}, u32[]{:S(2)}) collective-permute-start(bf16[3088,128]{1,0:T(8,128)(2,1)S(1)} %fusion.2.refs_0_.rest_0_), channel_id=1, source_target_pairs={{0,4},{4,8},{8,12},{12,0},{16,20},{20,24},{24,28},{28,16},{1,5},{5... | collective-permute-start | bytes 2371592 | tf_op jit(solution)/shard_map/ppermute | solution.py:161
  14.6 3.4 %collective-permute-start.1 = (bf16[3088,128]{1,0:T(8,128)(2,1)S(1)}, bf16[3088,128]{1,0:T(8,128)(2,1)S(1)}, u32[]{:S(2)}, u32[]{:S(2)}) collective-permute-start(bf16[3088,128]{1,0:T(8,128)(2,1)S(1)} %fusion.2.refs_0_.rest_0_), channel_id=1, source_target_pairs={{0,12},{4,0},{8,4},{12,8},{16,28},{20,16},{24,20},{28,24},{1,13},{... | collective-permute-start | bytes 2371592 | tf_op jit(solution)/shard_map/ppermute | solution.py:161
  18.0 13.0 %all_gather.9 = s32[1,4,2,8,2]{3,4,2,0,1:T(2,128)S(1)} all-gather(s32[1,1,2,8,2]{3,4,2,0,1:T(2,128)S(1)} %pad_add_fusion), channel_id=1, replica_groups=mesh['row'=16,'col'=8,'depth'=4] {'depth'}, dimensions={1}, use_global_device_ids=true | all-gather | bytes 640 | tf_op jit(solution)/shard_map/all_gather | solution.py:152
  31.0 1.9 %collective-permute-start.3 = (bf16[3088,128]{1,0:T(8,128)(2,1)S(1)}, bf16[3088,128]{1,0:T(8,128)(2,1)}, u32[]{:S(2)}, u32[]{:S(2)}) collective-permute-start(bf16[3088,128]{1,0:T(8,128)(2,1)S(1)} %fusion.2.refs_0_.rest_0_), channel_id=1, source_target_pairs={{0,16},{4,20},{8,24},{12,28},{16,0},{20,4},{24,8},{28,12},{1,17},{... | collective-permute-start | bytes 2371592 | tf_op jit(solution)/shard_map/ppermute | solution.py:161
  32.9 1.9 %collective-permute-start.4 = (bf16[3088,128]{1,0:T(8,128)(2,1)S(1)}, bf16[3088,128]{1,0:T(8,128)(2,1)}, u32[]{:S(2)}, u32[]{:S(2)}) collective-permute-start(bf16[3088,128]{1,0:T(8,128)(2,1)S(1)} %fusion.2.refs_0_.rest_0_), channel_id=1, source_target_pairs={{0,20},{4,24},{8,28},{12,16},{16,4},{20,8},{24,12},{28,0},{1,21},{... | collective-permute-start | bytes 2371592 | tf_op jit(solution)/shard_map/ppermute | solution.py:161
  34.8 3.7 %collective-permute-start.5 = (bf16[3088,128]{1,0:T(8,128)(2,1)S(1)}, bf16[3088,128]{1,0:T(8,128)(2,1)}, u32[]{:S(2)}, u32[]{:S(2)}) collective-permute-start(bf16[3088,128]{1,0:T(8,128)(2,1)S(1)} %fusion.2.refs_0_.rest_0_), channel_id=1, source_target_pairs={{0,24},{4,28},{8,16},{12,20},{16,8},{20,12},{24,0},{28,4},{1,25},{... | collective-permute-start | bytes 2371592 | tf_op jit(solution)/shard_map/ppermute | solution.py:161
  38.6 4.2 %collective-permute-start.2 = (bf16[3088,128]{1,0:T(8,128)(2,1)S(1)}, bf16[3088,128]{1,0:T(8,128)(2,1)}, u32[]{:S(2)}, u32[]{:S(2)}) collective-permute-start(bf16[3088,128]{1,0:T(8,128)(2,1)S(1)} %fusion.2.refs_0_.rest_0_), channel_id=1, source_target_pairs={{0,8},{4,12},{8,0},{12,4},{16,24},{20,28},{24,16},{28,20},{1,9},{5... | collective-permute-start | bytes 2371592 | tf_op jit(solution)/shard_map/ppermute | solution.py:161
  42.8 5.5 %collective-permute-start.6 = (bf16[3088,128]{1,0:T(8,128)(2,1)S(1)}, bf16[3088,128]{1,0:T(8,128)(2,1)}, u32[]{:S(2)}, u32[]{:S(2)}) collective-permute-start(bf16[3088,128]{1,0:T(8,128)(2,1)S(1)} %fusion.2.refs_0_.rest_0_), channel_id=1, source_target_pairs={{0,28},{4,16},{8,20},{12,24},{16,12},{20,0},{24,4},{28,8},{1,29},{... | collective-permute-start | bytes 2371592 | tf_op jit(solution)/shard_map/ppermute | solution.py:161
  49.8 26.4 %all_gather.10 = s32[16,1,2,8,2]{3,4,2,1,0:T(2,128)S(1)} all-gather(s32[1,1,2,8,2]{3,4,2,1,0:T(2,128)S(1)} %bitcast.30), channel_id=1, replica_groups=mesh['row'=16,'col'=8,'depth'=4] {'row'}, dimensions={0}, use_global_device_ids=true | all-gather | bytes 2176 | tf_op jit(solution)/shard_map/all_gather | solution.py:173
  77.0 8.2 %collective-permute-done.5.refs_6_.rest_6_ = bf16[3088,128]{1,0:T(8,128)(2,1)} collective-permute-done((bf16[3088,128]{1,0:T(8,128)(2,1)S(1)}, bf16[3088,128]{1,0:T(8,128)(2,1)}, u32[]{:S(2)}, u32[]{:S(2)}) %collective-permute-start.5) | collective-permute-done | bytes 790560 | tf_op jit(solution)/shard_map/ppermute | solution.py:161
  85.2 12.4 %collective-permute-done.2.refs_2_.rest_2_ = bf16[3088,128]{1,0:T(8,128)(2,1)} collective-permute-done((bf16[3088,128]{1,0:T(8,128)(2,1)S(1)}, bf16[3088,128]{1,0:T(8,128)(2,1)}, u32[]{:S(2)}, u32[]{:S(2)}) %collective-permute-start.2) | collective-permute-done | bytes 790560 | tf_op jit(solution)/shard_map/ppermute | solution.py:161
  97.6 5.4 %collective-permute-done.6.refs_7_.rest_7_ = bf16[3088,128]{1,0:T(8,128)(2,1)} collective-permute-done((bf16[3088,128]{1,0:T(8,128)(2,1)S(1)}, bf16[3088,128]{1,0:T(8,128)(2,1)}, u32[]{:S(2)}, u32[]{:S(2)}) %collective-permute-start.6) | collective-permute-done | bytes 790560 | tf_op jit(solution)/shard_map/ppermute | solution.py:161
  103.0 1.4 keys.1.ham
  104.5 4.9 %pairs.1 = s32[512]{0:T(512)} custom-call(s32[2]{0:T(128)} %pad_add_fusion.1.where, s32[16,128]{1,0:T(8,128)} %keys.1.ham, s32[16,16]{1,0:T(8,128)} %copy.21.iterate, s32[64]{0:T(128)} %select_n.19.aim), custom_call_target="tpu_custom_call" | custom-call | tf_op jit(solution)/shard_map/pairs/pallas_call | solution.py:190
  109.4 11.7 %all-gather.3.cloned.1.call-done = bf16[16,1,1,8,2,128,128]{6,5,4,3,2,1,0:T(8,128)(2,1)} async-done(((bf16[1,1,1,8,2,128,128]{6,5,4,3,2,1,0:T(8,128)(2,1)}), bf16[16,1,1,8,2,128,128]{6,5,4,3,2,1,0:T(8,128)(2,1)}) %all-gather.3.cloned.1.call-update) | async-done | bytes 8388624 | tf_op jit(solution)/shard_map/all_gather | solution.py:149
  121.1 2.5 %products.1 = (bf16[16,128,128]{2,1,0:T(8,128)(2,1)S(1)}, bf16[16,128,128]{2,1,0:T(8,128)(2,1)S(1)}, bf16[2,16,128,128]{3,2,1,0:T(8,128)(2,1)S(1)}) custom-call(s32[512]{0:T(512)} %pairs.1, bf16[256,128,128]{2,1,0:T(8,128)(2,1)} %bitcast.27, bf16[3088,128]{1,0:T(8,128)(2,1)} %copy-done, bf16[3088,128]{1,0:T(8,128)(2,1)} %copy-done.1, ...), custom_call_target="tpu_custom_call" | custom-call | tf_op jit(solution)/shard_map/products/pallas_call | solution.py:199
  123.6 2.6 %collective-permute-start.8 = (bf16[16,128,128]{2,1,0:T(8,128)(2,1)S(1)}, bf16[16,128,128]{2,1,0:T(8,128)(2,1)}, u32[]{:S(2)}, u32[]{:S(2)}) collective-permute-start(bf16[16,128,128]{2,1,0:T(8,128)(2,1)S(1)} %get-tuple-element.24), channel_id=1, source_target_pairs={{0,1},{1,0},{2,3},{3,2},{4,5},{5,4},{6,7},{7,6},{8,9},{9,8},{10,11... | collective-permute-start | bytes 1572872 | tf_op jit(solution)/shard_map/ppermute | solution.py:215
  126.2 1.9 %collective-permute-start.7 = (bf16[16,128,128]{2,1,0:T(8,128)(2,1)S(1)}, bf16[16,128,128]{2,1,0:T(8,128)(2,1)S(1)}, u32[]{:S(2)}, u32[]{:S(2)}) collective-permute-start(bf16[16,128,128]{2,1,0:T(8,128)(2,1)S(1)} %get-tuple-element.23), channel_id=1, source_target_pairs={{0,1},{1,0},{2,3},{3,2},{4,5},{5,4},{6,7},{7,6},{8,9},{9,8},{10,11... | collective-permute-start | bytes 1572872 | tf_op jit(solution)/shard_map/ppermute | solution.py:216
  128.3 1.2 fusion.4
  129.5 5.2 %collective-permute-start.10 = (bf16[8,128,128]{2,1,0:T(8,128)(2,1)S(1)}, bf16[8,128,128]{2,1,0:T(8,128)(2,1)S(1)}, u32[]{:S(2)}, u32[]{:S(2)}) collective-permute-start(bf16[8,128,128]{2,1,0:T(8,128)(2,1)S(1)} %get-tuple-element.26), channel_id=1, source_target_pairs={{0,2},{1,3},{2,0},{3,1},{4,6},{5,7},{6,4},{7,5},{8,10},{9,11},{10,... | collective-permute-start | bytes 786440 | tf_op jit(solution)/shard_map/ppermute | solution.py:220
  134.7 1.9 %collective-permute-start.9 = (bf16[8,128,128]{2,1,0:T(8,128)(2,1)S(1)}, bf16[8,128,128]{2,1,0:T(8,128)(2,1)S(1)}, u32[]{:S(2)}, u32[]{:S(2)}) collective-permute-start(bf16[8,128,128]{2,1,0:T(8,128)(2,1)S(1)} %get-tuple-element.25), channel_id=1, source_target_pairs={{0,2},{1,3},{2,0},{3,1},{4,6},{5,7},{6,4},{7,5},{8,10},{9,11},{10,... | collective-permute-start | bytes 786440 | tf_op jit(solution)/shard_map/ppermute | solution.py:220
  136.9 4.0 %collective-permute-done.10 = bf16[8,128,128]{2,1,0:T(8,128)(2,1)S(1)} collective-permute-done((bf16[8,128,128]{2,1,0:T(8,128)(2,1)S(1)}, bf16[8,128,128]{2,1,0:T(8,128)(2,1)S(1)}, u32[]{:S(2)}, u32[]{:S(2)}) %collective-permute-start.10) | collective-permute-done | bytes 262176 | tf_op jit(solution)/shard_map/ppermute | solution.py:220
  140.9 5.6 %collective-permute-done.9 = bf16[8,128,128]{2,1,0:T(8,128)(2,1)S(1)} collective-permute-done((bf16[8,128,128]{2,1,0:T(8,128)(2,1)S(1)}, bf16[8,128,128]{2,1,0:T(8,128)(2,1)S(1)}, u32[]{:S(2)}, u32[]{:S(2)}) %collective-permute-start.9) | collective-permute-done | bytes 262176 | tf_op jit(solution)/shard_map/ppermute | solution.py:220
  (38 shorter events, 6.4 us)
Async XLA Ops:
  6.5 11.4 %copy-start.5 = (s32[1,1,1,8,2]{3,4,2,1,0:T(2,128)S(1)}, s32[1,1,1,8,2]{3,4,2,1,0:T(2,128)}, u32[]{:S(2)}) copy-start(s32[1,1,1,8,2]{3,4,2,1,0:T(2,128)} %param.13) | copy-start | bytes 196
  6.5 11.4 %copy-start.4 = (s32[1,1,1,8,2]{3,4,2,1,0:T(2,128)S(1)}, s32[1,1,1,8,2]{3,4,2,1,0:T(2,128)}, u32[]{:S(2)}) copy-start(s32[1,1,1,8,2]{3,4,2,1,0:T(2,128)} %param.14) | copy-start | bytes 196
  6.5 114.5 %all-gather.3.cloned.1.call-start = ((), (), s32[]{:S(2)}) async-start(), calls=%async_computation | async-start | bytes 8912896 | tf_op jit(solution)/shard_map/all_gather | solution.py:149
  10.5 92.5 %copy-start = (bf16[3088,128]{1,0:T(8,128)(2,1)}, bf16[3088,128]{1,0:T(8,128)(2,1)S(1)}, u32[]{:S(2)}) copy-start(bf16[3088,128]{1,0:T(8,128)(2,1)S(1)} %fusion.2.refs_0_.rest_0_) | copy-start | bytes 2371588
  10.5 28.0 %collective-permute-start = (bf16[3088,128]{1,0:T(8,128)(2,1)S(1)}, bf16[3088,128]{1,0:T(8,128)(2,1)S(1)}, u32[]{:S(2)}, u32[]{:S(2)}) collective-permute-start(bf16[3088,128]{1,0:T(8,128)(2,1)S(1)} %fusion.2.refs_0_.rest_0_), channel_id=1, source_target_pairs={{0,4},{4,8},{8,12},{12,0},{16,20},{20,24},{24,28},{28,16},{1,5},{5... | collective-permute-start | bytes 2371592 | tf_op jit(solution)/shard_map/ppermute | solution.py:161
  14.6 24.0 %collective-permute-start.1 = (bf16[3088,128]{1,0:T(8,128)(2,1)S(1)}, bf16[3088,128]{1,0:T(8,128)(2,1)S(1)}, u32[]{:S(2)}, u32[]{:S(2)}) collective-permute-start(bf16[3088,128]{1,0:T(8,128)(2,1)S(1)} %fusion.2.refs_0_.rest_0_), channel_id=1, source_target_pairs={{0,12},{4,0},{8,4},{12,8},{16,28},{20,16},{24,20},{28,24},{1,13},{... | collective-permute-start | bytes 2371592 | tf_op jit(solution)/shard_map/ppermute | solution.py:161
  31.0 46.0 %collective-permute-start.3 = (bf16[3088,128]{1,0:T(8,128)(2,1)S(1)}, bf16[3088,128]{1,0:T(8,128)(2,1)}, u32[]{:S(2)}, u32[]{:S(2)}) collective-permute-start(bf16[3088,128]{1,0:T(8,128)(2,1)S(1)} %fusion.2.refs_0_.rest_0_), channel_id=1, source_target_pairs={{0,16},{4,20},{8,24},{12,28},{16,0},{20,4},{24,8},{28,12},{1,17},{... | collective-permute-start | bytes 2371592 | tf_op jit(solution)/shard_map/ppermute | solution.py:161
  32.9 44.1 %collective-permute-start.4 = (bf16[3088,128]{1,0:T(8,128)(2,1)S(1)}, bf16[3088,128]{1,0:T(8,128)(2,1)}, u32[]{:S(2)}, u32[]{:S(2)}) collective-permute-start(bf16[3088,128]{1,0:T(8,128)(2,1)S(1)} %fusion.2.refs_0_.rest_0_), channel_id=1, source_target_pairs={{0,20},{4,24},{8,28},{12,16},{16,4},{20,8},{24,12},{28,0},{1,21},{... | collective-permute-start | bytes 2371592 | tf_op jit(solution)/shard_map/ppermute | solution.py:161
  34.8 50.4 %collective-permute-start.5 = (bf16[3088,128]{1,0:T(8,128)(2,1)S(1)}, bf16[3088,128]{1,0:T(8,128)(2,1)}, u32[]{:S(2)}, u32[]{:S(2)}) collective-permute-start(bf16[3088,128]{1,0:T(8,128)(2,1)S(1)} %fusion.2.refs_0_.rest_0_), channel_id=1, source_target_pairs={{0,24},{4,28},{8,16},{12,20},{16,8},{20,12},{24,0},{28,4},{1,25},{... | collective-permute-start | bytes 2371592 | tf_op jit(solution)/shard_map/ppermute | solution.py:161
  38.6 64.5 %copy-start.1 = (bf16[3088,128]{1,0:T(8,128)(2,1)}, bf16[3088,128]{1,0:T(8,128)(2,1)S(1)}, u32[]{:S(2)}) copy-start(bf16[3088,128]{1,0:T(8,128)(2,1)S(1)} %collective-permute-done.refs_1_.rest_1_) | copy-start | bytes 2371588
  38.6 64.4 %copy-start.2 = (bf16[3088,128]{1,0:T(8,128)(2,1)}, bf16[3088,128]{1,0:T(8,128)(2,1)S(1)}, u32[]{:S(2)}) copy-start(bf16[3088,128]{1,0:T(8,128)(2,1)S(1)} %collective-permute-done.1.refs_3_.rest_3_) | copy-start | bytes 2371588
  38.6 59.0 %collective-permute-start.2 = (bf16[3088,128]{1,0:T(8,128)(2,1)S(1)}, bf16[3088,128]{1,0:T(8,128)(2,1)}, u32[]{:S(2)}, u32[]{:S(2)}) collective-permute-start(bf16[3088,128]{1,0:T(8,128)(2,1)S(1)} %fusion.2.refs_0_.rest_0_), channel_id=1, source_target_pairs={{0,8},{4,12},{8,0},{12,4},{16,24},{20,28},{24,16},{28,20},{1,9},{5... | collective-permute-start | bytes 2371592 | tf_op jit(solution)/shard_map/ppermute | solution.py:161
  42.8 60.2 %collective-permute-start.6 = (bf16[3088,128]{1,0:T(8,128)(2,1)S(1)}, bf16[3088,128]{1,0:T(8,128)(2,1)}, u32[]{:S(2)}, u32[]{:S(2)}) collective-permute-start(bf16[3088,128]{1,0:T(8,128)(2,1)S(1)} %fusion.2.refs_0_.rest_0_), channel_id=1, source_target_pairs={{0,28},{4,16},{8,20},{12,24},{16,12},{20,0},{24,4},{28,8},{1,29},{... | collective-permute-start | bytes 2371592 | tf_op jit(solution)/shard_map/ppermute | solution.py:161
  123.6 13.0 %copy-start.3 = (bf16[1,1,1,8,2,128,128]{6,5,4,3,2,1,0:T(8,128)(2,1)S(1)}, bf16[1,1,1,8,2,128,128]{6,5,4,3,2,1,0:T(8,128)(2,1)}, u32[]{:S(2)}) copy-start(bf16[1,1,1,8,2,128,128]{6,5,4,3,2,1,0:T(8,128)(2,1)} %param.15) | copy-start | bytes 1572868
  123.6 4.7 %collective-permute-start.8 = (bf16[16,128,128]{2,1,0:T(8,128)(2,1)S(1)}, bf16[16,128,128]{2,1,0:T(8,128)(2,1)}, u32[]{:S(2)}, u32[]{:S(2)}) collective-permute-start(bf16[16,128,128]{2,1,0:T(8,128)(2,1)S(1)} %get-tuple-element.24), channel_id=1, source_target_pairs={{0,1},{1,0},{2,3},{3,2},{4,5},{5,4},{6,7},{7,6},{8,9},{9,8},{10,11... | collective-permute-start | bytes 1572872 | tf_op jit(solution)/shard_map/ppermute | solution.py:215
  126.2 10.4 %collective-permute-start.7 = (bf16[16,128,128]{2,1,0:T(8,128)(2,1)S(1)}, bf16[16,128,128]{2,1,0:T(8,128)(2,1)S(1)}, u32[]{:S(2)}, u32[]{:S(2)}) collective-permute-start(bf16[16,128,128]{2,1,0:T(8,128)(2,1)S(1)} %get-tuple-element.23), channel_id=1, source_target_pairs={{0,1},{1,0},{2,3},{3,2},{4,5},{5,4},{6,7},{7,6},{8,9},{9,8},{10,11... | collective-permute-start | bytes 1572872 | tf_op jit(solution)/shard_map/ppermute | solution.py:216
  129.5 11.4 %collective-permute-start.10 = (bf16[8,128,128]{2,1,0:T(8,128)(2,1)S(1)}, bf16[8,128,128]{2,1,0:T(8,128)(2,1)S(1)}, u32[]{:S(2)}, u32[]{:S(2)}) collective-permute-start(bf16[8,128,128]{2,1,0:T(8,128)(2,1)S(1)} %get-tuple-element.26), channel_id=1, source_target_pairs={{0,2},{1,3},{2,0},{3,1},{4,6},{5,7},{6,4},{7,5},{8,10},{9,11},{10,... | collective-permute-start | bytes 786440 | tf_op jit(solution)/shard_map/ppermute | solution.py:220
  134.7 11.8 %collective-permute-start.9 = (bf16[8,128,128]{2,1,0:T(8,128)(2,1)S(1)}, bf16[8,128,128]{2,1,0:T(8,128)(2,1)S(1)}, u32[]{:S(2)}, u32[]{:S(2)}) collective-permute-start(bf16[8,128,128]{2,1,0:T(8,128)(2,1)S(1)} %get-tuple-element.25), channel_id=1, source_target_pairs={{0,2},{1,3},{2,0},{3,1},{4,6},{5,7},{6,4},{7,5},{8,10},{9,11},{10,... | collective-permute-start | bytes 786440 | tf_op jit(solution)/shard_map/ppermute | solution.py:220
Sparse Core Ops, SparseCore 0:
  9.4 111.5 all-gather.2

commit v11 on v8

--- a/solution.py
+++ b/solution.py
@@ -109,14 +109,15 @@
 
     lax.fori_loop(0, half, clear, 0, unroll=4)
 
-    def multiply(at, carry):
+    def arrive(at):
         slot = at % WINDOW
         pltpu.make_async_copy(hams[0].at[pl.ds(0, size)], ham_buf.at[slot], ham_sem.at[slot]).wait()
         pltpu.make_async_copy(iterate.at[0], it_buf.at[slot], it_sem.at[slot]).wait()
+
+    def store(at, product):
         goal = pairs[at] // 65536
         seen = goal >= 64
         goal = goal % 64
-        product = jnp.dot(ham_buf[slot], it_buf[slot], preferred_element_type=jnp.float32)
         product = jnp.where(seen, total[goal], 0.0) + product
         total[goal] = product
         owner = goal // half
@@ -134,9 +135,26 @@
         def _():
             start(at + WINDOW)
 
-        return carry
-
-    lax.fori_loop(0, count, multiply, 0)
+    def two(step, carry):
+        at = 2 * step
+        more = at + 1 < count
+        arrive(at)
+
+        @pl.when(more)
+        def _():
+            arrive(at + 1)
+
+        slots_now = (at % WINDOW, (at + 1) % WINDOW)
+        products = [jnp.dot(ham_buf[k], it_buf[k], preferred_element_type=jnp.float32) for k in slots_now]
+        store(at, products[0])
+
+        @pl.when(more)
+        def _():
+            store(at + 1, products[1])
+
+        return carry
+
+    lax.fori_loop(0, (count + 1) // 2, two, 0)
 
 
 def body(h_blocks, h_rows, h_cols, h_flags, x_blocks, x_cols, x_flags, previous):

time: 156 us -> 156 us (level)
  no operation moved by 1% of the time
where the time goes in v11:
time: 156 us; the launch traced here: 155 us
  waiting for transfers between devices  52.8 us (34%)
  blocking collectives  39.5 us (25%)
  starting transfers between devices  32.7 us (21%)
  between operations  13.6 us (9%)
  Pallas kernels  8.83 us (6%)
  other arithmetic  6.06 us (4%)
  local copies, waits for them, and re-layouts  1.76 us (1%)
    all_gather x1, blocking collectives, body(): it_ints = lax.all_gather(it_ints, 'row', axis=0, tiled=True)  26.5 us
    ppermute x7, waiting for transfers between devices, send(): return lax.ppermute(source, 'col', route)  26 us
    ppermute x7, starting transfers between devices, send(): return lax.ppermute(source, 'col', route)  24.7 us
    all_gather x1, blocking collectives, body(): aim_ints = lax.all_gather(it_ints, 'depth', axis=1, tiled=True)  13 us
    all_gather x1, waiting for transfers between devices, body(): iterate = lax.all_gather(x_blocks[0, 0, 0], 'row', axis=0)  12.1 us
    ppermute x1, waiting for transfers between devices, body(): far = lax.ppermute(onward, 'depth', [(d, d ^ 2) for d in range(n_depth)])  11.7 us
    ppermute x1, starting transfers between devices, body(): far = lax.ppermute(onward, 'depth', [(d, d ^ 2) for d in range(n_depth)])  5.54 us
    pallas_call x1, Pallas kernels, body(): pl.pallas_call(pair_kernel, out_shape=jax.ShapeDtypeStruct((512,), jnp.in...  4.53 us
  transfers between devices with their start and end apart: 10, of which 6 were waited for; matrix products, arithmetic and copies ran while one was open for 4% of the time, Pallas kernels for 4%

profile of v11, /device:TPU:1, one launch (start us, length us, event | category | flops | bytes accessed | tf_op | source)
XLA Modules:
  0.0 155.3 jit_solution(12185426436431078696)
XLA Ops:
  6.5 0.7 all-gather.3.cloned.1.call-update
  9.3 1.2 fusion.1.refs_0_.rest_0_
  10.5 4.0 %collective-permute-start = (bf16[3088,128]{1,0:T(8,128)(2,1)S(1)}, bf16[3088,128]{1,0:T(8,128)(2,1)S(1)}, u32[]{:S(2)}, u32[]{:S(2)}) collective-permute-start(bf16[3088,128]{1,0:T(8,128)(2,1)S(1)} %fusion.1.refs_0_.rest_0_), channel_id=1, source_target_pairs={{0,4},{4,8},{8,12},{12,0},{16,20},{20,24},{24,28},{28,16},{1,5},{5... | collective-permute-start | bytes 2371592 | tf_op jit(solution)/shard_map/ppermute | solution.py:176
  14.6 3.4 %collective-permute-start.1 = (bf16[3088,128]{1,0:T(8,128)(2,1)S(1)}, bf16[3088,128]{1,0:T(8,128)(2,1)S(1)}, u32[]{:S(2)}, u32[]{:S(2)}) collective-permute-start(bf16[3088,128]{1,0:T(8,128)(2,1)S(1)} %fusion.1.refs_0_.rest_0_), channel_id=1, source_target_pairs={{0,12},{4,0},{8,4},{12,8},{16,28},{20,16},{24,20},{28,24},{1,13},{... | collective-permute-start | bytes 2371592 | tf_op jit(solution)/shard_map/ppermute | solution.py:176
  18.0 13.0 %all_gather.9 = s32[1,4,2,8,2]{3,4,2,0,1:T(2,128)S(1)} all-gather(s32[1,1,2,8,2]{3,4,2,0,1:T(2,128)S(1)} %pad_add_fusion), channel_id=1, replica_groups=mesh['row'=16,'col'=8,'depth'=4] {'depth'}, dimensions={1}, use_global_device_ids=true | all-gather | bytes 640 | tf_op jit(solution)/shard_map/all_gather | solution.py:167
  31.0 1.9 %collective-permute-start.3 = (bf16[3088,128]{1,0:T(8,128)(2,1)S(1)}, bf16[3088,128]{1,0:T(8,128)(2,1)S(1)}, u32[]{:S(2)}, u32[]{:S(2)}) collective-permute-start(bf16[3088,128]{1,0:T(8,128)(2,1)S(1)} %fusion.1.refs_0_.rest_0_), channel_id=1, source_target_pairs={{0,16},{4,20},{8,24},{12,28},{16,0},{20,4},{24,8},{28,12},{1,17},{... | collective-permute-start | bytes 2371592 | tf_op jit(solution)/shard_map/ppermute | solution.py:176
  32.9 1.9 %collective-permute-start.4 = (bf16[3088,128]{1,0:T(8,128)(2,1)S(1)}, bf16[3088,128]{1,0:T(8,128)(2,1)}, u32[]{:S(2)}, u32[]{:S(2)}) collective-permute-start(bf16[3088,128]{1,0:T(8,128)(2,1)S(1)} %fusion.1.refs_0_.rest_0_), channel_id=1, source_target_pairs={{0,20},{4,24},{8,28},{12,16},{16,4},{20,8},{24,12},{28,0},{1,21},{... | collective-permute-start | bytes 2371592 | tf_op jit(solution)/shard_map/ppermute | solution.py:176
  34.8 3.7 %collective-permute-start.5 = (bf16[3088,128]{1,0:T(8,128)(2,1)S(1)}, bf16[3088,128]{1,0:T(8,128)(2,1)}, u32[]{:S(2)}, u32[]{:S(2)}) collective-permute-start(bf16[3088,128]{1,0:T(8,128)(2,1)S(1)} %fusion.1.refs_0_.rest_0_), channel_id=1, source_target_pairs={{0,24},{4,28},{8,16},{12,20},{16,8},{20,12},{24,0},{28,4},{1,25},{... | collective-permute-start | bytes 2371592 | tf_op jit(solution)/shard_map/ppermute | solution.py:176
  38.6 4.2 %collective-permute-start.2 = (bf16[3088,128]{1,0:T(8,128)(2,1)S(1)}, bf16[3088,128]{1,0:T(8,128)(2,1)}, u32[]{:S(2)}, u32[]{:S(2)}) collective-permute-start(bf16[3088,128]{1,0:T(8,128)(2,1)S(1)} %fusion.1.refs_0_.rest_0_), channel_id=1, source_target_pairs={{0,8},{4,12},{8,0},{12,4},{16,24},{20,28},{24,16},{28,20},{1,9},{5... | collective-permute-start | bytes 2371592 | tf_op jit(solution)/shard_map/ppermute | solution.py:176
  42.8 5.5 %collective-permute-start.6 = (bf16[3088,128]{1,0:T(8,128)(2,1)S(1)}, bf16[3088,128]{1,0:T(8,128)(2,1)}, u32[]{:S(2)}, u32[]{:S(2)}) collective-permute-start(bf16[3088,128]{1,0:T(8,128)(2,1)S(1)} %fusion.1.refs_0_.rest_0_), channel_id=1, source_target_pairs={{0,28},{4,16},{8,20},{12,24},{16,12},{20,0},{24,4},{28,8},{1,29},{... | collective-permute-start | bytes 2371592 | tf_op jit(solution)/shard_map/ppermute | solution.py:176
  49.8 26.5 %all_gather.10 = s32[16,1,2,8,2]{3,4,2,1,0:T(2,128)S(1)} all-gather(s32[1,1,2,8,2]{3,4,2,1,0:T(2,128)S(1)} %bitcast.25), channel_id=1, replica_groups=mesh['row'=16,'col'=8,'depth'=4] {'row'}, dimensions={0}, use_global_device_ids=true | all-gather | bytes 2176 | tf_op jit(solution)/shard_map/all_gather | solution.py:188
  77.0 8.2 %collective-permute-done.5.refs_6_.rest_6_ = bf16[3088,128]{1,0:T(8,128)(2,1)} collective-permute-done((bf16[3088,128]{1,0:T(8,128)(2,1)S(1)}, bf16[3088,128]{1,0:T(8,128)(2,1)}, u32[]{:S(2)}, u32[]{:S(2)}) %collective-permute-start.5) | collective-permute-done | bytes 790560 | tf_op jit(solution)/shard_map/ppermute | solution.py:176
  85.2 12.4 %collective-permute-done.2.refs_2_.rest_2_ = bf16[3088,128]{1,0:T(8,128)(2,1)} collective-permute-done((bf16[3088,128]{1,0:T(8,128)(2,1)S(1)}, bf16[3088,128]{1,0:T(8,128)(2,1)}, u32[]{:S(2)}, u32[]{:S(2)}) %collective-permute-start.2) | collective-permute-done | bytes 790560 | tf_op jit(solution)/shard_map/ppermute | solution.py:176
  97.6 5.4 %collective-permute-done.6.refs_7_.rest_7_ = bf16[3088,128]{1,0:T(8,128)(2,1)} collective-permute-done((bf16[3088,128]{1,0:T(8,128)(2,1)S(1)}, bf16[3088,128]{1,0:T(8,128)(2,1)}, u32[]{:S(2)}, u32[]{:S(2)}) %collective-permute-start.6) | collective-permute-done | bytes 790560 | tf_op jit(solution)/shard_map/ppermute | solution.py:176
  103.0 1.4 keys.1.ham
  104.5 4.5 %pairs.1 = s32[512]{0:T(512)} custom-call(s32[2]{0:T(128)} %pad_add_fusion.1.where, s32[16,128]{1,0:T(8,128)} %keys.1.ham, s32[16,16]{1,0:T(8,128)} %copy.21.iterate, s32[64]{0:T(128)} %select_n.19.aim), custom_call_target="tpu_custom_call" | custom-call | tf_op jit(solution)/shard_map/pairs/pallas_call | solution.py:205
  109.0 12.1 %all-gather.3.cloned.1.call-done = bf16[16,1,1,8,2,128,128]{6,5,4,3,2,1,0:T(8,128)(2,1)} async-done(((bf16[1,1,1,8,2,128,128]{6,5,4,3,2,1,0:T(8,128)(2,1)}), bf16[16,1,1,8,2,128,128]{6,5,4,3,2,1,0:T(8,128)(2,1)}) %all-gather.3.cloned.1.call-update) | async-done | bytes 8388624 | tf_op jit(solution)/shard_map/all_gather | solution.py:164
  121.1 2.9 %products.1 = (bf16[2,16,128,128]{3,2,1,0:T(8,128)(2,1)S(1)}, bf16[2,16,128,128]{3,2,1,0:T(8,128)(2,1)S(1)}) custom-call(s32[512]{0:T(512)} %pairs.1, bf16[256,128,128]{2,1,0:T(8,128)(2,1)} %bitcast.22, bf16[3088,128]{1,0:T(8,128)(2,1)} %copy-done, bf16[3088,128]{1,0:T(8,128)(2,1)} %copy-done.1, bf16[3088,128]{1,0:T(8,128)(2,1)} %collective-permute-done.2.refs_2_.rest_2_, ...), custom_call_target="tpu_custom_call" | custom-call | tf_op jit(solution)/shard_map/products/pallas_call | solution.py:213
  124.0 2.5 %collective-permute-start.7 = (bf16[2,16,128,128]{3,2,1,0:T(8,128)(2,1)S(1)}, bf16[2,16,128,128]{3,2,1,0:T(8,128)(2,1)S(1)}, u32[]{:S(2)}, u32[]{:S(2)}) collective-permute-start(bf16[2,16,128,128]{3,2,1,0:T(8,128)(2,1)S(1)} %get-tuple-element.22), channel_id=1, source_target_pairs={{0,1},{1,0},{2,3},{3,2},{4,5},{5,4},{6,7},{7,6},{8,9},{9,8},{10,11... | collective-permute-start | bytes 3145736 | tf_op jit(solution)/shard_map/ppermute | solution.py:228
  126.5 2.3 %collective-permute-done.7 = bf16[2,16,128,128]{3,2,1,0:T(8,128)(2,1)S(1)} collective-permute-done((bf16[2,16,128,128]{3,2,1,0:T(8,128)(2,1)S(1)}, bf16[2,16,128,128]{3,2,1,0:T(8,128)(2,1)S(1)}, u32[]{:S(2)}, u32[]{:S(2)}) %collective-permute-start.7) | collective-permute-done | bytes 1048608 | tf_op jit(solution)/shard_map/ppermute | solution.py:228
  128.8 0.9 fusion.2
  129.7 5.5 %collective-permute-start.8 = (bf16[16,128,128]{2,1,0:T(8,128)(2,1)}, bf16[16,128,128]{2,1,0:T(8,128)(2,1)S(1)}, u32[]{:S(2)}, u32[]{:S(2)}) collective-permute-start(bf16[16,128,128]{2,1,0:T(8,128)(2,1)} %fusion.2), channel_id=1, source_target_pairs={{0,2},{1,3},{2,0},{3,1},{4,6},{5,7},{6,4},{7,5},{8,10},{9,11},{10,... | collective-permute-start | bytes 1572872 | tf_op jit(solution)/shard_map/ppermute | solution.py:230
  135.7 11.7 %collective-permute-done.8 = bf16[16,128,128]{2,1,0:T(8,128)(2,1)S(1)} collective-permute-done((bf16[16,128,128]{2,1,0:T(8,128)(2,1)}, bf16[16,128,128]{2,1,0:T(8,128)(2,1)S(1)}, u32[]{:S(2)}, u32[]{:S(2)}) %collective-permute-start.8) | collective-permute-done | bytes 524320 | tf_op jit(solution)/shard_map/ppermute | solution.py:230
  147.4 1.0 multiply_convert_fusion
  (36 shorter events, 4.7 us)
Async XLA Ops:
  6.5 11.4 %copy-start.6 = (s32[1,1,1,8,2]{3,4,2,1,0:T(2,128)S(1)}, s32[1,1,1,8,2]{3,4,2,1,0:T(2,128)}, u32[]{:S(2)}) copy-start(s32[1,1,1,8,2]{3,4,2,1,0:T(2,128)} %param.13) | copy-start | bytes 196
  6.5 11.4 %copy-start.5 = (s32[1,1,1,8,2]{3,4,2,1,0:T(2,128)S(1)}, s32[1,1,1,8,2]{3,4,2,1,0:T(2,128)}, u32[]{:S(2)}) copy-start(s32[1,1,1,8,2]{3,4,2,1,0:T(2,128)} %param.14) | copy-start | bytes 196
  6.5 114.5 %all-gather.3.cloned.1.call-start = ((), (), s32[]{:S(2)}) async-start(), calls=%async_computation | async-start | bytes 8912896 | tf_op jit(solution)/shard_map/all_gather | solution.py:164
  10.5 92.5 %copy-start = (bf16[3088,128]{1,0:T(8,128)(2,1)}, bf16[3088,128]{1,0:T(8,128)(2,1)S(1)}, u32[]{:S(2)}) copy-start(bf16[3088,128]{1,0:T(8,128)(2,1)S(1)} %fusion.1.refs_0_.rest_0_) | copy-start | bytes 2371588
  10.5 28.0 %collective-permute-start = (bf16[3088,128]{1,0:T(8,128)(2,1)S(1)}, bf16[3088,128]{1,0:T(8,128)(2,1)S(1)}, u32[]{:S(2)}, u32[]{:S(2)}) collective-permute-start(bf16[3088,128]{1,0:T(8,128)(2,1)S(1)} %fusion.1.refs_0_.rest_0_), channel_id=1, source_target_pairs={{0,4},{4,8},{8,12},{12,0},{16,20},{20,24},{24,28},{28,16},{1,5},{5... | collective-permute-start | bytes 2371592 | tf_op jit(solution)/shard_map/ppermute | solution.py:176
  14.6 24.0 %collective-permute-start.1 = (bf16[3088,128]{1,0:T(8,128)(2,1)S(1)}, bf16[3088,128]{1,0:T(8,128)(2,1)S(1)}, u32[]{:S(2)}, u32[]{:S(2)}) collective-permute-start(bf16[3088,128]{1,0:T(8,128)(2,1)S(1)} %fusion.1.refs_0_.rest_0_), channel_id=1, source_target_pairs={{0,12},{4,0},{8,4},{12,8},{16,28},{20,16},{24,20},{28,24},{1,13},{... | collective-permute-start | bytes 2371592 | tf_op jit(solution)/shard_map/ppermute | solution.py:176
  31.0 46.0 %collective-permute-start.3 = (bf16[3088,128]{1,0:T(8,128)(2,1)S(1)}, bf16[3088,128]{1,0:T(8,128)(2,1)S(1)}, u32[]{:S(2)}, u32[]{:S(2)}) collective-permute-start(bf16[3088,128]{1,0:T(8,128)(2,1)S(1)} %fusion.1.refs_0_.rest_0_), channel_id=1, source_target_pairs={{0,16},{4,20},{8,24},{12,28},{16,0},{20,4},{24,8},{28,12},{1,17},{... | collective-permute-start | bytes 2371592 | tf_op jit(solution)/shard_map/ppermute | solution.py:176
  32.9 44.1 %collective-permute-start.4 = (bf16[3088,128]{1,0:T(8,128)(2,1)S(1)}, bf16[3088,128]{1,0:T(8,128)(2,1)}, u32[]{:S(2)}, u32[]{:S(2)}) collective-permute-start(bf16[3088,128]{1,0:T(8,128)(2,1)S(1)} %fusion.1.refs_0_.rest_0_), channel_id=1, source_target_pairs={{0,20},{4,24},{8,28},{12,16},{16,4},{20,8},{24,12},{28,0},{1,21},{... | collective-permute-start | bytes 2371592 | tf_op jit(solution)/shard_map/ppermute | solution.py:176
  34.8 50.4 %collective-permute-start.5 = (bf16[3088,128]{1,0:T(8,128)(2,1)S(1)}, bf16[3088,128]{1,0:T(8,128)(2,1)}, u32[]{:S(2)}, u32[]{:S(2)}) collective-permute-start(bf16[3088,128]{1,0:T(8,128)(2,1)S(1)} %fusion.1.refs_0_.rest_0_), channel_id=1, source_target_pairs={{0,24},{4,28},{8,16},{12,20},{16,8},{20,12},{24,0},{28,4},{1,25},{... | collective-permute-start | bytes 2371592 | tf_op jit(solution)/shard_map/ppermute | solution.py:176
  38.6 64.5 %copy-start.1 = (bf16[3088,128]{1,0:T(8,128)(2,1)}, bf16[3088,128]{1,0:T(8,128)(2,1)S(1)}, u32[]{:S(2)}) copy-start(bf16[3088,128]{1,0:T(8,128)(2,1)S(1)} %collective-permute-done.refs_1_.rest_1_) | copy-start | bytes 2371588
  38.6 64.4 %copy-start.2 = (bf16[3088,128]{1,0:T(8,128)(2,1)}, bf16[3088,128]{1,0:T(8,128)(2,1)S(1)}, u32[]{:S(2)}) copy-start(bf16[3088,128]{1,0:T(8,128)(2,1)S(1)} %collective-permute-done.1.refs_3_.rest_3_) | copy-start | bytes 2371588
  38.6 59.0 %collective-permute-start.2 = (bf16[3088,128]{1,0:T(8,128)(2,1)S(1)}, bf16[3088,128]{1,0:T(8,128)(2,1)}, u32[]{:S(2)}, u32[]{:S(2)}) collective-permute-start(bf16[3088,128]{1,0:T(8,128)(2,1)S(1)} %fusion.1.refs_0_.rest_0_), channel_id=1, source_target_pairs={{0,8},{4,12},{8,0},{12,4},{16,24},{20,28},{24,16},{28,20},{1,9},{5... | collective-permute-start | bytes 2371592 | tf_op jit(solution)/shard_map/ppermute | solution.py:176
  42.8 60.2 %collective-permute-start.6 = (bf16[3088,128]{1,0:T(8,128)(2,1)S(1)}, bf16[3088,128]{1,0:T(8,128)(2,1)}, u32[]{:S(2)}, u32[]{:S(2)}) collective-permute-start(bf16[3088,128]{1,0:T(8,128)(2,1)S(1)} %fusion.1.refs_0_.rest_0_), channel_id=1, source_target_pairs={{0,28},{4,16},{8,20},{12,24},{16,12},{20,0},{24,4},{28,8},{1,29},{... | collective-permute-start | bytes 2371592 | tf_op jit(solution)/shard_map/ppermute | solution.py:176
  77.0 26.0 %copy-start.3 = (bf16[3088,128]{1,0:T(8,128)(2,1)}, bf16[3088,128]{1,0:T(8,128)(2,1)S(1)}, u32[]{:S(2)}) copy-start(bf16[3088,128]{1,0:T(8,128)(2,1)S(1)} %collective-permute-done.3.refs_4_.rest_4_) | copy-start | bytes 2371588
  123.9 11.5 %copy-start.4 = (bf16[1,1,1,8,2,128,128]{6,5,4,3,2,1,0:T(8,128)(2,1)S(1)}, bf16[1,1,1,8,2,128,128]{6,5,4,3,2,1,0:T(8,128)(2,1)}, u32[]{:S(2)}) copy-start(bf16[1,1,1,8,2,128,128]{6,5,4,3,2,1,0:T(8,128)(2,1)} %param.15) | copy-start | bytes 1572868
  124.0 4.8 %collective-permute-start.7 = (bf16[2,16,128,128]{3,2,1,0:T(8,128)(2,1)S(1)}, bf16[2,16,128,128]{3,2,1,0:T(8,128)(2,1)S(1)}, u32[]{:S(2)}, u32[]{:S(2)}) collective-permute-start(bf16[2,16,128,128]{3,2,1,0:T(8,128)(2,1)S(1)} %get-tuple-element.22), channel_id=1, source_target_pairs={{0,1},{1,0},{2,3},{3,2},{4,5},{5,4},{6,7},{7,6},{8,9},{9,8},{10,11... | collective-permute-start | bytes 3145736 | tf_op jit(solution)/shard_map/ppermute | solution.py:228
  129.7 17.7 %collective-permute-start.8 = (bf16[16,128,128]{2,1,0:T(8,128)(2,1)}, bf16[16,128,128]{2,1,0:T(8,128)(2,1)S(1)}, u32[]{:S(2)}, u32[]{:S(2)}) collective-permute-start(bf16[16,128,128]{2,1,0:T(8,128)(2,1)} %fusion.2), channel_id=1, source_target_pairs={{0,2},{1,3},{2,0},{3,1},{4,6},{5,7},{6,4},{7,5},{8,10},{9,11},{10,... | collective-permute-start | bytes 1572872 | tf_op jit(solution)/shard_map/ppermute | solution.py:230
Sparse Core Ops, SparseCore 0:
  9.4 111.5 all-gather.2

commit v12 on v10

--- a/solution.py
+++ b/solution.py
@@ -214,11 +214,9 @@
     to_core = [(d, d ^ 1) for d in range(n_depth)]
     near_on = lax.ppermute(sent_on, "depth", to_core)
     near_keep = lax.ppermute(sent_keep, "depth", to_core)
-    far = []
-    for rows in (slice(0, results // 2), slice(results // 2, results)):
-        onward = kept[0, rows].astype(jnp.float32) + near_on[rows].astype(jnp.float32)
-        far.append(lax.ppermute(onward.astype(jnp.bfloat16), "depth", [(d, d ^ 2) for d in range(n_depth)]))
-    far = jnp.concatenate(far, axis=0)
+    onward = (kept[0].astype(jnp.float32) + near_on.astype(jnp.float32)).astype(jnp.bfloat16)
+    onward, kept = lax.optimization_barrier((onward, kept))
+    far = lax.ppermute(onward, "depth", [(d, d ^ 2) for d in range(n_depth)])
     prior = previous.reshape(results, block, block).astype(jnp.float32)
     live = x_flags.reshape(results, 1, 1).astype(jnp.float32)
     base = 2.0 * (kept[1].astype(jnp.float32) + near_keep.astype(jnp.float32)) - prior

time: 156 us -> 156 us (level)
  waiting for transfers between devices: 48 us -> 50.8 us
  starting transfers between devices: 36.3 us -> 33.9 us
    ppermute x2 -> x1, starting transfers between devices: 7.09 us -> 4.46 us  [body(): far = lax.ppermute(onward, 'depth', [(d, d ^ 2) for d in range(n_depth)])]
    ppermute x2 -> x1, waiting for transfers between devices: 9.62 us -> 11.6 us  [body(): far = lax.ppermute(onward, 'depth', [(d, d ^ 2) for d in range(n_depth)])]
  transfers between devices with their start and end apart: 12 -> 11, of which waited for: 6 -> 5; matrix products, arithmetic and copies ran while one was open for 5% -> 4% of each run, Pallas kernels for 4% -> 4%
where the time goes in v12:
time: 156 us; the launch traced here: 154 us
  waiting for transfers between devices  50.8 us (33%)
  blocking collectives  39.5 us (25%)
  starting transfers between devices  33.9 us (22%)
  between operations  13.6 us (9%)
  Pallas kernels  8.45 us (5%)
  other arithmetic  6.3 us (4%)
  local copies, waits for them, and re-layouts  1.76 us (1%)
    all_gather x1, blocking collectives, body(): it_ints = lax.all_gather(it_ints, 'row', axis=0, tiled=True)  26.5 us
    ppermute x7, waiting for transfers between devices, send(): return lax.ppermute(source, 'col', route)  26 us
    ppermute x7, starting transfers between devices, send(): return lax.ppermute(source, 'col', route)  24.7 us
    all_gather x1, blocking collectives, body(): aim_ints = lax.all_gather(it_ints, 'depth', axis=1, tiled=True)  13 us
    all_gather x1, waiting for transfers between devices, body(): iterate = lax.all_gather(x_blocks[0, 0, 0], 'row', axis=0)  12.5 us
    ppermute x1, waiting for transfers between devices, body(): far = lax.ppermute(onward, 'depth', [(d, d ^ 2) for d in range(n_depth)])  11.6 us
    ppermute x1, starting transfers between devices, body(): far = lax.ppermute(onward, 'depth', [(d, d ^ 2) for d in range(n_depth)])  4.46 us
    pallas_call x1, Pallas kernels, body(): pl.pallas_call(pair_kernel, out_shape=jax.ShapeDtypeStruct((512,), jnp.in...  4.09 us
  transfers between devices with their start and end apart: 11, of which 5 were waited for; matrix products, arithmetic and copies ran while one was open for 4% of the time, Pallas kernels for 4%

profile of v12, /device:TPU:1, one launch (start us, length us, event | category | flops | bytes accessed | tf_op | source)
XLA Modules:
  0.0 154.4 jit_solution(14486318394588745550)
XLA Ops:
  6.5 0.7 all-gather.3.cloned.1.call-update
  9.3 1.2 fusion.3.refs_0_.rest_0_
  10.5 4.0 %collective-permute-start = (bf16[3088,128]{1,0:T(8,128)(2,1)S(1)}, bf16[3088,128]{1,0:T(8,128)(2,1)S(1)}, u32[]{:S(2)}, u32[]{:S(2)}) collective-permute-start(bf16[3088,128]{1,0:T(8,128)(2,1)S(1)} %fusion.3.refs_0_.rest_0_), channel_id=1, source_target_pairs={{0,4},{4,8},{8,12},{12,0},{16,20},{20,24},{24,28},{28,16},{1,5},{5... | collective-permute-start | bytes 2371592 | tf_op jit(solution)/shard_map/ppermute | solution.py:161
  14.6 3.4 %collective-permute-start.1 = (bf16[3088,128]{1,0:T(8,128)(2,1)S(1)}, bf16[3088,128]{1,0:T(8,128)(2,1)S(1)}, u32[]{:S(2)}, u32[]{:S(2)}) collective-permute-start(bf16[3088,128]{1,0:T(8,128)(2,1)S(1)} %fusion.3.refs_0_.rest_0_), channel_id=1, source_target_pairs={{0,12},{4,0},{8,4},{12,8},{16,28},{20,16},{24,20},{28,24},{1,13},{... | collective-permute-start | bytes 2371592 | tf_op jit(solution)/shard_map/ppermute | solution.py:161
  18.0 13.0 %all_gather.9 = s32[1,4,2,8,2]{3,4,2,0,1:T(2,128)S(1)} all-gather(s32[1,1,2,8,2]{3,4,2,0,1:T(2,128)S(1)} %pad_add_fusion), channel_id=1, replica_groups=mesh['row'=16,'col'=8,'depth'=4] {'depth'}, dimensions={1}, use_global_device_ids=true | all-gather | bytes 640 | tf_op jit(solution)/shard_map/all_gather | solution.py:152
  31.0 1.9 %collective-permute-start.3 = (bf16[3088,128]{1,0:T(8,128)(2,1)S(1)}, bf16[3088,128]{1,0:T(8,128)(2,1)}, u32[]{:S(2)}, u32[]{:S(2)}) collective-permute-start(bf16[3088,128]{1,0:T(8,128)(2,1)S(1)} %fusion.3.refs_0_.rest_0_), channel_id=1, source_target_pairs={{0,16},{4,20},{8,24},{12,28},{16,0},{20,4},{24,8},{28,12},{1,17},{... | collective-permute-start | bytes 2371592 | tf_op jit(solution)/shard_map/ppermute | solution.py:161
  32.9 1.9 %collective-permute-start.4 = (bf16[3088,128]{1,0:T(8,128)(2,1)S(1)}, bf16[3088,128]{1,0:T(8,128)(2,1)}, u32[]{:S(2)}, u32[]{:S(2)}) collective-permute-start(bf16[3088,128]{1,0:T(8,128)(2,1)S(1)} %fusion.3.refs_0_.rest_0_), channel_id=1, source_target_pairs={{0,20},{4,24},{8,28},{12,16},{16,4},{20,8},{24,12},{28,0},{1,21},{... | collective-permute-start | bytes 2371592 | tf_op jit(solution)/shard_map/ppermute | solution.py:161
  34.8 3.7 %collective-permute-start.5 = (bf16[3088,128]{1,0:T(8,128)(2,1)S(1)}, bf16[3088,128]{1,0:T(8,128)(2,1)}, u32[]{:S(2)}, u32[]{:S(2)}) collective-permute-start(bf16[3088,128]{1,0:T(8,128)(2,1)S(1)} %fusion.3.refs_0_.rest_0_), channel_id=1, source_target_pairs={{0,24},{4,28},{8,16},{12,20},{16,8},{20,12},{24,0},{28,4},{1,25},{... | collective-permute-start | bytes 2371592 | tf_op jit(solution)/shard_map/ppermute | solution.py:161
  38.6 4.2 %collective-permute-start.2 = (bf16[3088,128]{1,0:T(8,128)(2,1)S(1)}, bf16[3088,128]{1,0:T(8,128)(2,1)}, u32[]{:S(2)}, u32[]{:S(2)}) collective-permute-start(bf16[3088,128]{1,0:T(8,128)(2,1)S(1)} %fusion.3.refs_0_.rest_0_), channel_id=1, source_target_pairs={{0,8},{4,12},{8,0},{12,4},{16,24},{20,28},{24,16},{28,20},{1,9},{5... | collective-permute-start | bytes 2371592 | tf_op jit(solution)/shard_map/ppermute | solution.py:161
  42.8 5.5 %collective-permute-start.6 = (bf16[3088,128]{1,0:T(8,128)(2,1)S(1)}, bf16[3088,128]{1,0:T(8,128)(2,1)}, u32[]{:S(2)}, u32[]{:S(2)}) collective-permute-start(bf16[3088,128]{1,0:T(8,128)(2,1)S(1)} %fusion.3.refs_0_.rest_0_), channel_id=1, source_target_pairs={{0,28},{4,16},{8,20},{12,24},{16,12},{20,0},{24,4},{28,8},{1,29},{... | collective-permute-start | bytes 2371592 | tf_op jit(solution)/shard_map/ppermute | solution.py:161
  48.4 0.7 select_n.19.aim
  49.8 26.5 %all_gather.10 = s32[16,1,2,8,2]{3,4,2,1,0:T(2,128)S(1)} all-gather(s32[1,1,2,8,2]{3,4,2,1,0:T(2,128)S(1)} %bitcast.27), channel_id=1, replica_groups=mesh['row'=16,'col'=8,'depth'=4] {'row'}, dimensions={0}, use_global_device_ids=true | all-gather | bytes 2176 | tf_op jit(solution)/shard_map/all_gather | solution.py:173
  77.0 8.2 %collective-permute-done.5.refs_6_.rest_6_ = bf16[3088,128]{1,0:T(8,128)(2,1)} collective-permute-done((bf16[3088,128]{1,0:T(8,128)(2,1)S(1)}, bf16[3088,128]{1,0:T(8,128)(2,1)}, u32[]{:S(2)}, u32[]{:S(2)}) %collective-permute-start.5) | collective-permute-done | bytes 790560 | tf_op jit(solution)/shard_map/ppermute | solution.py:161
  85.2 12.4 %collective-permute-done.2.refs_2_.rest_2_ = bf16[3088,128]{1,0:T(8,128)(2,1)} collective-permute-done((bf16[3088,128]{1,0:T(8,128)(2,1)S(1)}, bf16[3088,128]{1,0:T(8,128)(2,1)}, u32[]{:S(2)}, u32[]{:S(2)}) %collective-permute-start.2) | collective-permute-done | bytes 790560 | tf_op jit(solution)/shard_map/ppermute | solution.py:161
  97.6 5.4 %collective-permute-done.6.refs_7_.rest_7_ = bf16[3088,128]{1,0:T(8,128)(2,1)} collective-permute-done((bf16[3088,128]{1,0:T(8,128)(2,1)S(1)}, bf16[3088,128]{1,0:T(8,128)(2,1)}, u32[]{:S(2)}, u32[]{:S(2)}) %collective-permute-start.6) | collective-permute-done | bytes 790560 | tf_op jit(solution)/shard_map/ppermute | solution.py:161
  103.0 1.4 keys.1.ham
  104.5 4.1 %pairs.1 = s32[512]{0:T(512)} custom-call(s32[2]{0:T(128)} %pad_add_fusion.1.where, s32[16,128]{1,0:T(8,128)} %keys.1.ham, s32[16,16]{1,0:T(8,128)} %copy.21.iterate, s32[64]{0:T(128)} %select_n.19.aim), custom_call_target="tpu_custom_call" | custom-call | tf_op jit(solution)/shard_map/pairs/pallas_call | solution.py:190
  108.5 12.5 %all-gather.3.cloned.1.call-done = bf16[16,1,1,8,2,128,128]{6,5,4,3,2,1,0:T(8,128)(2,1)} async-done(((bf16[1,1,1,8,2,128,128]{6,5,4,3,2,1,0:T(8,128)(2,1)}), bf16[16,1,1,8,2,128,128]{6,5,4,3,2,1,0:T(8,128)(2,1)}) %all-gather.3.cloned.1.call-update) | async-done | bytes 8388624 | tf_op jit(solution)/shard_map/all_gather | solution.py:149
  121.1 2.9 %products.1 = (bf16[16,128,128]{2,1,0:T(8,128)(2,1)S(1)}, bf16[16,128,128]{2,1,0:T(8,128)(2,1)S(1)}, bf16[2,16,128,128]{3,2,1,0:T(8,128)(2,1)S(1)}) custom-call(s32[512]{0:T(512)} %pairs.1, bf16[256,128,128]{2,1,0:T(8,128)(2,1)} %bitcast.24, bf16[3088,128]{1,0:T(8,128)(2,1)} %copy-done, bf16[3088,128]{1,0:T(8,128)(2,1)} %copy-done.1, ...), custom_call_target="tpu_custom_call" | custom-call | tf_op jit(solution)/shard_map/products/pallas_call | solution.py:199
  124.0 2.9 %collective-permute-start.7 = (bf16[16,128,128]{2,1,0:T(8,128)(2,1)S(1)}, bf16[16,128,128]{2,1,0:T(8,128)(2,1)S(1)}, u32[]{:S(2)}, u32[]{:S(2)}) collective-permute-start(bf16[16,128,128]{2,1,0:T(8,128)(2,1)S(1)} %get-tuple-element.25), channel_id=1, source_target_pairs={{0,1},{1,0},{2,3},{3,2},{4,5},{5,4},{6,7},{7,6},{8,9},{9,8},{10,11... | collective-permute-start | bytes 1572872 | tf_op jit(solution)/shard_map/ppermute | solution.py:215
  126.9 1.9 %collective-permute-start.8 = (bf16[16,128,128]{2,1,0:T(8,128)(2,1)S(1)}, bf16[16,128,128]{2,1,0:T(8,128)(2,1)S(1)}, u32[]{:S(2)}, u32[]{:S(2)}) collective-permute-start(bf16[16,128,128]{2,1,0:T(8,128)(2,1)S(1)} %get-tuple-element.27), channel_id=1, source_target_pairs={{0,1},{1,0},{2,3},{3,2},{4,5},{5,4},{6,7},{7,6},{8,9},{9,8},{10,11... | collective-permute-start | bytes 1572872 | tf_op jit(solution)/shard_map/ppermute | solution.py:216
  129.0 4.5 %collective-permute-start.9 = (bf16[16,128,128]{2,1,0:T(8,128)(2,1)S(1)}, bf16[16,128,128]{2,1,0:T(8,128)(2,1)}, u32[]{:S(2)}, u32[]{:S(2)}) collective-permute-start(bf16[16,128,128]{2,1,0:T(8,128)(2,1)S(1)} %fusion.2), channel_id=1, source_target_pairs={{0,2},{1,3},{2,0},{3,1},{4,6},{5,7},{6,4},{7,5},{8,10},{9,11},{10,... | collective-permute-start | bytes 1572872 | tf_op jit(solution)/shard_map/ppermute | solution.py:219
  133.9 11.6 %collective-permute-done.9 = bf16[16,128,128]{2,1,0:T(8,128)(2,1)} collective-permute-done((bf16[16,128,128]{2,1,0:T(8,128)(2,1)S(1)}, bf16[16,128,128]{2,1,0:T(8,128)(2,1)}, u32[]{:S(2)}, u32[]{:S(2)}) %collective-permute-start.9) | collective-permute-done | bytes 524320 | tf_op jit(solution)/shard_map/ppermute | solution.py:219
  145.5 2.0 %multiply_convert_fusion = bf16[16,128,128]{2,1,0:T(8,128)(2,1)} fusion(f32[16,128,128]{2,1,0:T(8,128)S(1)} %convert_subtract_fusion, bf16[16,128,128]{2,1,0:T(8,128)(2,1)} %collective-permute-done.9, f32[16]{0:T(128)S(1)} %convert_element_type.62), kind=kLoop, calls=%fused_computation.7 | loop fusion | flops 1310720 | bytes 2097216 | tf_op jit(solution)/shard_map/convert_element_type | solution.py:225
  (36 shorter events, 4.2 us)
Async XLA Ops:
  6.5 11.4 %copy-start.5 = (s32[1,1,1,8,2]{3,4,2,1,0:T(2,128)S(1)}, s32[1,1,1,8,2]{3,4,2,1,0:T(2,128)}, u32[]{:S(2)}) copy-start(s32[1,1,1,8,2]{3,4,2,1,0:T(2,128)} %param.13) | copy-start | bytes 196
  6.5 11.4 %copy-start.4 = (s32[1,1,1,8,2]{3,4,2,1,0:T(2,128)S(1)}, s32[1,1,1,8,2]{3,4,2,1,0:T(2,128)}, u32[]{:S(2)}) copy-start(s32[1,1,1,8,2]{3,4,2,1,0:T(2,128)} %param.14) | copy-start | bytes 196
  6.5 114.5 %all-gather.3.cloned.1.call-start = ((), (), s32[]{:S(2)}) async-start(), calls=%async_computation | async-start | bytes 8912896 | tf_op jit(solution)/shard_map/all_gather | solution.py:149
  10.5 92.5 %copy-start = (bf16[3088,128]{1,0:T(8,128)(2,1)}, bf16[3088,128]{1,0:T(8,128)(2,1)S(1)}, u32[]{:S(2)}) copy-start(bf16[3088,128]{1,0:T(8,128)(2,1)S(1)} %fusion.3.refs_0_.rest_0_) | copy-start | bytes 2371588
  10.5 28.0 %collective-permute-start = (bf16[3088,128]{1,0:T(8,128)(2,1)S(1)}, bf16[3088,128]{1,0:T(8,128)(2,1)S(1)}, u32[]{:S(2)}, u32[]{:S(2)}) collective-permute-start(bf16[3088,128]{1,0:T(8,128)(2,1)S(1)} %fusion.3.refs_0_.rest_0_), channel_id=1, source_target_pairs={{0,4},{4,8},{8,12},{12,0},{16,20},{20,24},{24,28},{28,16},{1,5},{5... | collective-permute-start | bytes 2371592 | tf_op jit(solution)/shard_map/ppermute | solution.py:161
  14.6 24.0 %collective-permute-start.1 = (bf16[3088,128]{1,0:T(8,128)(2,1)S(1)}, bf16[3088,128]{1,0:T(8,128)(2,1)S(1)}, u32[]{:S(2)}, u32[]{:S(2)}) collective-permute-start(bf16[3088,128]{1,0:T(8,128)(2,1)S(1)} %fusion.3.refs_0_.rest_0_), channel_id=1, source_target_pairs={{0,12},{4,0},{8,4},{12,8},{16,28},{20,16},{24,20},{28,24},{1,13},{... | collective-permute-start | bytes 2371592 | tf_op jit(solution)/shard_map/ppermute | solution.py:161
  31.0 46.0 %collective-permute-start.3 = (bf16[3088,128]{1,0:T(8,128)(2,1)S(1)}, bf16[3088,128]{1,0:T(8,128)(2,1)}, u32[]{:S(2)}, u32[]{:S(2)}) collective-permute-start(bf16[3088,128]{1,0:T(8,128)(2,1)S(1)} %fusion.3.refs_0_.rest_0_), channel_id=1, source_target_pairs={{0,16},{4,20},{8,24},{12,28},{16,0},{20,4},{24,8},{28,12},{1,17},{... | collective-permute-start | bytes 2371592 | tf_op jit(solution)/shard_map/ppermute | solution.py:161
  32.9 44.1 %collective-permute-start.4 = (bf16[3088,128]{1,0:T(8,128)(2,1)S(1)}, bf16[3088,128]{1,0:T(8,128)(2,1)}, u32[]{:S(2)}, u32[]{:S(2)}) collective-permute-start(bf16[3088,128]{1,0:T(8,128)(2,1)S(1)} %fusion.3.refs_0_.rest_0_), channel_id=1, source_target_pairs={{0,20},{4,24},{8,28},{12,16},{16,4},{20,8},{24,12},{28,0},{1,21},{... | collective-permute-start | bytes 2371592 | tf_op jit(solution)/shard_map/ppermute | solution.py:161
  34.8 50.4 %collective-permute-start.5 = (bf16[3088,128]{1,0:T(8,128)(2,1)S(1)}, bf16[3088,128]{1,0:T(8,128)(2,1)}, u32[]{:S(2)}, u32[]{:S(2)}) collective-permute-start(bf16[3088,128]{1,0:T(8,128)(2,1)S(1)} %fusion.3.refs_0_.rest_0_), channel_id=1, source_target_pairs={{0,24},{4,28},{8,16},{12,20},{16,8},{20,12},{24,0},{28,4},{1,25},{... | collective-permute-start | bytes 2371592 | tf_op jit(solution)/shard_map/ppermute | solution.py:161
  38.6 64.5 %copy-start.1 = (bf16[3088,128]{1,0:T(8,128)(2,1)}, bf16[3088,128]{1,0:T(8,128)(2,1)S(1)}, u32[]{:S(2)}) copy-start(bf16[3088,128]{1,0:T(8,128)(2,1)S(1)} %collective-permute-done.refs_1_.rest_1_) | copy-start | bytes 2371588
  38.6 64.4 %copy-start.2 = (bf16[3088,128]{1,0:T(8,128)(2,1)}, bf16[3088,128]{1,0:T(8,128)(2,1)S(1)}, u32[]{:S(2)}) copy-start(bf16[3088,128]{1,0:T(8,128)(2,1)S(1)} %collective-permute-done.1.refs_3_.rest_3_) | copy-start | bytes 2371588
  38.6 59.0 %collective-permute-start.2 = (bf16[3088,128]{1,0:T(8,128)(2,1)S(1)}, bf16[3088,128]{1,0:T(8,128)(2,1)}, u32[]{:S(2)}, u32[]{:S(2)}) collective-permute-start(bf16[3088,128]{1,0:T(8,128)(2,1)S(1)} %fusion.3.refs_0_.rest_0_), channel_id=1, source_target_pairs={{0,8},{4,12},{8,0},{12,4},{16,24},{20,28},{24,16},{28,20},{1,9},{5... | collective-permute-start | bytes 2371592 | tf_op jit(solution)/shard_map/ppermute | solution.py:161
  42.8 60.2 %collective-permute-start.6 = (bf16[3088,128]{1,0:T(8,128)(2,1)S(1)}, bf16[3088,128]{1,0:T(8,128)(2,1)}, u32[]{:S(2)}, u32[]{:S(2)}) collective-permute-start(bf16[3088,128]{1,0:T(8,128)(2,1)S(1)} %fusion.3.refs_0_.rest_0_), channel_id=1, source_target_pairs={{0,28},{4,16},{8,20},{12,24},{16,12},{20,0},{24,4},{28,8},{1,29},{... | collective-permute-start | bytes 2371592 | tf_op jit(solution)/shard_map/ppermute | solution.py:161
  124.0 9.7 %copy-start.3 = (bf16[1,1,1,8,2,128,128]{6,5,4,3,2,1,0:T(8,128)(2,1)S(1)}, bf16[1,1,1,8,2,128,128]{6,5,4,3,2,1,0:T(8,128)(2,1)}, u32[]{:S(2)}) copy-start(bf16[1,1,1,8,2,128,128]{6,5,4,3,2,1,0:T(8,128)(2,1)} %param.15) | copy-start | bytes 1572868
  124.0 4.8 %collective-permute-start.7 = (bf16[16,128,128]{2,1,0:T(8,128)(2,1)S(1)}, bf16[16,128,128]{2,1,0:T(8,128)(2,1)S(1)}, u32[]{:S(2)}, u32[]{:S(2)}) collective-permute-start(bf16[16,128,128]{2,1,0:T(8,128)(2,1)S(1)} %get-tuple-element.25), channel_id=1, source_target_pairs={{0,1},{1,0},{2,3},{3,2},{4,5},{5,4},{6,7},{7,6},{8,9},{9,8},{10,11... | collective-permute-start | bytes 1572872 | tf_op jit(solution)/shard_map/ppermute | solution.py:215
  126.9 6.7 %collective-permute-start.8 = (bf16[16,128,128]{2,1,0:T(8,128)(2,1)S(1)}, bf16[16,128,128]{2,1,0:T(8,128)(2,1)S(1)}, u32[]{:S(2)}, u32[]{:S(2)}) collective-permute-start(bf16[16,128,128]{2,1,0:T(8,128)(2,1)S(1)} %get-tuple-element.27), channel_id=1, source_target_pairs={{0,1},{1,0},{2,3},{3,2},{4,5},{5,4},{6,7},{7,6},{8,9},{9,8},{10,11... | collective-permute-start | bytes 1572872 | tf_op jit(solution)/shard_map/ppermute | solution.py:216
  129.0 16.5 %collective-permute-start.9 = (bf16[16,128,128]{2,1,0:T(8,128)(2,1)S(1)}, bf16[16,128,128]{2,1,0:T(8,128)(2,1)}, u32[]{:S(2)}, u32[]{:S(2)}) collective-permute-start(bf16[16,128,128]{2,1,0:T(8,128)(2,1)S(1)} %fusion.2), channel_id=1, source_target_pairs={{0,2},{1,3},{2,0},{3,1},{4,6},{5,7},{6,4},{7,5},{8,10},{9,11},{10,... | collective-permute-start | bytes 1572872 | tf_op jit(solution)/shard_map/ppermute | solution.py:219
Sparse Core Ops, SparseCore 0:
  9.4 111.5 all-gather.2

commit v13 on v8

--- a/solution.py
+++ b/solution.py
@@ -209,11 +209,11 @@
     )(*[pltpu.with_memory_space_constraint(x, pltpu.HBM) for x in (pairs, iterate)], *hams)
     near = lax.ppermute(sent, "depth", [(d, d ^ 1) for d in range(n_depth)])
     onward = (kept[0].astype(jnp.float32) + near[0].astype(jnp.float32)).astype(jnp.bfloat16)
-    far = lax.ppermute(onward, "depth", [(d, d ^ 2) for d in range(n_depth)])
     prior = previous.reshape(results, block, block).astype(jnp.float32)
     live = x_flags.reshape(results, 1, 1).astype(jnp.float32)
     base = 2.0 * (kept[1].astype(jnp.float32) + near[1].astype(jnp.float32)) - prior
-    base = lax.optimization_barrier(base)
+    onward, base = lax.optimization_barrier((onward, base))
+    far = lax.ppermute(onward, "depth", [(d, d ^ 2) for d in range(n_depth)])
     result = (base + 2.0 * far.astype(jnp.float32)) * live
     return result.astype(jnp.bfloat16).reshape(previous.shape)
 

time: 156 us -> 155 us (level)
  no operation moved by 1% of the time
where the time goes in v13:
time: 155 us; the launch traced here: 154 us
  waiting for transfers between devices  53.4 us (34%)
  blocking collectives  39.5 us (25%)
  starting transfers between devices  32 us (21%)
  between operations  13.6 us (9%)
  Pallas kernels  8.26 us (5%)
  other arithmetic  5.26 us (3%)
  local copies, waits for them, and re-layouts  1.76 us (1%)
    all_gather x1, blocking collectives, body(): it_ints = lax.all_gather(it_ints, 'row', axis=0, tiled=True)  26.5 us
    ppermute x7, waiting for transfers between devices, send(): return lax.ppermute(source, 'col', route)  26 us
    ppermute x7, starting transfers between devices, send(): return lax.ppermute(source, 'col', route)  24.7 us
    all_gather x1, blocking collectives, body(): aim_ints = lax.all_gather(it_ints, 'depth', axis=1, tiled=True)  13 us
    all_gather x1, waiting for transfers between devices, body(): iterate = lax.all_gather(x_blocks[0, 0, 0], 'row', axis=0)  12.6 us
    ppermute x1, waiting for transfers between devices, body(): far = lax.ppermute(onward, 'depth', [(d, d ^ 2) for d in range(n_depth)])  11.9 us
    ppermute x1, starting transfers between devices, body(): far = lax.ppermute(onward, 'depth', [(d, d ^ 2) for d in range(n_depth)])  4.48 us
    pallas_call x1, Pallas kernels, body(): pl.pallas_call(pair_kernel, out_shape=jax.ShapeDtypeStruct((512,), jnp.in...  4.04 us
  transfers between devices with their start and end apart: 10, of which 6 were waited for; matrix products, arithmetic and copies ran while one was open for 4% of the time, Pallas kernels for 4%

profile of v13, /device:TPU:1, one launch (start us, length us, event | category | flops | bytes accessed | tf_op | source)
XLA Modules:
  0.0 153.8 jit_solution(9096736747930979827)
XLA Ops:
  6.5 0.7 all-gather.3.cloned.1.call-update
  9.3 1.2 fusion.1.refs_0_.rest_0_
  10.5 4.0 %collective-permute-start = (bf16[3088,128]{1,0:T(8,128)(2,1)S(1)}, bf16[3088,128]{1,0:T(8,128)(2,1)S(1)}, u32[]{:S(2)}, u32[]{:S(2)}) collective-permute-start(bf16[3088,128]{1,0:T(8,128)(2,1)S(1)} %fusion.1.refs_0_.rest_0_), channel_id=1, source_target_pairs={{0,4},{4,8},{8,12},{12,0},{16,20},{20,24},{24,28},{28,16},{1,5},{5... | collective-permute-start | bytes 2371592 | tf_op jit(solution)/shard_map/ppermute | solution.py:158
  14.6 3.4 %collective-permute-start.1 = (bf16[3088,128]{1,0:T(8,128)(2,1)S(1)}, bf16[3088,128]{1,0:T(8,128)(2,1)S(1)}, u32[]{:S(2)}, u32[]{:S(2)}) collective-permute-start(bf16[3088,128]{1,0:T(8,128)(2,1)S(1)} %fusion.1.refs_0_.rest_0_), channel_id=1, source_target_pairs={{0,12},{4,0},{8,4},{12,8},{16,28},{20,16},{24,20},{28,24},{1,13},{... | collective-permute-start | bytes 2371592 | tf_op jit(solution)/shard_map/ppermute | solution.py:158
  18.0 13.0 %all_gather.9 = s32[1,4,2,8,2]{3,4,2,0,1:T(2,128)S(1)} all-gather(s32[1,1,2,8,2]{3,4,2,0,1:T(2,128)S(1)} %pad_add_fusion), channel_id=1, replica_groups=mesh['row'=16,'col'=8,'depth'=4] {'depth'}, dimensions={1}, use_global_device_ids=true | all-gather | bytes 640 | tf_op jit(solution)/shard_map/all_gather | solution.py:149
  31.0 1.9 %collective-permute-start.3 = (bf16[3088,128]{1,0:T(8,128)(2,1)S(1)}, bf16[3088,128]{1,0:T(8,128)(2,1)S(1)}, u32[]{:S(2)}, u32[]{:S(2)}) collective-permute-start(bf16[3088,128]{1,0:T(8,128)(2,1)S(1)} %fusion.1.refs_0_.rest_0_), channel_id=1, source_target_pairs={{0,16},{4,20},{8,24},{12,28},{16,0},{20,4},{24,8},{28,12},{1,17},{... | collective-permute-start | bytes 2371592 | tf_op jit(solution)/shard_map/ppermute | solution.py:158
  32.9 1.9 %collective-permute-start.4 = (bf16[3088,128]{1,0:T(8,128)(2,1)S(1)}, bf16[3088,128]{1,0:T(8,128)(2,1)}, u32[]{:S(2)}, u32[]{:S(2)}) collective-permute-start(bf16[3088,128]{1,0:T(8,128)(2,1)S(1)} %fusion.1.refs_0_.rest_0_), channel_id=1, source_target_pairs={{0,20},{4,24},{8,28},{12,16},{16,4},{20,8},{24,12},{28,0},{1,21},{... | collective-permute-start | bytes 2371592 | tf_op jit(solution)/shard_map/ppermute | solution.py:158
  34.8 3.7 %collective-permute-start.5 = (bf16[3088,128]{1,0:T(8,128)(2,1)S(1)}, bf16[3088,128]{1,0:T(8,128)(2,1)}, u32[]{:S(2)}, u32[]{:S(2)}) collective-permute-start(bf16[3088,128]{1,0:T(8,128)(2,1)S(1)} %fusion.1.refs_0_.rest_0_), channel_id=1, source_target_pairs={{0,24},{4,28},{8,16},{12,20},{16,8},{20,12},{24,0},{28,4},{1,25},{... | collective-permute-start | bytes 2371592 | tf_op jit(solution)/shard_map/ppermute | solution.py:158
  38.6 4.2 %collective-permute-start.2 = (bf16[3088,128]{1,0:T(8,128)(2,1)S(1)}, bf16[3088,128]{1,0:T(8,128)(2,1)}, u32[]{:S(2)}, u32[]{:S(2)}) collective-permute-start(bf16[3088,128]{1,0:T(8,128)(2,1)S(1)} %fusion.1.refs_0_.rest_0_), channel_id=1, source_target_pairs={{0,8},{4,12},{8,0},{12,4},{16,24},{20,28},{24,16},{28,20},{1,9},{5... | collective-permute-start | bytes 2371592 | tf_op jit(solution)/shard_map/ppermute | solution.py:158
  42.8 5.5 %collective-permute-start.6 = (bf16[3088,128]{1,0:T(8,128)(2,1)S(1)}, bf16[3088,128]{1,0:T(8,128)(2,1)}, u32[]{:S(2)}, u32[]{:S(2)}) collective-permute-start(bf16[3088,128]{1,0:T(8,128)(2,1)S(1)} %fusion.1.refs_0_.rest_0_), channel_id=1, source_target_pairs={{0,28},{4,16},{8,20},{12,24},{16,12},{20,0},{24,4},{28,8},{1,29},{... | collective-permute-start | bytes 2371592 | tf_op jit(solution)/shard_map/ppermute | solution.py:158
  48.4 0.7 select_n.19.aim
  49.8 26.5 %all_gather.10 = s32[16,1,2,8,2]{3,4,2,1,0:T(2,128)S(1)} all-gather(s32[1,1,2,8,2]{3,4,2,1,0:T(2,128)S(1)} %bitcast.25), channel_id=1, replica_groups=mesh['row'=16,'col'=8,'depth'=4] {'row'}, dimensions={0}, use_global_device_ids=true | all-gather | bytes 2176 | tf_op jit(solution)/shard_map/all_gather | solution.py:170
  77.0 8.2 %collective-permute-done.5.refs_6_.rest_6_ = bf16[3088,128]{1,0:T(8,128)(2,1)} collective-permute-done((bf16[3088,128]{1,0:T(8,128)(2,1)S(1)}, bf16[3088,128]{1,0:T(8,128)(2,1)}, u32[]{:S(2)}, u32[]{:S(2)}) %collective-permute-start.5) | collective-permute-done | bytes 790560 | tf_op jit(solution)/shard_map/ppermute | solution.py:158
  85.2 12.4 %collective-permute-done.2.refs_2_.rest_2_ = bf16[3088,128]{1,0:T(8,128)(2,1)} collective-permute-done((bf16[3088,128]{1,0:T(8,128)(2,1)S(1)}, bf16[3088,128]{1,0:T(8,128)(2,1)}, u32[]{:S(2)}, u32[]{:S(2)}) %collective-permute-start.2) | collective-permute-done | bytes 790560 | tf_op jit(solution)/shard_map/ppermute | solution.py:158
  97.6 5.4 %collective-permute-done.6.refs_7_.rest_7_ = bf16[3088,128]{1,0:T(8,128)(2,1)} collective-permute-done((bf16[3088,128]{1,0:T(8,128)(2,1)S(1)}, bf16[3088,128]{1,0:T(8,128)(2,1)}, u32[]{:S(2)}, u32[]{:S(2)}) %collective-permute-start.6) | collective-permute-done | bytes 790560 | tf_op jit(solution)/shard_map/ppermute | solution.py:158
  103.0 1.4 keys.1.ham
  104.5 4.0 %pairs.1 = s32[512]{0:T(512)} custom-call(s32[2]{0:T(128)} %pad_add_fusion.1.where, s32[16,128]{1,0:T(8,128)} %keys.1.ham, s32[16,16]{1,0:T(8,128)} %copy.21.iterate, s32[64]{0:T(128)} %select_n.19.aim), custom_call_target="tpu_custom_call" | custom-call | tf_op jit(solution)/shard_map/pairs/pallas_call | solution.py:187
  108.5 12.6 %all-gather.3.cloned.1.call-done = bf16[16,1,1,8,2,128,128]{6,5,4,3,2,1,0:T(8,128)(2,1)} async-done(((bf16[1,1,1,8,2,128,128]{6,5,4,3,2,1,0:T(8,128)(2,1)}), bf16[16,1,1,8,2,128,128]{6,5,4,3,2,1,0:T(8,128)(2,1)}) %all-gather.3.cloned.1.call-update) | async-done | bytes 8388624 | tf_op jit(solution)/shard_map/all_gather | solution.py:146
  121.1 2.8 %products.1 = (bf16[2,16,128,128]{3,2,1,0:T(8,128)(2,1)S(1)}, bf16[2,16,128,128]{3,2,1,0:T(8,128)(2,1)S(1)}) custom-call(s32[512]{0:T(512)} %pairs.1, bf16[256,128,128]{2,1,0:T(8,128)(2,1)} %bitcast.22, bf16[3088,128]{1,0:T(8,128)(2,1)} %copy-done, bf16[3088,128]{1,0:T(8,128)(2,1)} %copy-done.1, bf16[3088,128]{1,0:T(8,128)(2,1)} %collective-permute-done.2.refs_2_.rest_2_, ...), custom_call_target="tpu_custom_call" | custom-call | tf_op jit(solution)/shard_map/products/pallas_call | solution.py:195
  123.9 2.9 %collective-permute-start.7 = (bf16[2,16,128,128]{3,2,1,0:T(8,128)(2,1)S(1)}, bf16[2,16,128,128]{3,2,1,0:T(8,128)(2,1)S(1)}, u32[]{:S(2)}, u32[]{:S(2)}) collective-permute-start(bf16[2,16,128,128]{3,2,1,0:T(8,128)(2,1)S(1)} %get-tuple-element.24), channel_id=1, source_target_pairs={{0,1},{1,0},{2,3},{3,2},{4,5},{5,4},{6,7},{7,6},{8,9},{9,8},{10,11... | collective-permute-start | bytes 3145736 | tf_op jit(solution)/shard_map/ppermute | solution.py:210
  126.8 2.3 %collective-permute-done.7 = bf16[2,16,128,128]{3,2,1,0:T(8,128)(2,1)S(1)} collective-permute-done((bf16[2,16,128,128]{3,2,1,0:T(8,128)(2,1)S(1)}, bf16[2,16,128,128]{3,2,1,0:T(8,128)(2,1)S(1)}, u32[]{:S(2)}, u32[]{:S(2)}) %collective-permute-start.7) | collective-permute-done | bytes 1048608 | tf_op jit(solution)/shard_map/ppermute | solution.py:210
  129.5 4.5 %collective-permute-start.8 = (bf16[16,128,128]{2,1,0:T(8,128)(2,1)S(1)}, bf16[16,128,128]{2,1,0:T(8,128)(2,1)S(1)}, u32[]{:S(2)}, u32[]{:S(2)}) collective-permute-start(bf16[16,128,128]{2,1,0:T(8,128)(2,1)S(1)} %fusion.2), channel_id=1, source_target_pairs={{0,2},{1,3},{2,0},{3,1},{4,6},{5,7},{6,4},{7,5},{8,10},{9,11},{10,... | collective-permute-start | bytes 1572872 | tf_op jit(solution)/shard_map/ppermute | solution.py:216
  134.1 11.9 %collective-permute-done.8 = bf16[16,128,128]{2,1,0:T(8,128)(2,1)S(1)} collective-permute-done((bf16[16,128,128]{2,1,0:T(8,128)(2,1)S(1)}, bf16[16,128,128]{2,1,0:T(8,128)(2,1)S(1)}, u32[]{:S(2)}, u32[]{:S(2)}) %collective-permute-start.8) | collective-permute-done | bytes 524320 | tf_op jit(solution)/shard_map/ppermute | solution.py:216
  146.0 1.0 multiply_convert_fusion
  (36 shorter events, 4.2 us)
Async XLA Ops:
  6.5 11.4 %copy-start.6 = (s32[1,1,1,8,2]{3,4,2,1,0:T(2,128)S(1)}, s32[1,1,1,8,2]{3,4,2,1,0:T(2,128)}, u32[]{:S(2)}) copy-start(s32[1,1,1,8,2]{3,4,2,1,0:T(2,128)} %param.13) | copy-start | bytes 196
  6.5 11.4 %copy-start.5 = (s32[1,1,1,8,2]{3,4,2,1,0:T(2,128)S(1)}, s32[1,1,1,8,2]{3,4,2,1,0:T(2,128)}, u32[]{:S(2)}) copy-start(s32[1,1,1,8,2]{3,4,2,1,0:T(2,128)} %param.14) | copy-start | bytes 196
  6.5 114.5 %all-gather.3.cloned.1.call-start = ((), (), s32[]{:S(2)}) async-start(), calls=%async_computation | async-start | bytes 8912896 | tf_op jit(solution)/shard_map/all_gather | solution.py:146
  10.5 92.5 %copy-start = (bf16[3088,128]{1,0:T(8,128)(2,1)}, bf16[3088,128]{1,0:T(8,128)(2,1)S(1)}, u32[]{:S(2)}) copy-start(bf16[3088,128]{1,0:T(8,128)(2,1)S(1)} %fusion.1.refs_0_.rest_0_) | copy-start | bytes 2371588
  10.5 28.0 %collective-permute-start = (bf16[3088,128]{1,0:T(8,128)(2,1)S(1)}, bf16[3088,128]{1,0:T(8,128)(2,1)S(1)}, u32[]{:S(2)}, u32[]{:S(2)}) collective-permute-start(bf16[3088,128]{1,0:T(8,128)(2,1)S(1)} %fusion.1.refs_0_.rest_0_), channel_id=1, source_target_pairs={{0,4},{4,8},{8,12},{12,0},{16,20},{20,24},{24,28},{28,16},{1,5},{5... | collective-permute-start | bytes 2371592 | tf_op jit(solution)/shard_map/ppermute | solution.py:158
  14.6 24.0 %collective-permute-start.1 = (bf16[3088,128]{1,0:T(8,128)(2,1)S(1)}, bf16[3088,128]{1,0:T(8,128)(2,1)S(1)}, u32[]{:S(2)}, u32[]{:S(2)}) collective-permute-start(bf16[3088,128]{1,0:T(8,128)(2,1)S(1)} %fusion.1.refs_0_.rest_0_), channel_id=1, source_target_pairs={{0,12},{4,0},{8,4},{12,8},{16,28},{20,16},{24,20},{28,24},{1,13},{... | collective-permute-start | bytes 2371592 | tf_op jit(solution)/shard_map/ppermute | solution.py:158
  31.0 46.0 %collective-permute-start.3 = (bf16[3088,128]{1,0:T(8,128)(2,1)S(1)}, bf16[3088,128]{1,0:T(8,128)(2,1)S(1)}, u32[]{:S(2)}, u32[]{:S(2)}) collective-permute-start(bf16[3088,128]{1,0:T(8,128)(2,1)S(1)} %fusion.1.refs_0_.rest_0_), channel_id=1, source_target_pairs={{0,16},{4,20},{8,24},{12,28},{16,0},{20,4},{24,8},{28,12},{1,17},{... | collective-permute-start | bytes 2371592 | tf_op jit(solution)/shard_map/ppermute | solution.py:158
  32.9 44.1 %collective-permute-start.4 = (bf16[3088,128]{1,0:T(8,128)(2,1)S(1)}, bf16[3088,128]{1,0:T(8,128)(2,1)}, u32[]{:S(2)}, u32[]{:S(2)}) collective-permute-start(bf16[3088,128]{1,0:T(8,128)(2,1)S(1)} %fusion.1.refs_0_.rest_0_), channel_id=1, source_target_pairs={{0,20},{4,24},{8,28},{12,16},{16,4},{20,8},{24,12},{28,0},{1,21},{... | collective-permute-start | bytes 2371592 | tf_op jit(solution)/shard_map/ppermute | solution.py:158
  34.8 50.4 %collective-permute-start.5 = (bf16[3088,128]{1,0:T(8,128)(2,1)S(1)}, bf16[3088,128]{1,0:T(8,128)(2,1)}, u32[]{:S(2)}, u32[]{:S(2)}) collective-permute-start(bf16[3088,128]{1,0:T(8,128)(2,1)S(1)} %fusion.1.refs_0_.rest_0_), channel_id=1, source_target_pairs={{0,24},{4,28},{8,16},{12,20},{16,8},{20,12},{24,0},{28,4},{1,25},{... | collective-permute-start | bytes 2371592 | tf_op jit(solution)/shard_map/ppermute | solution.py:158
  38.6 64.5 %copy-start.1 = (bf16[3088,128]{1,0:T(8,128)(2,1)}, bf16[3088,128]{1,0:T(8,128)(2,1)S(1)}, u32[]{:S(2)}) copy-start(bf16[3088,128]{1,0:T(8,128)(2,1)S(1)} %collective-permute-done.refs_1_.rest_1_) | copy-start | bytes 2371588
  38.6 64.4 %copy-start.2 = (bf16[3088,128]{1,0:T(8,128)(2,1)}, bf16[3088,128]{1,0:T(8,128)(2,1)S(1)}, u32[]{:S(2)}) copy-start(bf16[3088,128]{1,0:T(8,128)(2,1)S(1)} %collective-permute-done.1.refs_3_.rest_3_) | copy-start | bytes 2371588
  38.6 59.0 %collective-permute-start.2 = (bf16[3088,128]{1,0:T(8,128)(2,1)S(1)}, bf16[3088,128]{1,0:T(8,128)(2,1)}, u32[]{:S(2)}, u32[]{:S(2)}) collective-permute-start(bf16[3088,128]{1,0:T(8,128)(2,1)S(1)} %fusion.1.refs_0_.rest_0_), channel_id=1, source_target_pairs={{0,8},{4,12},{8,0},{12,4},{16,24},{20,28},{24,16},{28,20},{1,9},{5... | collective-permute-start | bytes 2371592 | tf_op jit(solution)/shard_map/ppermute | solution.py:158
  42.8 60.2 %collective-permute-start.6 = (bf16[3088,128]{1,0:T(8,128)(2,1)S(1)}, bf16[3088,128]{1,0:T(8,128)(2,1)}, u32[]{:S(2)}, u32[]{:S(2)}) collective-permute-start(bf16[3088,128]{1,0:T(8,128)(2,1)S(1)} %fusion.1.refs_0_.rest_0_), channel_id=1, source_target_pairs={{0,28},{4,16},{8,20},{12,24},{16,12},{20,0},{24,4},{28,8},{1,29},{... | collective-permute-start | bytes 2371592 | tf_op jit(solution)/shard_map/ppermute | solution.py:158
  77.0 26.0 %copy-start.3 = (bf16[3088,128]{1,0:T(8,128)(2,1)}, bf16[3088,128]{1,0:T(8,128)(2,1)S(1)}, u32[]{:S(2)}) copy-start(bf16[3088,128]{1,0:T(8,128)(2,1)S(1)} %collective-permute-done.3.refs_4_.rest_4_) | copy-start | bytes 2371588
  123.9 5.3 %copy-start.4 = (bf16[1,1,1,8,2,128,128]{6,5,4,3,2,1,0:T(8,128)(2,1)S(1)}, bf16[1,1,1,8,2,128,128]{6,5,4,3,2,1,0:T(8,128)(2,1)}, u32[]{:S(2)}) copy-start(bf16[1,1,1,8,2,128,128]{6,5,4,3,2,1,0:T(8,128)(2,1)} %param.15) | copy-start | bytes 1572868
  123.9 5.1 %collective-permute-start.7 = (bf16[2,16,128,128]{3,2,1,0:T(8,128)(2,1)S(1)}, bf16[2,16,128,128]{3,2,1,0:T(8,128)(2,1)S(1)}, u32[]{:S(2)}, u32[]{:S(2)}) collective-permute-start(bf16[2,16,128,128]{3,2,1,0:T(8,128)(2,1)S(1)} %get-tuple-element.24), channel_id=1, source_target_pairs={{0,1},{1,0},{2,3},{3,2},{4,5},{5,4},{6,7},{7,6},{8,9},{9,8},{10,11... | collective-permute-start | bytes 3145736 | tf_op jit(solution)/shard_map/ppermute | solution.py:210
  129.5 16.5 %collective-permute-start.8 = (bf16[16,128,128]{2,1,0:T(8,128)(2,1)S(1)}, bf16[16,128,128]{2,1,0:T(8,128)(2,1)S(1)}, u32[]{:S(2)}, u32[]{:S(2)}) collective-permute-start(bf16[16,128,128]{2,1,0:T(8,128)(2,1)S(1)} %fusion.2), channel_id=1, source_target_pairs={{0,2},{1,3},{2,0},{3,1},{4,6},{5,7},{6,4},{7,5},{8,10},{9,11},{10,... | collective-permute-start | bytes 1572872 | tf_op jit(solution)/shard_map/ppermute | solution.py:216
Sparse Core Ops, SparseCore 0:
  9.4 111.5 all-gather.2
